TPU v7x, 32 devices: a whole 2x2x4 slice. The times are simulated.
32 devices in a mesh: ctx: 16 (over z, x, core), fsdp: 2 (over y).
Axes of the slice: x: 2, y: 2, z: 4, core: 2. Of those that a mesh axis runs over, the one named last changes fastest.
Arguments:
- tokens: bfloat16 [2, 2048, 1536], P('fsdp', 'ctx'), may hold values from -6 to 6
- cotangent: bfloat16 [2, 2048, 1536], P('fsdp', 'ctx'), may hold values from -6 to 6
- norm_gain1: bfloat16 [1536], P(('ctx', 'fsdp')), may hold values from 0.5 to 1.5
- w_query: bfloat16 [1536, 1536], P(('ctx', 'fsdp')), may hold values from -0.15625 to 0.15625
- key_weight: bfloat16 [1536, 768], P(('ctx', 'fsdp')), may hold values from -0.15625 to 0.15625
- value_weight: bfloat16 [1536, 768], P(('ctx', 'fsdp')), may hold values from -0.15625 to 0.15625
- w_out: bfloat16 [1536, 1536], P(('ctx', 'fsdp')), may hold values from -1.5 to 1.5
- norm_gain2: bfloat16 [1536], P(('ctx', 'fsdp')), may hold values from 0.5 to 1.5
- w_gate: bfloat16 [1536, 4096], P(('ctx', 'fsdp')), may hold values from -0.15625 to 0.15625
- w_up: bfloat16 [1536, 4096], P(('ctx', 'fsdp')), may hold values from -0.15625 to 0.15625
- w_down: bfloat16 [4096, 1536], P(('ctx', 'fsdp')), may hold values from -0.09375 to 0.09375
Outputs:
- output: bfloat16 [2, 2048, 1536], P('fsdp', 'ctx')
- input_grad: float32 [2, 2048, 1536], P('fsdp', 'ctx')
- grad_gain1: float32 [1536], P(('ctx', 'fsdp'))
- grad_query: float32 [1536, 1536], P(('ctx', 'fsdp'))
- grad_key: float32 [1536, 768], P(('ctx', 'fsdp'))
- grad_value: float32 [1536, 768], P(('ctx', 'fsdp'))
- grad_out: float32 [1536, 1536], P(('ctx', 'fsdp'))
- grad_gain2: float32 [1536], P(('ctx', 'fsdp'))
- grad_gate: float32 [1536, 4096], P(('ctx', 'fsdp'))
- grad_up: float32 [1536, 4096], P(('ctx', 'fsdp'))
- grad_down: float32 [4096, 1536], P(('ctx', 'fsdp'))
All inputs are finite; a program needn't handle non-finite values.
Results may differ from a plain program's by a relative error of at most 0.025.
Values may be sent and summed in bfloat16 or wider, within the bound.
No kernel may reach another device: no remote copies, remote signals or barrier semaphores. Data moves between devices by JAX's collectives and lax.ppermute only.
A program may use at most 384 MiB of HBM per device.

v0:
```python
import jax
import jax.numpy as jnp
from jax import lax
from jax.sharding import PartitionSpec as P

QUERY_HEADS = 16
KEY_VALUE_HEADS = 8
HEAD_SIZE = 96


rope_base = 100000.0
norm_eps = 1e-05
masked_value = -1e30
key_block = 512


def rms_norm(value_rows, gain):
    return (
        value_rows
        * lax.rsqrt(jnp.mean(value_rows * value_rows, axis=-1, keepdims=True) + norm_eps)
        * gain
    )


def apply_rotary(value_rows, token_position):
    half = value_rows.shape[-1] // 2
    exponent = jnp.arange(half, dtype=jnp.float32) * (2.0 / value_rows.shape[-1])
    freq = rope_base ** (-exponent)
    angle = token_position[:, None] * freq[None, :]
    cosine = jnp.cos(angle)[:, None, :]
    sine = jnp.sin(angle)[:, None, :]
    first = value_rows[..., :half]
    second = value_rows[..., half:]
    return jnp.concatenate(
        [first * cosine - second * sine, second * cosine + first * sine], axis=-1
    )


def matmul(left, right):
    return jnp.dot(left, right, preferred_element_type=jnp.float32)


def key_pieces(key_rows, value_rows, key_value_heads, head_dim):
    count = key_rows.shape[0]
    number = count // key_block
    key_sets = key_rows.reshape(number, key_block, key_value_heads, head_dim)
    value_sets = value_rows.reshape(number, key_block, key_value_heads, head_dim)
    starts = jnp.arange(number, dtype=jnp.int32) * key_block
    return (key_sets, value_sets, starts, key_block)


def fold_keys(carry, key_rows, value_rows, query_rows, query_pos):
    key_value_heads = query_rows.shape[1]
    head_dim = query_rows.shape[3]
    scale = head_dim ** (-0.5)
    key_sets, value_sets, starts, size = key_pieces(key_rows, value_rows, key_value_heads, head_dim)

    def fold_one_piece(state, item):
        key_set, value_set, begin = item

        def fold_live(state):
            top, total, summed = state
            scores = (
                jnp.einsum(
                    "tkgd,skd->kgts", query_rows, key_set, preferred_element_type=jnp.float32
                )
                * scale
            )
            visible = (begin + jnp.arange(size, dtype=jnp.int32))[None, :] <= query_pos[:, None]
            scores = jnp.where(visible, scores, masked_value)
            new_top = jnp.maximum(top, jnp.max(scores, axis=-1))
            weights = jnp.where(visible, jnp.exp(scores - new_top[..., None]), 0.0)
            factor = jnp.exp(top - new_top)
            total = total * factor + jnp.sum(weights, axis=-1)
            summed = summed * factor[..., None] + jnp.einsum(
                "kgts,skd->kgtd",
                weights.astype(jnp.bfloat16),
                value_set,
                preferred_element_type=jnp.float32,
            )
            return (new_top, total, summed)

        def fold_skipped(state):
            return state

        return (lax.cond(begin <= query_pos[-1], fold_live, fold_skipped, state), None)

    carry, _ = lax.scan(fold_one_piece, carry, (key_sets, value_sets, starts))
    return carry


def back_keys(key_rows, value_rows, query_rows, query_pos, d_heads, log_total, delta):
    rows, key_value_heads, groups, head_dim = query_rows.shape
    scale = head_dim ** (-0.5)
    key_sets, value_sets, starts, size = key_pieces(key_rows, value_rows, key_value_heads, head_dim)

    def back_one_piece(d_query, item):
        key_set, value_set, begin = item

        def back_live(d_query):
            scores = (
                jnp.einsum(
                    "tkgd,skd->kgts", query_rows, key_set, preferred_element_type=jnp.float32
                )
                * scale
            )
            visible = (begin + jnp.arange(size, dtype=jnp.int32))[None, :] <= query_pos[:, None]
            prob = jnp.where(visible, jnp.exp(scores - log_total[..., None]), 0.0)
            d_prob = jnp.einsum(
                "tkgd,skd->kgts", d_heads, value_set, preferred_element_type=jnp.float32
            )
            d_scores = (prob * (d_prob - delta[..., None])).astype(jnp.bfloat16)
            d_query = d_query + scale * jnp.einsum(
                "kgts,skd->tkgd", d_scores, key_set, preferred_element_type=jnp.float32
            )
            d_key = scale * jnp.einsum(
                "kgts,tkgd->skd", d_scores, query_rows, preferred_element_type=jnp.float32
            )
            d_value = jnp.einsum(
                "kgts,tkgd->skd",
                prob.astype(jnp.bfloat16),
                d_heads,
                preferred_element_type=jnp.float32,
            )
            return (
                d_query,
                (
                    d_key.reshape(size, key_value_heads * head_dim),
                    d_value.reshape(size, key_value_heads * head_dim),
                ),
            )

        def back_skipped(d_query):
            empty = jnp.zeros((size, key_value_heads * head_dim), jnp.float32)
            return (d_query, (empty, empty))

        return lax.cond(begin <= query_pos[-1], back_live, back_skipped, d_query)

    start_grad = jnp.zeros((rows, key_value_heads, groups, head_dim), jnp.float32)
    d_query, (d_keys, d_values) = lax.scan(
        back_one_piece, start_grad, (key_sets, value_sets, starts)
    )
    return (
        d_query,
        d_keys.reshape(key_rows.shape[0], key_value_heads * head_dim),
        d_values.reshape(key_rows.shape[0], key_value_heads * head_dim),
    )


def local(
    tokens,
    cotangent,
    norm_gain1,
    w_query,
    key_weight,
    value_weight,
    w_out,
    norm_gain2,
    w_gate,
    w_up,
    w_down,
):
    rows = tokens.shape[1]
    key_value_heads = KEY_VALUE_HEADS
    heads = QUERY_HEADS
    head_dim = HEAD_SIZE
    groups = heads // key_value_heads
    first_row = lax.axis_index("ctx") * rows
    query_pos = first_row + jnp.arange(rows, dtype=jnp.int32)
    token_position = query_pos.astype(jnp.float32)
    inputs = tokens[0].astype(jnp.float32)
    gathered = (
        lax.all_gather(norm_gain1, ("ctx", "fsdp"), axis=0, tiled=True),
        lax.all_gather(w_query, ("ctx", "fsdp"), axis=0, tiled=True),
        lax.all_gather(key_weight, ("ctx", "fsdp"), axis=0, tiled=True),
        lax.all_gather(value_weight, ("ctx", "fsdp"), axis=0, tiled=True),
        lax.all_gather(w_out, ("ctx", "fsdp"), axis=0, tiled=True),
        lax.all_gather(norm_gain2, ("ctx", "fsdp"), axis=0, tiled=True),
        lax.all_gather(w_gate, ("ctx", "fsdp"), axis=0, tiled=True),
        lax.all_gather(w_up, ("ctx", "fsdp"), axis=0, tiled=True),
        lax.all_gather(w_down, ("ctx", "fsdp"), axis=0, tiled=True),
    )
    gain_one = gathered[0].astype(jnp.float32)
    gain_two = gathered[5].astype(jnp.float32)
    normed1 = rms_norm(inputs, gain_one).astype(jnp.bfloat16)
    query_pre = matmul(normed1, gathered[1]).reshape(rows, heads, head_dim)
    key_pre = matmul(normed1, gathered[2]).reshape(rows, key_value_heads, head_dim)
    value = matmul(normed1, gathered[3]).astype(jnp.bfloat16)
    query_rows = (
        apply_rotary(query_pre, token_position)
        .astype(jnp.bfloat16)
        .reshape(rows, key_value_heads, groups, head_dim)
    )
    key_rows = (
        apply_rotary(key_pre, token_position)
        .reshape(rows, key_value_heads * head_dim)
        .astype(jnp.bfloat16)
    )
    start_state = (
        jnp.full((key_value_heads, groups, rows), masked_value, jnp.float32),
        jnp.zeros((key_value_heads, groups, rows), jnp.float32),
        jnp.zeros((key_value_heads, groups, rows, head_dim), jnp.float32),
    )
    top, total, summed = fold_keys(
        start_state,
        lax.all_gather(key_rows, "ctx", axis=0, tiled=True),
        lax.all_gather(value, "ctx", axis=0, tiled=True),
        query_rows,
        query_pos,
    )
    mixed_heads = jnp.transpose(summed / total[..., None], (2, 0, 1, 3))
    log_total = top + jnp.log(total)
    mixed_low = mixed_heads.reshape(rows, heads * head_dim).astype(jnp.bfloat16)
    middle = inputs + matmul(mixed_low, gathered[4])
    normed2 = rms_norm(middle, gain_two).astype(jnp.bfloat16)
    gate = matmul(normed2, gathered[6])
    upper = matmul(normed2, gathered[7])
    hidden = (jax.nn.silu(gate) * upper).astype(jnp.bfloat16)
    result = middle + matmul(hidden, gathered[8])
    gathered = (
        lax.all_gather(norm_gain1, ("ctx", "fsdp"), axis=0, tiled=True),
        lax.all_gather(w_query, ("ctx", "fsdp"), axis=0, tiled=True),
        lax.all_gather(key_weight, ("ctx", "fsdp"), axis=0, tiled=True),
        lax.all_gather(value_weight, ("ctx", "fsdp"), axis=0, tiled=True),
        lax.all_gather(w_out, ("ctx", "fsdp"), axis=0, tiled=True),
        lax.all_gather(norm_gain2, ("ctx", "fsdp"), axis=0, tiled=True),
        lax.all_gather(w_gate, ("ctx", "fsdp"), axis=0, tiled=True),
        lax.all_gather(w_up, ("ctx", "fsdp"), axis=0, tiled=True),
        lax.all_gather(w_down, ("ctx", "fsdp"), axis=0, tiled=True),
    )
    incoming = cotangent[0].astype(jnp.float32)
    incoming_low = incoming.astype(jnp.bfloat16)
    grad_down = matmul(hidden.T, incoming_low)
    d_hidden = matmul(incoming_low, gathered[8].T)
    _, swiglu_back = jax.vjp(lambda gate_in, upper_in: jax.nn.silu(gate_in) * upper_in, gate, upper)
    d_gate, d_upper = swiglu_back(d_hidden)
    d_gate = d_gate.astype(jnp.bfloat16)
    d_upper = d_upper.astype(jnp.bfloat16)
    grad_gate = matmul(normed2.T, d_gate)
    grad_up = matmul(normed2.T, d_upper)
    d_normed2 = matmul(d_gate, gathered[6].T) + matmul(d_upper, gathered[7].T)
    _, norm_back2 = jax.vjp(rms_norm, middle, gain_two)
    d_middle, grad_gain2 = norm_back2(d_normed2)
    d_middle = d_middle + incoming
    owned_gain2, owned_gate, owned_up, owned_down = (
        lax.psum_scatter(grad_gain2, ("ctx", "fsdp"), scatter_dimension=0, tiled=True),
        lax.psum_scatter(grad_gate, ("ctx", "fsdp"), scatter_dimension=0, tiled=True),
        lax.psum_scatter(grad_up, ("ctx", "fsdp"), scatter_dimension=0, tiled=True),
        lax.psum_scatter(grad_down, ("ctx", "fsdp"), scatter_dimension=0, tiled=True),
    )
    d_middle_low = d_middle.astype(jnp.bfloat16)
    grad_out = matmul(mixed_low.T, d_middle_low)
    d_mixed = matmul(d_middle_low, gathered[4].T).astype(jnp.bfloat16)
    d_heads = d_mixed.reshape(rows, key_value_heads, groups, head_dim)
    delta = jnp.transpose(jnp.sum(d_heads.astype(jnp.float32) * mixed_heads, axis=-1), (1, 2, 0))
    back_keys_all, back_values_all = (
        lax.all_gather(key_rows, "ctx", axis=0, tiled=True),
        lax.all_gather(value, "ctx", axis=0, tiled=True),
    )
    d_query_rot, d_keys_all, d_values_all = back_keys(
        back_keys_all, back_values_all, query_rows, query_pos, d_heads, log_total, delta
    )
    d_keys_rot, d_value = (
        lax.psum_scatter(d_keys_all, "ctx", scatter_dimension=0, tiled=True),
        lax.psum_scatter(d_values_all, "ctx", scatter_dimension=0, tiled=True),
    )
    _, rotate_back_query = jax.vjp(
        lambda values_in: apply_rotary(values_in, token_position), query_pre
    )
    _, rotate_back_key = jax.vjp(lambda values_in: apply_rotary(values_in, token_position), key_pre)
    d_query = (
        rotate_back_query(d_query_rot.reshape(rows, heads, head_dim))[0]
        .reshape(rows, heads * head_dim)
        .astype(jnp.bfloat16)
    )
    d_key = (
        rotate_back_key(d_keys_rot.reshape(rows, key_value_heads, head_dim))[0]
        .reshape(rows, key_value_heads * head_dim)
        .astype(jnp.bfloat16)
    )
    d_value = d_value.astype(jnp.bfloat16)
    grad_query = matmul(normed1.T, d_query)
    grad_key = matmul(normed1.T, d_key)
    grad_value = matmul(normed1.T, d_value)
    d_normed1 = (
        matmul(d_query, gathered[1].T)
        + matmul(d_key, gathered[2].T)
        + matmul(d_value, gathered[3].T)
    )
    _, norm_back1 = jax.vjp(rms_norm, inputs, gain_one)
    d_inputs, grad_gain1 = norm_back1(d_normed1)
    input_grad = d_inputs + d_middle
    owned_gain1, owned_query, owned_key, owned_value, owned_out = (
        lax.psum_scatter(grad_gain1, ("ctx", "fsdp"), scatter_dimension=0, tiled=True),
        lax.psum_scatter(grad_query, ("ctx", "fsdp"), scatter_dimension=0, tiled=True),
        lax.psum_scatter(grad_key, ("ctx", "fsdp"), scatter_dimension=0, tiled=True),
        lax.psum_scatter(grad_value, ("ctx", "fsdp"), scatter_dimension=0, tiled=True),
        lax.psum_scatter(grad_out, ("ctx", "fsdp"), scatter_dimension=0, tiled=True),
    )
    return (
        result.astype(jnp.bfloat16)[None],
        input_grad[None],
        owned_gain1,
        owned_query,
        owned_key,
        owned_value,
        owned_out,
        owned_gain2,
        owned_gate,
        owned_up,
        owned_down,
    )


def solution(mesh):
    in_specs = (
        P("fsdp", "ctx", None),
        P("fsdp", "ctx", None),
        P(("ctx", "fsdp")),
        P(("ctx", "fsdp"), None),
        P(("ctx", "fsdp"), None),
        P(("ctx", "fsdp"), None),
        P(("ctx", "fsdp"), None),
        P(("ctx", "fsdp")),
        P(("ctx", "fsdp"), None),
        P(("ctx", "fsdp"), None),
        P(("ctx", "fsdp"), None),
    )
    out_specs = (
        P("fsdp", "ctx", None),
        P("fsdp", "ctx", None),
        P(("ctx", "fsdp")),
        P(("ctx", "fsdp"), None),
        P(("ctx", "fsdp"), None),
        P(("ctx", "fsdp"), None),
        P(("ctx", "fsdp"), None),
        P(("ctx", "fsdp")),
        P(("ctx", "fsdp"), None),
        P(("ctx", "fsdp"), None),
        P(("ctx", "fsdp"), None),
    )
    return jax.shard_map(local, mesh=mesh, in_specs=in_specs, out_specs=out_specs, check_vma=False)
```

profile of v0, /device:TPU:10, one launch (start us, length us, event | category | flops | bytes accessed | tf_op | source)
XLA Modules:
  0.0 2205.8 jit_solution(5016868738364606262)
XLA Ops:
  11.2 41.6 %all-reduce.9 = (bf16[1536]{0:T(1024)(128)(2,1)S(1)}, bf16[1536]{0:T(1024)(128)(2,1)S(1)}) all-reduce(bf16[1536]{0:T(1024)(128)(2,1)S(1)} %dynamic-update-slice, bf16[1536]{0:T(1024)(128)(2,1)S(1)} %dynamic-update-slice.1), channel_id=1, replica_groups=mesh['ctx'=16,'fsdp'=2] {'ctx','fsdp'}, use_global_device_ids=true, to_apply=%add.4 | all-reduce | flops 3072 | bytes 12288
  54.1 14.2 all-gather.10.cloned.1.call-done
  72.9 54.7 %all-gather.16.cloned.1.call-done = bf16[1536,768]{1,0:T(8,128)(2,1)} async-done(((bf16[48,768]{1,0:T(8,128)(2,1)}), bf16[1536,768]{1,0:T(8,128)(2,1)}) %all-gather.16.cloned.1.call-update) | async-done | bytes 2359312 | tf_op jit(solution)/shard_map/all_gather | solution.py:176
  133.9 60.6 %all-gather.14.cloned.1.call-done = bf16[1536,1536]{1,0:T(8,128)(2,1)} async-done(((bf16[48,1536]{1,0:T(8,128)(2,1)}), bf16[1536,1536]{1,0:T(8,128)(2,1)}) %all-gather.14.cloned.1.call-update) | async-done | bytes 4718608 | tf_op jit(solution)/shard_map/all_gather | solution.py:174
  205.2 35.4 %all-gather.12.cloned.1.call-done = bf16[2048,768]{0,1:T(8,128)(2,1)} async-done(((bf16[128,768]{0,1:T(8,128)(2,1)}), bf16[2048,768]{0,1:T(8,128)(2,1)}) %all-gather.12.cloned.1.call-update) | async-done | bytes 3145744 | tf_op jit(solution)/shard_map/all_gather | solution.py:206
  251.1 37.3 %all-gather.18.cloned.1.call-done = bf16[2048,768]{1,0:T(8,128)(2,1)} async-done(((bf16[128,768]{1,0:T(8,128)(2,1)}), bf16[2048,768]{1,0:T(8,128)(2,1)}) %all-gather.18.cloned.1.call-update) | async-done | bytes 3145744 | tf_op jit(solution)/shard_map/all_gather | solution.py:207
  288.4 8.2 reshape.259
  304.1 25.4 %while.31 = (s32[]{:T(128)}, f32[8,2,128]{2,1,0:T(2,128)S(1)}, f32[8,2,128]{2,1,0:T(2,128)S(1)}, f32[8,2,128,96]{2,3,1,0:T(8,128)S(1)}, s32[4]{0:T(128)}, /*inde...) while((s32[]{:T(128)}, f32[8,2,128]{2,1,0:T(2,128)S(1)}, ...), condition=%wide.region_6.7_spmd, body=%wide.region_1.6_spmd.sunk | while | flops 416748032 | bytes 16520979 | solution.py:88
  329.5 25.0 %all-gather.20.cloned.1.call-done = bf16[1536,1536]{1,0:T(8,128)(2,1)} async-done(((bf16[48,1536]{1,0:T(8,128)(2,1)}), bf16[1536,1536]{1,0:T(8,128)(2,1)}) %all-gather.20.cloned.1.call-update) | async-done | bytes 4718608 | tf_op jit(solution)/shard_map/all_gather | solution.py:177
  358.6 92.7 %all-gather.22.cloned.1.call-done = bf16[1536,4096]{1,0:T(8,128)(2,1)} async-done(((bf16[48,4096]{1,0:T(8,128)(2,1)}), bf16[1536,4096]{1,0:T(8,128)(2,1)}) %all-gather.22.cloned.1.call-update) | async-done | bytes 12582928 | tf_op jit(solution)/shard_map/all_gather | solution.py:179
  459.0 89.5 %all-gather.24.cloned.1.call-done = bf16[1536,4096]{1,0:T(8,128)(2,1)} async-done(((bf16[48,4096]{1,0:T(8,128)(2,1)}), bf16[1536,4096]{1,0:T(8,128)(2,1)}) %all-gather.24.cloned.1.call-update) | async-done | bytes 12582928 | tf_op jit(solution)/shard_map/all_gather | solution.py:180
  556.1 89.5 %all-gather.26.cloned.1.call-done = bf16[4096,1536]{1,0:T(8,128)(2,1)} async-done(((bf16[128,1536]{1,0:T(8,128)(2,1)}), bf16[4096,1536]{1,0:T(8,128)(2,1)}) %all-gather.26.cloned.1.call-update) | async-done | bytes 12582928 | tf_op jit(solution)/shard_map/all_gather | solution.py:181
  645.6 11.1 multiply_convert_fusion
  656.7 9.6 fusion.95
  666.4 9.8 multiply_reduce_fusion
  680.9 59.7 %while.32 = (s32[]{:T(128)}, f32[128,8,2,96]{0,3,2,1:T(8,128)}, f32[4,512,768]{2,1,0:T(8,128)}, f32[4,512,768]{2,1,0:T(8,128)}, s32[4]{0:T(128)}, /*index=5*/s32...) while((s32[]{:T(128)}, f32[128,8,2,96]{0,3,2,1:T(8,128)}, ...), condition=%wide.region_13.14_spmd, body=%wide.region_10.13_spmd.sunk | while | flops 1017971200 | bytes 57703412 | solution.py:140
  684.0 10.1 conditional.5
  703.8 10.1 conditional.5
  753.6 90.1 %reduce-scatter.10.cloned.1.call-done = f32[128,768]{1,0:T(8,128)} async-done(((f32[2048,768]{1,0:T(8,128)}), f32[128,768]{1,0:T(8,128)}) %reduce-scatter.10.cloned.1.call-update) | async-done | bytes 393232 | tf_op jit(solution)/shard_map/reduce_scatter | solution.py:264
  848.1 84.5 %reduce-scatter.12.cloned.1.call-done = f32[128,768]{1,0:T(8,128)} async-done(((f32[2048,768]{1,0:T(8,128)}), f32[128,768]{1,0:T(8,128)}) %reduce-scatter.12.cloned.1.call-update) | async-done | bytes 393232 | tf_op jit(solution)/shard_map/reduce_scatter | solution.py:265
  936.7 10.5 fusion.97
  948.5 11.0 fusion.98
  960.9 11.0 fusion.66
  976.2 7.8 fusion.45
  986.8 43.3 %all-reduce.8 = (f32[1536]{0:T(1024)S(1)}, f32[1536]{0:T(1024)S(1)}) all-reduce(f32[1536]{0:T(1024)S(1)} %get-tuple-element.365, f32[1536]{0:T(1024)S(1)} %copy-done.33), channel_id=4, replica_groups=mesh['ctx'=16,'fsdp'=2] {'ctx','fsdp'}, use_global_device_ids=true, to_apply=%region_18.19.clone | all-reduce | flops 3072 | bytes 24576
  1032.4 42.5 %reduce-scatter.14.cloned.1.call-done = f32[48,1536]{1,0:T(8,128)} async-done(((f32[1536,1536]{1,0:T(8,128)}), f32[48,1536]{1,0:T(8,128)}) %reduce-scatter.14.cloned.1.call-update) | async-done | bytes 294928 | tf_op jit(solution)/shard_map/reduce_scatter | solution.py:295
  1074.9 142.1 %reduce-scatter.20.cloned.1.call-done = f32[48,1536]{1,0:T(8,128)} async-done(((f32[1536,1536]{1,0:T(8,128)}), f32[48,1536]{1,0:T(8,128)}) %reduce-scatter.20.cloned.1.call-update) | async-done | bytes 294928 | tf_op jit(solution)/shard_map/reduce_scatter | solution.py:298
  1217.0 112.2 %reduce-scatter.16.cloned.1.call-done = f32[48,768]{1,0:T(8,128)} async-done(((f32[1536,768]{1,0:T(8,128)}), f32[48,768]{1,0:T(8,128)}) %reduce-scatter.16.cloned.1.call-update) | async-done | bytes 147472 | tf_op jit(solution)/shard_map/reduce_scatter | solution.py:296
  1329.1 112.9 %reduce-scatter.18.cloned.1.call-done = f32[48,768]{1,0:T(8,128)} async-done(((f32[1536,768]{1,0:T(8,128)}), f32[48,768]{1,0:T(8,128)}) %reduce-scatter.18.cloned.1.call-update) | async-done | bytes 147472 | tf_op jit(solution)/shard_map/reduce_scatter | solution.py:297
  1442.1 251.5 %reduce-scatter.22.cloned.1.call-done = f32[48,4096]{1,0:T(8,128)} async-done(((f32[1536,4096]{1,0:T(8,128)}), f32[48,4096]{1,0:T(8,128)}) %reduce-scatter.22.cloned.1.call-update) | async-done | bytes 786448 | tf_op jit(solution)/shard_map/reduce_scatter | solution.py:247
  1693.6 253.0 %reduce-scatter.24.cloned.1.call-done = f32[48,4096]{1,0:T(8,128)} async-done(((f32[1536,4096]{1,0:T(8,128)}), f32[48,4096]{1,0:T(8,128)}) %reduce-scatter.24.cloned.1.call-update) | async-done | bytes 786448 | tf_op jit(solution)/shard_map/reduce_scatter | solution.py:248
  1946.6 251.9 %reduce-scatter.26.cloned.1.call-done = f32[128,1536]{1,0:T(8,128)} async-done(((f32[4096,1536]{1,0:T(8,128)}), f32[128,1536]{1,0:T(8,128)}) %reduce-scatter.26.cloned.1.call-update) | async-done | bytes 786448 | tf_op jit(solution)/shard_map/reduce_scatter | solution.py:249
  (272 shorter events, 189.4 us)
Async XLA Ops:
  7.2 64.0 %copy-start.1 = (bf16[1,128,1536]{2,1,0:T(8,128)(2,1)S(1)}, bf16[1,128,1536]{2,1,0:T(8,128)(2,1)}, u32[]{:S(2)}) copy-start(bf16[1,128,1536]{2,1,0:T(8,128)(2,1)} %param.19) | copy-start | bytes 1179652
  7.2 61.2 %all-gather.10.cloned.1.call-start = ((), (), s32[]{:S(2)}) async-start(), calls=%async_computation.9 | async-start | bytes 2433024 | tf_op jit(solution)/shard_map/all_gather | solution.py:175
  7.9 119.6 %all-gather.16.cloned.1.call-start = ((), (), s32[]{:S(2)}) async-start(), calls=%async_computation.12 | async-start | bytes 2433024 | tf_op jit(solution)/shard_map/all_gather | solution.py:176
  8.7 185.9 %all-gather.14.cloned.1.call-start = ((), (), s32[]{:S(2)}) async-start(), calls=%async_computation.11 | async-start | bytes 4866048 | tf_op jit(solution)/shard_map/all_gather | solution.py:174
  9.4 231.2 %all-gather.12.cloned.1.call-start = ((), (), s32[]{:S(2)}) async-start(), calls=%async_computation.10 | async-start | bytes 3342336 | tf_op jit(solution)/shard_map/all_gather | solution.py:206
  53.9 14.4 copy-start.36
  54.1 150.9 %copy-start.29 = (f32[128,48]{0,1:T(8,128)}, f32[128,48]{0,1:T(8,128)S(1)}, u32[]{:S(2)}) copy-start(f32[128,48]{0,1:T(8,128)S(1)} %get-tuple-element.430) | copy-start | bytes 73732
  54.1 150.9 %copy-start.31 = (f32[128,48]{0,1:T(8,128)}, f32[128,48]{0,1:T(8,128)S(1)}, u32[]{:S(2)}) copy-start(f32[128,48]{0,1:T(8,128)S(1)} %get-tuple-element.431) | copy-start | bytes 73732
  72.8 215.6 %all-gather.18.cloned.1.call-start = ((), (), s32[]{:S(2)}) async-start(), calls=%async_computation.13 | async-start | bytes 3342336 | tf_op jit(solution)/shard_map/all_gather | solution.py:207
  130.5 224.1 %all-gather.20.cloned.1.call-start = ((), (), s32[]{:S(2)}) async-start(), calls=%async_computation.14 | async-start | bytes 4866048 | tf_op jit(solution)/shard_map/all_gather | solution.py:177
  131.0 320.2 %all-gather.22.cloned.1.call-start = ((), (), s32[]{:S(2)}) async-start(), calls=%async_computation.15 | async-start | bytes 12976128 | tf_op jit(solution)/shard_map/all_gather | solution.py:179
  131.8 416.6 %all-gather.24.cloned.1.call-start = ((), (), s32[]{:S(2)}) async-start(), calls=%async_computation.16 | async-start | bytes 12976128 | tf_op jit(solution)/shard_map/all_gather | solution.py:180
  132.5 513.1 %all-gather.26.cloned.1.call-start = ((), (), s32[]{:S(2)}) async-start(), calls=%async_computation.17 | async-start | bytes 12976128 | tf_op jit(solution)/shard_map/all_gather | solution.py:181
  133.3 710.5 %reduce-scatter.10.cloned.1.call-start = ((), (), s32[]{:S(2)}) async-start(), calls=%async_computation.18 | async-start | bytes 6684672 | tf_op jit(solution)/shard_map/reduce_scatter | solution.py:264
  329.5 129.4 %copy-start.15 = (bf16[128,8,2,96]{0,3,2,1:T(8,128)(2,1)}, bf16[128,8,2,96]{0,3,2,1:T(8,128)(2,1)S(1)}, u32[]{:S(2)}) copy-start(bf16[128,8,2,96]{0,3,2,1:T(8,128)(2,1)S(1)} %bitcast_convert_fusion) | copy-start | bytes 1179652
  357.7 318.4 %copy-start.6 = (f32[128,1536]{1,0:T(8,128)}, f32[128,1536]{1,0:T(8,128)S(1)}, u32[]{:S(2)}) copy-start(f32[128,1536]{1,0:T(8,128)S(1)} %get-tuple-element.433) | copy-start | bytes 2359300
  358.6 189.8 %copy-start.8 = (bf16[128,1536]{1,0:T(8,128)(2,1)}, bf16[128,1536]{1,0:T(8,128)(2,1)S(1)}, u32[]{:S(2)}) copy-start(bf16[128,1536]{1,0:T(8,128)(2,1)S(1)} %multiply_convert_fusion.2) | copy-start | bytes 1179652
  459.0 186.6 %copy-start.26 = (bf16[1,128,1536]{2,1,0:T(8,128)(2,1)S(1)}, bf16[1,128,1536]{2,1,0:T(8,128)(2,1)}, u32[]{:S(2)}) copy-start(bf16[1,128,1536]{2,1,0:T(8,128)(2,1)} %param.20) | copy-start | bytes 1179652
  656.7 9.7 copy-start.17
  656.7 20.6 slice-start
  666.4 11.0 slice-start.1
  740.7 191.9 %reduce-scatter.12.cloned.1.call-start = ((), (), s32[]{:S(2)}) async-start(), calls=%async_computation.19 | async-start | bytes 6684672 | tf_op jit(solution)/shard_map/reduce_scatter | solution.py:265
  741.4 333.5 %reduce-scatter.14.cloned.1.call-start = ((), (), s32[]{:S(2)}) async-start(), calls=%async_computation.20 | async-start | bytes 9732096 | tf_op jit(solution)/shard_map/reduce_scatter | solution.py:295
  747.2 469.8 %reduce-scatter.20.cloned.1.call-start = ((), (), s32[]{:S(2)}) async-start(), calls=%async_computation.23 | async-start | bytes 9732096 | tf_op jit(solution)/shard_map/reduce_scatter | solution.py:298
  753.3 575.8 %reduce-scatter.16.cloned.1.call-start = ((), (), s32[]{:S(2)}) async-start(), calls=%async_computation.21 | async-start | bytes 4866048 | tf_op jit(solution)/shard_map/reduce_scatter | solution.py:296
  848.0 88.6 %copy-start.9 = (bf16[128,1536]{1,0:T(8,128)(2,1)S(1)}, bf16[128,1536]{1,0:T(8,128)(2,1)}, u32[]{:S(2)}) copy-start(bf16[128,1536]{1,0:T(8,128)(2,1)} %copy-done.8) | copy-start | bytes 1179652
  848.0 88.6 %copy-start.20 = (bf16[128,4096]{1,0:T(8,128)(2,1)S(1)}, bf16[128,4096]{1,0:T(8,128)(2,1)}, u32[]{:S(2)}) copy-start(bf16[128,4096]{1,0:T(8,128)(2,1)} %copy-done.19) | copy-start | bytes 3145732
  848.1 594.0 %reduce-scatter.18.cloned.1.call-start = ((), (), s32[]{:S(2)}) async-start(), calls=%async_computation.22 | async-start | bytes 4866048 | tf_op jit(solution)/shard_map/reduce_scatter | solution.py:297
  936.6 756.9 %reduce-scatter.22.cloned.1.call-start = ((), (), s32[]{:S(2)}) async-start(), calls=%async_computation.24 | async-start | bytes 25952256 | tf_op jit(solution)/shard_map/reduce_scatter | solution.py:247
  947.2 999.4 %reduce-scatter.24.cloned.1.call-start = ((), (), s32[]{:S(2)}) async-start(), calls=%async_computation.25 | async-start | bytes 25952256 | tf_op jit(solution)/shard_map/reduce_scatter | solution.py:248
  959.5 1239.0 %reduce-scatter.26.cloned.1.call-start = ((), (), s32[]{:S(2)}) async-start(), calls=%async_computation.26 | async-start | bytes 25952256 | tf_op jit(solution)/shard_map/reduce_scatter | solution.py:249
  984.0 47.2 %copy-start.37 = (f32[128]{0:T(128)S(1)}, f32[128]{0:T(128)}, u32[]{:S(2)}) copy-start(f32[128]{0:T(128)} %copy-done.36) | copy-start | bytes 1540
  (40 other events, 116.2 us)
Sparse Core Ops, SparseCore 0:
  10.9 57.3 all-gather.9
  71.3 56.2 all-gather.15
  130.5 63.9 all-gather.13
  197.1 43.4 all-gather.11
  243.3 45.0 all-gather.17
  291.2 63.3 all-gather.19
  357.4 93.7 all-gather.21
  454.1 94.2 all-gather.23
  551.3 94.2 all-gather.25
  740.8 102.9 reduce-scatter.9
  848.2 84.2 reduce-scatter.11
  938.9 135.9 reduce-scatter.13
  1082.4 134.5 reduce-scatter.19
  1222.9 106.2 reduce-scatter.15
  1335.9 106.0 reduce-scatter.17
  1448.9 244.6 reduce-scatter.21
  1701.5 245.0 reduce-scatter.23
  1953.4 244.9 reduce-scatter.25
where the time goes:
time: 2220 us; the launch traced here: 2210 us
  waiting for transfers between devices  1840 us (83%)
  matrix products  149 us (7%)
  local copies, waits for them, and re-layouts  88.4 us (4%)
  blocking collectives  84.9 us (4%)
    reduce_scatter x1, waiting for transfers between devices, local(): lax.psum_scatter(grad_up, ('ctx', 'fsdp'), scatter_dimension=0, tiled=True)  253 us
    reduce_scatter x1, waiting for transfers between devices, local(): lax.psum_scatter(grad_down, ('ctx', 'fsdp'), scatter_dimension=0, tiled=T...  252 us
    reduce_scatter x1, waiting for transfers between devices, local(): lax.psum_scatter(grad_gate, ('ctx', 'fsdp'), scatter_dimension=0, tiled=T...  252 us
    reduce_scatter x1, waiting for transfers between devices, local(): lax.psum_scatter(grad_out, ('ctx', 'fsdp'), scatter_dimension=0, tiled=True)  142 us
    dot_general x21, matrix products, matmul(): return jnp.dot(left, right, preferred_element_type=jnp.float32)  122 us
    reduce_scatter x1, waiting for transfers between devices, local(): lax.psum_scatter(grad_value, ('ctx', 'fsdp'), scatter_dimension=0, tiled=...  113 us
    reduce_scatter x1, waiting for transfers between devices, local(): lax.psum_scatter(grad_key, ('ctx', 'fsdp'), scatter_dimension=0, tiled=True)  112 us
    all_gather x1, waiting for transfers between devices, local(): lax.all_gather(w_gate, ('ctx', 'fsdp'), axis=0, tiled=True)  92.7 us
  transfers between devices with their start and end apart: 18, of which 18 were waited for; matrix products, arithmetic and copies ran while one was open for 7% of the time, Pallas kernels for 0%

commit v1 on v0

--- a/solution.py
+++ b/solution.py
@@ -1,6 +1,12 @@
+import functools
+
 import jax
 import jax.numpy as jnp
+import numpy as np
 from jax import lax
+from jax.experimental import pallas as pl
+from jax.experimental.pallas import tpu as pltpu
+from jax.sharding import Mesh
 from jax.sharding import PartitionSpec as P
 
 QUERY_HEADS = 16
@@ -312,6 +318,412 @@
     )
 
 
+bf16 = jnp.bfloat16
+f32 = jnp.float32
+score_scale = HEAD_SIZE ** (-0.5)
+log2_e = 1.4426950408889634
+ln_2 = 0.6931471805599453
+
+
+def dot_at(left, right, left_dim, right_dim):
+    return lax.dot_general(
+        left, right, (((left_dim,), (right_dim,)), ((), ())), preferred_element_type=jnp.float32
+    )
+
+
+def heads_forward_kernel(step, q_ref, k_ref, v_ref, mixed_ref, prob_ref):
+    tokens = q_ref.shape[1]
+    offset = 0
+    for begin in range(0, tokens, step):
+        end = begin + step
+        scores = dot_at(k_ref[:, 0:end], q_ref[:, begin:end], 0, 0)
+        key = lax.broadcasted_iota(jnp.int32, (step, step), 0)
+        query = lax.broadcasted_iota(jnp.int32, (step, step), 1)
+        last = jnp.where(key <= query, scores[begin:end], masked_value)
+        top = jnp.max(last, axis=0, keepdims=True)
+        if begin:
+            top = jnp.maximum(top, jnp.max(scores[:begin], axis=0, keepdims=True))
+        last = jnp.exp2(last - top)
+        total = jnp.sum(last, axis=0, keepdims=True)
+        if begin:
+            first = jnp.exp2(scores[:begin] - top)
+            total = total + jnp.sum(first, axis=0, keepdims=True)
+        inverse = 1.0 / total
+        prob_ref[offset + begin : offset + end, :] = (last * inverse).astype(bf16)
+        if begin:
+            prob_ref[offset : offset + begin, :] = (first * inverse).astype(bf16)
+        mixed_ref[:, begin:end] = dot_at(
+            v_ref[:, 0:end], prob_ref[offset : offset + end, :], 1, 0
+        )
+        offset += end
+
+
+def heads_backward_kernel(
+    step, q_ref, k_ref, v_ref, prob_ref, mixed_ref, d_mixed_ref, d_q_ref, d_k_ref, d_v_ref
+):
+    tokens = q_ref.shape[1]
+    offset = 0
+    for begin in range(0, tokens, step):
+        end = begin + step
+        d_mixed = d_mixed_ref[:, begin:end]
+        delta = jnp.sum(d_mixed.astype(f32) * mixed_ref[:, begin:end], axis=0, keepdims=True)
+        prob = prob_ref[offset : offset + end, :]
+        d_prob = dot_at(v_ref[:, 0:end], d_mixed, 0, 0)
+        d_scores = (prob.astype(f32) * (d_prob - delta)).astype(bf16)
+        d_q_ref[:, begin:end] = dot_at(k_ref[:, 0:end], d_scores, 1, 0) * score_scale
+        d_v = dot_at(d_mixed, prob, 1, 1)
+        d_k = dot_at(q_ref[:, begin:end], d_scores, 1, 1) * ln_2
+        if begin:
+            d_v_ref[:, 0:begin] += d_v[:, 0:begin]
+            d_k_ref[:, 0:begin] += d_k[:, 0:begin]
+        d_v_ref[:, begin:end] = d_v[:, begin:end]
+        d_k_ref[:, begin:end] = d_k[:, begin:end]
+        offset += end
+
+
+def heads_forward(q, k, v, step):
+    size, tokens = q.shape
+    blocks = tokens // step
+    pairs = step * blocks * (blocks + 1) // 2
+    whole = pl.BlockSpec(memory_space=pltpu.VMEM)
+    return pl.pallas_call(
+        functools.partial(heads_forward_kernel, step),
+        out_shape=(
+            jax.ShapeDtypeStruct((size, tokens), f32),
+            jax.ShapeDtypeStruct((pairs, step), bf16),
+        ),
+        in_specs=[whole] * 3,
+        out_specs=(whole, whole),
+        compiler_params=pltpu.CompilerParams(vmem_limit_bytes=40 * 2**20),
+        cost_estimate=pl.CostEstimate(
+            flops=4 * size * pairs * step, bytes_accessed=pairs * step * 2, transcendentals=pairs * step
+        ),
+        name="heads_forward",
+    )(q, k, v)
+
+
+def heads_backward(q, k, v, prob, mixed, d_mixed, step):
+    size, tokens = q.shape
+    whole = pl.BlockSpec(memory_space=pltpu.VMEM)
+    return pl.pallas_call(
+        functools.partial(heads_backward_kernel, step),
+        out_shape=(jax.ShapeDtypeStruct((size, tokens), f32),) * 3,
+        in_specs=[whole] * 6,
+        out_specs=(whole,) * 3,
+        compiler_params=pltpu.CompilerParams(vmem_limit_bytes=40 * 2**20),
+        cost_estimate=pl.CostEstimate(
+            flops=8 * size * prob.size, bytes_accessed=prob.size * 2, transcendentals=0
+        ),
+        name="heads_backward",
+    )(q, k, v, prob, mixed, d_mixed)
+
+
+def ring_of(count):
+    order = list(range(0, count, 2)) + list(range(count - 1, 0, -2))
+    forward = [(order[i], order[(i + 1) % count]) for i in range(count)]
+    backward = [(there, here) for here, there in forward]
+    return order, forward, backward
+
+
+def ring_gather(shards, count):
+    order, forward, backward = ring_of(count)
+    order = jnp.array(order, jnp.int32)
+    place = jnp.argsort(order)[lax.axis_index("d")]
+    outs = []
+    for shard in shards:
+        out = jnp.zeros((count,) + shard.shape, shard.dtype)
+        outs.append(lax.dynamic_update_slice_in_dim(out, shard[None], lax.axis_index("d"), 0))
+    ahead = list(shards)
+    behind = list(shards)
+    for hop in range(1, count // 2 + 1):
+        left = order[(place + count - hop) % count]
+        right = order[(place + hop) % count]
+        if hop < count // 2:
+            ahead = [lax.ppermute(a, "d", forward) for a in ahead]
+            behind = [lax.ppermute(b, "d", backward) for b in behind]
+            ahead, behind = lax.optimization_barrier((ahead, behind))
+            outs = [
+                lax.dynamic_update_slice_in_dim(o, a[None], left, 0) for o, a in zip(outs, ahead)
+            ]
+            outs = [
+                lax.dynamic_update_slice_in_dim(o, b[None], right, 0) for o, b in zip(outs, behind)
+            ]
+        else:
+            half = [a.shape[0] // 2 for a in ahead]
+            ahead = [lax.ppermute(a[:h], "d", forward) for a, h in zip(ahead, half)]
+            behind = [lax.ppermute(b[h:], "d", backward) for b, h in zip(behind, half)]
+            outs = [
+                lax.dynamic_update_slice(o, a[None], (left,) + (0,) * a.ndim)
+                for o, a in zip(outs, ahead)
+            ]
+            outs = [
+                lax.dynamic_update_slice(o, b[None], (left, h) + (0,) * (b.ndim - 1))
+                for o, b, h in zip(outs, behind, half)
+            ]
+    return outs
+
+
+def ring_scatter(terms, count):
+    order, forward, backward = ring_of(count)
+    order = jnp.array(order, jnp.int32)
+    place = jnp.argsort(order)[lax.axis_index("d")]
+
+    def part(term, position, side):
+        half = term.shape[1] // 2
+        start = (order[position % count], side * half) + (0,) * (term.ndim - 2)
+        return lax.dynamic_slice(term, start, (1, half) + term.shape[2:])[0]
+
+    ahead = [part(t, place + count - 1, 0) for t in terms]
+    behind = [part(t, place + 1, 1) for t in terms]
+    for hop in range(1, count):
+        ahead = [lax.ppermute(a, "d", forward) for a in ahead]
+        behind = [lax.ppermute(b, "d", backward) for b in behind]
+        ahead, behind = lax.optimization_barrier((ahead, behind))
+        kind = f32 if hop == count - 1 else bf16
+        ahead = [
+            (a.astype(f32) + part(t, place + 2 * count - 1 - hop, 0).astype(f32)).astype(kind)
+            for a, t in zip(ahead, terms)
+        ]
+        behind = [
+            (b.astype(f32) + part(t, place + 1 + hop, 1).astype(f32)).astype(kind)
+            for b, t in zip(behind, terms)
+        ]
+    return [jnp.concatenate([a, b], axis=0) for a, b in zip(ahead, behind)]
+
+
+def swap(values, axis):
+    return lax.ppermute(values, axis, [(0, 1), (1, 0)])
+
+
+def rows_of_group(own):
+    pair = lax.all_gather(own, "y", axis=0)
+    return lax.all_gather(pair, "core", axis=1)
+
+
+def own_rows_sum(terms):
+    core = lax.axis_index("core")
+    seq = lax.axis_index("y")
+    away = lax.dynamic_index_in_dim(terms, 1 - core, 1, False).astype(bf16)
+    kept = lax.dynamic_index_in_dim(terms, core, 1, False)
+    pair = kept + swap(away, "core").astype(f32)
+    away = lax.dynamic_index_in_dim(pair, 1 - seq, 0, False).astype(bf16)
+    kept = lax.dynamic_index_in_dim(pair, seq, 0, False)
+    return kept + swap(away, "y").astype(f32)
+
+
+def all_to_all(values, axes):
+    return lax.all_to_all(values, axes, 0, 0, tiled=True)
+
+
+def inverse_rms(values):
+    return lax.rsqrt(jnp.mean(values * values, axis=-1, keepdims=True) + norm_eps)
+
+
+def head_layer(
+    count,
+    tokens,
+    cotangent,
+    norm_gain1,
+    w_query,
+    key_weight,
+    value_weight,
+    w_out,
+    norm_gain2,
+    w_gate,
+    w_up,
+    w_down,
+):
+    rows, width = tokens.shape[1:]
+    own = w_query.shape[0]
+    ff_own = w_down.shape[0]
+    half = HEAD_SIZE // 2
+    quarter = HEAD_SIZE // 4
+    group = 4 * own
+    seq_rows = 2 * rows
+    length = count * seq_rows
+    step = seq_rows
+
+    gain1 = norm_gain1.astype(f32)[:, None]
+    gain2 = norm_gain2.astype(f32)[:, None]
+
+    with jax.named_scope("attention_weights"):
+        query_cols = (gain1 * w_query.astype(f32)).astype(bf16)
+        key_cols = (gain1 * key_weight.astype(f32)).astype(bf16)
+        value_cols = (gain1 * value_weight.astype(f32)).astype(bf16)
+        qkv_cols = jnp.concatenate(
+            [
+                query_cols.reshape(own, count, 4, half).transpose(2, 0, 1, 3),
+                key_cols.reshape(own, count, 4, quarter).transpose(2, 0, 1, 3),
+                value_cols.reshape(own, count, 4, quarter).transpose(2, 0, 1, 3),
+            ],
+            axis=-1,
+        ).reshape(4, own, count * HEAD_SIZE)
+        qkv_rows = all_to_all(qkv_cols, ("core", "y")).reshape(group, count * HEAD_SIZE)
+        (qkv_weight,) = ring_gather([qkv_rows], count)
+        qkv_weight = qkv_weight.reshape(width, count * HEAD_SIZE)
+    with jax.named_scope("feed_forward_weights"):
+        gate_cols = (gain2 * w_gate.astype(f32)).astype(bf16)
+        up_cols = (gain2 * w_up.astype(f32)).astype(bf16)
+        pair_cols = jnp.concatenate(
+            [
+                gate_cols.reshape(own, count, 4, ff_own).transpose(2, 0, 1, 3),
+                up_cols.reshape(own, count, 4, ff_own).transpose(2, 0, 1, 3),
+            ],
+            axis=2,
+        ).reshape(4, own, 2 * count * ff_own)
+        pair_rows = all_to_all(pair_cols, ("core", "y")).reshape(group, 2 * count * ff_own)
+        pair_rows, own_out, own_down, qkv_weight = lax.optimization_barrier(
+            (pair_rows, w_out, w_down, qkv_weight)
+        )
+        pair_weight, out_weight, down_weight = ring_gather([pair_rows, own_out, own_down], count)
+        pair_weight = pair_weight.reshape(width, 2 * count * ff_own)
+        out_weight = out_weight.reshape(count * own, width)
+        down_weight = down_weight.reshape(count * ff_own, width)
+
+    inputs = tokens[0].astype(f32)
+    r1 = inverse_rms(inputs)
+    n1_own = (inputs * r1).astype(bf16)
+    n1 = rows_of_group(n1_own).reshape(2 * seq_rows, width)
+    d_out = rows_of_group(cotangent[0]).reshape(2 * seq_rows, width)
+    qkv = dot_at(qkv_weight, n1, 0, 1).astype(bf16)
+    qkv = qkv.reshape(count, HEAD_SIZE, 2, seq_rows).transpose(0, 2, 1, 3)
+    qkv = all_to_all(qkv.reshape(2 * count, HEAD_SIZE, seq_rows), ("d", "y"))
+    qkv = qkv.reshape(count, 2, HEAD_SIZE, seq_rows)
+    q_parts = qkv[:, :, :half].transpose(1, 2, 0, 3).reshape(2, half, length)
+    kv = lax.all_gather(qkv[:, :, half:], "core", axis=0)
+    kv = kv.reshape(2, count, 2, 2, quarter, seq_rows).transpose(3, 0, 2, 4, 1, 5)
+    k_parts, v_parts = kv.reshape(2, 2, half, length)
+    position = jnp.arange(length, dtype=f32)
+    exponent = jnp.arange(half, dtype=f32) * (2.0 / HEAD_SIZE)
+    angle = (rope_base ** (-exponent))[:, None] * position[None, :]
+    cosine = jnp.cos(angle)
+    sine = jnp.sin(angle)
+
+    def rotate(first, second):
+        return jnp.concatenate(
+            [first * cosine - second * sine, second * cosine + first * sine], axis=0
+        )
+
+    def rotate_back(turned):
+        first = turned[:half]
+        second = turned[half:]
+        return jnp.stack(
+            [first * cosine + second * sine, second * cosine - first * sine], axis=0
+        )
+
+    q_parts = q_parts.astype(f32)
+    k_parts = k_parts.astype(f32)
+    q = (rotate(q_parts[0], q_parts[1]) * (score_scale * log2_e)).astype(bf16)
+    k = rotate(k_parts[0], k_parts[1]).astype(bf16)
+    v = v_parts.reshape(HEAD_SIZE, length)
+    mixed, prob = heads_forward(q, k, v, step)
+    mixed_send = mixed.astype(bf16).reshape(2, half, count, seq_rows).transpose(2, 0, 1, 3)
+    mixed_low = all_to_all(mixed_send.reshape(2 * count, half, seq_rows), ("d", "y"))
+    mixed_low = mixed_low.reshape(count, 2, half, seq_rows).transpose(0, 2, 1, 3)
+    mixed_low = mixed_low.reshape(count * half, 2 * seq_rows)
+    branch = dot_at(mixed_low, out_weight, 0, 0).reshape(2, 2, rows, width)
+    middle = inputs + own_rows_sum(branch)
+
+    r2 = inverse_rms(middle)
+    n2_own = middle * r2
+    n2 = rows_of_group(n2_own.astype(bf16)).reshape(2 * seq_rows, width)
+    both = dot_at(n2, pair_weight, 1, 0)
+    gate = both[:, : count * ff_own]
+    upper = both[:, count * ff_own :]
+    sigma = jax.nn.sigmoid(gate)
+    silu = gate * sigma
+    hidden = (silu * upper).astype(bf16)
+    d_hidden = dot_at(d_out, down_weight, 1, 1)
+    d_gate = (d_hidden * upper * (sigma + silu * (1.0 - sigma))).astype(bf16)
+    d_upper = (d_hidden * silu).astype(bf16)
+    d_both = jnp.concatenate([d_gate, d_upper], axis=1)
+    d_normed2 = own_rows_sum(dot_at(d_both, pair_weight, 1, 1).reshape(2, 2, rows, width))
+    incoming = cotangent[0].astype(f32)
+    d_middle = incoming + r2 * (
+        d_normed2 - n2_own * jnp.mean(d_normed2 * n2_own, axis=-1, keepdims=True)
+    )
+    grad_down = dot_at(hidden, d_out, 0, 0).astype(bf16).reshape(count, ff_own, width)
+    grad_both = dot_at(n2, d_both, 0, 0).astype(bf16).reshape(count, group, 2 * count * ff_own)
+    owned_down, owned_both = ring_scatter([grad_down, grad_both], count)
+    result = middle + own_rows_sum(dot_at(hidden, down_weight, 1, 0).reshape(2, 2, rows, width))
+
+    d_mid = rows_of_group(d_middle.astype(bf16)).reshape(2 * seq_rows, width)
+    d_mixed = dot_at(out_weight, d_mid, 1, 1).astype(bf16)
+    d_mixed = d_mixed.reshape(count, half, 2, seq_rows).transpose(0, 2, 1, 3)
+    d_mixed = all_to_all(d_mixed.reshape(2 * count, half, seq_rows), ("d", "y"))
+    d_mixed = d_mixed.reshape(count, 2, half, seq_rows).transpose(1, 2, 0, 3)
+    d_mixed = d_mixed.reshape(HEAD_SIZE, length)
+    d_q, d_k, d_v = heads_backward(q, k, v, prob, mixed, d_mixed, step)
+    core = lax.axis_index("core")
+    d_kv = jnp.stack([rotate_back(d_k), d_v.reshape(2, half, length)], axis=1)
+    away = lax.dynamic_index_in_dim(d_kv, 1 - core, 0, False).astype(bf16)
+    kept = lax.dynamic_index_in_dim(d_kv, core, 0, False)
+    d_kv = (kept + swap(away, "core").astype(f32)).astype(bf16)
+    d_kv = d_kv.reshape(2, 2, quarter, count, seq_rows).transpose(3, 1, 0, 2, 4)
+    d_kv = d_kv.reshape(count, 2, half, seq_rows)
+    d_q = rotate_back(d_q).astype(bf16).reshape(2, half, count, seq_rows).transpose(2, 0, 1, 3)
+    d_qkv = jnp.concatenate([d_q, d_kv], axis=2).reshape(2 * count, HEAD_SIZE, seq_rows)
+    d_qkv = all_to_all(d_qkv, ("d", "y")).reshape(count, 2, HEAD_SIZE, seq_rows)
+    d_qkv = d_qkv.transpose(0, 2, 1, 3).reshape(count * HEAD_SIZE, 2 * seq_rows)
+    grad_out = dot_at(mixed_low, d_mid, 1, 0).astype(bf16).reshape(count, own, width)
+    grad_qkv = dot_at(n1, d_qkv, 0, 1).astype(bf16).reshape(count, group, count * HEAD_SIZE)
+    grad_out, grad_qkv, owned_down, owned_both = lax.optimization_barrier(
+        (grad_out, grad_qkv, owned_down, owned_both)
+    )
+    owned_out, owned_qkv = ring_scatter([grad_out, grad_qkv], count)
+    d_normed1 = own_rows_sum(dot_at(d_qkv, qkv_weight, 0, 1).reshape(2, 2, rows, width))
+    n1_wide = inputs * r1
+    input_grad = d_middle + r1 * (
+        d_normed1 - n1_wide * jnp.mean(d_normed1 * n1_wide, axis=-1, keepdims=True)
+    )
+
+    own_both = all_to_all(owned_both.astype(bf16).reshape(4, own, -1), ("core", "y")).astype(f32)
+    own_both = own_both.reshape(4, own, 2, count, ff_own).transpose(2, 1, 3, 0, 4)
+    own_gate, own_up = own_both.reshape(2, own, 4 * count * ff_own)
+    owned_gain2 = jnp.sum(own_gate * w_gate.astype(f32), axis=1) + jnp.sum(
+        own_up * w_up.astype(f32), axis=1
+    )
+    own_qkv = all_to_all(owned_qkv.astype(bf16).reshape(4, own, -1), ("core", "y")).astype(f32)
+    own_qkv = own_qkv.reshape(4, own, count, HEAD_SIZE).transpose(1, 2, 0, 3)
+    own_query = own_qkv[..., :half].reshape(own, -1)
+    own_key = own_qkv[..., half : half + quarter].reshape(own, -1)
+    own_value = own_qkv[..., half + quarter :].reshape(own, -1)
+    owned_gain1 = (
+        jnp.sum(own_query * w_query.astype(f32), axis=1)
+        + jnp.sum(own_key * key_weight.astype(f32), axis=1)
+        + jnp.sum(own_value * value_weight.astype(f32), axis=1)
+    )
+    return (
+        result.astype(bf16)[None],
+        input_grad[None],
+        owned_gain1,
+        gain1 * own_query,
+        gain1 * own_key,
+        gain1 * own_value,
+        owned_out,
+        owned_gain2,
+        gain2 * own_gate,
+        gain2 * own_up,
+        owned_down,
+    )
+
+
+def by_heads(mesh):
+    count = mesh.shape["ctx"] // 2
+    parts = Mesh(mesh.devices.reshape(count, 2, 2), ("d", "core", "y"))
+    owner = ("d", "core", "y")
+    row_spec = P("y", ("d", "core"), None)
+    in_specs = (row_spec, row_spec) + (P(owner),) * 9
+    out_specs = (row_spec, row_spec) + (P(owner),) * 9
+    return jax.shard_map(
+        functools.partial(head_layer, count),
+        mesh=parts,
+        in_specs=in_specs,
+        out_specs=out_specs,
+        check_vma=False,
+    )
+
+
 def solution(mesh):
     in_specs = (
         P("fsdp", "ctx", None),
@@ -339,4 +751,6 @@
         P(("ctx", "fsdp"), None),
         P(("ctx", "fsdp"), None),
     )
+    if mesh.shape["ctx"] == QUERY_HEADS and mesh.shape["fsdp"] == 2:
+        return by_heads(mesh)
     return jax.shard_map(local, mesh=mesh, in_specs=in_specs, out_specs=out_specs, check_vma=False)

time: 2220 us -> 627 us (0.28)
  the two profiles are of different devices: /device:TPU:10 before, /device:TPU:0 now
where the time goes in v1:
time: 627 us; the launch traced here: 616 us
  waiting for transfers between devices  163 us (26%)
  starting transfers between devices  145 us (23%)
  local copies, waits for them, and re-layouts  88.5 us (14%)
  other arithmetic  55.8 us (9%)
  between operations  51.8 us (8%)
  blocking collectives  50.1 us (8%)
  matrix products  48.7 us (8%)
  Pallas kernels  13.2 us (2%)
    ppermute x12, waiting for transfers between devices, ring_gather(): ahead = [lax.ppermute(a, 'd', forward) for a in ahead]  51.8 us
    dot_general x12, matrix products, dot_at(): lax.dot_general(left, right, (((left_dim,), (right_dim,)), ((), ())), pre...  48.7 us
    all_gather x4, blocking collectives, rows_of_group(): pair = lax.all_gather(own, 'y', axis=0)  47.5 us
    all_to_all x8, starting transfers between devices, all_to_all(): return lax.all_to_all(values, axes, 0, 0, tiled=True)  38.9 us
    ppermute x28, starting transfers between devices, ring_scatter(): ahead = [lax.ppermute(a, 'd', forward) for a in ahead]  37.9 us
    convert_element_type x24, other arithmetic, ring_scatter(): (b.astype(f32) + part(t, place + 1 + hop, 1).astype(f32)).astype(kind)  28.8 us
    ppermute x28, waiting for transfers between devices, ring_scatter(): ahead = [lax.ppermute(a, 'd', forward) for a in ahead]  28.4 us
    ppermute x28, waiting for transfers between devices, ring_scatter(): behind = [lax.ppermute(b, 'd', backward) for b in behind]  26.7 us
  transfers between devices with their start and end apart: 109, of which 42 were waited for; matrix products, arithmetic and copies ran while one was open for 22% of the time, Pallas kernels for 2%

profile of v1, /device:TPU:0, one launch (start us, length us, event | category | flops | bytes accessed | tf_op | source)
XLA Modules:
  0.0 616.1 jit_solution(16429027168883264169)
XLA Ops:
  12.7 4.2 all-to-all-start.1
  19.6 4.3 all-to-all-done.1
  29.9 17.6 %all_gather.49 = bf16[2,128,1536]{2,1,0:T(8,128)(2,1)} all-gather(bf16[1,128,1536]{2,1,0:T(8,128)(2,1)S(1)} %fusion.20), channel_id=1, replica_groups=mesh['d'=8,'core'=2,'y'=2] {'y'}, dimensions={0}, use_global_device_ids=true | all-gather | bytes 1179648 | tf_op jit(solution)/shard_map/all_gather | solution.py:499
  77.6 4.9 collective-permute-done.2
  86.1 5.3 collective-permute-done.4
  107.4 15.0 %collective-permute-done.9 = bf16[48,1536]{1,0:T(8,128)(2,1)} collective-permute-done((bf16[48,1536]{1,0:T(8,128)(2,1)}, bf16[48,1536]{1,0:T(8,128)(2,1)}, u32[]{:S(2)}, u32[]{:S(2)}) %collective-permute-start.9) | collective-permute-done | bytes 147488 | tf_op jit(solution)/shard_map/feed_forward_weights/ppermute | solution.py:442
  122.8 4.4 convolution_convert_fusion.4
  130.5 5.2 all-to-all-start.2
  142.7 20.8 %collective-permute-done.15 = bf16[48,1536]{1,0:T(8,128)(2,1)} collective-permute-done((bf16[48,1536]{1,0:T(8,128)(2,1)}, bf16[48,1536]{1,0:T(8,128)(2,1)}, u32[]{:S(2)}, u32[]{:S(2)}) %collective-permute-start.15) | collective-permute-done | bytes 147488 | tf_op jit(solution)/shard_map/feed_forward_weights/ppermute | solution.py:442
  168.1 7.6 %collective-permute-done.19 = bf16[128,1536]{1,0:T(8,128)(2,1)} collective-permute-done((bf16[128,1536]{1,0:T(8,128)(2,1)}, bf16[128,1536]{1,0:T(8,128)(2,1)}, u32[]{:S(2)}, u32[]{:S(2)}) %collective-permute-start.19) | collective-permute-done | bytes 393248 | tf_op jit(solution)/shard_map/feed_forward_weights/ppermute | solution.py:443
  175.6 3.9 collective-permute-start.20
  191.5 5.9 collective-permute-done.21
  197.6 7.3 %heads_forward.1 = (f32[96,2048]{1,0:T(8,128)S(1)}, bf16[9216,256]{1,0:T(8,128)(2,1)S(1)}) custom-call(bf16[96,2048]{1,0:T(8,128)(2,1)S(1)} %fusion.31.q_ref, bf16[96,2048]{1,0:T(8,128)(2,1)S(1)} %pad_maximum_fusion.6.k_ref, bf16[96,2048]{1,0:T(8,128)(2,1)S(1)} %bitcast.572), custom_call_target="tpu_custom_call" | custom-call | flops 905969664 | bytes 4718592 | tf_op jit(solution)/shard_map/heads_forward/pallas_call | solution.py:389
  208.0 6.3 %all-to-all-start.3 = ((bf16[16,48,256]{2,1,0:T(8,128)(2,1)}), bf16[16,48,256]{2,1,0:T(8,128)(2,1)}, u32[]{:S(2)}, u32[]{:S(2)}) async-start(bf16[16,48,256]{2,1,0:T(8,128)(2,1)} %bitcast.622), calls=%async_computation.3 | async-start | bytes 786432 | tf_op jit(solution)/shard_map/all_to_all | solution.py:515
  240.2 9.8 %collective-permute-done.29 = bf16[128,1536]{1,0:T(8,128)(2,1)} collective-permute-done((bf16[128,1536]{1,0:T(8,128)(2,1)S(1)}, bf16[128,1536]{1,0:T(8,128)(2,1)}, u32[]{:S(2)}, u32[]{:S(2)}) %collective-permute-start.29) | collective-permute-done | bytes 393248 | tf_op jit(solution)/shard_map/ppermute | solution.py:495
  251.6 11.1 %all-gather.2 = bf16[256,1536]{1,0:T(8,128)(2,1)} all-gather(bf16[128,1536]{1,0:T(8,128)(2,1)S(1)} %multiply_convert_fusion.1), channel_id=4, replica_groups=mesh['d'=8,'core'=2,'y'=2] {'y'}, dimensions={0}, use_global_device_ids=true | all-gather | bytes 1179648 | tf_op jit(solution)/shard_map/all_gather | solution.py:499
  262.8 10.2 %all_gather.58 = bf16[2,128,1536]{2,1,0:T(8,128)(2,1)} all-gather(bf16[1,128,1536]{2,1,0:T(8,128)(2,1)S(1)} %copy-done.21), channel_id=1, replica_groups=mesh['d'=8,'core'=2,'y'=2] {'y'}, dimensions={0}, use_global_device_ids=true | all-gather | bytes 1179648 | tf_op jit(solution)/shard_map/all_gather | solution.py:499
  325.9 8.7 %fusion.108 = f32[512,2048]{1,0:T(8,128)} fusion(bf16[512,1536]{1,0:T(8,128)(2,1)} %bitcast.663, bf16[1536,2048]{1,0:T(8,128)(2,1)} %bitcast.75), kind=kOutput, calls=%fused_computation.291 | convolution fusion | flops 3221225472 | bytes 12058624 | tf_op jit(solution)/shard_map/dot_general | solution.py:329
  334.5 6.0 fusion.3
  342.0 3.8 convolution_convert_fusion
  345.8 8.1 %fusion.110 = f32[2,2,128,1536]{3,2,1,0:T(8,128)S(1)} fusion(bf16[2,2,128,2048]{3,2,1,0:T(8,128)(2,1)S(1)} %bitcast.618, bf16[1536,2048,1,1]{1,0,3,2:T(8,128)(2,1)} %bitcast.99), kind=kOutput, calls=%fused_computation.293 | convolution fusion | flops 3221225472 | bytes 11534336 | tf_op jit(solution)/shard_map/dot_general | solution.py:329
  360.4 3.7 fusion.109
  367.0 4.8 collective-permute-done.42
  383.8 5.0 collective-permute-done.46
  399.1 3.6 collective-permute-done.50
  411.3 8.5 %all-gather.5 = bf16[256,1536]{1,0:T(8,128)(2,1)} all-gather(bf16[128,1536]{1,0:T(8,128)(2,1)S(1)} %get-tuple-element.238), channel_id=7, replica_groups=mesh['d'=8,'core'=2,'y'=2] {'y'}, dimensions={0}, use_global_device_ids=true | all-gather | bytes 1179648 | tf_op jit(solution)/shard_map/all_gather | solution.py:499
  443.3 7.0 %all-to-all-start.4 = ((bf16[16,48,256]{2,1,0:T(8,128)(2,1)}), bf16[16,48,256]{2,1,0:T(8,128)(2,1)S(1)}, u32[]{:S(2)}, u32[]{:S(2)}) async-start(bf16[16,48,256]{2,1,0:T(8,128)(2,1)} %bitcast.107), calls=%async_computation.4 | async-start | bytes 786432 | tf_op jit(solution)/shard_map/all_to_all | solution.py:515
  466.7 5.9 heads_backward.1
  481.3 5.7 all-to-all-start.5
  490.2 7.2 %collective-permute-done.68 = bf16[96,2048]{1,0:T(8,128)(2,1)S(1)} collective-permute-done((bf16[96,2048]{1,0:T(8,128)(2,1)S(1)}, bf16[96,2048]{1,0:T(8,128)(2,1)S(1)}, u32[]{:S(2)}, u32[]{:S(2)}) %collective-permute-start.68) | collective-permute-done | bytes 393248 | tf_op jit(solution)/shard_map/ppermute | solution.py:480
  501.9 7.8 %all-to-all-done.5 = bf16[16,96,256]{2,1,0:T(8,128)(2,1)S(1)} async-done(((bf16[16,96,256]{2,1,0:T(8,128)(2,1)}), bf16[16,96,256]{2,1,0:T(8,128)(2,1)S(1)}, u32[]{:S(2)}, u32[]{:S(2)}) %all-to-all-start.5) | async-done | bytes 786464 | tf_op jit(solution)/shard_map/all_to_all | solution.py:515
  561.8 4.1 all-to-all-done.7
  (482 shorter events, 330.4 us)
Async XLA Ops:
  23.9 75.9 %all-to-all-start = ((bf16[4,48,2048]{2,1,0:T(8,128)(2,1)}), bf16[4,48,2048]{2,1,0:T(8,128)(2,1)S(1)}, u32[]{:S(2)}, u32[]{:S(2)}) async-start(bf16[4,48,2048]{2,1,0:T(8,128)(2,1)} %reshape.447), calls=%async_computation | async-start | bytes 1572864 | tf_op jit(solution)/shard_map/feed_forward_weights/all_to_all | solution.py:515
  27.4 95.4 %all-gather.12.cloned.1.call-start = ((), (), s32[]{:S(2)}) async-start(), calls=%async_computation.8 | async-start | bytes 2359296 | tf_op jit(solution)/shard_map/all_gather | solution.py:500
  27.4 45.6 %collective-permute-start = (bf16[192,768]{1,0:T(8,128)(2,1)}, bf16[192,768]{1,0:T(8,128)(2,1)}, u32[]{:S(2)}, u32[]{:S(2)}) collective-permute-start(bf16[192,768]{1,0:T(8,128)(2,1)} %bitcast.10), channel_id=1, source_target_pairs={{0,8},{8,16},{16,24},{24,28},{28,20},{20,12},{12,4},{4,0},{1,9},{9... | collective-permute-start | bytes 884744 | tf_op jit(solution)/shard_map/attention_weights/ppermute | solution.py:442
  29.9 43.2 %collective-permute-start.1 = (bf16[192,768]{1,0:T(8,128)(2,1)}, bf16[192,768]{1,0:T(8,128)(2,1)}, u32[]{:S(2)}, u32[]{:S(2)}) collective-permute-start(bf16[192,768]{1,0:T(8,128)(2,1)} %bitcast.10), channel_id=1, source_target_pairs={{8,0},{16,8},{24,16},{28,24},{20,28},{12,20},{4,12},{0,4},{9,1},{1... | collective-permute-start | bytes 884744 | tf_op jit(solution)/shard_map/attention_weights/ppermute | solution.py:443
  99.8 35.9 %collective-permute-start.8 = (bf16[192,2048]{1,0:T(8,128)(2,1)S(1)}, bf16[192,2048]{1,0:T(8,128)(2,1)}, u32[]{:S(2)}, u32[]{:S(2)}) collective-permute-start(bf16[192,2048]{1,0:T(8,128)(2,1)S(1)} %bitcast.588), channel_id=1, source_target_pairs={{0,8},{8,16},{16,24},{24,28},{28,20},{20,12},{12,4},{4,0},{1,9},{9... | collective-permute-start | bytes 2359304 | tf_op jit(solution)/shard_map/feed_forward_weights/ppermute | solution.py:442
  102.3 33.5 %collective-permute-start.11 = (bf16[192,2048]{1,0:T(8,128)(2,1)S(1)}, bf16[192,2048]{1,0:T(8,128)(2,1)}, u32[]{:S(2)}, u32[]{:S(2)}) collective-permute-start(bf16[192,2048]{1,0:T(8,128)(2,1)S(1)} %bitcast.589), channel_id=1, source_target_pairs={{8,0},{16,8},{24,16},{28,24},{20,28},{12,20},{4,12},{0,4},{9,1},{1... | collective-permute-start | bytes 2359304 | tf_op jit(solution)/shard_map/feed_forward_weights/ppermute | solution.py:443
  102.3 20.1 %collective-permute-start.9 = (bf16[48,1536]{1,0:T(8,128)(2,1)}, bf16[48,1536]{1,0:T(8,128)(2,1)}, u32[]{:S(2)}, u32[]{:S(2)}) collective-permute-start(bf16[48,1536]{1,0:T(8,128)(2,1)} %param.21), channel_id=1, source_target_pairs={{0,8},{8,16},{16,24},{24,28},{28,20},{20,12},{12,4},{4,0},{1,9},{9... | collective-permute-start | bytes 442376 | tf_op jit(solution)/shard_map/feed_forward_weights/ppermute | solution.py:442
  104.3 31.4 %collective-permute-start.12 = (bf16[48,1536]{1,0:T(8,128)(2,1)}, bf16[48,1536]{1,0:T(8,128)(2,1)}, u32[]{:S(2)}, u32[]{:S(2)}) collective-permute-start(bf16[48,1536]{1,0:T(8,128)(2,1)} %param.21), channel_id=1, source_target_pairs={{8,0},{16,8},{24,16},{28,24},{20,28},{12,20},{4,12},{0,4},{9,1},{1... | collective-permute-start | bytes 442376 | tf_op jit(solution)/shard_map/feed_forward_weights/ppermute | solution.py:443
  105.3 30.4 %collective-permute-start.10 = (bf16[128,1536]{1,0:T(8,128)(2,1)}, bf16[128,1536]{1,0:T(8,128)(2,1)S(1)}, u32[]{:S(2)}, u32[]{:S(2)}) collective-permute-start(bf16[128,1536]{1,0:T(8,128)(2,1)} %param.25), channel_id=1, source_target_pairs={{0,8},{8,16},{16,24},{24,28},{28,20},{20,12},{12,4},{4,0},{1,9},{9... | collective-permute-start | bytes 1179656 | tf_op jit(solution)/shard_map/feed_forward_weights/ppermute | solution.py:442
  130.5 55.3 %all-to-all-start.2 = ((bf16[16,96,256]{2,1,0:T(8,128)(2,1)}), bf16[16,96,256]{2,1,0:T(8,128)(2,1)S(1)}, u32[]{:S(2)}, u32[]{:S(2)}) async-start(bf16[16,96,256]{2,1,0:T(8,128)(2,1)} %bitcast.36), calls=%async_computation.2 | async-start | bytes 1572864 | tf_op jit(solution)/shard_map/all_to_all | solution.py:515
  135.7 39.9 %collective-permute-start.14 = (bf16[192,2048]{1,0:T(8,128)(2,1)}, bf16[192,2048]{1,0:T(8,128)(2,1)}, u32[]{:S(2)}, u32[]{:S(2)}) collective-permute-start(bf16[192,2048]{1,0:T(8,128)(2,1)} %collective-permute-done.8), channel_id=1, source_target_pairs={{0,8},{8,16},{16,24},{24,28},{28,20},{20,12},{12,4},{4,0},{1,9},{9... | collective-permute-start | bytes 2359304 | tf_op jit(solution)/shard_map/feed_forward_weights/ppermute | solution.py:442
  137.7 25.8 %collective-permute-start.15 = (bf16[48,1536]{1,0:T(8,128)(2,1)}, bf16[48,1536]{1,0:T(8,128)(2,1)}, u32[]{:S(2)}, u32[]{:S(2)}) collective-permute-start(bf16[48,1536]{1,0:T(8,128)(2,1)} %collective-permute-done.9), channel_id=1, source_target_pairs={{0,8},{8,16},{16,24},{24,28},{28,20},{20,12},{12,4},{4,0},{1,9},{9... | collective-permute-start | bytes 442376 | tf_op jit(solution)/shard_map/feed_forward_weights/ppermute | solution.py:442
  139.2 36.5 %collective-permute-start.17 = (bf16[192,2048]{1,0:T(8,128)(2,1)}, bf16[192,2048]{1,0:T(8,128)(2,1)}, u32[]{:S(2)}, u32[]{:S(2)}) collective-permute-start(bf16[192,2048]{1,0:T(8,128)(2,1)} %collective-permute-done.11), channel_id=1, source_target_pairs={{8,0},{16,8},{24,16},{28,24},{20,28},{12,20},{4,12},{0,4},{9,1},{1... | collective-permute-start | bytes 2359304 | tf_op jit(solution)/shard_map/feed_forward_weights/ppermute | solution.py:443
  140.7 27.4 %collective-permute-start.16 = (bf16[128,1536]{1,0:T(8,128)(2,1)S(1)}, bf16[128,1536]{1,0:T(8,128)(2,1)}, u32[]{:S(2)}, u32[]{:S(2)}) collective-permute-start(bf16[128,1536]{1,0:T(8,128)(2,1)S(1)} %collective-permute-done.10), channel_id=1, source_target_pairs={{0,8},{8,16},{16,24},{24,28},{28,20},{20,12},{12,4},{4,0},{1,9},{9... | collective-permute-start | bytes 1179656 | tf_op jit(solution)/shard_map/feed_forward_weights/ppermute | solution.py:442
  142.2 25.9 %collective-permute-start.18 = (bf16[48,1536]{1,0:T(8,128)(2,1)}, bf16[48,1536]{1,0:T(8,128)(2,1)}, u32[]{:S(2)}, u32[]{:S(2)}) collective-permute-start(bf16[48,1536]{1,0:T(8,128)(2,1)} %collective-permute-done.12), channel_id=1, source_target_pairs={{8,0},{16,8},{24,16},{28,24},{20,28},{12,20},{4,12},{0,4},{9,1},{1... | collective-permute-start | bytes 442376 | tf_op jit(solution)/shard_map/feed_forward_weights/ppermute | solution.py:443
  175.6 38.8 %collective-permute-start.20 = (bf16[192,2048]{1,0:T(8,128)(2,1)}, bf16[192,2048]{1,0:T(8,128)(2,1)}, u32[]{:S(2)}, u32[]{:S(2)}) collective-permute-start(bf16[192,2048]{1,0:T(8,128)(2,1)} %collective-permute-done.14), channel_id=1, source_target_pairs={{0,8},{8,16},{16,24},{24,28},{28,20},{20,12},{12,4},{4,0},{1,9},{9... | collective-permute-start | bytes 2359304 | tf_op jit(solution)/shard_map/feed_forward_weights/ppermute | solution.py:442
  181.9 32.6 %collective-permute-start.22 = (bf16[128,1536]{1,0:T(8,128)(2,1)}, bf16[128,1536]{1,0:T(8,128)(2,1)}, u32[]{:S(2)}, u32[]{:S(2)}) collective-permute-start(bf16[128,1536]{1,0:T(8,128)(2,1)} %collective-permute-done.16), channel_id=1, source_target_pairs={{0,8},{8,16},{16,24},{24,28},{28,20},{20,12},{12,4},{4,0},{1,9},{9... | collective-permute-start | bytes 1179656 | tf_op jit(solution)/shard_map/feed_forward_weights/ppermute | solution.py:442
  181.9 32.5 %collective-permute-start.23 = (bf16[192,2048]{1,0:T(8,128)(2,1)}, bf16[192,2048]{1,0:T(8,128)(2,1)}, u32[]{:S(2)}, u32[]{:S(2)}) collective-permute-start(bf16[192,2048]{1,0:T(8,128)(2,1)} %collective-permute-done.17), channel_id=1, source_target_pairs={{8,0},{16,8},{24,16},{28,24},{20,28},{12,20},{4,12},{0,4},{9,1},{1... | collective-permute-start | bytes 2359304 | tf_op jit(solution)/shard_map/feed_forward_weights/ppermute | solution.py:443
  183.9 30.6 %collective-permute-start.25 = (bf16[128,1536]{1,0:T(8,128)(2,1)}, bf16[128,1536]{1,0:T(8,128)(2,1)}, u32[]{:S(2)}, u32[]{:S(2)}) collective-permute-start(bf16[128,1536]{1,0:T(8,128)(2,1)} %collective-permute-done.19), channel_id=1, source_target_pairs={{8,0},{16,8},{24,16},{28,24},{20,28},{12,20},{4,12},{0,4},{9,1},{1... | collective-permute-start | bytes 1179656 | tf_op jit(solution)/shard_map/feed_forward_weights/ppermute | solution.py:443
  214.4 111.5 %all-gather.14.cloned.1.call-start = ((), (), s32[]{:S(2)}) async-start(), calls=%async_computation.9 | async-start | bytes 2359296 | tf_op jit(solution)/shard_map/all_gather | solution.py:500
  262.7 71.8 %all-gather.16.cloned.1.call-start = ((), (), s32[]{:S(2)}) async-start(), calls=%async_computation.10 | async-start | bytes 2359296 | tf_op jit(solution)/shard_map/all_gather | solution.py:500
  273.0 165.5 %all-gather.18.cloned.1.call-start = ((), (), s32[]{:S(2)}) async-start(), calls=%async_computation.11 | async-start | bytes 2359296 | tf_op jit(solution)/shard_map/all_gather | solution.py:500
  354.0 23.2 %collective-permute-start.36 = (bf16[2,128,1536]{2,1,0:T(8,128)(2,1)S(1)}, bf16[2,128,1536]{2,1,0:T(8,128)(2,1)S(1)}, u32[]{:S(2)}, u32[]{:S(2)}) collective-permute-start(bf16[2,128,1536]{2,1,0:T(8,128)(2,1)S(1)} %fusion.22), channel_id=1, source_target_pairs={{0,2},{2,0},{1,3},{3,1},{4,6},{6,4},{5,7},{7,5},{8,10},{10,8},{9,1... | collective-permute-start | bytes 2359304 | tf_op jit(solution)/shard_map/ppermute | solution.py:495
  364.2 28.4 %collective-permute-start.34 = (bf16[2,128,1536]{2,1,0:T(8,128)(2,1)S(1)}, bf16[2,128,1536]{2,1,0:T(8,128)(2,1)S(1)}, u32[]{:S(2)}, u32[]{:S(2)}) collective-permute-start(bf16[2,128,1536]{2,1,0:T(8,128)(2,1)S(1)} %fusion.23), channel_id=1, source_target_pairs={{0,2},{2,0},{1,3},{3,1},{4,6},{6,4},{5,7},{7,5},{8,10},{10,8},{9,1... | collective-permute-start | bytes 2359304 | tf_op jit(solution)/shard_map/ppermute | solution.py:495
  382.3 26.6 %collective-permute-start.37 = (bf16[128,1536]{1,0:T(8,128)(2,1)S(1)}, bf16[128,1536]{1,0:T(8,128)(2,1)S(1)}, u32[]{:S(2)}, u32[]{:S(2)}) collective-permute-start(bf16[128,1536]{1,0:T(8,128)(2,1)S(1)} %fusion.52), channel_id=1, source_target_pairs={{0,1},{1,0},{2,3},{3,2},{4,5},{5,4},{6,7},{7,6},{8,9},{9,8},{10,11... | collective-permute-start | bytes 1179656 | tf_op jit(solution)/shard_map/ppermute | solution.py:495
  436.5 23.8 %collective-permute-start.62 = (bf16[96,2048]{1,0:T(8,128)(2,1)}, bf16[96,2048]{1,0:T(8,128)(2,1)}, u32[]{:S(2)}, u32[]{:S(2)}) collective-permute-start(bf16[96,2048]{1,0:T(8,128)(2,1)} %get-tuple-element.247), channel_id=1, source_target_pairs={{0,8},{8,16},{16,24},{24,28},{28,20},{20,12},{12,4},{4,0},{1,9},{9... | collective-permute-start | bytes 1179656 | tf_op jit(solution)/shard_map/ppermute | solution.py:479
  438.2 22.1 %collective-permute-start.64 = (bf16[96,2048]{1,0:T(8,128)(2,1)}, bf16[96,2048]{1,0:T(8,128)(2,1)}, u32[]{:S(2)}, u32[]{:S(2)}) collective-permute-start(bf16[96,2048]{1,0:T(8,128)(2,1)} %get-tuple-element.246), channel_id=1, source_target_pairs={{8,0},{16,8},{24,16},{28,24},{20,28},{12,20},{4,12},{0,4},{9,1},{1... | collective-permute-start | bytes 1179656 | tf_op jit(solution)/shard_map/ppermute | solution.py:480
  443.3 20.7 %all-to-all-start.4 = ((bf16[16,48,256]{2,1,0:T(8,128)(2,1)}), bf16[16,48,256]{2,1,0:T(8,128)(2,1)S(1)}, u32[]{:S(2)}, u32[]{:S(2)}) async-start(bf16[16,48,256]{2,1,0:T(8,128)(2,1)} %bitcast.107), calls=%async_computation.4 | async-start | bytes 786432 | tf_op jit(solution)/shard_map/all_to_all | solution.py:515
  462.1 28.1 %collective-permute-start.65 = (bf16[64,1536]{1,0:T(8,128)(2,1)}, bf16[64,1536]{1,0:T(8,128)(2,1)S(1)}, u32[]{:S(2)}, u32[]{:S(2)}) collective-permute-start(bf16[64,1536]{1,0:T(8,128)(2,1)} %get-tuple-element.264), channel_id=1, source_target_pairs={{0,8},{8,16},{16,24},{24,28},{28,20},{20,12},{12,4},{4,0},{1,9},{9... | collective-permute-start | bytes 589832 | tf_op jit(solution)/shard_map/ppermute | solution.py:479
  478.8 18.6 %collective-permute-start.68 = (bf16[96,2048]{1,0:T(8,128)(2,1)S(1)}, bf16[96,2048]{1,0:T(8,128)(2,1)S(1)}, u32[]{:S(2)}, u32[]{:S(2)}) collective-permute-start(bf16[96,2048]{1,0:T(8,128)(2,1)S(1)} %get-tuple-element.244), channel_id=1, source_target_pairs={{8,0},{16,8},{24,16},{28,24},{20,28},{12,20},{4,12},{0,4},{9,1},{1... | collective-permute-start | bytes 1179656 | tf_op jit(solution)/shard_map/ppermute | solution.py:480
  481.3 28.4 %all-to-all-start.5 = ((bf16[16,96,256]{2,1,0:T(8,128)(2,1)}), bf16[16,96,256]{2,1,0:T(8,128)(2,1)S(1)}, u32[]{:S(2)}, u32[]{:S(2)}) async-start(bf16[16,96,256]{2,1,0:T(8,128)(2,1)} %pad_maximum_fusion.3), calls=%async_computation.5 | async-start | bytes 1572864 | tf_op jit(solution)/shard_map/all_to_all | solution.py:515
  550.9 25.6 %collective-permute-start.39 = (bf16[2,128,1536]{2,1,0:T(8,128)(2,1)}, bf16[2,128,1536]{2,1,0:T(8,128)(2,1)}, u32[]{:S(2)}, u32[]{:S(2)}) collective-permute-start(bf16[2,128,1536]{2,1,0:T(8,128)(2,1)} %fusion.24), channel_id=1, source_target_pairs={{0,2},{2,0},{1,3},{3,1},{4,6},{6,4},{5,7},{7,5},{8,10},{10,8},{9,1... | collective-permute-start | bytes 2359304 | tf_op jit(solution)/shard_map/ppermute | solution.py:495
  (118 other events, 1277.8 us)
Sparse Core Ops, SparseCore 0:
  47.7 10.9 all-gather.11
  262.9 9.7 all-gather.13
  274.2 10.9 all-gather.15
  420.0 10.6 all-gather.17

commit v2 on v1

--- a/solution.py
+++ b/solution.py
@@ -418,77 +418,545 @@
     )(q, k, v, prob, mixed, d_mixed)
 
 
+def on_chip(kernel, out_shape, args, flops, blocks=(), scratch=(), name=None):
+    moved = sum(a.size * a.dtype.itemsize for a in list(args) + list(blocks))
+    moved += sum(o.size * o.dtype.itemsize for o in out_shape)
+    near = pl.BlockSpec(memory_space=pltpu.VMEM)
+    return pl.pallas_call(
+        kernel,
+        out_shape=tuple(out_shape),
+        in_specs=[pl.BlockSpec(memory_space=pltpu.SMEM)]
+        + [near] * (len(args) - 1)
+        + [pl.BlockSpec(memory_space=pltpu.HBM)] * len(blocks),
+        out_specs=(near,) * len(out_shape),
+        scratch_shapes=scratch,
+        compiler_params=pltpu.CompilerParams(vmem_limit_bytes=48 * 2**20),
+        cost_estimate=pl.CostEstimate(flops=flops, bytes_accessed=moved, transcendentals=0),
+        name=name,
+    )(*args, *blocks)
+
+
+def like(dtype, *shape):
+    return jax.ShapeDtypeStruct(shape, dtype)
+
+
+def block_copies(at_ref, block_refs, whole_ref, sem_ref, first=0):
+    size = whole_ref.shape[0] // len(block_refs)
+    copies = []
+    for k, block_ref in enumerate(block_refs):
+        start = pl.multiple_of(at_ref[k] * size, size)
+        copies.append(
+            pltpu.make_async_copy(
+                block_ref.at[pl.ds(first, size), :], whole_ref.at[pl.ds(start, size), :], sem_ref.at[k]
+            )
+        )
+    return copies
+
+
+def core_rows(at_ref, count, rows, seq, other):
+    core = at_ref[2 * count]
+    start = seq * 2 * rows + (1 - core if other else core) * rows
+    return pl.ds(pl.multiple_of(start, rows), rows)
+
+
+def join_rows(at_ref, count, own_ref, other_ref, whole_ref):
+    rows = own_ref.shape[1]
+    for seq in range(2):
+        whole_ref[core_rows(at_ref, count, rows, seq, False), :] = own_ref[seq]
+        whole_ref[core_rows(at_ref, count, rows, seq, True), :] = other_ref[seq]
+
+
+def part_rows(at_ref, count, whole_ref, kept_ref, away_ref):
+    rows = kept_ref.shape[1]
+    for seq in range(2):
+        kept_ref[seq] = whole_ref[core_rows(at_ref, count, rows, seq, False), :]
+        away_ref[seq] = whole_ref[core_rows(at_ref, count, rows, seq, True), :].astype(bf16)
+
+
+def query_columns_kernel(at_ref, gain_ref, query_ref, key_ref, value_ref, out_ref):
+    gain = gain_ref[...]
+    query = query_ref[...].astype(f32) * gain
+    key = key_ref[...].astype(f32) * gain
+    value = value_ref[...].astype(f32) * gain
+    half = HEAD_SIZE // 2
+    quarter = HEAD_SIZE // 4
+    groups = out_ref.shape[2] // HEAD_SIZE
+    for t in range(4):
+        pieces = []
+        for group in range(groups):
+            place = 4 * group + t
+            pieces.append(query[:, place * half : (place + 1) * half])
+            pieces.append(key[:, place * quarter : (place + 1) * quarter])
+            pieces.append(value[:, place * quarter : (place + 1) * quarter])
+        out_ref[t] = jnp.concatenate(pieces, axis=1).astype(bf16)
+
+
+def query_columns(at, gain, query, key, value):
+    own, width = query.shape
+    (out,) = on_chip(
+        query_columns_kernel,
+        [like(bf16, 4, own, (width + 2 * key.shape[1]) // 4)],
+        [at, gain, query, key, value],
+        own * width,
+        name="query_columns",
+    )
+    return out
+
+
+def pair_columns_kernel(size, at_ref, gain_ref, gate_ref, up_ref, out_ref):
+    gain = gain_ref[...]
+    half = out_ref.shape[2] // 2
+    for t in range(4):
+        for position in range(half // size):
+            columns = pl.ds((4 * position + t) * size, size)
+            for side, ref in enumerate((gate_ref, up_ref)):
+                out_ref[t, :, pl.ds(side * half + position * size, size)] = (
+                    ref[:, columns].astype(f32) * gain
+                ).astype(bf16)
+
+
+def pair_columns(at, gain, gate, up, size):
+    own, ff = gate.shape
+    (out,) = on_chip(
+        functools.partial(pair_columns_kernel, size),
+        [like(bf16, 4, own, ff // 2)],
+        [at, gain, gate, up],
+        own * ff,
+        name="pair_columns",
+    )
+    return out
+
+
+def project_heads_kernel(at_ref, own_ref, other_ref, *refs):
+    blocks, (n_ref, weight_ref, heads_ref, sem_ref) = refs[:-4], refs[-4:]
+    copies = block_copies(at_ref, blocks, weight_ref, sem_ref)
+    for copy in copies:
+        copy.start()
+    join_rows(at_ref, len(blocks), own_ref, other_ref, n_ref)
+    for copy in copies:
+        copy.wait()
+    size, rows = heads_ref.shape[1:]
+    for seq in range(2):
+        part = dot_at(weight_ref[...], n_ref[seq * rows : (seq + 1) * rows, :], 0, 1).astype(bf16)
+        for head in range(heads_ref.shape[0] // 2):
+            heads_ref[2 * head + seq] = part[head * size : (head + 1) * size, :]
+
+
+def project_heads(at, own, other, blocks):
+    count = len(blocks)
+    _, rows, width = own.shape
+    columns = blocks[0].shape[1]
+    return on_chip(
+        project_heads_kernel,
+        [
+            like(bf16, 4 * rows, width),
+            like(bf16, width, columns),
+            like(bf16, 2 * count, columns // count, 2 * rows),
+        ],
+        [at, own, other],
+        8 * rows * width * columns,
+        blocks=blocks,
+        scratch=[pltpu.SemaphoreType.DMA((count,))],
+        name="project_heads",
+    )
+
+
+def join_heads(heads_ref, joined_ref):
+    size, rows = heads_ref.shape[1:]
+    for seq in range(2):
+        for head in range(heads_ref.shape[0] // 2):
+            joined_ref[head * size : (head + 1) * size, seq * rows : (seq + 1) * rows] = heads_ref[
+                2 * head + seq
+            ]
+
+
+def project_out_kernel(first, at_ref, heads_ref, *refs):
+    blocks, (weight_ref, joined_ref, kept_ref, away_ref, out_ref, sem_ref) = refs[:-6], refs[-6:]
+    copies = block_copies(at_ref, blocks, weight_ref, sem_ref, first=first)
+    for copy in copies:
+        copy.start()
+    join_heads(heads_ref, joined_ref)
+    for copy in copies:
+        copy.wait()
+    out_ref[...] = dot_at(joined_ref[...], weight_ref[...], 0, 0)
+    part_rows(at_ref, len(blocks), out_ref, kept_ref, away_ref)
+
+
+def project_out(at, heads, blocks, first):
+    count = len(blocks)
+    own, width = blocks[0].shape
+    own -= first
+    rows = heads.shape[2] // 2
+    return on_chip(
+        functools.partial(project_out_kernel, first),
+        [
+            like(bf16, count * own, width),
+            like(bf16, count * own, 4 * rows),
+            like(f32, 2, rows, width),
+            like(bf16, 2, rows, width),
+        ],
+        [at, heads],
+        8 * rows * width * count * own,
+        blocks=blocks,
+        scratch=[pltpu.VMEM((4 * rows, width), f32), pltpu.SemaphoreType.DMA((count,))],
+        name="project_out",
+    )
+
+
+def hidden_gradient_kernel(at_ref, own_ref, other_ref, *refs):
+    blocks, (d_out_ref, weight_ref, d_hidden_ref, sem_ref) = refs[:-4], refs[-4:]
+    copies = block_copies(at_ref, blocks, weight_ref, sem_ref)
+    for copy in copies:
+        copy.start()
+    join_rows(at_ref, len(blocks), own_ref, other_ref, d_out_ref)
+    for copy in copies:
+        copy.wait()
+    d_hidden_ref[...] = dot_at(d_out_ref[...], weight_ref[...], 1, 1).astype(bf16)
+
+
+def hidden_gradient(at, d_out_own, d_out_other, blocks, own):
+    count = len(blocks)
+    _, rows, width = d_out_own.shape
+    return on_chip(
+        hidden_gradient_kernel,
+        [
+            like(bf16, 4 * rows, width),
+            like(bf16, count * own, width),
+            like(bf16, 4 * rows, count * own),
+        ],
+        [at, d_out_own, d_out_other],
+        8 * rows * width * count * own,
+        blocks=blocks,
+        scratch=[pltpu.SemaphoreType.DMA((count,))],
+        name="hidden_gradient",
+    )
+
+
+def feed_forward_kernel(step, at_ref, own_ref, other_ref, d_hidden_ref, *refs):
+    blocks = refs[:-8]
+    n_ref, hidden_ref, d_both_ref, kept_ref, away_ref, d_n_ref, whole_ref, sem_ref = refs[-8:]
+    ff = hidden_ref.shape[1]
+    copies = block_copies(at_ref, blocks, whole_ref, sem_ref)
+    for copy in copies:
+        copy.start()
+    join_rows(at_ref, len(blocks), own_ref, other_ref, n_ref)
+    for copy in copies:
+        copy.wait()
+    for begin in range(0, n_ref.shape[0], step):
+        rows = slice(begin, begin + step)
+        both = dot_at(n_ref[rows, :], whole_ref[...], 1, 0)
+        gate = both[:, :ff]
+        upper = both[:, ff:]
+        sigma = 1.0 / (1.0 + jnp.exp(-gate))
+        silu = gate * sigma
+        hidden_ref[rows, :] = (silu * upper).astype(bf16)
+        d_hidden = d_hidden_ref[rows, :].astype(f32)
+        d_both_ref[rows, :ff] = (d_hidden * upper * (sigma + silu * (1.0 - sigma))).astype(bf16)
+        d_both_ref[rows, ff:] = (d_hidden * silu).astype(bf16)
+        d_n_ref[rows, :] = dot_at(d_both_ref[rows, :], whole_ref[...], 1, 1)
+    part_rows(at_ref, len(blocks), d_n_ref, kept_ref, away_ref)
+
+
+def feed_forward(at, own, other, d_hidden, blocks):
+    _, rows, width = own.shape
+    ff = d_hidden.shape[1]
+    return on_chip(
+        functools.partial(feed_forward_kernel, min(256, 4 * rows)),
+        [
+            like(bf16, 4 * rows, width),
+            like(bf16, 4 * rows, ff),
+            like(bf16, 4 * rows, 2 * ff),
+            like(f32, 2, rows, width),
+            like(bf16, 2, rows, width),
+        ],
+        [at, own, other, d_hidden],
+        32 * rows * width * ff,
+        blocks=blocks,
+        scratch=[
+            pltpu.VMEM((4 * rows, width), f32),
+            pltpu.VMEM((width, 2 * ff), bf16),
+            pltpu.SemaphoreType.DMA((len(blocks),)),
+        ],
+        name="feed_forward",
+    )
+
+
+def feed_forward_grads_kernel(at_ref, n_ref, d_both_ref, hidden_ref, d_out_ref, both_ref, down_ref):
+    count, block, _ = both_ref.shape
+    own = down_ref.shape[1]
+    for k in range(count):
+        down_ref[k] = dot_at(
+            hidden_ref[:, pl.ds(pl.multiple_of(at_ref[k] * own, own), own)], d_out_ref[...], 0, 0
+        ).astype(bf16)
+    for position in range(count):
+        columns = slice(position * block, (position + 1) * block)
+        both_ref[at_ref[count + position]] = dot_at(
+            n_ref[:, columns], d_both_ref[...], 0, 0
+        ).astype(bf16)
+
+
+def feed_forward_grads(at, n, d_both, hidden, d_out, count):
+    rows, width = n.shape
+    ff = hidden.shape[1]
+    return on_chip(
+        feed_forward_grads_kernel,
+        [like(bf16, count, width // count, 2 * ff), like(bf16, count, ff // count, width)],
+        [at, n, d_both, hidden, d_out],
+        6 * rows * width * ff,
+        name="feed_forward_grads",
+    )
+
+
+def split_heads_kernel(at_ref, own_ref, other_ref, weight_ref, d_mid_ref, heads_ref):
+    join_rows(at_ref, heads_ref.shape[0] // 2, own_ref, other_ref, d_mid_ref)
+    size, rows = heads_ref.shape[1:]
+    for seq in range(2):
+        part = dot_at(weight_ref[...], d_mid_ref[seq * rows : (seq + 1) * rows, :], 1, 1)
+        part = part.astype(bf16)
+        for head in range(heads_ref.shape[0] // 2):
+            heads_ref[2 * head + seq] = part[head * size : (head + 1) * size, :]
+
+
+def split_heads(at, own, other, weight, heads):
+    _, rows, width = own.shape
+    return on_chip(
+        split_heads_kernel,
+        [
+            like(bf16, 4 * rows, width),
+            like(bf16, 2 * heads, weight.shape[0] // heads, 2 * rows),
+        ],
+        [at, own, other, weight],
+        8 * rows * width * weight.shape[0],
+        name="split_heads",
+    )
+
+
+def heads_grad_kernel(at_ref, heads_ref, n_ref, joined_ref, grad_ref):
+    join_heads(heads_ref, joined_ref)
+    grad_ref[...] = dot_at(n_ref[...], joined_ref[...], 0, 1).astype(bf16)
+
+
+def heads_grad(at, heads, n):
+    rows, width = n.shape
+    columns = heads.shape[0] // 2 * heads.shape[1]
+    return on_chip(
+        heads_grad_kernel,
+        [like(bf16, columns, rows), like(bf16, width, columns)],
+        [at, heads, n],
+        2 * rows * width * columns,
+        name="heads_grad",
+    )
+
+
+def heads_input_kernel(at_ref, joined_ref, weight_ref, kept_ref, away_ref, out_ref):
+    out_ref[...] = dot_at(joined_ref[...], weight_ref[...], 0, 1)
+    count = weight_ref.shape[1] // HEAD_SIZE
+    part_rows(at_ref, count, out_ref, kept_ref, away_ref)
+
+
+def heads_input(at, joined, weight):
+    width, columns = weight.shape
+    rows = joined.shape[1] // 4
+    return on_chip(
+        heads_input_kernel,
+        [like(f32, 2, rows, width), like(bf16, 2, rows, width)],
+        [at, joined, weight],
+        0,
+        scratch=[pltpu.VMEM((4 * rows, width), f32)],
+        name="heads_input",
+    )
+
+
+def layer_output_kernel(count, at_ref, hidden_ref, weight_ref, kept_ref, away_ref, out_ref):
+    out_ref[...] = dot_at(hidden_ref[...], weight_ref[...], 1, 0)
+    part_rows(at_ref, count, out_ref, kept_ref, away_ref)
+
+
+def layer_output(at, hidden, weight, count):
+    ff, width = weight.shape
+    rows = hidden.shape[0] // 4
+    return on_chip(
+        functools.partial(layer_output_kernel, count),
+        [like(f32, 2, rows, width), like(bf16, 2, rows, width)],
+        [at, hidden, weight],
+        0,
+        scratch=[pltpu.VMEM((4 * rows, width), f32)],
+        name="layer_output",
+    )
+
+
+def query_rows_kernel(
+    at_ref, terms_ref, gain_ref, query_ref, key_ref, value_ref, d_query, d_key, d_value, d_gain
+):
+    half = HEAD_SIZE // 2
+    quarter = HEAD_SIZE // 4
+    positions = terms_ref.shape[0] // 4
+    groups = terms_ref.shape[2] // HEAD_SIZE
+    parts = []
+    for t in range(4):
+        total = terms_ref[t].astype(f32)
+        for position in range(1, positions):
+            total = total + terms_ref[4 * position + t].astype(f32)
+        parts.append(total)
+    pieces = ([], [], [])
+    for group in range(groups):
+        for t in range(4):
+            start = group * HEAD_SIZE
+            pieces[0].append(parts[t][:, start : start + half])
+            pieces[1].append(parts[t][:, start + half : start + half + quarter])
+            pieces[2].append(parts[t][:, start + half + quarter : start + HEAD_SIZE])
+    gain = gain_ref[...]
+    rows_sum = None
+    outs = (d_query, d_key, d_value)
+    for pieces_of, weight_ref, out_ref in zip(pieces, (query_ref, key_ref, value_ref), outs):
+        grad = jnp.concatenate(pieces_of, axis=1)
+        out_ref[...] = gain * grad
+        part = jnp.sum(grad * weight_ref[...].astype(f32), axis=1, keepdims=True)
+        rows_sum = part if rows_sum is None else rows_sum + part
+    d_gain[...] = rows_sum
+
+
+def query_rows_grads(at, terms, gain, query, key, value):
+    own = query.shape[0]
+    return on_chip(
+        query_rows_kernel,
+        [
+            like(f32, *query.shape),
+            like(f32, *key.shape),
+            like(f32, *value.shape),
+            like(f32, own, 1),
+        ],
+        [at, terms, gain, query, key, value],
+        terms.size,
+        name="query_rows_grads",
+    )
+
+
+def pair_rows_kernel(
+    size, count, at_ref, terms_ref, gain_ref, gate_ref, up_ref, d_gate, d_up, d_gain
+):
+    gain = gain_ref[...]
+    core = at_ref[2 * count]
+    seq = at_ref[2 * count + 1]
+    half = terms_ref.shape[2] // 2
+    rows_sum = jnp.zeros_like(gain)
+    for side, (weight_ref, out_ref) in enumerate(((gate_ref, d_gate), (up_ref, d_up))):
+        for position in range(half // size):
+            for t in range(4):
+                columns = slice((4 * position + t) * size, (4 * position + t + 1) * size)
+                start = side * half + position * size
+                block = (core + t // 2) % 2 * 2 + (seq + t % 2) % 2
+                grad = terms_ref[block, :, start : start + size].astype(f32)
+                out_ref[:, columns] = gain * grad
+                rows_sum = rows_sum + jnp.sum(
+                    grad * weight_ref[:, columns].astype(f32), axis=1, keepdims=True
+                )
+    d_gain[...] = rows_sum
+
+
+def pair_rows_grads(at, terms, gain, gate, up, size, count):
+    own = gate.shape[0]
+    return on_chip(
+        functools.partial(pair_rows_kernel, size, count),
+        [like(f32, *gate.shape), like(f32, *up.shape), like(f32, own, 1)],
+        [at, terms, gain, gate, up],
+        terms.size,
+        name="pair_rows_grads",
+    )
+
+
 def ring_of(count):
     order = list(range(0, count, 2)) + list(range(count - 1, 0, -2))
     forward = [(order[i], order[(i + 1) % count]) for i in range(count)]
     backward = [(there, here) for here, there in forward]
-    return order, forward, backward
-
-
-def ring_gather(shards, count):
-    order, forward, backward = ring_of(count)
-    order = jnp.array(order, jnp.int32)
-    place = jnp.argsort(order)[lax.axis_index("d")]
-    outs = []
-    for shard in shards:
-        out = jnp.zeros((count,) + shard.shape, shard.dtype)
-        outs.append(lax.dynamic_update_slice_in_dim(out, shard[None], lax.axis_index("d"), 0))
-    ahead = list(shards)
-    behind = list(shards)
-    for hop in range(1, count // 2 + 1):
-        left = order[(place + count - hop) % count]
-        right = order[(place + hop) % count]
-        if hop < count // 2:
-            ahead = [lax.ppermute(a, "d", forward) for a in ahead]
-            behind = [lax.ppermute(b, "d", backward) for b in behind]
-            ahead, behind = lax.optimization_barrier((ahead, behind))
-            outs = [
-                lax.dynamic_update_slice_in_dim(o, a[None], left, 0) for o, a in zip(outs, ahead)
-            ]
-            outs = [
-                lax.dynamic_update_slice_in_dim(o, b[None], right, 0) for o, b in zip(outs, behind)
-            ]
+    return forward, backward
+
+
+def place_of(position, count):
+    return jnp.where(position % 2 == 0, position // 2, count - (position + 1) // 2)
+
+
+def position_at(place, count):
+    place = lax.rem(place, count)
+    return jnp.where(place < count // 2, 2 * place, 2 * (count - place) - 1)
+
+
+def tie(*values):
+    return lax.optimization_barrier(values)
+
+
+def after(value, *others):
+    return lax.optimization_barrier((value,) + others)[0]
+
+
+class GatherRing:
+    def __init__(self, shard, count):
+        self.count = count
+        self.forward, self.backward = ring_of(count)
+        self.parts = [shard] + [None] * (count - 1)
+        self.ahead = self.behind = shard
+        self.hops = 0
+
+    def start(self, *others):
+        self.hops += 1
+        ahead, behind = self.ahead, self.behind
+        if self.hops == self.count // 2:
+            half = ahead.shape[0] // 2
+            ahead, behind = ahead[:half], behind[half:]
+        if others:
+            ahead, behind = lax.optimization_barrier((ahead, behind) + others)[:2]
+        self.ahead = lax.ppermute(ahead, "d", self.forward)
+        self.behind = lax.ppermute(behind, "d", self.backward)
+
+    def settle(self, *others):
+        out = lax.optimization_barrier((self.ahead, self.behind) + others)
+        self.ahead, self.behind = out[:2]
+        if self.hops == self.count // 2:
+            self.parts[self.hops] = jnp.concatenate(out[:2], axis=0)
         else:
-            half = [a.shape[0] // 2 for a in ahead]
-            ahead = [lax.ppermute(a[:h], "d", forward) for a, h in zip(ahead, half)]
-            behind = [lax.ppermute(b[h:], "d", backward) for b, h in zip(behind, half)]
-            outs = [
-                lax.dynamic_update_slice(o, a[None], (left,) + (0,) * a.ndim)
-                for o, a in zip(outs, ahead)
-            ]
-            outs = [
-                lax.dynamic_update_slice(o, b[None], (left, h) + (0,) * (b.ndim - 1))
-                for o, b, h in zip(outs, behind, half)
-            ]
-    return outs
-
-
-def ring_scatter(terms, count):
-    order, forward, backward = ring_of(count)
-    order = jnp.array(order, jnp.int32)
-    place = jnp.argsort(order)[lax.axis_index("d")]
-
-    def part(term, position, side):
+            self.parts[self.count - self.hops] = self.ahead
+            self.parts[self.hops] = self.behind
+        return out[2] if len(others) == 1 else out[2:]
+
+
+class ScatterRing:
+    def __init__(self, terms, count):
+        self.count = count
+        self.terms = terms
+        self.forward, self.backward = ring_of(count)
+        self.ahead = [self.part(t, count - 1, 0) for t in terms]
+        self.behind = [self.part(t, 1, 1) for t in terms]
+        self.hops = 0
+
+    def part(self, term, at, side):
         half = term.shape[1] // 2
-        start = (order[position % count], side * half) + (0,) * (term.ndim - 2)
-        return lax.dynamic_slice(term, start, (1, half) + term.shape[2:])[0]
-
-    ahead = [part(t, place + count - 1, 0) for t in terms]
-    behind = [part(t, place + 1, 1) for t in terms]
-    for hop in range(1, count):
-        ahead = [lax.ppermute(a, "d", forward) for a in ahead]
-        behind = [lax.ppermute(b, "d", backward) for b in behind]
-        ahead, behind = lax.optimization_barrier((ahead, behind))
-        kind = f32 if hop == count - 1 else bf16
-        ahead = [
-            (a.astype(f32) + part(t, place + 2 * count - 1 - hop, 0).astype(f32)).astype(kind)
-            for a, t in zip(ahead, terms)
+        return term[at % self.count, side * half : (side + 1) * half]
+
+    def start(self, *others):
+        self.hops += 1
+        ahead, behind = self.ahead, self.behind
+        if others:
+            ahead, behind = lax.optimization_barrier((ahead, behind) + others)[:2]
+        self.ahead = [lax.ppermute(a, "d", self.forward) for a in ahead]
+        self.behind = [lax.ppermute(b, "d", self.backward) for b in behind]
+
+    def settle(self, *others):
+        out = lax.optimization_barrier((self.ahead, self.behind) + others)
+        ahead, behind = out[:2]
+        kind = f32 if self.hops == self.count - 1 else bf16
+        place = self.count - 1 - self.hops
+        self.ahead = [
+            (a.astype(f32) + self.part(t, place, 0).astype(f32)).astype(kind)
+            for a, t in zip(ahead, self.terms)
         ]
-        behind = [
-            (b.astype(f32) + part(t, place + 1 + hop, 1).astype(f32)).astype(kind)
-            for b, t in zip(behind, terms)
+        self.behind = [
+            (b.astype(f32) + self.part(t, 1 + self.hops, 1).astype(f32)).astype(kind)
+            for b, t in zip(behind, self.terms)
         ]
-    return [jnp.concatenate([a, b], axis=0) for a, b in zip(ahead, behind)]
+        return out[2] if len(others) == 1 else out[2:]
+
+    def sums(self):
+        return [jnp.concatenate([a, b], axis=0) for a, b in zip(self.ahead, self.behind)]
 
 
 def swap(values, axis):
@@ -500,15 +968,35 @@
     return lax.all_gather(pair, "core", axis=1)
 
 
-def own_rows_sum(terms):
+def core_sum(kept, away):
+    return kept + swap(away, "core").astype(f32)
+
+
+def both_rows_sum(pair):
+    return pair + swap(pair.astype(bf16), "y").astype(f32)
+
+
+def own_rows_sum(pair):
+    seq = lax.axis_index("y")
+    away = lax.dynamic_index_in_dim(pair, 1 - seq, 0, False).astype(bf16)
+    return lax.dynamic_index_in_dim(pair, seq, 0, False) + swap(away, "y").astype(f32)
+
+
+def own_columns(blocks):
     core = lax.axis_index("core")
     seq = lax.axis_index("y")
-    away = lax.dynamic_index_in_dim(terms, 1 - core, 1, False).astype(bf16)
-    kept = lax.dynamic_index_in_dim(terms, core, 1, False)
-    pair = kept + swap(away, "core").astype(f32)
-    away = lax.dynamic_index_in_dim(pair, 1 - seq, 0, False).astype(bf16)
-    kept = lax.dynamic_index_in_dim(pair, seq, 0, False)
-    return kept + swap(away, "y").astype(f32)
+    away = lax.dynamic_index_in_dim(blocks, 1 - seq, 1, False)
+    kept = lax.dynamic_index_in_dim(blocks, seq, 1, False)
+    pair = jnp.stack([kept, swap(away, "y")])
+    away = lax.dynamic_index_in_dim(pair, 1 - core, 1, False)
+    kept = lax.dynamic_index_in_dim(pair, core, 1, False)
+    return jnp.concatenate([kept, swap(away, "core")])
+
+
+def both_rows(own, *others):
+    other = after(swap(own, "y"), *others)
+    first = lax.axis_index("y") == 0
+    return jnp.stack([jnp.where(first, own, other), jnp.where(first, other, own)])
 
 
 def all_to_all(values, axes):
@@ -546,53 +1034,56 @@
     gain1 = norm_gain1.astype(f32)[:, None]
     gain2 = norm_gain2.astype(f32)[:, None]
 
-    with jax.named_scope("attention_weights"):
-        query_cols = (gain1 * w_query.astype(f32)).astype(bf16)
-        key_cols = (gain1 * key_weight.astype(f32)).astype(bf16)
-        value_cols = (gain1 * value_weight.astype(f32)).astype(bf16)
-        qkv_cols = jnp.concatenate(
-            [
-                query_cols.reshape(own, count, 4, half).transpose(2, 0, 1, 3),
-                key_cols.reshape(own, count, 4, quarter).transpose(2, 0, 1, 3),
-                value_cols.reshape(own, count, 4, quarter).transpose(2, 0, 1, 3),
-            ],
-            axis=-1,
-        ).reshape(4, own, count * HEAD_SIZE)
-        qkv_rows = all_to_all(qkv_cols, ("core", "y")).reshape(group, count * HEAD_SIZE)
-        (qkv_weight,) = ring_gather([qkv_rows], count)
-        qkv_weight = qkv_weight.reshape(width, count * HEAD_SIZE)
-    with jax.named_scope("feed_forward_weights"):
-        gate_cols = (gain2 * w_gate.astype(f32)).astype(bf16)
-        up_cols = (gain2 * w_up.astype(f32)).astype(bf16)
-        pair_cols = jnp.concatenate(
-            [
-                gate_cols.reshape(own, count, 4, ff_own).transpose(2, 0, 1, 3),
-                up_cols.reshape(own, count, 4, ff_own).transpose(2, 0, 1, 3),
-            ],
-            axis=2,
-        ).reshape(4, own, 2 * count * ff_own)
-        pair_rows = all_to_all(pair_cols, ("core", "y")).reshape(group, 2 * count * ff_own)
-        pair_rows, own_out, own_down, qkv_weight = lax.optimization_barrier(
-            (pair_rows, w_out, w_down, qkv_weight)
-        )
-        pair_weight, out_weight, down_weight = ring_gather([pair_rows, own_out, own_down], count)
-        pair_weight = pair_weight.reshape(width, 2 * count * ff_own)
-        out_weight = out_weight.reshape(count * own, width)
-        down_weight = down_weight.reshape(count * ff_own, width)
-
-    inputs = tokens[0].astype(f32)
+    place = place_of(lax.axis_index("d"), count)
+    steps = jnp.arange(count, dtype=jnp.int32)
+    core = lax.axis_index("core")
+    seq = lax.axis_index("y")
+    at = jnp.concatenate(
+        [
+            position_at(place + steps, count),
+            lax.rem(place_of(steps, count) - place + count, count),
+            jnp.stack([core, seq]).astype(jnp.int32),
+        ]
+    )
+
+    out_down = GatherRing(jnp.concatenate([w_down, w_out], axis=0), count)
+    out_down.start()
+    qkv_cols = query_columns(at, gain1, w_query, key_weight, value_weight)
+    qkv_rows = all_to_all(qkv_cols, ("core", "y")).reshape(group, count * HEAD_SIZE)
+    qkv_rows = out_down.settle(qkv_rows)
+    tokens_pair = both_rows(tokens[0], qkv_rows)
+    qkv_ring = GatherRing(qkv_rows, count)
+    qkv_ring.start()
+    inputs = tokens_pair.astype(f32)
     r1 = inverse_rms(inputs)
     n1_own = (inputs * r1).astype(bf16)
-    n1 = rows_of_group(n1_own).reshape(2 * seq_rows, width)
-    d_out = rows_of_group(cotangent[0]).reshape(2 * seq_rows, width)
-    qkv = dot_at(qkv_weight, n1, 0, 1).astype(bf16)
-    qkv = qkv.reshape(count, HEAD_SIZE, 2, seq_rows).transpose(0, 2, 1, 3)
-    qkv = all_to_all(qkv.reshape(2 * count, HEAD_SIZE, seq_rows), ("d", "y"))
-    qkv = qkv.reshape(count, 2, HEAD_SIZE, seq_rows)
+    n1_other = swap(n1_own, "core")
+    pair_cols = pair_columns(at, gain2, w_gate, w_up, ff_own)
+    n1_own, n1_other, pair_cols = qkv_ring.settle(n1_own, n1_other, pair_cols)
+    qkv_ring.start()
+    pair_rows = all_to_all(pair_cols, ("core", "y")).reshape(group, 2 * count * ff_own)
+    qkv_ring.settle()
+    qkv_ring.start()
+    pair_rows = qkv_ring.settle(pair_rows)
+    qkv_ring.start()
+    n1_own = qkv_ring.settle(n1_own)
+
+    out_down.start(n1_own)
+    n1, qkv_weight, qkv = project_heads(at, n1_own, n1_other, qkv_ring.parts)
+    cotangent_pair = both_rows(after(cotangent[0], pair_rows), n1_own)
+    cotangent_other = swap(cotangent_pair, "core")
+    qkv = all_to_all(qkv, ("d", "y")).reshape(count, 2, HEAD_SIZE, seq_rows)
+    out_down.settle()
+    out_down.start()
+    qkv, cotangent_other = out_down.settle(qkv, cotangent_other)
+    out_down.start()
     q_parts = qkv[:, :, :half].transpose(1, 2, 0, 3).reshape(2, half, length)
-    kv = lax.all_gather(qkv[:, :, half:], "core", axis=0)
-    kv = kv.reshape(2, count, 2, 2, quarter, seq_rows).transpose(3, 0, 2, 4, 1, 5)
-    k_parts, v_parts = kv.reshape(2, 2, half, length)
+    kv_own = qkv[:, :, half:].reshape(count, 2, 2, quarter, seq_rows).transpose(2, 1, 3, 0, 4)
+    kv_own = kv_own.reshape(2, half, length)
+    kv_other = swap(kv_own, "core")
+    kv_first = jnp.where(core == 0, kv_own, kv_other)
+    kv_second = jnp.where(core == 0, kv_other, kv_own)
+    k_parts = (kv_first[0], kv_second[0])
     position = jnp.arange(length, dtype=f32)
     exponent = jnp.arange(half, dtype=f32) * (2.0 / HEAD_SIZE)
     angle = (rope_base ** (-exponent))[:, None] * position[None, :]
@@ -612,98 +1103,113 @@
         )
 
     q_parts = q_parts.astype(f32)
-    k_parts = k_parts.astype(f32)
+    k_parts = [part.astype(f32) for part in k_parts]
     q = (rotate(q_parts[0], q_parts[1]) * (score_scale * log2_e)).astype(bf16)
     k = rotate(k_parts[0], k_parts[1]).astype(bf16)
-    v = v_parts.reshape(HEAD_SIZE, length)
+    v = jnp.concatenate([kv_first[1], kv_second[1]], axis=0)
+    pair_ring = GatherRing(pair_rows, count)
+    pair_ring.start(qkv)
     mixed, prob = heads_forward(q, k, v, step)
+    mixed = out_down.settle(mixed)
+    mixed = pair_ring.settle(mixed)
+    pair_ring.start()
     mixed_send = mixed.astype(bf16).reshape(2, half, count, seq_rows).transpose(2, 0, 1, 3)
     mixed_low = all_to_all(mixed_send.reshape(2 * count, half, seq_rows), ("d", "y"))
-    mixed_low = mixed_low.reshape(count, 2, half, seq_rows).transpose(0, 2, 1, 3)
-    mixed_low = mixed_low.reshape(count * half, 2 * seq_rows)
-    branch = dot_at(mixed_low, out_weight, 0, 0).reshape(2, 2, rows, width)
-    middle = inputs + own_rows_sum(branch)
+    mixed_low = pair_ring.settle(mixed_low)
+    pair_ring.start()
+    out_weight, mixed_low, kept, away = project_out(at, mixed_low, out_down.parts, ff_own)
+    branch = pair_ring.settle(core_sum(kept, away))
+    pair_ring.start()
+    branch = both_rows_sum(branch)
+    d_out, down_weight, d_hidden = hidden_gradient(
+        at, cotangent_pair, cotangent_other, out_down.parts, ff_own
+    )
+    branch, d_hidden = tie(branch, d_hidden)
+    middle = inputs + branch
 
     r2 = inverse_rms(middle)
-    n2_own = middle * r2
-    n2 = rows_of_group(n2_own.astype(bf16)).reshape(2 * seq_rows, width)
-    both = dot_at(n2, pair_weight, 1, 0)
-    gate = both[:, : count * ff_own]
-    upper = both[:, count * ff_own :]
-    sigma = jax.nn.sigmoid(gate)
-    silu = gate * sigma
-    hidden = (silu * upper).astype(bf16)
-    d_hidden = dot_at(d_out, down_weight, 1, 1)
-    d_gate = (d_hidden * upper * (sigma + silu * (1.0 - sigma))).astype(bf16)
-    d_upper = (d_hidden * silu).astype(bf16)
-    d_both = jnp.concatenate([d_gate, d_upper], axis=1)
-    d_normed2 = own_rows_sum(dot_at(d_both, pair_weight, 1, 1).reshape(2, 2, rows, width))
-    incoming = cotangent[0].astype(f32)
-    d_middle = incoming + r2 * (
-        d_normed2 - n2_own * jnp.mean(d_normed2 * n2_own, axis=-1, keepdims=True)
-    )
-    grad_down = dot_at(hidden, d_out, 0, 0).astype(bf16).reshape(count, ff_own, width)
-    grad_both = dot_at(n2, d_both, 0, 0).astype(bf16).reshape(count, group, 2 * count * ff_own)
-    owned_down, owned_both = ring_scatter([grad_down, grad_both], count)
-    result = middle + own_rows_sum(dot_at(hidden, down_weight, 1, 0).reshape(2, 2, rows, width))
-
-    d_mid = rows_of_group(d_middle.astype(bf16)).reshape(2 * seq_rows, width)
-    d_mixed = dot_at(out_weight, d_mid, 1, 1).astype(bf16)
-    d_mixed = d_mixed.reshape(count, half, 2, seq_rows).transpose(0, 2, 1, 3)
-    d_mixed = all_to_all(d_mixed.reshape(2 * count, half, seq_rows), ("d", "y"))
+    n2_pair = middle * r2
+    n2_own = n2_pair.astype(bf16)
+    n2_other = swap(n2_own, "core")
+    n2_own, n2_other = pair_ring.settle(n2_own, n2_other)
+    n2, hidden, d_both, kept, away = feed_forward(at, n2_own, n2_other, d_hidden, pair_ring.parts)
+    d_n2 = core_sum(kept, away)
+    grad_both, grad_down = feed_forward_grads(
+        at, n2, d_both, after(hidden, d_n2), d_out, count
+    )
+    d_normed2 = both_rows_sum(d_n2)
+    ff_ring = ScatterRing([grad_both, grad_down], count)
+    ff_ring.start()
+    d_normed2 = ff_ring.settle(d_normed2)
+    ff_ring.start()
+    d_middle = cotangent_pair.astype(f32) + r2 * (
+        d_normed2 - n2_pair * jnp.mean(d_normed2 * n2_pair, axis=-1, keepdims=True)
+    )
+
+    d_mid_own = d_middle.astype(bf16)
+    d_mid_other = swap(d_mid_own, "core")
+    d_mid, d_mixed = split_heads(at, d_mid_own, d_mid_other, out_weight, count)
+    d_mixed = ff_ring.settle(d_mixed)
+    ff_ring.start()
+    d_mixed = all_to_all(d_mixed, ("d", "y"))
+    d_mixed = ff_ring.settle(d_mixed)
+    ff_ring.start()
     d_mixed = d_mixed.reshape(count, 2, half, seq_rows).transpose(1, 2, 0, 3)
     d_mixed = d_mixed.reshape(HEAD_SIZE, length)
+    grad_out = dot_at(after(mixed_low, d_mixed), d_mid, 1, 0).astype(bf16)
+    owned_out = all_to_all(grad_out.reshape(count, own, width), "d")
     d_q, d_k, d_v = heads_backward(q, k, v, prob, mixed, d_mixed, step)
-    core = lax.axis_index("core")
     d_kv = jnp.stack([rotate_back(d_k), d_v.reshape(2, half, length)], axis=1)
     away = lax.dynamic_index_in_dim(d_kv, 1 - core, 0, False).astype(bf16)
     kept = lax.dynamic_index_in_dim(d_kv, core, 0, False)
-    d_kv = (kept + swap(away, "core").astype(f32)).astype(bf16)
+    d_kv = core_sum(kept, away).astype(bf16)
     d_kv = d_kv.reshape(2, 2, quarter, count, seq_rows).transpose(3, 1, 0, 2, 4)
     d_kv = d_kv.reshape(count, 2, half, seq_rows)
     d_q = rotate_back(d_q).astype(bf16).reshape(2, half, count, seq_rows).transpose(2, 0, 1, 3)
     d_qkv = jnp.concatenate([d_q, d_kv], axis=2).reshape(2 * count, HEAD_SIZE, seq_rows)
-    d_qkv = all_to_all(d_qkv, ("d", "y")).reshape(count, 2, HEAD_SIZE, seq_rows)
-    d_qkv = d_qkv.transpose(0, 2, 1, 3).reshape(count * HEAD_SIZE, 2 * seq_rows)
-    grad_out = dot_at(mixed_low, d_mid, 1, 0).astype(bf16).reshape(count, own, width)
-    grad_qkv = dot_at(n1, d_qkv, 0, 1).astype(bf16).reshape(count, group, count * HEAD_SIZE)
-    grad_out, grad_qkv, owned_down, owned_both = lax.optimization_barrier(
-        (grad_out, grad_qkv, owned_down, owned_both)
-    )
-    owned_out, owned_qkv = ring_scatter([grad_out, grad_qkv], count)
-    d_normed1 = own_rows_sum(dot_at(d_qkv, qkv_weight, 0, 1).reshape(2, 2, rows, width))
-    n1_wide = inputs * r1
-    input_grad = d_middle + r1 * (
+    d_qkv, owned_out = ff_ring.settle(d_qkv, owned_out)
+    ff_ring.start()
+    d_qkv = all_to_all(d_qkv, ("d", "y"))
+    ff_ring.settle()
+    ff_ring.start()
+    d_qkv = ff_ring.settle(d_qkv)
+    d_qkv, grad_qkv = heads_grad(at, d_qkv, n1)
+    grad_qkv = grad_qkv.reshape(4 * count, own, count * HEAD_SIZE)
+    ff_ring.start(grad_qkv)
+    own_qkv = all_to_all(grad_qkv, ("d", "core", "y"))
+    ff_ring.settle()
+    owned_both, owned_down = ff_ring.sums()
+    own_both = own_columns(owned_both.astype(bf16).reshape(2, 2, own, -1))
+    kept, away = heads_input(at, d_qkv, qkv_weight)
+    d_normed1 = own_rows_sum(core_sum(kept, away))
+    kept, away = layer_output(at, hidden, down_weight, count)
+    n1_wide, r1_own, d_middle_own, middle_own = (
+        lax.dynamic_index_in_dim(value, seq, 0, False)
+        for value in (inputs * r1, r1, d_middle, middle)
+    )
+    input_grad = d_middle_own + r1_own * (
         d_normed1 - n1_wide * jnp.mean(d_normed1 * n1_wide, axis=-1, keepdims=True)
     )
-
-    own_both = all_to_all(owned_both.astype(bf16).reshape(4, own, -1), ("core", "y")).astype(f32)
-    own_both = own_both.reshape(4, own, 2, count, ff_own).transpose(2, 1, 3, 0, 4)
-    own_gate, own_up = own_both.reshape(2, own, 4 * count * ff_own)
-    owned_gain2 = jnp.sum(own_gate * w_gate.astype(f32), axis=1) + jnp.sum(
-        own_up * w_up.astype(f32), axis=1
-    )
-    own_qkv = all_to_all(owned_qkv.astype(bf16).reshape(4, own, -1), ("core", "y")).astype(f32)
-    own_qkv = own_qkv.reshape(4, own, count, HEAD_SIZE).transpose(1, 2, 0, 3)
-    own_query = own_qkv[..., :half].reshape(own, -1)
-    own_key = own_qkv[..., half : half + quarter].reshape(own, -1)
-    own_value = own_qkv[..., half + quarter :].reshape(own, -1)
-    owned_gain1 = (
-        jnp.sum(own_query * w_query.astype(f32), axis=1)
-        + jnp.sum(own_key * key_weight.astype(f32), axis=1)
-        + jnp.sum(own_value * value_weight.astype(f32), axis=1)
+    result = middle_own + own_rows_sum(core_sum(kept, away))
+    own_qkv, own_both = tie(own_qkv, own_both)
+    owned_out = jnp.sum(owned_out.astype(f32), axis=0)
+    grad_gate, grad_up, grad_gain2 = pair_rows_grads(
+        at, own_both, gain2, w_gate, w_up, ff_own, count
+    )
+    grad_query, grad_key, grad_value, grad_gain1 = query_rows_grads(
+        at, own_qkv, gain1, w_query, key_weight, value_weight
     )
     return (
         result.astype(bf16)[None],
         input_grad[None],
-        owned_gain1,
-        gain1 * own_query,
-        gain1 * own_key,
-        gain1 * own_value,
+        grad_gain1[:, 0],
+        grad_query,
+        grad_key,
+        grad_value,
         owned_out,
-        owned_gain2,
-        gain2 * own_gate,
-        gain2 * own_up,
+        grad_gain2[:, 0],
+        grad_gate,
+        grad_up,
         owned_down,
     )
 

time: 627 us -> 538 us (0.86)
  the two profiles are of different devices: /device:TPU:0 before, /device:TPU:10 now
where the time goes in v2:
time: 538 us; the launch traced here: 530 us
  waiting for transfers between devices  262 us (49%)
  starting transfers between devices  106 us (20%)
  Pallas kernels  68.9 us (13%)
  other arithmetic  50.7 us (9%)
  local copies, waits for them, and re-layouts  39.3 us (7%)
    ppermute x14, waiting for transfers between devices, start(): self.ahead = [lax.ppermute(a, 'd', self.forward) for a in ahead]  113 us
    ppermute x12, waiting for transfers between devices, start(): self.ahead = lax.ppermute(ahead, 'd', self.forward)  85.8 us
    pallas_call x13, Pallas kernels, on_chip(): pl.pallas_call(kernel, out_shape=tuple(out_shape), in_specs=[pl.BlockSpec...  55.6 us
    all_to_all x8, starting transfers between devices, all_to_all(): return lax.all_to_all(values, axes, 0, 0, tiled=True)  42.2 us
    ppermute x18, waiting for transfers between devices, swap(): return lax.ppermute(values, axis, [(0, 1), (1, 0)])  32.3 us
    unnamed x159, local copies, waits for them, and re-layouts  30.4 us
    all_to_all x8, waiting for transfers between devices, all_to_all(): return lax.all_to_all(values, axes, 0, 0, tiled=True)  24.1 us
    ppermute x14, starting transfers between devices, start(): self.behind = [lax.ppermute(b, 'd', self.backward) for b in behind]  23.3 us
  transfers between devices with their start and end apart: 78, of which 36 were waited for; matrix products, arithmetic and copies ran while one was open for 9% of the time, Pallas kernels for 9%

profile of v2, /device:TPU:10, one launch (start us, length us, event | category | flops | bytes accessed | tf_op | source)
XLA Modules:
  0.0 530.4 jit_solution(10372490713267608790)
XLA Ops:
  14.9 6.3 %all-to-all-done = bf16[4,48,768]{2,1,0:T(8,128)(2,1)S(1)} async-done(((bf16[4,48,768]{2,1,0:T(8,128)(2,1)}), bf16[4,48,768]{2,1,0:T(8,128)(2,1)S(1)}, u32[]{:S(2)}, u32[]{:S(2)}) %all-to-all-start) | async-done | bytes 294944 | tf_op jit(solution)/shard_map/all_to_all | solution.py:1003
  26.9 5.6 %collective-permute-done.3.refs_7_ = bf16[192,768]{1,0:T(8,128)(2,1)} collective-permute-done((bf16[192,768]{1,0:T(8,128)(2,1)S(1)}, bf16[192,768]{1,0:T(8,128)(2,1)}, u32[]{:S(2)}, u32[]{:S(2)}) %collective-permute-start.3) | collective-permute-done | bytes 294944 | tf_op jit(solution)/shard_map/ppermute | solution.py:908
  43.7 5.5 %collective-permute-done.8.refs_5_ = bf16[192,768]{1,0:T(8,128)(2,1)S(1)} collective-permute-done((bf16[192,768]{1,0:T(8,128)(2,1)}, bf16[192,768]{1,0:T(8,128)(2,1)S(1)}, u32[]{:S(2)}, u32[]{:S(2)}) %collective-permute-start.8) | collective-permute-done | bytes 294944 | tf_op jit(solution)/shard_map/ppermute | solution.py:908
  61.8 7.1 %all-to-all-start.2 = ((bf16[16,96,256]{2,1,0:T(8,128)(2,1)}), bf16[16,96,256]{2,1,0:T(8,128)(2,1)}, u32[]{:S(2)}, u32[]{:S(2)}) async-start(bf16[16,96,256]{2,1,0:T(8,128)(2,1)} %get-tuple-element.158), calls=%async_computation.2 | async-start | bytes 1572864 | tf_op jit(solution)/shard_map/all_to_all | solution.py:1003
  72.2 25.5 %collective-permute-done.12.refs_6_ = bf16[176,1536]{1,0:T(8,128)(2,1)S(1)} collective-permute-done((bf16[176,1536]{1,0:T(8,128)(2,1)}, bf16[176,1536]{1,0:T(8,128)(2,1)S(1)}, u32[]{:S(2)}, u32[]{:S(2)}) %collective-permute-start.12) | collective-permute-done | bytes 540704 | tf_op jit(solution)/shard_map/ppermute | solution.py:908
  102.2 8.4 %collective-permute-done.14.refs_5_ = bf16[176,1536]{1,0:T(8,128)(2,1)S(1)} collective-permute-done((bf16[176,1536]{1,0:T(8,128)(2,1)S(1)}, bf16[176,1536]{1,0:T(8,128)(2,1)S(1)}, u32[]{:S(2)}, u32[]{:S(2)}) %collective-permute-start.14) | collective-permute-done | bytes 540704 | tf_op jit(solution)/shard_map/ppermute | solution.py:908
  123.0 7.4 %heads_forward.1 = (f32[96,2048]{1,0:T(8,128)S(1)}, bf16[9216,256]{1,0:T(8,128)(2,1)S(1)}) custom-call(bf16[96,2048]{1,0:T(8,128)(2,1)S(1)} %fusion.7.q_ref, bf16[96,2048]{1,0:T(8,128)(2,1)S(1)} %pad_maximum_fusion.7.k_ref, bf16[96,2048]{1,0:T(8,128)(2,1)S(1)} %pad_maximum_fusion.8.v_ref), custom_call_target="tpu_custom_call" | custom-call | flops 905969664 | bytes 4718592 | tf_op jit(solution)/shard_map/heads_forward/pallas_call | solution.py:389
  132.7 9.5 %collective-permute-done.18.refs_7_ = bf16[192,2048]{1,0:T(8,128)(2,1)} collective-permute-done((bf16[192,2048]{1,0:T(8,128)(2,1)}, bf16[192,2048]{1,0:T(8,128)(2,1)}, u32[]{:S(2)}, u32[]{:S(2)}) %collective-permute-start.18) | collective-permute-done | bytes 786464 | tf_op jit(solution)/shard_map/ppermute | solution.py:908
  145.7 7.0 %all-to-all-start.3 = ((bf16[16,48,256]{2,1,0:T(8,128)(2,1)}), bf16[16,48,256]{2,1,0:T(8,128)(2,1)S(1)}, u32[]{:S(2)}, u32[]{:S(2)}) async-start(bf16[16,48,256]{2,1,0:T(8,128)(2,1)} %bitcast.258), calls=%async_computation.3 | async-start | bytes 786432 | tf_op jit(solution)/shard_map/all_to_all | solution.py:1003
  155.5 17.1 %all-to-all-done.3.heads_ref = bf16[16,48,256]{2,1,0:T(8,128)(2,1)S(1)} async-done(((bf16[16,48,256]{2,1,0:T(8,128)(2,1)}), bf16[16,48,256]{2,1,0:T(8,128)(2,1)S(1)}, u32[]{:S(2)}, u32[]{:S(2)}) %all-to-all-start.3) | async-done | bytes 393248 | tf_op jit(solution)/shard_map/all_to_all | solution.py:1003
  177.8 5.4 %project_out.1 = (bf16[384,1536]{1,0:T(8,128)(2,1)}, bf16[384,512]{1,0:T(8,128)(2,1)S(1)}, f32[2,128,1536]{2,1,0:T(8,128)}, bf16[2,128,1536]{2,1,0:T(8,128)(2,1)S(1)}) custom-call(s32[18]{0:T(128)S(1)} %pad_add_fusion.at_ref, bf16[16,48,256]{2,1,0:T(8,128)(2,1)S(1)} %all-to-all-done.3.heads_ref, ...), custom_call_target="tpu_custom_call" | custom-call | flops 603979776 | bytes 8650824 | tf_op jit(solution)/shard_map/project_out/pallas_call | solution.py:425
  188.1 16.1 %collective-permute-done.25.refs_5_ = bf16[192,2048]{1,0:T(8,128)(2,1)S(1)} collective-permute-done((bf16[192,2048]{1,0:T(8,128)(2,1)}, bf16[192,2048]{1,0:T(8,128)(2,1)S(1)}, u32[]{:S(2)}, u32[]{:S(2)}) %collective-permute-start.25) | collective-permute-done | bytes 786464 | tf_op jit(solution)/shard_map/ppermute | solution.py:908
  205.6 5.6 %hidden_gradient.1 = (bf16[512,1536]{1,0:T(8,128)(2,1)}, bf16[1024,1536]{1,0:T(8,128)(2,1)}, bf16[512,1024]{1,0:T(8,128)(2,1)}) custom-call(s32[18]{0:T(128)S(1)} %pad_add_fusion.at_ref, bf16[2,128,1536]{2,1,0:T(8,128)(2,1)S(1)} %copy-done.22, bf16[2,128,1536]{2,1,0:T(8,128)(2,1)S(1)} %copy-done.43, ...), custom_call_target="tpu_custom_call" | custom-call | flops 1610612736 | bytes 11665480 | tf_op jit(solution)/shard_map/hidden_gradient/pallas_call | solution.py:425
  211.3 12.6 %collective-permute-done.28 = bf16[2,128,1536]{2,1,0:T(8,128)(2,1)S(1)} collective-permute-done((bf16[2,128,1536]{2,1,0:T(8,128)(2,1)S(1)}, bf16[2,128,1536]{2,1,0:T(8,128)(2,1)S(1)}, u32[]{:S(2)}, u32[]{:S(2)}) %collective-permute-start.28) | collective-permute-done | bytes 786464 | tf_op jit(solution)/shard_map/ppermute | solution.py:963
  227.0 9.2 %collective-permute-done.29 = bf16[96,2048]{1,0:T(8,128)(2,1)S(1)} collective-permute-done((bf16[96,2048]{1,0:T(8,128)(2,1)S(1)}, bf16[96,2048]{1,0:T(8,128)(2,1)S(1)}, u32[]{:S(2)}, u32[]{:S(2)}) %collective-permute-start.29) | collective-permute-done | bytes 393248 | tf_op jit(solution)/shard_map/ppermute | solution.py:908
  237.8 12.4 %feed_forward.1 = (bf16[512,1536]{1,0:T(8,128)(2,1)}, bf16[512,1024]{1,0:T(8,128)(2,1)}, bf16[512,2048]{1,0:T(8,128)(2,1)}, f32[2,128,1536]{2,1,0:T(8,128)}, bf16[2,128,1536]{2,1,0:T(8,128)(2,1)S(1)}) custom-call(s32[18]{0:T(128)S(1)} %pad_add_fusion.at_ref, bf16[2,128,1536]{2,1,0:T(8,128)(2,1)S(1)} %multiply_convert_fusion.own_ref, ...), custom_call_target="tpu_custom_call" | custom-call | flops 6442450944 | bytes 15990856 | tf_op jit(solution)/shard_map/feed_forward/pallas_call | solution.py:425
  255.2 9.5 %feed_forward_grads.1 = (bf16[8,192,2048]{2,1,0:T(8,128)(2,1)}, bf16[8,128,1536]{2,1,0:T(8,128)(2,1)}) custom-call(s32[18]{0:T(128)S(1)} %pad_add_fusion.at_ref, bf16[512,1536]{1,0:T(8,128)(2,1)S(1)} %copy-done.48, bf16[512,2048]{1,0:T(8,128)(2,1)} %get-tuple-element.194.d_both_ref, bf16[512,1024]{1,0:T(8,128)(2,1)S(1)} %copy-done.19, ...), custom_call_target="tpu_custom_call" | custom-call | flops 4831838208 | bytes 15728712 | tf_op jit(solution)/shard_map/feed_forward_grads/pallas_call | solution.py:425
  274.2 7.0 %collective-permute-done.36 = bf16[64,1536]{1,0:T(8,128)(2,1)S(1)} collective-permute-done((bf16[64,1536]{1,0:T(8,128)(2,1)S(1)}, bf16[64,1536]{1,0:T(8,128)(2,1)S(1)}, u32[]{:S(2)}, u32[]{:S(2)}) %collective-permute-start.36) | collective-permute-done | bytes 196640 | tf_op jit(solution)/shard_map/ppermute | solution.py:940
  293.9 7.0 %collective-permute-done.41 = bf16[64,1536]{1,0:T(8,128)(2,1)S(1)} collective-permute-done((bf16[64,1536]{1,0:T(8,128)(2,1)S(1)}, bf16[64,1536]{1,0:T(8,128)(2,1)S(1)}, u32[]{:S(2)}, u32[]{:S(2)}) %collective-permute-start.41) | collective-permute-done | bytes 196640 | tf_op jit(solution)/shard_map/ppermute | solution.py:940
  302.3 5.8 %all-to-all-start.4 = ((bf16[16,48,256]{2,1,0:T(8,128)(2,1)}), bf16[16,48,256]{2,1,0:T(8,128)(2,1)S(1)}, u32[]{:S(2)}, u32[]{:S(2)}) async-start(bf16[16,48,256]{2,1,0:T(8,128)(2,1)} %get-tuple-element.212), calls=%async_computation.4 | async-start | bytes 786432 | tf_op jit(solution)/shard_map/all_to_all | solution.py:1003
  317.7 4.8 layer_output.1
  323.7 6.8 %collective-permute-done.46 = bf16[64,1536]{1,0:T(8,128)(2,1)S(1)} collective-permute-done((bf16[64,1536]{1,0:T(8,128)(2,1)}, bf16[64,1536]{1,0:T(8,128)(2,1)S(1)}, u32[]{:S(2)}, u32[]{:S(2)}) %collective-permute-start.46) | collective-permute-done | bytes 196640 | tf_op jit(solution)/shard_map/ppermute | solution.py:940
  340.3 5.9 %heads_backward.1 = (f32[96,2048]{1,0:T(8,128)S(1)}, f32[96,2048]{1,0:T(8,128)S(1)}, f32[96,2048]{1,0:T(8,128)S(1)}) custom-call(bf16[96,2048]{1,0:T(8,128)(2,1)S(1)} %fusion.7.q_ref, bf16[96,2048]{1,0:T(8,128)(2,1)S(1)} %pad_maximum_fusion.7.k_ref, bf16[96,2048]{1,0:T(8,128)(2,1)S(1)} %pad_maximum_fusion.8.v_ref, bf16[9216,256]{1,0:T(8,128)(2,1)S(1)} %copy-done.1, ...), custom_call_target="tpu_custom_call" | custom-call | flops 1811939328 | bytes 4718592 | tf_op jit(solution)/shard_map/heads_backward/pallas_call | solution.py:408
  357.1 12.7 %collective-permute-done.50 = bf16[64,1536]{1,0:T(8,128)(2,1)S(1)} collective-permute-done((bf16[64,1536]{1,0:T(8,128)(2,1)S(1)}, bf16[64,1536]{1,0:T(8,128)(2,1)S(1)}, u32[]{:S(2)}, u32[]{:S(2)}) %collective-permute-start.50) | collective-permute-done | bytes 196640 | tf_op jit(solution)/shard_map/ppermute | solution.py:940
  369.7 7.4 %collective-permute-done.49 = bf16[96,2048]{1,0:T(8,128)(2,1)S(1)} collective-permute-done((bf16[96,2048]{1,0:T(8,128)(2,1)S(1)}, bf16[96,2048]{1,0:T(8,128)(2,1)S(1)}, u32[]{:S(2)}, u32[]{:S(2)}) %collective-permute-start.49) | collective-permute-done | bytes 393248 | tf_op jit(solution)/shard_map/ppermute | solution.py:940
  385.2 5.1 all-to-all-start.6
  391.7 6.8 %collective-permute-done.54 = bf16[96,2048]{1,0:T(8,128)(2,1)S(1)} collective-permute-done((bf16[96,2048]{1,0:T(8,128)(2,1)}, bf16[96,2048]{1,0:T(8,128)(2,1)S(1)}, u32[]{:S(2)}, u32[]{:S(2)}) %collective-permute-start.54) | collective-permute-done | bytes 393248 | tf_op jit(solution)/shard_map/ppermute | solution.py:940
  409.6 13.3 %collective-permute-done.59 = bf16[64,1536]{1,0:T(8,128)(2,1)S(1)} collective-permute-done((bf16[64,1536]{1,0:T(8,128)(2,1)S(1)}, bf16[64,1536]{1,0:T(8,128)(2,1)S(1)}, u32[]{:S(2)}, u32[]{:S(2)}) %collective-permute-start.59) | collective-permute-done | bytes 196640 | tf_op jit(solution)/shard_map/ppermute | solution.py:940
  427.9 5.2 all-to-all-start.7
  446.6 52.4 %collective-permute-done.65 = bf16[64,1536]{1,0:T(8,128)(2,1)S(1)} collective-permute-done((bf16[64,1536]{1,0:T(8,128)(2,1)S(1)}, bf16[64,1536]{1,0:T(8,128)(2,1)S(1)}, u32[]{:S(2)}, u32[]{:S(2)}) %collective-permute-start.65) | collective-permute-done | bytes 196640 | tf_op jit(solution)/shard_map/ppermute | solution.py:940
  504.2 8.5 %collective-permute-done.68 = bf16[2,48,2048]{2,1,0:T(8,128)(2,1)S(1)} collective-permute-done((bf16[2,48,2048]{2,1,0:T(8,128)(2,1)S(1)}, bf16[2,48,2048]{2,1,0:T(8,128)(2,1)S(1)}, u32[]{:S(2)}, u32[]{:S(2)}) %collective-permute-start.68) | collective-permute-done | bytes 393248 | tf_op jit(solution)/shard_map/ppermute | solution.py:963
  513.8 6.0 %collective-permute-done.63 = bf16[128,1536]{1,0:T(8,128)(2,1)S(1)} collective-permute-done((bf16[128,1536]{1,0:T(8,128)(2,1)S(1)}, bf16[128,1536]{1,0:T(8,128)(2,1)S(1)}, u32[]{:S(2)}, u32[]{:S(2)}) %collective-permute-start.63) | collective-permute-done | bytes 393248 | tf_op jit(solution)/shard_map/ppermute | solution.py:963
  (389 shorter events, 203.1 us)
Async XLA Ops:
  50.7 20.2 %collective-permute-start.16 = (bf16[128,1536]{1,0:T(8,128)(2,1)}, bf16[128,1536]{1,0:T(8,128)(2,1)}, u32[]{:S(2)}, u32[]{:S(2)}) collective-permute-start(bf16[128,1536]{1,0:T(8,128)(2,1)} %bitcast.275), channel_id=1, source_target_pairs={{0,1},{1,0},{2,3},{3,2},{4,5},{5,4},{6,7},{7,6},{8,9},{9,8},{10,11... | collective-permute-start | bytes 1179656 | tf_op jit(solution)/shard_map/ppermute | solution.py:963
  61.8 49.7 %all-to-all-start.2 = ((bf16[16,96,256]{2,1,0:T(8,128)(2,1)}), bf16[16,96,256]{2,1,0:T(8,128)(2,1)}, u32[]{:S(2)}, u32[]{:S(2)}) async-start(bf16[16,96,256]{2,1,0:T(8,128)(2,1)} %get-tuple-element.158), calls=%async_computation.2 | async-start | bytes 1572864 | tf_op jit(solution)/shard_map/all_to_all | solution.py:1003
  68.9 28.8 %collective-permute-start.12 = (bf16[176,1536]{1,0:T(8,128)(2,1)}, bf16[176,1536]{1,0:T(8,128)(2,1)S(1)}, u32[]{:S(2)}, u32[]{:S(2)}) collective-permute-start(bf16[176,1536]{1,0:T(8,128)(2,1)} %collective-permute-done.1.refs_7_), channel_id=1, source_target_pairs={{0,8},{8,16},{16,24},{24,28},{28,20},{20,12},{12,4},{4,0},{1,9},{9... | collective-permute-start | bytes 1622024 | tf_op jit(solution)/shard_map/ppermute | solution.py:908
  69.5 28.2 %collective-permute-start.13 = (bf16[176,1536]{1,0:T(8,128)(2,1)}, bf16[176,1536]{1,0:T(8,128)(2,1)S(1)}, u32[]{:S(2)}, u32[]{:S(2)}) collective-permute-start(bf16[176,1536]{1,0:T(8,128)(2,1)} %collective-permute-done.2.refs_1_), channel_id=1, source_target_pairs={{8,0},{16,8},{24,16},{28,24},{20,28},{12,20},{4,12},{0,4},{9,1},{1... | collective-permute-start | bytes 1622024 | tf_op jit(solution)/shard_map/ppermute | solution.py:909
  72.1 29.2 %collective-permute-start.17 = (bf16[2,128,1536]{2,1,0:T(8,128)(2,1)S(1)}, bf16[2,128,1536]{2,1,0:T(8,128)(2,1)S(1)}, u32[]{:S(2)}, u32[]{:S(2)}) collective-permute-start(bf16[2,128,1536]{2,1,0:T(8,128)(2,1)S(1)} %pad_maximum_fusion.1.own_ref), channel_id=1, source_target_pairs={{0,2},{2,0},{1,3},{3,1},{4,6},{6,4},{5,7},{7,5},{8,10},{10,8},{9,1... | collective-permute-start | bytes 2359304 | tf_op jit(solution)/shard_map/ppermute | solution.py:963
  118.4 23.7 %collective-permute-start.18 = (bf16[192,2048]{1,0:T(8,128)(2,1)}, bf16[192,2048]{1,0:T(8,128)(2,1)}, u32[]{:S(2)}, u32[]{:S(2)}) collective-permute-start(bf16[192,2048]{1,0:T(8,128)(2,1)} %bitcast.8.refs_0_), channel_id=1, source_target_pairs={{0,8},{8,16},{16,24},{24,28},{28,20},{20,12},{12,4},{4,0},{1,9},{9... | collective-permute-start | bytes 2359304 | tf_op jit(solution)/shard_map/ppermute | solution.py:908
  119.2 23.5 %collective-permute-start.19 = (bf16[192,2048]{1,0:T(8,128)(2,1)}, bf16[192,2048]{1,0:T(8,128)(2,1)}, u32[]{:S(2)}, u32[]{:S(2)}) collective-permute-start(bf16[192,2048]{1,0:T(8,128)(2,1)} %bitcast.8.refs_0_), channel_id=1, source_target_pairs={{8,0},{16,8},{24,16},{28,24},{20,28},{12,20},{4,12},{0,4},{9,1},{1... | collective-permute-start | bytes 2359304 | tf_op jit(solution)/shard_map/ppermute | solution.py:909
  142.8 29.8 %collective-permute-start.23 = (bf16[192,2048]{1,0:T(8,128)(2,1)}, bf16[192,2048]{1,0:T(8,128)(2,1)}, u32[]{:S(2)}, u32[]{:S(2)}) collective-permute-start(bf16[192,2048]{1,0:T(8,128)(2,1)} %collective-permute-done.18.refs_7_), channel_id=1, source_target_pairs={{0,8},{8,16},{16,24},{24,28},{28,20},{20,12},{12,4},{4,0},{1,9},{9... | collective-permute-start | bytes 2359304 | tf_op jit(solution)/shard_map/ppermute | solution.py:908
  144.5 28.1 %collective-permute-start.24 = (bf16[192,2048]{1,0:T(8,128)(2,1)}, bf16[192,2048]{1,0:T(8,128)(2,1)}, u32[]{:S(2)}, u32[]{:S(2)}) collective-permute-start(bf16[192,2048]{1,0:T(8,128)(2,1)} %collective-permute-done.19.refs_1_), channel_id=1, source_target_pairs={{8,0},{16,8},{24,16},{28,24},{20,28},{12,20},{4,12},{0,4},{9,1},{1... | collective-permute-start | bytes 2359304 | tf_op jit(solution)/shard_map/ppermute | solution.py:909
  145.7 26.9 %all-to-all-start.3 = ((bf16[16,48,256]{2,1,0:T(8,128)(2,1)}), bf16[16,48,256]{2,1,0:T(8,128)(2,1)S(1)}, u32[]{:S(2)}, u32[]{:S(2)}) async-start(bf16[16,48,256]{2,1,0:T(8,128)(2,1)} %bitcast.258), calls=%async_computation.3 | async-start | bytes 786432 | tf_op jit(solution)/shard_map/all_to_all | solution.py:1003
  184.0 20.2 %collective-permute-start.25 = (bf16[192,2048]{1,0:T(8,128)(2,1)}, bf16[192,2048]{1,0:T(8,128)(2,1)S(1)}, u32[]{:S(2)}, u32[]{:S(2)}) collective-permute-start(bf16[192,2048]{1,0:T(8,128)(2,1)} %collective-permute-done.23.refs_6_), channel_id=1, source_target_pairs={{0,8},{8,16},{16,24},{24,28},{28,20},{20,12},{12,4},{4,0},{1,9},{9... | collective-permute-start | bytes 2359304 | tf_op jit(solution)/shard_map/ppermute | solution.py:908
  184.9 19.9 %collective-permute-start.26 = (bf16[192,2048]{1,0:T(8,128)(2,1)}, bf16[192,2048]{1,0:T(8,128)(2,1)S(1)}, u32[]{:S(2)}, u32[]{:S(2)}) collective-permute-start(bf16[192,2048]{1,0:T(8,128)(2,1)} %collective-permute-done.24.refs_2_), channel_id=1, source_target_pairs={{8,0},{16,8},{24,16},{28,24},{20,28},{12,20},{4,12},{0,4},{9,1},{1... | collective-permute-start | bytes 2359304 | tf_op jit(solution)/shard_map/ppermute | solution.py:909
  254.4 19.6 %collective-permute-start.39 = (bf16[2,128,1536]{2,1,0:T(8,128)(2,1)S(1)}, bf16[2,128,1536]{2,1,0:T(8,128)(2,1)S(1)}, u32[]{:S(2)}, u32[]{:S(2)}) collective-permute-start(bf16[2,128,1536]{2,1,0:T(8,128)(2,1)S(1)} %get-tuple-element.265), channel_id=1, source_target_pairs={{0,1},{1,0},{2,3},{3,2},{4,5},{5,4},{6,7},{7,6},{8,9},{9,8},{10,11... | collective-permute-start | bytes 2359304 | tf_op jit(solution)/shard_map/ppermute | solution.py:963
  302.3 28.2 %all-to-all-start.4 = ((bf16[16,48,256]{2,1,0:T(8,128)(2,1)}), bf16[16,48,256]{2,1,0:T(8,128)(2,1)S(1)}, u32[]{:S(2)}, u32[]{:S(2)}) async-start(bf16[16,48,256]{2,1,0:T(8,128)(2,1)} %get-tuple-element.212), calls=%async_computation.4 | async-start | bytes 786432 | tf_op jit(solution)/shard_map/all_to_all | solution.py:1003
  310.5 19.9 %collective-permute-start.45 = (bf16[96,2048]{1,0:T(8,128)(2,1)}, bf16[96,2048]{1,0:T(8,128)(2,1)}, u32[]{:S(2)}, u32[]{:S(2)}) collective-permute-start(bf16[96,2048]{1,0:T(8,128)(2,1)} %get-tuple-element.280), channel_id=1, source_target_pairs={{0,8},{8,16},{16,24},{24,28},{28,20},{20,12},{12,4},{4,0},{1,9},{9... | collective-permute-start | bytes 1179656 | tf_op jit(solution)/shard_map/ppermute | solution.py:940
  311.1 19.4 %collective-permute-start.47 = (bf16[96,2048]{1,0:T(8,128)(2,1)}, bf16[96,2048]{1,0:T(8,128)(2,1)}, u32[]{:S(2)}, u32[]{:S(2)}) collective-permute-start(bf16[96,2048]{1,0:T(8,128)(2,1)} %get-tuple-element.279), channel_id=1, source_target_pairs={{8,0},{16,8},{24,16},{28,24},{20,28},{12,20},{4,12},{0,4},{9,1},{1... | collective-permute-start | bytes 1179656 | tf_op jit(solution)/shard_map/ppermute | solution.py:941
  323.7 66.6 %collective-permute-start.32 = (bf16[2,128,1536]{2,1,0:T(8,128)(2,1)}, bf16[2,128,1536]{2,1,0:T(8,128)(2,1)}, u32[]{:S(2)}, u32[]{:S(2)}) collective-permute-start(bf16[2,128,1536]{2,1,0:T(8,128)(2,1)} %get-tuple-element.192), channel_id=1, source_target_pairs={{0,2},{2,0},{1,3},{3,1},{4,6},{6,4},{5,7},{7,5},{8,10},{10,8},{9,1... | collective-permute-start | bytes 2359304 | tf_op jit(solution)/shard_map/ppermute | solution.py:963
  333.7 43.4 %all-to-all-start.5 = ((bf16[8,48,1536]{2,1,0:T(8,128)(2,1)}), bf16[8,48,1536]{2,1,0:T(8,128)(2,1)}, u32[]{:S(2)}, u32[]{:S(2)}) async-start(bf16[8,48,1536]{2,1,0:T(8,128)(2,1)} %bitcast.269), calls=%async_computation.5 | async-start | bytes 2359296 | tf_op jit(solution)/shard_map/all_to_all | solution.py:1003
  349.7 20.0 %collective-permute-start.50 = (bf16[64,1536]{1,0:T(8,128)(2,1)S(1)}, bf16[64,1536]{1,0:T(8,128)(2,1)S(1)}, u32[]{:S(2)}, u32[]{:S(2)}) collective-permute-start(bf16[64,1536]{1,0:T(8,128)(2,1)S(1)} %get-tuple-element.294), channel_id=1, source_target_pairs={{0,8},{8,16},{16,24},{24,28},{28,20},{20,12},{12,4},{4,0},{1,9},{9... | collective-permute-start | bytes 589832 | tf_op jit(solution)/shard_map/ppermute | solution.py:940
  350.3 19.4 %collective-permute-start.52 = (bf16[64,1536]{1,0:T(8,128)(2,1)S(1)}, bf16[64,1536]{1,0:T(8,128)(2,1)S(1)}, u32[]{:S(2)}, u32[]{:S(2)}) collective-permute-start(bf16[64,1536]{1,0:T(8,128)(2,1)S(1)} %get-tuple-element.293), channel_id=1, source_target_pairs={{8,0},{16,8},{24,16},{28,24},{20,28},{12,20},{4,12},{0,4},{9,1},{1... | collective-permute-start | bytes 589832 | tf_op jit(solution)/shard_map/ppermute | solution.py:941
  353.4 23.7 %collective-permute-start.49 = (bf16[96,2048]{1,0:T(8,128)(2,1)S(1)}, bf16[96,2048]{1,0:T(8,128)(2,1)S(1)}, u32[]{:S(2)}, u32[]{:S(2)}) collective-permute-start(bf16[96,2048]{1,0:T(8,128)(2,1)S(1)} %get-tuple-element.278), channel_id=1, source_target_pairs={{0,8},{8,16},{16,24},{24,28},{28,20},{20,12},{12,4},{4,0},{1,9},{9... | collective-permute-start | bytes 1179656 | tf_op jit(solution)/shard_map/ppermute | solution.py:940
  354.4 22.7 %collective-permute-start.51 = (bf16[96,2048]{1,0:T(8,128)(2,1)S(1)}, bf16[96,2048]{1,0:T(8,128)(2,1)S(1)}, u32[]{:S(2)}, u32[]{:S(2)}) collective-permute-start(bf16[96,2048]{1,0:T(8,128)(2,1)S(1)} %get-tuple-element.277), channel_id=1, source_target_pairs={{8,0},{16,8},{24,16},{28,24},{20,28},{12,20},{4,12},{0,4},{9,1},{1... | collective-permute-start | bytes 1179656 | tf_op jit(solution)/shard_map/ppermute | solution.py:941
  385.2 39.3 %all-to-all-start.6 = ((bf16[16,96,256]{2,1,0:T(8,128)(2,1)}), bf16[16,96,256]{2,1,0:T(8,128)(2,1)S(1)}, u32[]{:S(2)}, u32[]{:S(2)}) async-start(bf16[16,96,256]{2,1,0:T(8,128)(2,1)} %pad_maximum_fusion.3), calls=%async_computation.6 | async-start | bytes 1572864 | tf_op jit(solution)/shard_map/all_to_all | solution.py:1003
  400.0 23.0 %collective-permute-start.58 = (bf16[96,2048]{1,0:T(8,128)(2,1)S(1)}, bf16[96,2048]{1,0:T(8,128)(2,1)S(1)}, u32[]{:S(2)}, u32[]{:S(2)}) collective-permute-start(bf16[96,2048]{1,0:T(8,128)(2,1)S(1)} %get-tuple-element.274), channel_id=1, source_target_pairs={{0,8},{8,16},{16,24},{24,28},{28,20},{20,12},{12,4},{4,0},{1,9},{9... | collective-permute-start | bytes 1179656 | tf_op jit(solution)/shard_map/ppermute | solution.py:940
  400.1 24.4 %collective-permute-start.60 = (bf16[96,2048]{1,0:T(8,128)(2,1)S(1)}, bf16[96,2048]{1,0:T(8,128)(2,1)}, u32[]{:S(2)}, u32[]{:S(2)}) collective-permute-start(bf16[96,2048]{1,0:T(8,128)(2,1)S(1)} %get-tuple-element.273), channel_id=1, source_target_pairs={{8,0},{16,8},{24,16},{28,24},{20,28},{12,20},{4,12},{0,4},{9,1},{1... | collective-permute-start | bytes 1179656 | tf_op jit(solution)/shard_map/ppermute | solution.py:941
  408.2 32.2 %collective-permute-start.33 = (bf16[128,1536]{1,0:T(8,128)(2,1)}, bf16[128,1536]{1,0:T(8,128)(2,1)}, u32[]{:S(2)}, u32[]{:S(2)}) collective-permute-start(bf16[128,1536]{1,0:T(8,128)(2,1)} %fusion.33), channel_id=1, source_target_pairs={{0,1},{1,0},{2,3},{3,2},{4,5},{5,4},{6,7},{7,6},{8,9},{9,8},{10,11... | collective-permute-start | bytes 1179656 | tf_op jit(solution)/shard_map/ppermute | solution.py:963
  427.9 94.3 %all-to-all-start.7 = ((bf16[32,48,768]{2,1,0:T(8,128)(2,1)}), bf16[32,48,768]{2,1,0:T(8,128)(2,1)S(1)}, u32[]{:S(2)}, u32[]{:S(2)}) async-start(bf16[32,48,768]{2,1,0:T(8,128)(2,1)} %bitcast.249), calls=%async_computation.7 | async-start | bytes 4718592 | tf_op jit(solution)/shard_map/all_to_all | solution.py:1003
  436.2 62.8 %collective-permute-start.64 = (bf16[96,2048]{1,0:T(8,128)(2,1)S(1)}, bf16[96,2048]{1,0:T(8,128)(2,1)S(1)}, u32[]{:S(2)}, u32[]{:S(2)}) collective-permute-start(bf16[96,2048]{1,0:T(8,128)(2,1)S(1)} %get-tuple-element.245), channel_id=1, source_target_pairs={{0,8},{8,16},{16,24},{24,28},{28,20},{20,12},{12,4},{4,0},{1,9},{9... | collective-permute-start | bytes 1179656 | tf_op jit(solution)/shard_map/ppermute | solution.py:940
  436.8 62.2 %collective-permute-start.66 = (bf16[96,2048]{1,0:T(8,128)(2,1)S(1)}, bf16[96,2048]{1,0:T(8,128)(2,1)S(1)}, u32[]{:S(2)}, u32[]{:S(2)}) collective-permute-start(bf16[96,2048]{1,0:T(8,128)(2,1)S(1)} %get-tuple-element.247), channel_id=1, source_target_pairs={{8,0},{16,8},{24,16},{28,24},{20,28},{12,20},{4,12},{0,4},{9,1},{1... | collective-permute-start | bytes 1179656 | tf_op jit(solution)/shard_map/ppermute | solution.py:941
  438.3 60.7 %collective-permute-start.65 = (bf16[64,1536]{1,0:T(8,128)(2,1)S(1)}, bf16[64,1536]{1,0:T(8,128)(2,1)S(1)}, u32[]{:S(2)}, u32[]{:S(2)}) collective-permute-start(bf16[64,1536]{1,0:T(8,128)(2,1)S(1)} %get-tuple-element.246), channel_id=1, source_target_pairs={{0,8},{8,16},{16,24},{24,28},{28,20},{20,12},{12,4},{4,0},{1,9},{9... | collective-permute-start | bytes 589832 | tf_op jit(solution)/shard_map/ppermute | solution.py:940
  438.9 60.1 %collective-permute-start.67 = (bf16[64,1536]{1,0:T(8,128)(2,1)S(1)}, bf16[64,1536]{1,0:T(8,128)(2,1)S(1)}, u32[]{:S(2)}, u32[]{:S(2)}) collective-permute-start(bf16[64,1536]{1,0:T(8,128)(2,1)S(1)} %get-tuple-element.248), channel_id=1, source_target_pairs={{8,0},{16,8},{24,16},{28,24},{20,28},{12,20},{4,12},{0,4},{9,1},{1... | collective-permute-start | bytes 589832 | tf_op jit(solution)/shard_map/ppermute | solution.py:941
  446.6 56.7 %collective-permute-start.62 = (bf16[2,128,1536]{2,1,0:T(8,128)(2,1)S(1)}, bf16[2,128,1536]{2,1,0:T(8,128)(2,1)S(1)}, u32[]{:S(2)}, u32[]{:S(2)}) collective-permute-start(bf16[2,128,1536]{2,1,0:T(8,128)(2,1)S(1)} %get-tuple-element.239), channel_id=1, source_target_pairs={{0,2},{2,0},{1,3},{3,1},{4,6},{6,4},{5,7},{7,5},{8,10},{10,8},{9,1... | collective-permute-start | bytes 2359304 | tf_op jit(solution)/shard_map/ppermute | solution.py:963
  (121 other events, 1158.5 us)

commit v3 on v2

--- a/solution.py
+++ b/solution.py
@@ -331,10 +331,35 @@
     )
 
 
-def heads_forward_kernel(step, q_ref, k_ref, v_ref, mixed_ref, prob_ref):
-    tokens = q_ref.shape[1]
+def rotate(values, cosine, sine):
+    half = values.shape[0] // 2
+    first, second = values[:half], values[half:]
+    return jnp.concatenate([first * cosine - second * sine, second * cosine + first * sine], axis=0)
+
+
+def rotate_back(values, cosine, sine):
+    half = values.shape[0] // 2
+    first, second = values[:half], values[half:]
+    return jnp.concatenate([first * cosine + second * sine, second * cosine - first * sine], axis=0)
+
+
+def heads_forward_kernel(
+    count, at_ref, q_ref, own_ref, other_ref, cos_ref, sin_ref,
+    send_ref, mixed_ref, prob_ref, k_ref, v_ref, turn_ref,
+):
+    core = at_ref[2 * count]
+    half = own_ref.shape[1]
+    here = pl.ds(pl.multiple_of(core * half, half), half)
+    there = pl.ds(pl.multiple_of((1 - core) * half, half), half)
+    turn_ref[here, :] = own_ref[0].astype(f32)
+    turn_ref[there, :] = other_ref[0].astype(f32)
+    k_ref[...] = rotate(turn_ref[...], cos_ref[...], sin_ref[...]).astype(bf16)
+    v_ref[here, :] = own_ref[1]
+    v_ref[there, :] = other_ref[1]
+    step = send_ref.shape[2]
     offset = 0
-    for begin in range(0, tokens, step):
+    for block in range(count):
+        begin = block * step
         end = begin + step
         scores = dot_at(k_ref[:, 0:end], q_ref[:, begin:end], 0, 0)
         key = lax.broadcasted_iota(jnp.int32, (step, step), 0)
@@ -352,25 +377,50 @@
         prob_ref[offset + begin : offset + end, :] = (last * inverse).astype(bf16)
         if begin:
             prob_ref[offset : offset + begin, :] = (first * inverse).astype(bf16)
-        mixed_ref[:, begin:end] = dot_at(
-            v_ref[:, 0:end], prob_ref[offset : offset + end, :], 1, 0
-        )
+        mixed = dot_at(v_ref[:, 0:end], prob_ref[offset : offset + end, :], 1, 0)
+        mixed_ref[:, begin:end] = mixed
+        send_ref[2 * block] = mixed[:half].astype(bf16)
+        send_ref[2 * block + 1] = mixed[half:].astype(bf16)
         offset += end
 
 
+def heads_forward(at, q, own, other, cosine, sine, count):
+    size, tokens = q.shape
+    step = tokens // count
+    pairs = step * count * (count + 1) // 2
+    return on_chip(
+        functools.partial(heads_forward_kernel, count),
+        [
+            like(bf16, 2 * count, size // 2, step),
+            like(f32, size, tokens),
+            like(bf16, pairs, step),
+            like(bf16, size, tokens),
+            like(bf16, size, tokens),
+        ],
+        [at, q, own, other, cosine, sine],
+        4 * size * pairs * step,
+        scratch=[pltpu.VMEM((size, tokens), f32)],
+        name="heads_forward",
+    )
+
+
 def heads_backward_kernel(
-    step, q_ref, k_ref, v_ref, prob_ref, mixed_ref, d_mixed_ref, d_q_ref, d_k_ref, d_v_ref
+    count, at_ref, q_ref, k_ref, v_ref, prob_ref, mixed_ref, back_ref, cos_ref, sin_ref,
+    d_q_ref, kept_ref, away_ref, d_k_ref, d_v_ref,
 ):
-    tokens = q_ref.shape[1]
+    core = at_ref[2 * count]
+    half, step = back_ref.shape[1:]
     offset = 0
-    for begin in range(0, tokens, step):
+    for block in range(count):
+        begin = block * step
         end = begin + step
-        d_mixed = d_mixed_ref[:, begin:end]
+        d_mixed = jnp.concatenate([back_ref[2 * block], back_ref[2 * block + 1]], axis=0)
         delta = jnp.sum(d_mixed.astype(f32) * mixed_ref[:, begin:end], axis=0, keepdims=True)
         prob = prob_ref[offset : offset + end, :]
         d_prob = dot_at(v_ref[:, 0:end], d_mixed, 0, 0)
         d_scores = (prob.astype(f32) * (d_prob - delta)).astype(bf16)
-        d_q_ref[:, begin:end] = dot_at(k_ref[:, 0:end], d_scores, 1, 0) * score_scale
+        d_q = dot_at(k_ref[:, 0:end], d_scores, 1, 0) * score_scale
+        d_q_ref[:, begin:end] = rotate_back(d_q, cos_ref[:, begin:end], sin_ref[:, begin:end])
         d_v = dot_at(d_mixed, prob, 1, 1)
         d_k = dot_at(q_ref[:, begin:end], d_scores, 1, 1) * ln_2
         if begin:
@@ -379,43 +429,62 @@
         d_v_ref[:, begin:end] = d_v[:, begin:end]
         d_k_ref[:, begin:end] = d_k[:, begin:end]
         offset += end
-
-
-def heads_forward(q, k, v, step):
+    d_k_ref[...] = rotate_back(d_k_ref[...], cos_ref[...], sin_ref[...])
+    here = pl.ds(pl.multiple_of(core * half, half), half)
+    there = pl.ds(pl.multiple_of((1 - core) * half, half), half)
+    kept_ref[0] = d_k_ref[here, :]
+    kept_ref[1] = d_v_ref[here, :]
+    away_ref[0] = d_k_ref[there, :].astype(bf16)
+    away_ref[1] = d_v_ref[there, :].astype(bf16)
+
+
+def heads_backward(at, q, k, v, prob, mixed, d_mixed, cosine, sine, count):
     size, tokens = q.shape
-    blocks = tokens // step
-    pairs = step * blocks * (blocks + 1) // 2
-    whole = pl.BlockSpec(memory_space=pltpu.VMEM)
-    return pl.pallas_call(
-        functools.partial(heads_forward_kernel, step),
-        out_shape=(
-            jax.ShapeDtypeStruct((size, tokens), f32),
-            jax.ShapeDtypeStruct((pairs, step), bf16),
-        ),
-        in_specs=[whole] * 3,
-        out_specs=(whole, whole),
-        compiler_params=pltpu.CompilerParams(vmem_limit_bytes=40 * 2**20),
-        cost_estimate=pl.CostEstimate(
-            flops=4 * size * pairs * step, bytes_accessed=pairs * step * 2, transcendentals=pairs * step
-        ),
-        name="heads_forward",
-    )(q, k, v)
-
-
-def heads_backward(q, k, v, prob, mixed, d_mixed, step):
-    size, tokens = q.shape
-    whole = pl.BlockSpec(memory_space=pltpu.VMEM)
-    return pl.pallas_call(
-        functools.partial(heads_backward_kernel, step),
-        out_shape=(jax.ShapeDtypeStruct((size, tokens), f32),) * 3,
-        in_specs=[whole] * 6,
-        out_specs=(whole,) * 3,
-        compiler_params=pltpu.CompilerParams(vmem_limit_bytes=40 * 2**20),
-        cost_estimate=pl.CostEstimate(
-            flops=8 * size * prob.size, bytes_accessed=prob.size * 2, transcendentals=0
-        ),
+    return on_chip(
+        functools.partial(heads_backward_kernel, count),
+        [
+            like(f32, size, tokens),
+            like(f32, 2, size // 2, tokens),
+            like(bf16, 2, size // 2, tokens),
+        ],
+        [at, q, k, v, prob, mixed, d_mixed, cosine, sine],
+        8 * size * prob.size,
+        scratch=[pltpu.VMEM((size, tokens), f32)] * 2,
         name="heads_backward",
-    )(q, k, v, prob, mixed, d_mixed)
+    )
+
+
+def heads_send_kernel(at_ref, d_q_ref, kept_ref, other_ref, send_ref, joined_ref):
+    half = kept_ref.shape[1]
+    quarter = half // 2
+    step = send_ref.shape[2]
+    d_kv = kept_ref[...] + other_ref[...].astype(f32)
+    joined_ref[: 2 * half, :] = d_q_ref[...].astype(bf16)
+    joined_ref[2 * half : 3 * half, :] = d_kv[0].astype(bf16)
+    joined_ref[3 * half :, :] = d_kv[1].astype(bf16)
+    for block in range(send_ref.shape[0] // 2):
+        columns = slice(block * step, (block + 1) * step)
+        for side in range(2):
+            rows = slice(side * quarter, (side + 1) * quarter)
+            send_ref[2 * block + side] = jnp.concatenate(
+                [
+                    d_q_ref[side * half : (side + 1) * half, columns],
+                    d_kv[0, rows, columns],
+                    d_kv[1, rows, columns],
+                ],
+                axis=0,
+            ).astype(bf16)
+
+
+def heads_send(at, d_q, kept, other, count):
+    size, tokens = d_q.shape
+    return on_chip(
+        heads_send_kernel,
+        [like(bf16, 2 * count, size, tokens // count), like(bf16, 2 * size, tokens)],
+        [at, d_q, kept, other],
+        8 * d_q.size,
+        name="heads_send",
+    )
 
 
 def on_chip(kernel, out_shape, args, flops, blocks=(), scratch=(), name=None):
@@ -527,36 +596,76 @@
     return out
 
 
-def project_heads_kernel(at_ref, own_ref, other_ref, *refs):
-    blocks, (n_ref, weight_ref, heads_ref, sem_ref) = refs[:-4], refs[-4:]
-    copies = block_copies(at_ref, blocks, weight_ref, sem_ref)
+def head_columns_kernel(at_ref, gain_ref, query_ref, key_ref, value_ref, out_ref):
+    gain = gain_ref[...]
+    query = query_ref[...].astype(f32) * gain
+    key = key_ref[...].astype(f32) * gain
+    value = value_ref[...].astype(f32) * gain
+    half = HEAD_SIZE // 2
+    for head in range(out_ref.shape[0] // 2):
+        columns = jnp.concatenate(
+            [
+                query[:, head * HEAD_SIZE : (head + 1) * HEAD_SIZE],
+                key[:, head * half : (head + 1) * half],
+                value[:, head * half : (head + 1) * half],
+            ],
+            axis=1,
+        ).astype(bf16)
+        out_ref[2 * head] = columns
+        out_ref[2 * head + 1] = columns
+
+
+def head_columns(at, gain, query, key, value):
+    own, width = query.shape
+    (out,) = on_chip(
+        head_columns_kernel,
+        [like(bf16, 2 * (width // HEAD_SIZE), own, 2 * HEAD_SIZE)],
+        [at, gain, query, key, value],
+        own * width,
+        name="head_columns",
+    )
+    return out
+
+
+def sequence_copies(at_ref, block_refs, whole_ref, sem_ref):
+    count = len(block_refs) // 2
+    core = at_ref[2 * count]
+    rows = block_refs[0].shape[0]
+    copies = []
+    for i, block_ref in enumerate(block_refs):
+        side = core if i < count else 1 - core
+        start = pl.multiple_of((2 * at_ref[i % count] + side) * rows, rows)
+        copies.append(
+            pltpu.make_async_copy(block_ref, whole_ref.at[pl.ds(start, rows), :], sem_ref.at[i])
+        )
+    return copies
+
+
+def project_heads_kernel(at_ref, weight_ref, cos_ref, sin_ref, *refs):
+    blocks, (q_ref, kv_ref, n_ref, sem_ref) = refs[:-4], refs[-4:]
+    copies = sequence_copies(at_ref, blocks, n_ref, sem_ref)
     for copy in copies:
         copy.start()
-    join_rows(at_ref, len(blocks), own_ref, other_ref, n_ref)
     for copy in copies:
         copy.wait()
-    size, rows = heads_ref.shape[1:]
-    for seq in range(2):
-        part = dot_at(weight_ref[...], n_ref[seq * rows : (seq + 1) * rows, :], 0, 1).astype(bf16)
-        for head in range(heads_ref.shape[0] // 2):
-            heads_ref[2 * head + seq] = part[head * size : (head + 1) * size, :]
-
-
-def project_heads(at, own, other, blocks):
-    count = len(blocks)
-    _, rows, width = own.shape
-    columns = blocks[0].shape[1]
+    half = kv_ref.shape[1]
+    out = dot_at(weight_ref[...], n_ref[...], 0, 1)
+    q = rotate(out[: 2 * half], cos_ref[...], sin_ref[...])
+    q_ref[...] = (q * (score_scale * log2_e)).astype(bf16)
+    kv_ref[0] = out[2 * half : 3 * half].astype(bf16)
+    kv_ref[1] = out[3 * half :].astype(bf16)
+
+
+def project_heads(at, weight, cosine, sine, blocks):
+    half, tokens = cosine.shape
+    rows, width = blocks[0].shape
     return on_chip(
         project_heads_kernel,
-        [
-            like(bf16, 4 * rows, width),
-            like(bf16, width, columns),
-            like(bf16, 2 * count, columns // count, 2 * rows),
-        ],
-        [at, own, other],
-        8 * rows * width * columns,
+        [like(bf16, 2 * half, tokens), like(bf16, 2, half, tokens)],
+        [at, weight, cosine, sine],
+        8 * half * tokens * width,
         blocks=blocks,
-        scratch=[pltpu.SemaphoreType.DMA((count,))],
+        scratch=[pltpu.VMEM((tokens, width), bf16), pltpu.SemaphoreType.DMA((len(blocks),))],
         name="project_heads",
     )
 
@@ -731,38 +840,61 @@
     )
 
 
-def heads_grad_kernel(at_ref, heads_ref, n_ref, joined_ref, grad_ref):
+def heads_grad_kernel(at_ref, joined_ref, *refs):
+    blocks, (grad_ref, n_ref, sem_ref) = refs[:-3], refs[-3:]
+    copies = sequence_copies(at_ref, blocks, n_ref, sem_ref)
+    for copy in copies:
+        copy.start()
+    for copy in copies:
+        copy.wait()
+    grad_ref[...] = dot_at(n_ref[...], joined_ref[...], 0, 1).astype(bf16)
+
+
+def heads_grad(at, joined, blocks):
+    columns, tokens = joined.shape
+    width = blocks[0].shape[1]
+    (out,) = on_chip(
+        heads_grad_kernel,
+        [like(bf16, width, columns)],
+        [at, joined],
+        2 * tokens * width * columns,
+        blocks=blocks,
+        scratch=[pltpu.VMEM((tokens, width), bf16), pltpu.SemaphoreType.DMA((len(blocks),))],
+        name="heads_grad",
+    )
+    return out
+
+
+def heads_input_kernel(at_ref, heads_ref, *refs):
+    blocks = refs[:-6]
+    kept_ref, away_ref, out_ref, joined_ref, weight_ref, sem_ref = refs[-6:]
+    copies = block_copies(at_ref, blocks, weight_ref, sem_ref)
+    for copy in copies:
+        copy.start()
     join_heads(heads_ref, joined_ref)
-    grad_ref[...] = dot_at(n_ref[...], joined_ref[...], 0, 1).astype(bf16)
-
-
-def heads_grad(at, heads, n):
-    rows, width = n.shape
-    columns = heads.shape[0] // 2 * heads.shape[1]
-    return on_chip(
-        heads_grad_kernel,
-        [like(bf16, columns, rows), like(bf16, width, columns)],
-        [at, heads, n],
-        2 * rows * width * columns,
-        name="heads_grad",
-    )
-
-
-def heads_input_kernel(at_ref, joined_ref, weight_ref, kept_ref, away_ref, out_ref):
+    for copy in copies:
+        copy.wait()
     out_ref[...] = dot_at(joined_ref[...], weight_ref[...], 0, 1)
-    count = weight_ref.shape[1] // HEAD_SIZE
-    part_rows(at_ref, count, out_ref, kept_ref, away_ref)
-
-
-def heads_input(at, joined, weight):
-    width, columns = weight.shape
-    rows = joined.shape[1] // 4
+    part_rows(at_ref, len(blocks), out_ref, kept_ref, away_ref)
+
+
+def heads_input(at, heads, blocks):
+    count = len(blocks)
+    block, columns = blocks[0].shape
+    rows = heads.shape[2] // 2
+    width = count * block
     return on_chip(
         heads_input_kernel,
         [like(f32, 2, rows, width), like(bf16, 2, rows, width)],
-        [at, joined, weight],
+        [at, heads],
         0,
-        scratch=[pltpu.VMEM((4 * rows, width), f32)],
+        blocks=blocks,
+        scratch=[
+            pltpu.VMEM((4 * rows, width), f32),
+            pltpu.VMEM((columns, 4 * rows), bf16),
+            pltpu.VMEM((width, columns), bf16),
+            pltpu.SemaphoreType.DMA((count,)),
+        ],
         name="heads_input",
     )
 
@@ -789,22 +921,12 @@
     at_ref, terms_ref, gain_ref, query_ref, key_ref, value_ref, d_query, d_key, d_value, d_gain
 ):
     half = HEAD_SIZE // 2
-    quarter = HEAD_SIZE // 4
-    positions = terms_ref.shape[0] // 4
-    groups = terms_ref.shape[2] // HEAD_SIZE
-    parts = []
-    for t in range(4):
-        total = terms_ref[t].astype(f32)
-        for position in range(1, positions):
-            total = total + terms_ref[4 * position + t].astype(f32)
-        parts.append(total)
     pieces = ([], [], [])
-    for group in range(groups):
-        for t in range(4):
-            start = group * HEAD_SIZE
-            pieces[0].append(parts[t][:, start : start + half])
-            pieces[1].append(parts[t][:, start + half : start + half + quarter])
-            pieces[2].append(parts[t][:, start + half + quarter : start + HEAD_SIZE])
+    for head in range(terms_ref.shape[0] // 2):
+        part = terms_ref[2 * head].astype(f32) + terms_ref[2 * head + 1].astype(f32)
+        pieces[0].append(part[:, :HEAD_SIZE])
+        pieces[1].append(part[:, HEAD_SIZE : HEAD_SIZE + half])
+        pieces[2].append(part[:, HEAD_SIZE + half :])
     gain = gain_ref[...]
     rows_sum = None
     outs = (d_query, d_key, d_value)
@@ -1046,100 +1168,95 @@
         ]
     )
 
-    out_down = GatherRing(jnp.concatenate([w_down, w_out], axis=0), count)
-    out_down.start()
-    qkv_cols = query_columns(at, gain1, w_query, key_weight, value_weight)
-    qkv_rows = all_to_all(qkv_cols, ("core", "y")).reshape(group, count * HEAD_SIZE)
-    qkv_rows = out_down.settle(qkv_rows)
-    tokens_pair = both_rows(tokens[0], qkv_rows)
-    qkv_ring = GatherRing(qkv_rows, count)
-    qkv_ring.start()
-    inputs = tokens_pair.astype(f32)
-    r1 = inverse_rms(inputs)
-    n1_own = (inputs * r1).astype(bf16)
-    n1_other = swap(n1_own, "core")
-    pair_cols = pair_columns(at, gain2, w_gate, w_up, ff_own)
-    n1_own, n1_other, pair_cols = qkv_ring.settle(n1_own, n1_other, pair_cols)
-    qkv_ring.start()
-    pair_rows = all_to_all(pair_cols, ("core", "y")).reshape(group, 2 * count * ff_own)
-    qkv_ring.settle()
-    qkv_ring.start()
-    pair_rows = qkv_ring.settle(pair_rows)
-    qkv_ring.start()
-    n1_own = qkv_ring.settle(n1_own)
-
-    out_down.start(n1_own)
-    n1, qkv_weight, qkv = project_heads(at, n1_own, n1_other, qkv_ring.parts)
-    cotangent_pair = both_rows(after(cotangent[0], pair_rows), n1_own)
-    cotangent_other = swap(cotangent_pair, "core")
-    qkv = all_to_all(qkv, ("d", "y")).reshape(count, 2, HEAD_SIZE, seq_rows)
-    out_down.settle()
-    out_down.start()
-    qkv, cotangent_other = out_down.settle(qkv, cotangent_other)
-    out_down.start()
-    q_parts = qkv[:, :, :half].transpose(1, 2, 0, 3).reshape(2, half, length)
-    kv_own = qkv[:, :, half:].reshape(count, 2, 2, quarter, seq_rows).transpose(2, 1, 3, 0, 4)
-    kv_own = kv_own.reshape(2, half, length)
-    kv_other = swap(kv_own, "core")
-    kv_first = jnp.where(core == 0, kv_own, kv_other)
-    kv_second = jnp.where(core == 0, kv_other, kv_own)
-    k_parts = (kv_first[0], kv_second[0])
     position = jnp.arange(length, dtype=f32)
     exponent = jnp.arange(half, dtype=f32) * (2.0 / HEAD_SIZE)
     angle = (rope_base ** (-exponent))[:, None] * position[None, :]
     cosine = jnp.cos(angle)
     sine = jnp.sin(angle)
 
-    def rotate(first, second):
-        return jnp.concatenate(
-            [first * cosine - second * sine, second * cosine + first * sine], axis=0
-        )
-
-    def rotate_back(turned):
-        first = turned[:half]
-        second = turned[half:]
-        return jnp.stack(
-            [first * cosine + second * sine, second * cosine - first * sine], axis=0
-        )
-
-    q_parts = q_parts.astype(f32)
-    k_parts = [part.astype(f32) for part in k_parts]
-    q = (rotate(q_parts[0], q_parts[1]) * (score_scale * log2_e)).astype(bf16)
-    k = rotate(k_parts[0], k_parts[1]).astype(bf16)
-    v = jnp.concatenate([kv_first[1], kv_second[1]], axis=0)
+    own_rows = tokens[0].astype(f32)
+    n1_ring = GatherRing((own_rows * inverse_rms(own_rows)).astype(bf16), count)
+    n1_ring.start()
+    out_ring = GatherRing(w_out, count)
+    out_ring.start()
+    head_cols = head_columns(at, gain1, w_query, key_weight, value_weight)
+    head_weight = all_to_all(head_cols, ("d", "core", "y")).reshape(width, 2 * HEAD_SIZE)
+    out_ring.settle()
+    head_cols = n1_ring.settle(head_cols)
+    n1_ring.start()
+    out_ring.start()
+    tokens_pair = both_rows(tokens[0], head_cols)
+    pair_cols = pair_columns(at, gain2, w_gate, w_up, ff_own)
+    out_ring.settle()
+    head_weight, tokens_pair, pair_cols = n1_ring.settle(head_weight, tokens_pair, pair_cols)
+    n1_ring.start()
+    out_ring.start()
+    pair_rows = all_to_all(pair_cols, ("core", "y")).reshape(group, 2 * count * ff_own)
+    out_ring.settle()
+    n1_ring.settle()
+    n1_ring.start()
+    out_ring.start()
+    out_ring.settle()
+    pair_rows = n1_ring.settle(pair_rows)
+    n1_blocks = n1_ring.parts + [swap(part, "core") for part in n1_ring.parts]
+
     pair_ring = GatherRing(pair_rows, count)
-    pair_ring.start(qkv)
-    mixed, prob = heads_forward(q, k, v, step)
-    mixed = out_down.settle(mixed)
-    mixed = pair_ring.settle(mixed)
+    pair_ring.start(n1_blocks[count // 2])
+    down_ring = GatherRing(w_down, count)
+    down_ring.start(n1_blocks[count // 2])
+    q, kv_own = project_heads(at, head_weight, cosine, sine, n1_blocks)
+    kv_other = swap(kv_own, "core")
+    cotangent_pair = both_rows(after(cotangent[0], pair_rows), kv_own)
+    cotangent_other = swap(cotangent_pair, "core")
+    mixed_send, mixed, prob, k, v = heads_forward(at, q, kv_own, kv_other, cosine, sine, count)
+    mixed_send = pair_ring.settle(mixed_send)
+    down_ring.settle()
     pair_ring.start()
-    mixed_send = mixed.astype(bf16).reshape(2, half, count, seq_rows).transpose(2, 0, 1, 3)
-    mixed_low = all_to_all(mixed_send.reshape(2 * count, half, seq_rows), ("d", "y"))
-    mixed_low = pair_ring.settle(mixed_low)
+    down_ring.start()
+    mixed_low = all_to_all(mixed_send, ("d", "y"))
+    mixed_low, cotangent_other = pair_ring.settle(mixed_low, cotangent_other)
+    down_ring.settle()
     pair_ring.start()
-    out_weight, mixed_low, kept, away = project_out(at, mixed_low, out_down.parts, ff_own)
-    branch = pair_ring.settle(core_sum(kept, away))
+    down_ring.start()
+    out_weight, mixed_low, kept, away = project_out(at, mixed_low, out_ring.parts, 0)
+    branch = core_sum(kept, away)
+    branch = both_rows_sum(branch)
+    down_ring.settle()
+    branch = pair_ring.settle(branch)
     pair_ring.start()
-    branch = both_rows_sum(branch)
-    d_out, down_weight, d_hidden = hidden_gradient(
-        at, cotangent_pair, cotangent_other, out_down.parts, ff_own
-    )
-    branch, d_hidden = tie(branch, d_hidden)
+    down_ring.start()
+    inputs = tokens_pair.astype(f32)
     middle = inputs + branch
 
     r2 = inverse_rms(middle)
     n2_pair = middle * r2
     n2_own = n2_pair.astype(bf16)
     n2_other = swap(n2_own, "core")
-    n2_own, n2_other = pair_ring.settle(n2_own, n2_other)
+    down_ring.settle()
+    d_out, down_weight, d_hidden = hidden_gradient(
+        at, cotangent_pair, cotangent_other, down_ring.parts, ff_own
+    )
+    n2_own, n2_other, d_hidden = pair_ring.settle(n2_own, n2_other, d_hidden)
+    qkv_cols = query_columns(at, gain1, w_query, key_weight, value_weight)
+    qkv_rows = all_to_all(after(qkv_cols, pair_rows), ("core", "y"))
+    qkv_rows = qkv_rows.reshape(group, count * HEAD_SIZE)
+    n2_own, qkv_rows = tie(n2_own, qkv_rows)
+    qkv_ring = GatherRing(qkv_rows, count)
+    qkv_ring.start()
     n2, hidden, d_both, kept, away = feed_forward(at, n2_own, n2_other, d_hidden, pair_ring.parts)
-    d_n2 = core_sum(kept, away)
+    d_n2 = qkv_ring.settle(core_sum(kept, away))
+    qkv_ring.start()
     grad_both, grad_down = feed_forward_grads(
         at, n2, d_both, after(hidden, d_n2), d_out, count
     )
     d_normed2 = both_rows_sum(d_n2)
+    grad_down = qkv_ring.settle(grad_down)
+    qkv_ring.start()
     ff_ring = ScatterRing([grad_both, grad_down], count)
+    qkv_ring.settle()
+    qkv_ring.start()
     ff_ring.start()
+    qkv_ring.settle()
     d_normed2 = ff_ring.settle(d_normed2)
     ff_ring.start()
     d_middle = cotangent_pair.astype(f32) + r2 * (
@@ -1149,55 +1266,46 @@
     d_mid_own = d_middle.astype(bf16)
     d_mid_other = swap(d_mid_own, "core")
     d_mid, d_mixed = split_heads(at, d_mid_own, d_mid_other, out_weight, count)
-    d_mixed = ff_ring.settle(d_mixed)
-    ff_ring.start()
     d_mixed = all_to_all(d_mixed, ("d", "y"))
     d_mixed = ff_ring.settle(d_mixed)
     ff_ring.start()
-    d_mixed = d_mixed.reshape(count, 2, half, seq_rows).transpose(1, 2, 0, 3)
-    d_mixed = d_mixed.reshape(HEAD_SIZE, length)
     grad_out = dot_at(after(mixed_low, d_mixed), d_mid, 1, 0).astype(bf16)
     owned_out = all_to_all(grad_out.reshape(count, own, width), "d")
-    d_q, d_k, d_v = heads_backward(q, k, v, prob, mixed, d_mixed, step)
-    d_kv = jnp.stack([rotate_back(d_k), d_v.reshape(2, half, length)], axis=1)
-    away = lax.dynamic_index_in_dim(d_kv, 1 - core, 0, False).astype(bf16)
-    kept = lax.dynamic_index_in_dim(d_kv, core, 0, False)
-    d_kv = core_sum(kept, away).astype(bf16)
-    d_kv = d_kv.reshape(2, 2, quarter, count, seq_rows).transpose(3, 1, 0, 2, 4)
-    d_kv = d_kv.reshape(count, 2, half, seq_rows)
-    d_q = rotate_back(d_q).astype(bf16).reshape(2, half, count, seq_rows).transpose(2, 0, 1, 3)
-    d_qkv = jnp.concatenate([d_q, d_kv], axis=2).reshape(2 * count, HEAD_SIZE, seq_rows)
+    d_q, kept, away = heads_backward(at, q, k, v, prob, mixed, d_mixed, cosine, sine, count)
+    d_qkv, joined = heads_send(at, d_q, kept, swap(away, "core"), count)
     d_qkv, owned_out = ff_ring.settle(d_qkv, owned_out)
     ff_ring.start()
     d_qkv = all_to_all(d_qkv, ("d", "y"))
+    grad_heads = heads_grad(at, joined, n1_blocks)
+    grad_heads = ff_ring.settle(grad_heads)
+    ff_ring.start()
+    grad_heads, d_qkv = ff_ring.settle(grad_heads, d_qkv)
+    ff_ring.start()
+    grad_heads = all_to_all(grad_heads.reshape(4 * count, own, 2 * HEAD_SIZE), ("d", "core", "y"))
+    kept, away = heads_input(at, d_qkv, qkv_ring.parts)
+    d_normed1 = own_rows_sum(core_sum(kept, away))
     ff_ring.settle()
     ff_ring.start()
-    d_qkv = ff_ring.settle(d_qkv)
-    d_qkv, grad_qkv = heads_grad(at, d_qkv, n1)
-    grad_qkv = grad_qkv.reshape(4 * count, own, count * HEAD_SIZE)
-    ff_ring.start(grad_qkv)
-    own_qkv = all_to_all(grad_qkv, ("d", "core", "y"))
     ff_ring.settle()
     owned_both, owned_down = ff_ring.sums()
     own_both = own_columns(owned_both.astype(bf16).reshape(2, 2, own, -1))
-    kept, away = heads_input(at, d_qkv, qkv_weight)
-    d_normed1 = own_rows_sum(core_sum(kept, away))
     kept, away = layer_output(at, hidden, down_weight, count)
-    n1_wide, r1_own, d_middle_own, middle_own = (
-        lax.dynamic_index_in_dim(value, seq, 0, False)
-        for value in (inputs * r1, r1, d_middle, middle)
-    )
-    input_grad = d_middle_own + r1_own * (
+    d_middle_own, middle_own = (
+        lax.dynamic_index_in_dim(value, seq, 0, False) for value in (d_middle, middle)
+    )
+    r1 = inverse_rms(own_rows)
+    n1_wide = own_rows * r1
+    input_grad = d_middle_own + r1 * (
         d_normed1 - n1_wide * jnp.mean(d_normed1 * n1_wide, axis=-1, keepdims=True)
     )
     result = middle_own + own_rows_sum(core_sum(kept, away))
-    own_qkv, own_both = tie(own_qkv, own_both)
+    grad_heads, own_both = tie(grad_heads, own_both)
     owned_out = jnp.sum(owned_out.astype(f32), axis=0)
     grad_gate, grad_up, grad_gain2 = pair_rows_grads(
         at, own_both, gain2, w_gate, w_up, ff_own, count
     )
     grad_query, grad_key, grad_value, grad_gain1 = query_rows_grads(
-        at, own_qkv, gain1, w_query, key_weight, value_weight
+        at, grad_heads, gain1, w_query, key_weight, value_weight
     )
     return (
         result.astype(bf16)[None],

time: 538 us -> 502 us (0.933)
  waiting for transfers between devices: 262 us -> 184 us
  starting transfers between devices: 106 us -> 122 us
  Pallas kernels: 68.9 us -> 83.3 us
  local copies, waits for them, and re-layouts: 39.3 us -> 51.3 us
    ppermute x14, waiting for transfers between devices: 113 us -> 68.4 us  [start(): self.ahead = [lax.ppermute(a, 'd', self.forward) for a in ahead]]
    pallas_call x13 -> x17, Pallas kernels: 55.6 us -> 83.3 us  [on_chip(): pl.pallas_call(kernel, out_shape=tuple(out_shape), in_specs=[pl.BlockSpec...]
    all_to_all x8, waiting for transfers between devices: 24.1 us -> 0.98 us  [all_to_all(): return lax.all_to_all(values, axes, 0, 0, tiled=True)]
    ppermute x18 -> x25, waiting for transfers between devices: 32.3 us -> 10.8 us  [swap(): return lax.ppermute(values, axis, [(0, 1), (1, 0)])]
    pallas_call x2 -> x0, Pallas kernels: 13.3 us -> none  [the longest x1 7.36 us: heads_forward(): pl.pallas_call(functools.partial(heads_forward_kernel, step), out_shape=(...]
    unnamed x159 -> x253, local copies, waits for them, and re-layouts: 30.4 us -> 41.5 us
    ppermute x12 -> x20, waiting for transfers between devices: 85.8 us -> 95.1 us  [start(): self.ahead = lax.ppermute(ahead, 'd', self.forward)]
    ppermute x12 -> x20, starting transfers between devices: 15.5 us -> 23.6 us  [start(): self.behind = lax.ppermute(behind, 'd', self.backward)]
  transfers between devices with their start and end apart: 78 -> 101, of which waited for: 36 -> 38; matrix products, arithmetic and copies ran while one was open for 9% -> 10% of each run, Pallas kernels for 9% -> 12%
where the time goes in v3:
time: 502 us; the launch traced here: 496 us
  waiting for transfers between devices  184 us (37%)
  starting transfers between devices  122 us (24%)
  Pallas kernels  83.3 us (17%)
  local copies, waits for them, and re-layouts  51.3 us (10%)
  other arithmetic  49.6 us (10%)
    ppermute x20, waiting for transfers between devices, start(): self.ahead = lax.ppermute(ahead, 'd', self.forward)  95.1 us
    pallas_call x17, Pallas kernels, on_chip(): pl.pallas_call(kernel, out_shape=tuple(out_shape), in_specs=[pl.BlockSpec...  83.3 us
    ppermute x14, waiting for transfers between devices, start(): self.ahead = [lax.ppermute(a, 'd', self.forward) for a in ahead]  68.4 us
    unnamed x253, local copies, waits for them, and re-layouts  41.5 us
    all_to_all x8, starting transfers between devices, all_to_all(): return lax.all_to_all(values, axes, 0, 0, tiled=True)  40.1 us
    ppermute x20, starting transfers between devices, start(): self.behind = lax.ppermute(behind, 'd', self.backward)  23.6 us
    convert_element_type x12, other arithmetic, settle(): (b.astype(f32) + self.part(t, 1 + self.hops, 1).astype(f32)).astype(kind)  20.2 us
    ppermute x14, starting transfers between devices, start(): self.behind = [lax.ppermute(b, 'd', self.backward) for b in behind]  19.4 us
  transfers between devices with their start and end apart: 101, of which 38 were waited for; matrix products, arithmetic and copies ran while one was open for 10% of the time, Pallas kernels for 12%

profile of v3, /device:TPU:10, one launch (start us, length us, event | category | flops | bytes accessed | tf_op | source)
XLA Modules:
  0.0 496.0 jit_solution(17659953541071329202)
XLA Ops:
  11.8 5.1 %all-to-all-start = ((bf16[32,48,192]{2,1,0:T(8,128)(2,1)}), bf16[32,48,192]{2,1,0:T(8,128)(2,1)}, u32[]{:S(2)}, u32[]{:S(2)}) async-start(bf16[32,48,192]{2,1,0:T(8,128)(2,1)} %head_columns.1), calls=%async_computation | async-start | bytes 1572864 | tf_op jit(solution)/shard_map/all_to_all | solution.py:1125
  22.9 21.9 %collective-permute-done.2.refs_6_ = bf16[128,1536]{1,0:T(8,128)(2,1)S(1)} collective-permute-done((bf16[128,1536]{1,0:T(8,128)(2,1)S(1)}, bf16[128,1536]{1,0:T(8,128)(2,1)S(1)}, u32[]{:S(2)}, u32[]{:S(2)}) %collective-permute-start.2) | collective-permute-done | bytes 393248 | tf_op jit(solution)/shard_map/ppermute | solution.py:1030
  46.9 4.2 all-to-all-start.1
  51.1 4.4 collective-permute-done.5.refs_5_
  74.2 7.1 %project_heads.1 = (bf16[96,2048]{1,0:T(8,128)(2,1)S(1)}, bf16[2,48,2048]{2,1,0:T(8,128)(2,1)S(1)}) custom-call(s32[18]{0:T(128)S(1)} %pad_add_fusion.at_ref, bf16[1536,192]{1,0:T(8,128)(2,1)} %bitcast.4.weight_ref, f32[48,2048]{1,0:T(8,128)S(1)} %get-tuple-element.336.cos_ref, f32[48,2048]{1,0:T(8,128)S(1)} %get-tuple-element.335.sin_ref, ...), custom_call_target="tpu_custom_call" | custom-call | flops 1207959552 | bytes 8454216 | tf_op jit(solution)/shard_map/project_heads/pallas_call | solution.py:494
  83.1 9.8 %heads_forward.1 = (bf16[16,48,256]{2,1,0:T(8,128)(2,1)S(1)}, f32[96,2048]{1,0:T(8,128)S(1)}, bf16[9216,256]{1,0:T(8,128)(2,1)}, bf16[96,2048]{1,0:T(8,128)(2,1)S(1)}, bf16[96,2048]{1,0:T(8,128)(2,1)S(1)}) custom-call(s32[18]{0:T(128)S(1)} %pad_add_fusion.at_ref, bf16[96,2048]{1,0:T(8,128)(2,1)S(1)} %get-tuple-element.165.q_ref, ...), custom_call_target="tpu_custom_call" | custom-call | flops 905969664 | bytes 8650824 | tf_op jit(solution)/shard_map/heads_forward/pallas_call | solution.py:494
  100.1 6.4 %all-to-all-start.2 = ((bf16[16,48,256]{2,1,0:T(8,128)(2,1)}), bf16[16,48,256]{2,1,0:T(8,128)(2,1)}, u32[]{:S(2)}, u32[]{:S(2)}) async-start(bf16[16,48,256]{2,1,0:T(8,128)(2,1)} %copy-done.44), calls=%async_computation.2 | async-start | bytes 786432 | tf_op jit(solution)/shard_map/all_to_all | solution.py:1125
  106.5 13.9 %collective-permute-done.26.refs_7_ = bf16[48,1536]{1,0:T(8,128)(2,1)} collective-permute-done((bf16[48,1536]{1,0:T(8,128)(2,1)}, bf16[48,1536]{1,0:T(8,128)(2,1)}, u32[]{:S(2)}, u32[]{:S(2)}) %collective-permute-start.26) | collective-permute-done | bytes 147488 | tf_op jit(solution)/shard_map/ppermute | solution.py:1030
  123.7 6.9 %collective-permute-done.28.refs_6_ = bf16[48,1536]{1,0:T(8,128)(2,1)S(1)} collective-permute-done((bf16[48,1536]{1,0:T(8,128)(2,1)}, bf16[48,1536]{1,0:T(8,128)(2,1)S(1)}, u32[]{:S(2)}, u32[]{:S(2)}) %collective-permute-start.28) | collective-permute-done | bytes 147488 | tf_op jit(solution)/shard_map/ppermute | solution.py:1030
  149.1 4.3 project_out.1
  157.3 8.4 %collective-permute-done.39.refs_7_ = bf16[128,1536]{1,0:T(8,128)(2,1)S(1)} collective-permute-done((bf16[128,1536]{1,0:T(8,128)(2,1)S(1)}, bf16[128,1536]{1,0:T(8,128)(2,1)S(1)}, u32[]{:S(2)}, u32[]{:S(2)}) %collective-permute-start.39) | collective-permute-done | bytes 393248 | tf_op jit(solution)/shard_map/ppermute | solution.py:1030
  171.5 8.0 %collective-permute-done.41.refs_6_ = bf16[128,1536]{1,0:T(8,128)(2,1)S(1)} collective-permute-done((bf16[128,1536]{1,0:T(8,128)(2,1)S(1)}, bf16[128,1536]{1,0:T(8,128)(2,1)S(1)}, u32[]{:S(2)}, u32[]{:S(2)}) %collective-permute-start.41) | collective-permute-done | bytes 393248 | tf_op jit(solution)/shard_map/ppermute | solution.py:1030
  182.3 14.0 %collective-permute-done.24.refs_5_ = bf16[192,2048]{1,0:T(8,128)(2,1)S(1)} collective-permute-done((bf16[192,2048]{1,0:T(8,128)(2,1)}, bf16[192,2048]{1,0:T(8,128)(2,1)S(1)}, u32[]{:S(2)}, u32[]{:S(2)}) %collective-permute-start.24) | collective-permute-done | bytes 786464 | tf_op jit(solution)/shard_map/ppermute | solution.py:1030
  198.2 4.8 collective-permute-done.43.refs_5_
  212.1 4.1 all-to-all-start.3
  224.3 5.3 %hidden_gradient.1 = (bf16[512,1536]{1,0:T(8,128)(2,1)}, bf16[1024,1536]{1,0:T(8,128)(2,1)}, bf16[512,1024]{1,0:T(8,128)(2,1)S(1)}) custom-call(s32[18]{0:T(128)S(1)} %pad_add_fusion.at_ref, bf16[2,128,1536]{2,1,0:T(8,128)(2,1)} %pad_maximum_fusion.1.own_ref, bf16[2,128,1536]{2,1,0:T(8,128)(2,1)} %collective-permute-done.23.other_ref, ...), custom_call_target="tpu_custom_call" | custom-call | flops 1610612736 | bytes 10485832 | tf_op jit(solution)/shard_map/hidden_gradient/pallas_call | solution.py:494
  232.7 12.9 %feed_forward.1 = (bf16[512,1536]{1,0:T(8,128)(2,1)}, bf16[512,1024]{1,0:T(8,128)(2,1)}, bf16[512,2048]{1,0:T(8,128)(2,1)}, f32[2,128,1536]{2,1,0:T(8,128)}, bf16[2,128,1536]{2,1,0:T(8,128)(2,1)S(1)}) custom-call(s32[18]{0:T(128)S(1)} %pad_add_fusion.at_ref, bf16[2,128,1536]{2,1,0:T(8,128)(2,1)} %multiply_convert_fusion.own_ref, ...), custom_call_target="tpu_custom_call" | custom-call | flops 6442450944 | bytes 15990856 | tf_op jit(solution)/shard_map/feed_forward/pallas_call | solution.py:494
  250.0 5.4 %collective-permute-done.49.refs_7_ = bf16[192,768]{1,0:T(8,128)(2,1)S(1)} collective-permute-done((bf16[192,768]{1,0:T(8,128)(2,1)}, bf16[192,768]{1,0:T(8,128)(2,1)S(1)}, u32[]{:S(2)}, u32[]{:S(2)}) %collective-permute-start.49) | collective-permute-done | bytes 294944 | tf_op jit(solution)/shard_map/ppermute | solution.py:1030
  259.8 9.4 %feed_forward_grads.1 = (bf16[8,192,2048]{2,1,0:T(8,128)(2,1)}, bf16[8,128,1536]{2,1,0:T(8,128)(2,1)}) custom-call(s32[18]{0:T(128)S(1)} %pad_add_fusion.at_ref, bf16[512,1536]{1,0:T(8,128)(2,1)S(1)} %copy-done.84, bf16[512,2048]{1,0:T(8,128)(2,1)} %get-tuple-element.213.d_both_ref, bf16[512,1024]{1,0:T(8,128)(2,1)S(1)} %copy-done.22, ...), custom_call_target="tpu_custom_call" | custom-call | flops 4831838208 | bytes 15728712 | tf_op jit(solution)/shard_map/feed_forward_grads/pallas_call | solution.py:494
  276.6 5.5 %collective-permute-done.52 = bf16[96,2048]{1,0:T(8,128)(2,1)S(1)} collective-permute-done((bf16[96,2048]{1,0:T(8,128)(2,1)S(1)}, bf16[96,2048]{1,0:T(8,128)(2,1)S(1)}, u32[]{:S(2)}, u32[]{:S(2)}) %collective-permute-start.52) | collective-permute-done | bytes 393248 | tf_op jit(solution)/shard_map/ppermute | solution.py:1062
  292.8 5.8 %all-to-all-start.4 = ((bf16[16,48,256]{2,1,0:T(8,128)(2,1)}), bf16[16,48,256]{2,1,0:T(8,128)(2,1)}, u32[]{:S(2)}, u32[]{:S(2)}) async-start(bf16[16,48,256]{2,1,0:T(8,128)(2,1)} %copy-done.45), calls=%async_computation.4 | async-start | bytes 786432 | tf_op jit(solution)/shard_map/all_to_all | solution.py:1125
  305.5 16.2 %collective-permute-done.60 = bf16[64,1536]{1,0:T(8,128)(2,1)S(1)} collective-permute-done((bf16[64,1536]{1,0:T(8,128)(2,1)S(1)}, bf16[64,1536]{1,0:T(8,128)(2,1)S(1)}, u32[]{:S(2)}, u32[]{:S(2)}) %collective-permute-start.60) | collective-permute-done | bytes 196640 | tf_op jit(solution)/shard_map/ppermute | solution.py:1062
  325.9 4.2 all-to-all-start.5
  342.8 8.4 %heads_backward.1 = (f32[96,2048]{1,0:T(8,128)S(1)}, f32[2,48,2048]{2,1,0:T(8,128)S(1)}, bf16[2,48,2048]{2,1,0:T(8,128)(2,1)S(1)}) custom-call(s32[18]{0:T(128)S(1)} %pad_add_fusion.at_ref, bf16[96,2048]{1,0:T(8,128)(2,1)S(1)} %copy-done.39, bf16[96,2048]{1,0:T(8,128)(2,1)S(1)} %copy-done.41, bf16[96,2048]{1,0:T(8,128)(2,1)S(1)} %copy-done.43, ...), custom_call_target="tpu_custom_call" | custom-call | flops 1811939328 | bytes 9830472 | tf_op jit(solution)/shard_map/heads_backward/pallas_call | solution.py:494
  356.0 14.7 %collective-permute-done.65 = bf16[64,1536]{1,0:T(8,128)(2,1)S(1)} collective-permute-done((bf16[64,1536]{1,0:T(8,128)(2,1)S(1)}, bf16[64,1536]{1,0:T(8,128)(2,1)S(1)}, u32[]{:S(2)}, u32[]{:S(2)}) %collective-permute-start.65) | collective-permute-done | bytes 196640 | tf_op jit(solution)/shard_map/ppermute | solution.py:1062
  384.8 4.8 all-to-all-start.6
  394.6 7.8 %heads_grad.1 = bf16[1536,192]{1,0:T(8,128)(2,1)} custom-call(s32[18]{0:T(128)S(1)} %pad_add_fusion.at_ref, bf16[192,2048]{1,0:T(8,128)(2,1)} %copy-done.27, bf16[128,1536]{1,0:T(8,128)(2,1)S(1)} %fusion.3.refs_0_, bf16[128,1536]{1,0:T(8,128)(2,1)S(1)} %collective-permute-done.1.refs_1_, bf16[128,1536]{1,0:T(8,128)(2,1)S(1)} %copy-done.2, ...), custom_call_target="tpu_custom_call" | custom-call | flops 1207959552 | bytes 7667784 | tf_op jit(solution)/shard_map/heads_grad/pallas_call | solution.py:494
  414.2 7.1 %collective-permute-done.74 = bf16[64,1536]{1,0:T(8,128)(2,1)S(1)} collective-permute-done((bf16[64,1536]{1,0:T(8,128)(2,1)S(1)}, bf16[64,1536]{1,0:T(8,128)(2,1)S(1)}, u32[]{:S(2)}, u32[]{:S(2)}) %collective-permute-start.74) | collective-permute-done | bytes 196640 | tf_op jit(solution)/shard_map/ppermute | solution.py:1062
  432.9 4.4 heads_input.1
  437.3 5.5 %all-to-all-start.7 = ((bf16[32,48,192]{2,1,0:T(8,128)(2,1)}), bf16[32,48,192]{2,1,0:T(8,128)(2,1)S(1)}, u32[]{:S(2)}, u32[]{:S(2)}) async-start(bf16[32,48,192]{2,1,0:T(8,128)(2,1)} %bitcast.163), calls=%async_computation.7 | async-start | bytes 1572864 | tf_op jit(solution)/shard_map/all_to_all | solution.py:1125
  451.7 23.2 %collective-permute-done.88 = bf16[64,1536]{1,0:T(8,128)(2,1)S(1)} collective-permute-done((bf16[64,1536]{1,0:T(8,128)(2,1)S(1)}, bf16[64,1536]{1,0:T(8,128)(2,1)S(1)}, u32[]{:S(2)}, u32[]{:S(2)}) %collective-permute-start.88) | collective-permute-done | bytes 196640 | tf_op jit(solution)/shard_map/ppermute | solution.py:1062
  480.0 7.1 %collective-permute-done.91 = bf16[2,48,2048]{2,1,0:T(8,128)(2,1)S(1)} collective-permute-done((bf16[2,48,2048]{2,1,0:T(8,128)(2,1)S(1)}, bf16[2,48,2048]{2,1,0:T(8,128)(2,1)S(1)}, u32[]{:S(2)}, u32[]{:S(2)}) %collective-permute-start.91) | collective-permute-done | bytes 393248 | tf_op jit(solution)/shard_map/ppermute | solution.py:1085
  (514 shorter events, 222.8 us)
Async XLA Ops:
  11.8 33.0 %all-to-all-start = ((bf16[32,48,192]{2,1,0:T(8,128)(2,1)}), bf16[32,48,192]{2,1,0:T(8,128)(2,1)}, u32[]{:S(2)}, u32[]{:S(2)}) async-start(bf16[32,48,192]{2,1,0:T(8,128)(2,1)} %head_columns.1), calls=%async_computation | async-start | bytes 1572864 | tf_op jit(solution)/shard_map/all_to_all | solution.py:1125
  18.8 26.0 %collective-permute-start.2 = (bf16[128,1536]{1,0:T(8,128)(2,1)S(1)}, bf16[128,1536]{1,0:T(8,128)(2,1)S(1)}, u32[]{:S(2)}, u32[]{:S(2)}) collective-permute-start(bf16[128,1536]{1,0:T(8,128)(2,1)S(1)} %collective-permute-done.refs_7_), channel_id=1, source_target_pairs={{0,8},{8,16},{16,24},{24,28},{28,20},{20,12},{12,4},{4,0},{1,9},{9... | collective-permute-start | bytes 1179656 | tf_op jit(solution)/shard_map/ppermute | solution.py:1030
  19.4 25.4 %collective-permute-start.3 = (bf16[128,1536]{1,0:T(8,128)(2,1)S(1)}, bf16[128,1536]{1,0:T(8,128)(2,1)S(1)}, u32[]{:S(2)}, u32[]{:S(2)}) collective-permute-start(bf16[128,1536]{1,0:T(8,128)(2,1)S(1)} %collective-permute-done.1.refs_1_), channel_id=1, source_target_pairs={{8,0},{16,8},{24,16},{28,24},{20,28},{12,20},{4,12},{0,4},{9,1},{1... | collective-permute-start | bytes 1179656 | tf_op jit(solution)/shard_map/ppermute | solution.py:1031
  68.7 27.3 %collective-permute-start.9 = (bf16[192,2048]{1,0:T(8,128)(2,1)}, bf16[192,2048]{1,0:T(8,128)(2,1)}, u32[]{:S(2)}, u32[]{:S(2)}) collective-permute-start(bf16[192,2048]{1,0:T(8,128)(2,1)} %bitcast.8.refs_0_), channel_id=1, source_target_pairs={{0,8},{8,16},{16,24},{24,28},{28,20},{20,12},{12,4},{4,0},{1,9},{9... | collective-permute-start | bytes 2359304 | tf_op jit(solution)/shard_map/ppermute | solution.py:1030
  70.5 25.5 %collective-permute-start.10 = (bf16[192,2048]{1,0:T(8,128)(2,1)}, bf16[192,2048]{1,0:T(8,128)(2,1)}, u32[]{:S(2)}, u32[]{:S(2)}) collective-permute-start(bf16[192,2048]{1,0:T(8,128)(2,1)} %bitcast.8.refs_0_), channel_id=1, source_target_pairs={{8,0},{16,8},{24,16},{28,24},{20,28},{12,20},{4,12},{0,4},{9,1},{1... | collective-permute-start | bytes 2359304 | tf_op jit(solution)/shard_map/ppermute | solution.py:1031
  82.5 62.0 %collective-permute-start.23 = (bf16[2,128,1536]{2,1,0:T(8,128)(2,1)}, bf16[2,128,1536]{2,1,0:T(8,128)(2,1)}, u32[]{:S(2)}, u32[]{:S(2)}) collective-permute-start(bf16[2,128,1536]{2,1,0:T(8,128)(2,1)} %pad_maximum_fusion.1.own_ref), channel_id=1, source_target_pairs={{0,2},{2,0},{1,3},{3,1},{4,6},{6,4},{5,7},{7,5},{8,10},{10,8},{9,1... | collective-permute-start | bytes 2359304 | tf_op jit(solution)/shard_map/ppermute | solution.py:1085
  96.0 48.5 %collective-permute-start.20 = (bf16[192,2048]{1,0:T(8,128)(2,1)}, bf16[192,2048]{1,0:T(8,128)(2,1)}, u32[]{:S(2)}, u32[]{:S(2)}) collective-permute-start(bf16[192,2048]{1,0:T(8,128)(2,1)} %collective-permute-done.9.refs_7_), channel_id=1, source_target_pairs={{0,8},{8,16},{16,24},{24,28},{28,20},{20,12},{12,4},{4,0},{1,9},{9... | collective-permute-start | bytes 2359304 | tf_op jit(solution)/shard_map/ppermute | solution.py:1030
  97.8 46.8 %collective-permute-start.21 = (bf16[192,2048]{1,0:T(8,128)(2,1)}, bf16[192,2048]{1,0:T(8,128)(2,1)}, u32[]{:S(2)}, u32[]{:S(2)}) collective-permute-start(bf16[192,2048]{1,0:T(8,128)(2,1)} %collective-permute-done.10.refs_1_), channel_id=1, source_target_pairs={{8,0},{16,8},{24,16},{28,24},{20,28},{12,20},{4,12},{0,4},{9,1},{1... | collective-permute-start | bytes 2359304 | tf_op jit(solution)/shard_map/ppermute | solution.py:1031
  100.1 44.5 %all-to-all-start.2 = ((bf16[16,48,256]{2,1,0:T(8,128)(2,1)}), bf16[16,48,256]{2,1,0:T(8,128)(2,1)}, u32[]{:S(2)}, u32[]{:S(2)}) async-start(bf16[16,48,256]{2,1,0:T(8,128)(2,1)} %copy-done.44), calls=%async_computation.2 | async-start | bytes 786432 | tf_op jit(solution)/shard_map/all_to_all | solution.py:1125
  156.7 25.4 %collective-permute-start.35 = (bf16[2,128,1536]{2,1,0:T(8,128)(2,1)S(1)}, bf16[2,128,1536]{2,1,0:T(8,128)(2,1)S(1)}, u32[]{:S(2)}, u32[]{:S(2)}) collective-permute-start(bf16[2,128,1536]{2,1,0:T(8,128)(2,1)S(1)} %fusion), channel_id=1, source_target_pairs={{0,1},{1,0},{2,3},{3,2},{4,5},{5,4},{6,7},{7,6},{8,9},{9,8},{10,11... | collective-permute-start | bytes 2359304 | tf_op jit(solution)/shard_map/ppermute | solution.py:1085
  169.5 26.9 %collective-permute-start.24 = (bf16[192,2048]{1,0:T(8,128)(2,1)}, bf16[192,2048]{1,0:T(8,128)(2,1)S(1)}, u32[]{:S(2)}, u32[]{:S(2)}) collective-permute-start(bf16[192,2048]{1,0:T(8,128)(2,1)} %collective-permute-done.20.refs_6_), channel_id=1, source_target_pairs={{0,8},{8,16},{16,24},{24,28},{28,20},{20,12},{12,4},{4,0},{1,9},{9... | collective-permute-start | bytes 2359304 | tf_op jit(solution)/shard_map/ppermute | solution.py:1030
  169.8 26.9 %collective-permute-start.25 = (bf16[192,2048]{1,0:T(8,128)(2,1)}, bf16[192,2048]{1,0:T(8,128)(2,1)S(1)}, u32[]{:S(2)}, u32[]{:S(2)}) collective-permute-start(bf16[192,2048]{1,0:T(8,128)(2,1)} %collective-permute-done.21.refs_2_), channel_id=1, source_target_pairs={{8,0},{16,8},{24,16},{28,24},{20,28},{12,20},{4,12},{0,4},{9,1},{1... | collective-permute-start | bytes 2359304 | tf_op jit(solution)/shard_map/ppermute | solution.py:1031
  180.1 23.4 %collective-permute-start.44 = (bf16[128,1536]{1,0:T(8,128)(2,1)S(1)}, bf16[128,1536]{1,0:T(8,128)(2,1)S(1)}, u32[]{:S(2)}, u32[]{:S(2)}) collective-permute-start(bf16[128,1536]{1,0:T(8,128)(2,1)S(1)} %collective-permute-done.42.refs_2_), channel_id=1, source_target_pairs={{8,0},{16,8},{24,16},{28,24},{20,28},{12,20},{4,12},{0,4},{9,1},{1... | collective-permute-start | bytes 1179656 | tf_op jit(solution)/shard_map/ppermute | solution.py:1031
  198.2 32.4 %collective-permute-start.38 = (bf16[2,128,1536]{2,1,0:T(8,128)(2,1)}, bf16[2,128,1536]{2,1,0:T(8,128)(2,1)}, u32[]{:S(2)}, u32[]{:S(2)}) collective-permute-start(bf16[2,128,1536]{2,1,0:T(8,128)(2,1)} %multiply_convert_fusion.own_ref), channel_id=1, source_target_pairs={{0,2},{2,0},{1,3},{3,1},{4,6},{6,4},{5,7},{7,5},{8,10},{10,8},{9,1... | collective-permute-start | bytes 2359304 | tf_op jit(solution)/shard_map/ppermute | solution.py:1085
  292.8 29.7 %all-to-all-start.4 = ((bf16[16,48,256]{2,1,0:T(8,128)(2,1)}), bf16[16,48,256]{2,1,0:T(8,128)(2,1)}, u32[]{:S(2)}, u32[]{:S(2)}) async-start(bf16[16,48,256]{2,1,0:T(8,128)(2,1)} %copy-done.45), calls=%async_computation.4 | async-start | bytes 786432 | tf_op jit(solution)/shard_map/all_to_all | solution.py:1125
  325.9 45.6 %all-to-all-start.5 = ((bf16[8,48,1536]{2,1,0:T(8,128)(2,1)}), bf16[8,48,1536]{2,1,0:T(8,128)(2,1)}, u32[]{:S(2)}, u32[]{:S(2)}) async-start(bf16[8,48,1536]{2,1,0:T(8,128)(2,1)} %bitcast.164), calls=%async_computation.5 | async-start | bytes 2359296 | tf_op jit(solution)/shard_map/all_to_all | solution.py:1125
  337.1 33.6 %collective-permute-start.64 = (bf16[96,2048]{1,0:T(8,128)(2,1)S(1)}, bf16[96,2048]{1,0:T(8,128)(2,1)}, u32[]{:S(2)}, u32[]{:S(2)}) collective-permute-start(bf16[96,2048]{1,0:T(8,128)(2,1)S(1)} %get-tuple-element.306), channel_id=1, source_target_pairs={{0,8},{8,16},{16,24},{24,28},{28,20},{20,12},{12,4},{4,0},{1,9},{9... | collective-permute-start | bytes 1179656 | tf_op jit(solution)/shard_map/ppermute | solution.py:1062
  338.8 31.9 %collective-permute-start.65 = (bf16[64,1536]{1,0:T(8,128)(2,1)S(1)}, bf16[64,1536]{1,0:T(8,128)(2,1)S(1)}, u32[]{:S(2)}, u32[]{:S(2)}) collective-permute-start(bf16[64,1536]{1,0:T(8,128)(2,1)S(1)} %get-tuple-element.322), channel_id=1, source_target_pairs={{0,8},{8,16},{16,24},{24,28},{28,20},{20,12},{12,4},{4,0},{1,9},{9... | collective-permute-start | bytes 589832 | tf_op jit(solution)/shard_map/ppermute | solution.py:1062
  338.9 32.5 %collective-permute-start.66 = (bf16[96,2048]{1,0:T(8,128)(2,1)S(1)}, bf16[96,2048]{1,0:T(8,128)(2,1)}, u32[]{:S(2)}, u32[]{:S(2)}) collective-permute-start(bf16[96,2048]{1,0:T(8,128)(2,1)S(1)} %get-tuple-element.305), channel_id=1, source_target_pairs={{8,0},{16,8},{24,16},{28,24},{20,28},{12,20},{4,12},{0,4},{9,1},{1... | collective-permute-start | bytes 1179656 | tf_op jit(solution)/shard_map/ppermute | solution.py:1063
  340.9 29.8 %collective-permute-start.67 = (bf16[64,1536]{1,0:T(8,128)(2,1)S(1)}, bf16[64,1536]{1,0:T(8,128)(2,1)S(1)}, u32[]{:S(2)}, u32[]{:S(2)}) collective-permute-start(bf16[64,1536]{1,0:T(8,128)(2,1)S(1)} %get-tuple-element.321), channel_id=1, source_target_pairs={{8,0},{16,8},{24,16},{28,24},{20,28},{12,20},{4,12},{0,4},{9,1},{1... | collective-permute-start | bytes 589832 | tf_op jit(solution)/shard_map/ppermute | solution.py:1063
  353.0 26.9 %collective-permute-start.77 = (bf16[192,768]{1,0:T(8,128)(2,1)}, bf16[192,768]{1,0:T(8,128)(2,1)S(1)}, u32[]{:S(2)}, u32[]{:S(2)}) collective-permute-start(bf16[192,768]{1,0:T(8,128)(2,1)} %collective-permute-done.53.refs_6_), channel_id=1, source_target_pairs={{0,8},{8,16},{16,24},{24,28},{28,20},{20,12},{12,4},{4,0},{1,9},{9... | collective-permute-start | bytes 884744 | tf_op jit(solution)/shard_map/ppermute | solution.py:1030
  374.0 30.5 %collective-permute-start.69 = (bf16[96,2048]{1,0:T(8,128)(2,1)}, bf16[96,2048]{1,0:T(8,128)(2,1)}, u32[]{:S(2)}, u32[]{:S(2)}) collective-permute-start(bf16[96,2048]{1,0:T(8,128)(2,1)} %get-tuple-element.304), channel_id=1, source_target_pairs={{0,8},{8,16},{16,24},{24,28},{28,20},{20,12},{12,4},{4,0},{1,9},{9... | collective-permute-start | bytes 1179656 | tf_op jit(solution)/shard_map/ppermute | solution.py:1062
  376.0 28.5 %collective-permute-start.71 = (bf16[96,2048]{1,0:T(8,128)(2,1)}, bf16[96,2048]{1,0:T(8,128)(2,1)}, u32[]{:S(2)}, u32[]{:S(2)}) collective-permute-start(bf16[96,2048]{1,0:T(8,128)(2,1)} %get-tuple-element.303), channel_id=1, source_target_pairs={{8,0},{16,8},{24,16},{28,24},{20,28},{12,20},{4,12},{0,4},{9,1},{1... | collective-permute-start | bytes 1179656 | tf_op jit(solution)/shard_map/ppermute | solution.py:1063
  377.9 24.5 %collective-permute-start.70 = (bf16[64,1536]{1,0:T(8,128)(2,1)}, bf16[64,1536]{1,0:T(8,128)(2,1)}, u32[]{:S(2)}, u32[]{:S(2)}) collective-permute-start(bf16[64,1536]{1,0:T(8,128)(2,1)} %get-tuple-element.320), channel_id=1, source_target_pairs={{0,8},{8,16},{16,24},{24,28},{28,20},{20,12},{12,4},{4,0},{1,9},{9... | collective-permute-start | bytes 589832 | tf_op jit(solution)/shard_map/ppermute | solution.py:1062
  381.9 26.4 %collective-permute-start.48 = (bf16[128,1536]{1,0:T(8,128)(2,1)}, bf16[128,1536]{1,0:T(8,128)(2,1)}, u32[]{:S(2)}, u32[]{:S(2)}) collective-permute-start(bf16[128,1536]{1,0:T(8,128)(2,1)} %fusion.26), channel_id=1, source_target_pairs={{0,1},{1,0},{2,3},{3,2},{4,5},{5,4},{6,7},{7,6},{8,9},{9,8},{10,11... | collective-permute-start | bytes 1179656 | tf_op jit(solution)/shard_map/ppermute | solution.py:1085
  384.8 37.3 %all-to-all-start.6 = ((bf16[16,96,256]{2,1,0:T(8,128)(2,1)}), bf16[16,96,256]{2,1,0:T(8,128)(2,1)S(1)}, u32[]{:S(2)}, u32[]{:S(2)}) async-start(bf16[16,96,256]{2,1,0:T(8,128)(2,1)} %copy-done.24), calls=%async_computation.6 | async-start | bytes 1572864 | tf_op jit(solution)/shard_map/all_to_all | solution.py:1125
  437.3 52.6 %all-to-all-start.7 = ((bf16[32,48,192]{2,1,0:T(8,128)(2,1)}), bf16[32,48,192]{2,1,0:T(8,128)(2,1)S(1)}, u32[]{:S(2)}, u32[]{:S(2)}) async-start(bf16[32,48,192]{2,1,0:T(8,128)(2,1)} %bitcast.163), calls=%async_computation.7 | async-start | bytes 1572864 | tf_op jit(solution)/shard_map/all_to_all | solution.py:1125
  444.5 30.4 %collective-permute-start.87 = (bf16[96,2048]{1,0:T(8,128)(2,1)S(1)}, bf16[96,2048]{1,0:T(8,128)(2,1)S(1)}, u32[]{:S(2)}, u32[]{:S(2)}) collective-permute-start(bf16[96,2048]{1,0:T(8,128)(2,1)S(1)} %get-tuple-element.298), channel_id=1, source_target_pairs={{0,8},{8,16},{16,24},{24,28},{28,20},{20,12},{12,4},{4,0},{1,9},{9... | collective-permute-start | bytes 1179656 | tf_op jit(solution)/shard_map/ppermute | solution.py:1062
  446.4 28.5 %collective-permute-start.88 = (bf16[64,1536]{1,0:T(8,128)(2,1)S(1)}, bf16[64,1536]{1,0:T(8,128)(2,1)S(1)}, u32[]{:S(2)}, u32[]{:S(2)}) collective-permute-start(bf16[64,1536]{1,0:T(8,128)(2,1)S(1)} %get-tuple-element.314), channel_id=1, source_target_pairs={{0,8},{8,16},{16,24},{24,28},{28,20},{20,12},{12,4},{4,0},{1,9},{9... | collective-permute-start | bytes 589832 | tf_op jit(solution)/shard_map/ppermute | solution.py:1062
  446.7 28.2 %collective-permute-start.89 = (bf16[96,2048]{1,0:T(8,128)(2,1)S(1)}, bf16[96,2048]{1,0:T(8,128)(2,1)S(1)}, u32[]{:S(2)}, u32[]{:S(2)}) collective-permute-start(bf16[96,2048]{1,0:T(8,128)(2,1)S(1)} %get-tuple-element.297), channel_id=1, source_target_pairs={{8,0},{16,8},{24,16},{28,24},{20,28},{12,20},{4,12},{0,4},{9,1},{1... | collective-permute-start | bytes 1179656 | tf_op jit(solution)/shard_map/ppermute | solution.py:1063
  448.5 26.4 %collective-permute-start.90 = (bf16[64,1536]{1,0:T(8,128)(2,1)S(1)}, bf16[64,1536]{1,0:T(8,128)(2,1)S(1)}, u32[]{:S(2)}, u32[]{:S(2)}) collective-permute-start(bf16[64,1536]{1,0:T(8,128)(2,1)S(1)} %get-tuple-element.313), channel_id=1, source_target_pairs={{8,0},{16,8},{24,16},{28,24},{20,28},{12,20},{4,12},{0,4},{9,1},{1... | collective-permute-start | bytes 589832 | tf_op jit(solution)/shard_map/ppermute | solution.py:1063
  450.2 37.1 %collective-permute-start.82 = (bf16[128,1536]{1,0:T(8,128)(2,1)S(1)}, bf16[128,1536]{1,0:T(8,128)(2,1)S(1)}, u32[]{:S(2)}, u32[]{:S(2)}) collective-permute-start(bf16[128,1536]{1,0:T(8,128)(2,1)S(1)} %fusion.27), channel_id=1, source_target_pairs={{0,1},{1,0},{2,3},{3,2},{4,5},{5,4},{6,7},{7,6},{8,9},{9,8},{10,11... | collective-permute-start | bytes 1179656 | tf_op jit(solution)/shard_map/ppermute | solution.py:1085
  (195 other events, 1436.2 us)

commit v4 on v3

--- a/solution.py
+++ b/solution.py
@@ -344,18 +344,16 @@
 
 
 def heads_forward_kernel(
-    count, at_ref, q_ref, own_ref, other_ref, cos_ref, sin_ref,
-    send_ref, mixed_ref, prob_ref, k_ref, v_ref, turn_ref,
+    count, at_ref, kept_ref, other_ref, cos_ref, sin_ref,
+    send_ref, mixed_ref, prob_ref, q_ref, k_ref, v_ref,
 ):
-    core = at_ref[2 * count]
-    half = own_ref.shape[1]
-    here = pl.ds(pl.multiple_of(core * half, half), half)
-    there = pl.ds(pl.multiple_of((1 - core) * half, half), half)
-    turn_ref[here, :] = own_ref[0].astype(f32)
-    turn_ref[there, :] = other_ref[0].astype(f32)
-    k_ref[...] = rotate(turn_ref[...], cos_ref[...], sin_ref[...]).astype(bf16)
-    v_ref[here, :] = own_ref[1]
-    v_ref[there, :] = other_ref[1]
+    size = q_ref.shape[0]
+    half = size // 2
+    rows = kept_ref[...] + other_ref[...].astype(f32)
+    q = rotate(rows[:size], cos_ref[...], sin_ref[...])
+    q_ref[...] = (q * (score_scale * log2_e)).astype(bf16)
+    k_ref[...] = rotate(rows[size : 2 * size], cos_ref[...], sin_ref[...]).astype(bf16)
+    v_ref[...] = rows[2 * size :].astype(bf16)
     step = send_ref.shape[2]
     offset = 0
     for block in range(count):
@@ -384,8 +382,9 @@
         offset += end
 
 
-def heads_forward(at, q, own, other, cosine, sine, count):
-    size, tokens = q.shape
+def heads_forward(at, kept, other, cosine, sine, count):
+    tokens = kept.shape[1]
+    size = kept.shape[0] // 3
     step = tokens // count
     pairs = step * count * (count + 1) // 2
     return on_chip(
@@ -396,20 +395,23 @@
             like(bf16, pairs, step),
             like(bf16, size, tokens),
             like(bf16, size, tokens),
+            like(bf16, size, tokens),
         ],
-        [at, q, own, other, cosine, sine],
+        [at, kept, other, cosine, sine],
         4 * size * pairs * step,
-        scratch=[pltpu.VMEM((size, tokens), f32)],
         name="heads_forward",
+        room=32,
     )
 
 
 def heads_backward_kernel(
     count, at_ref, q_ref, k_ref, v_ref, prob_ref, mixed_ref, back_ref, cos_ref, sin_ref,
-    d_q_ref, kept_ref, away_ref, d_k_ref, d_v_ref,
+    kept_ref, away_ref,
 ):
-    core = at_ref[2 * count]
     half, step = back_ref.shape[1:]
+    size = 2 * half
+    d_k_ref = kept_ref.at[size : 2 * size]
+    d_v_ref = kept_ref.at[2 * size :]
     offset = 0
     for block in range(count):
         begin = block * step
@@ -420,7 +422,7 @@
         d_prob = dot_at(v_ref[:, 0:end], d_mixed, 0, 0)
         d_scores = (prob.astype(f32) * (d_prob - delta)).astype(bf16)
         d_q = dot_at(k_ref[:, 0:end], d_scores, 1, 0) * score_scale
-        d_q_ref[:, begin:end] = rotate_back(d_q, cos_ref[:, begin:end], sin_ref[:, begin:end])
+        kept_ref[:size, begin:end] = rotate_back(d_q, cos_ref[:, begin:end], sin_ref[:, begin:end])
         d_v = dot_at(d_mixed, prob, 1, 1)
         d_k = dot_at(q_ref[:, begin:end], d_scores, 1, 1) * ln_2
         if begin:
@@ -430,64 +432,59 @@
         d_k_ref[:, begin:end] = d_k[:, begin:end]
         offset += end
     d_k_ref[...] = rotate_back(d_k_ref[...], cos_ref[...], sin_ref[...])
-    here = pl.ds(pl.multiple_of(core * half, half), half)
-    there = pl.ds(pl.multiple_of((1 - core) * half, half), half)
-    kept_ref[0] = d_k_ref[here, :]
-    kept_ref[1] = d_v_ref[here, :]
-    away_ref[0] = d_k_ref[there, :].astype(bf16)
-    away_ref[1] = d_v_ref[there, :].astype(bf16)
+    away_ref[...] = kept_ref[...].astype(bf16)
 
 
 def heads_backward(at, q, k, v, prob, mixed, d_mixed, cosine, sine, count):
     size, tokens = q.shape
     return on_chip(
         functools.partial(heads_backward_kernel, count),
-        [
-            like(f32, size, tokens),
-            like(f32, 2, size // 2, tokens),
-            like(bf16, 2, size // 2, tokens),
-        ],
+        [like(f32, 3 * size, tokens), like(bf16, 3 * size, tokens)],
         [at, q, k, v, prob, mixed, d_mixed, cosine, sine],
         8 * size * prob.size,
-        scratch=[pltpu.VMEM((size, tokens), f32)] * 2,
         name="heads_backward",
-    )
-
-
-def heads_send_kernel(at_ref, d_q_ref, kept_ref, other_ref, send_ref, joined_ref):
-    half = kept_ref.shape[1]
+        room=32,
+    )
+
+
+def heads_send_kernel(count, at_ref, kept_ref, other_ref, send_ref, joined_ref, d_kv_ref):
+    core = at_ref[2 * count]
+    size = kept_ref.shape[0] // 3
+    half = size // 2
     quarter = half // 2
     step = send_ref.shape[2]
-    d_kv = kept_ref[...] + other_ref[...].astype(f32)
-    joined_ref[: 2 * half, :] = d_q_ref[...].astype(bf16)
-    joined_ref[2 * half : 3 * half, :] = d_kv[0].astype(bf16)
-    joined_ref[3 * half :, :] = d_kv[1].astype(bf16)
-    for block in range(send_ref.shape[0] // 2):
+    d_kv_ref[...] = kept_ref[size:, :] + other_ref[size:, :].astype(f32)
+    joined_ref[pl.ds(pl.multiple_of(core * size, size), size), :] = kept_ref[:size, :].astype(bf16)
+    joined_ref[pl.ds(pl.multiple_of((1 - core) * size, size), size), :] = other_ref[:size, :]
+    joined_ref[2 * size :, :] = d_kv_ref[...].astype(bf16)
+    for block in range(count):
         columns = slice(block * step, (block + 1) * step)
         for side in range(2):
-            rows = slice(side * quarter, (side + 1) * quarter)
+            start = pl.multiple_of(core * half + side * quarter, quarter)
             send_ref[2 * block + side] = jnp.concatenate(
                 [
-                    d_q_ref[side * half : (side + 1) * half, columns],
-                    d_kv[0, rows, columns],
-                    d_kv[1, rows, columns],
+                    kept_ref[side * half : (side + 1) * half, columns],
+                    d_kv_ref[pl.ds(start, quarter), columns],
+                    d_kv_ref[pl.ds(start + size, quarter), columns],
                 ],
                 axis=0,
             ).astype(bf16)
 
 
-def heads_send(at, d_q, kept, other, count):
-    size, tokens = d_q.shape
+def heads_send(at, kept, other, count):
+    size, tokens = kept.shape
+    size = size // 3
     return on_chip(
-        heads_send_kernel,
-        [like(bf16, 2 * count, size, tokens // count), like(bf16, 2 * size, tokens)],
-        [at, d_q, kept, other],
-        8 * d_q.size,
+        functools.partial(heads_send_kernel, count),
+        [like(bf16, 2 * count, size, tokens // count), like(bf16, 4 * size, tokens)],
+        [at, kept, other],
+        8 * kept.size,
+        scratch=[pltpu.VMEM((2 * size, tokens), f32)],
         name="heads_send",
     )
 
 
-def on_chip(kernel, out_shape, args, flops, blocks=(), scratch=(), name=None):
+def on_chip(kernel, out_shape, args, flops, blocks=(), scratch=(), name=None, room=24):
     moved = sum(a.size * a.dtype.itemsize for a in list(args) + list(blocks))
     moved += sum(o.size * o.dtype.itemsize for o in out_shape)
     near = pl.BlockSpec(memory_space=pltpu.VMEM)
@@ -499,7 +496,7 @@
         + [pl.BlockSpec(memory_space=pltpu.HBM)] * len(blocks),
         out_specs=(near,) * len(out_shape),
         scratch_shapes=scratch,
-        compiler_params=pltpu.CompilerParams(vmem_limit_bytes=48 * 2**20),
+        compiler_params=pltpu.CompilerParams(vmem_limit_bytes=room * 2**20),
         cost_estimate=pl.CostEstimate(flops=flops, bytes_accessed=moved, transcendentals=0),
         name=name,
     )(*args, *blocks)
@@ -601,25 +598,25 @@
     query = query_ref[...].astype(f32) * gain
     key = key_ref[...].astype(f32) * gain
     value = value_ref[...].astype(f32) * gain
-    half = HEAD_SIZE // 2
-    for head in range(out_ref.shape[0] // 2):
+    for group in range(out_ref.shape[0] // 2):
+        shared = slice(group * HEAD_SIZE, (group + 1) * HEAD_SIZE)
         columns = jnp.concatenate(
             [
-                query[:, head * HEAD_SIZE : (head + 1) * HEAD_SIZE],
-                key[:, head * half : (head + 1) * half],
-                value[:, head * half : (head + 1) * half],
+                query[:, 2 * group * HEAD_SIZE : 2 * (group + 1) * HEAD_SIZE],
+                key[:, shared],
+                value[:, shared],
             ],
             axis=1,
         ).astype(bf16)
-        out_ref[2 * head] = columns
-        out_ref[2 * head + 1] = columns
+        out_ref[2 * group] = columns
+        out_ref[2 * group + 1] = columns
 
 
 def head_columns(at, gain, query, key, value):
     own, width = query.shape
     (out,) = on_chip(
         head_columns_kernel,
-        [like(bf16, 2 * (width // HEAD_SIZE), own, 2 * HEAD_SIZE)],
+        [like(bf16, width // HEAD_SIZE, own, 4 * HEAD_SIZE)],
         [at, gain, query, key, value],
         own * width,
         name="head_columns",
@@ -627,45 +624,84 @@
     return out
 
 
+def normed_halves_kernel(count, at_ref, rows_ref, kept_ref, away_ref):
+    core = at_ref[2 * count]
+    rows = rows_ref[...].astype(f32)
+    mean = jnp.mean(rows * rows, axis=-1, keepdims=True)
+    normed = rows * lax.rsqrt(mean + norm_eps)
+    size = rows.shape[1] // (2 * count)
+    halves = [
+        jnp.concatenate(
+            [normed[:, (2 * i + c) * size : (2 * i + c + 1) * size] for i in range(count)], axis=1
+        )
+        for c in range(2)
+    ]
+    kept_ref[...] = jnp.where(core == 0, halves[0], halves[1]).astype(bf16)
+    away_ref[...] = jnp.where(core == 0, halves[1], halves[0]).astype(bf16)
+
+
+def normed_halves(at, rows, count):
+    tokens, width = rows.shape
+    return on_chip(
+        functools.partial(normed_halves_kernel, count),
+        [like(bf16, tokens, width // 2), like(bf16, tokens, width // 2)],
+        [at, rows],
+        8 * rows.size,
+        name="normed_halves",
+    )
+
+
 def sequence_copies(at_ref, block_refs, whole_ref, sem_ref):
-    count = len(block_refs) // 2
+    count = len(block_refs)
     core = at_ref[2 * count]
-    rows = block_refs[0].shape[0]
+    rows = whole_ref.shape[0] // (2 * count)
     copies = []
     for i, block_ref in enumerate(block_refs):
-        side = core if i < count else 1 - core
-        start = pl.multiple_of((2 * at_ref[i % count] + side) * rows, rows)
-        copies.append(
-            pltpu.make_async_copy(block_ref, whole_ref.at[pl.ds(start, rows), :], sem_ref.at[i])
-        )
+        for k, side in enumerate((core, 1 - core)):
+            start = pl.multiple_of((2 * at_ref[i] + side) * rows, rows)
+            copies.append(
+                pltpu.make_async_copy(
+                    block_ref.at[pl.ds(k * rows, rows), :],
+                    whole_ref.at[pl.ds(start, rows), :],
+                    sem_ref.at[2 * i + k],
+                )
+            )
     return copies
 
 
-def project_heads_kernel(at_ref, weight_ref, cos_ref, sin_ref, *refs):
-    blocks, (q_ref, kv_ref, n_ref, sem_ref) = refs[:-4], refs[-4:]
+def project_heads_kernel(at_ref, weight_ref, *refs):
+    blocks, (kept_ref, away_ref, n_ref, out_ref, sem_ref) = refs[:-5], refs[-5:]
     copies = sequence_copies(at_ref, blocks, n_ref, sem_ref)
     for copy in copies:
         copy.start()
     for copy in copies:
         copy.wait()
-    half = kv_ref.shape[1]
-    out = dot_at(weight_ref[...], n_ref[...], 0, 1)
-    q = rotate(out[: 2 * half], cos_ref[...], sin_ref[...])
-    q_ref[...] = (q * (score_scale * log2_e)).astype(bf16)
-    kv_ref[0] = out[2 * half : 3 * half].astype(bf16)
-    kv_ref[1] = out[3 * half :].astype(bf16)
-
-
-def project_heads(at, weight, cosine, sine, blocks):
-    half, tokens = cosine.shape
-    rows, width = blocks[0].shape
+    core = at_ref[2 * len(blocks)]
+    size = kept_ref.shape[0] // 3
+    out_ref[...] = dot_at(weight_ref[...], n_ref[...], 0, 1)
+    kept_ref[:size, :] = out_ref[pl.ds(pl.multiple_of(core * size, size), size), :]
+    kept_ref[size:, :] = out_ref[2 * size :, :]
+    there = pl.ds(pl.multiple_of((1 - core) * size, size), size)
+    away_ref[:size, :] = out_ref[there, :].astype(bf16)
+    away_ref[size:, :] = out_ref[2 * size :, :].astype(bf16)
+
+
+def project_heads(at, weight, blocks, rows):
+    count = len(blocks)
+    width, columns = weight.shape
+    tokens = 2 * count * rows
+    size = columns // 4
     return on_chip(
         project_heads_kernel,
-        [like(bf16, 2 * half, tokens), like(bf16, 2, half, tokens)],
-        [at, weight, cosine, sine],
-        8 * half * tokens * width,
+        [like(f32, 3 * size, tokens), like(bf16, 3 * size, tokens)],
+        [at, weight],
+        2 * columns * tokens * width,
         blocks=blocks,
-        scratch=[pltpu.VMEM((tokens, width), bf16), pltpu.SemaphoreType.DMA((len(blocks),))],
+        scratch=[
+            pltpu.VMEM((tokens, width), bf16),
+            pltpu.VMEM((columns, tokens), f32),
+            pltpu.SemaphoreType.DMA((2 * count,)),
+        ],
         name="project_heads",
     )
 
@@ -681,20 +717,32 @@
 
 def project_out_kernel(first, at_ref, heads_ref, *refs):
     blocks, (weight_ref, joined_ref, kept_ref, away_ref, out_ref, sem_ref) = refs[:-6], refs[-6:]
-    copies = block_copies(at_ref, blocks, weight_ref, sem_ref, first=first)
+    count = len(blocks)
+    own = weight_ref.shape[0] // count
+    width = weight_ref.shape[1] // 2
+    copies = []
+    for i, block_ref in enumerate(blocks):
+        start = pl.multiple_of(at_ref[i] * own, own)
+        for k in range(2):
+            copies.append(
+                pltpu.make_async_copy(
+                    block_ref.at[pl.ds(first + k * own, own), :],
+                    weight_ref.at[pl.ds(start, own), pl.ds(k * width, width)],
+                    sem_ref.at[2 * i + k],
+                )
+            )
     for copy in copies:
         copy.start()
     join_heads(heads_ref, joined_ref)
     for copy in copies:
         copy.wait()
     out_ref[...] = dot_at(joined_ref[...], weight_ref[...], 0, 0)
-    part_rows(at_ref, len(blocks), out_ref, kept_ref, away_ref)
-
-
-def project_out(at, heads, blocks, first):
+    part_rows(at_ref, count, out_ref, kept_ref, away_ref)
+
+
+def project_out(at, heads, blocks, first, own):
     count = len(blocks)
-    own, width = blocks[0].shape
-    own -= first
+    width = 2 * blocks[0].shape[1]
     rows = heads.shape[2] // 2
     return on_chip(
         functools.partial(project_out_kernel, first),
@@ -707,113 +755,166 @@
         [at, heads],
         8 * rows * width * count * own,
         blocks=blocks,
-        scratch=[pltpu.VMEM((4 * rows, width), f32), pltpu.SemaphoreType.DMA((count,))],
+        scratch=[pltpu.VMEM((4 * rows, width), f32), pltpu.SemaphoreType.DMA((2 * count,))],
         name="project_out",
     )
 
 
-def hidden_gradient_kernel(at_ref, own_ref, other_ref, *refs):
-    blocks, (d_out_ref, weight_ref, d_hidden_ref, sem_ref) = refs[:-4], refs[-4:]
-    copies = block_copies(at_ref, blocks, weight_ref, sem_ref)
-    for copy in copies:
-        copy.start()
-    join_rows(at_ref, len(blocks), own_ref, other_ref, d_out_ref)
-    for copy in copies:
-        copy.wait()
-    d_hidden_ref[...] = dot_at(d_out_ref[...], weight_ref[...], 1, 1).astype(bf16)
-
-
-def hidden_gradient(at, d_out_own, d_out_other, blocks, own):
-    count = len(blocks)
-    _, rows, width = d_out_own.shape
-    return on_chip(
-        hidden_gradient_kernel,
-        [
-            like(bf16, 4 * rows, width),
-            like(bf16, count * own, width),
-            like(bf16, 4 * rows, count * own),
-        ],
-        [at, d_out_own, d_out_other],
-        8 * rows * width * count * own,
-        blocks=blocks,
-        scratch=[pltpu.SemaphoreType.DMA((count,))],
-        name="hidden_gradient",
-    )
-
-
-def feed_forward_kernel(step, at_ref, own_ref, other_ref, d_hidden_ref, *refs):
-    blocks = refs[:-8]
-    n_ref, hidden_ref, d_both_ref, kept_ref, away_ref, d_n_ref, whole_ref, sem_ref = refs[-8:]
+def down_pieces(rows, width, wide):
+    left = wide // 2
+    right = width - left
+    pieces = [(i * rows // 2, 0, rows // 2, left, 0, i * left) for i in range(2)]
+    parts = wide // right
+    size = rows // parts
+    pieces += [(i * size, left, size, right, rows // 2, i * right) for i in range(parts)]
+    return pieces
+
+
+def pack_down_kernel(at_ref, down_ref, pair_ref, out_ref):
+    first = pair_ref.shape[0]
+    out_ref[:first, :] = pair_ref[...]
+    for row, column, rows, columns, to, place in down_pieces(*down_ref.shape, out_ref.shape[1]):
+        out_ref[first + to : first + to + rows, place : place + columns] = down_ref[
+            row : row + rows, column : column + columns
+        ]
+
+
+def pack_down(at, down, pair):
+    first, wide = pair.shape
+    (out,) = on_chip(
+        pack_down_kernel,
+        [like(bf16, first + down.size // wide, wide)],
+        [at, down, pair],
+        0,
+        name="pack_down",
+    )
+    return out
+
+
+def down_copies(at_ref, block_refs, first, down_ref, sem_ref):
+    own = down_ref.shape[0] // len(block_refs)
+    pieces = down_pieces(own, down_ref.shape[1], block_refs[0].shape[1])
+    copies = []
+    for i, block_ref in enumerate(block_refs):
+        for k, (row, column, rows, columns, to, place) in enumerate(pieces):
+            start = pl.multiple_of(at_ref[i] * own + row, rows)
+            copies.append(
+                pltpu.make_async_copy(
+                    block_ref.at[pl.ds(first + to, rows), pl.ds(place, columns)],
+                    down_ref.at[pl.ds(start, rows), pl.ds(column, columns)],
+                    sem_ref.at[i * len(pieces) + k],
+                )
+            )
+    return copies
+
+
+def feed_forward_kernel(step, at_ref, own_ref, other_ref, d_own_ref, d_other_ref, *refs):
+    blocks = refs[:-11]
+    n_ref, d_out_ref, hidden_ref, d_both_ref, kept_ref, away_ref = refs[-11:-5]
+    d_n_ref, whole_ref, down_ref, sem_ref, down_sem_ref = refs[-5:]
     ff = hidden_ref.shape[1]
-    copies = block_copies(at_ref, blocks, whole_ref, sem_ref)
+    first = whole_ref.shape[0] // len(blocks)
+    copies = down_copies(at_ref, blocks, first, down_ref, down_sem_ref)
+    copies += block_copies(at_ref, blocks, whole_ref, sem_ref)
     for copy in copies:
         copy.start()
     join_rows(at_ref, len(blocks), own_ref, other_ref, n_ref)
+    join_rows(at_ref, len(blocks), d_own_ref, d_other_ref, d_out_ref)
     for copy in copies:
         copy.wait()
     for begin in range(0, n_ref.shape[0], step):
         rows = slice(begin, begin + step)
+        d_hidden = dot_at(d_out_ref[rows, :], down_ref[...], 1, 1)
         both = dot_at(n_ref[rows, :], whole_ref[...], 1, 0)
         gate = both[:, :ff]
         upper = both[:, ff:]
         sigma = 1.0 / (1.0 + jnp.exp(-gate))
         silu = gate * sigma
         hidden_ref[rows, :] = (silu * upper).astype(bf16)
-        d_hidden = d_hidden_ref[rows, :].astype(f32)
         d_both_ref[rows, :ff] = (d_hidden * upper * (sigma + silu * (1.0 - sigma))).astype(bf16)
         d_both_ref[rows, ff:] = (d_hidden * silu).astype(bf16)
         d_n_ref[rows, :] = dot_at(d_both_ref[rows, :], whole_ref[...], 1, 1)
     part_rows(at_ref, len(blocks), d_n_ref, kept_ref, away_ref)
 
 
-def feed_forward(at, own, other, d_hidden, blocks):
+def feed_forward(at, own, other, d_own, d_other, blocks, ff):
     _, rows, width = own.shape
-    ff = d_hidden.shape[1]
+    count = len(blocks)
+    pieces = len(down_pieces(ff // count, width, 2 * ff))
     return on_chip(
         functools.partial(feed_forward_kernel, min(256, 4 * rows)),
         [
+            like(bf16, 4 * rows, width),
             like(bf16, 4 * rows, width),
             like(bf16, 4 * rows, ff),
             like(bf16, 4 * rows, 2 * ff),
             like(f32, 2, rows, width),
             like(bf16, 2, rows, width),
         ],
-        [at, own, other, d_hidden],
-        32 * rows * width * ff,
+        [at, own, other, d_own, d_other],
+        40 * rows * width * ff,
         blocks=blocks,
         scratch=[
             pltpu.VMEM((4 * rows, width), f32),
             pltpu.VMEM((width, 2 * ff), bf16),
-            pltpu.SemaphoreType.DMA((len(blocks),)),
+            pltpu.VMEM((ff, width), bf16),
+            pltpu.SemaphoreType.DMA((count,)),
+            pltpu.SemaphoreType.DMA((count * pieces,)),
         ],
         name="feed_forward",
-    )
-
-
-def feed_forward_grads_kernel(at_ref, n_ref, d_both_ref, hidden_ref, d_out_ref, both_ref, down_ref):
-    count, block, _ = both_ref.shape
-    own = down_ref.shape[1]
-    for k in range(count):
-        down_ref[k] = dot_at(
-            hidden_ref[:, pl.ds(pl.multiple_of(at_ref[k] * own, own), own)], d_out_ref[...], 0, 0
-        ).astype(bf16)
+        room=40,
+    )
+
+
+def feed_forward_grads_kernel(at_ref, n_ref, d_both_ref, hidden_ref, d_out_ref, grad_ref):
+    count, _, wide = grad_ref.shape
+    block = n_ref.shape[1] // count
+    own = hidden_ref.shape[1] // count
     for position in range(count):
+        place = at_ref[count + position]
         columns = slice(position * block, (position + 1) * block)
-        both_ref[at_ref[count + position]] = dot_at(
-            n_ref[:, columns], d_both_ref[...], 0, 0
-        ).astype(bf16)
+        grad_ref[place, :block, :] = dot_at(n_ref[:, columns], d_both_ref[...], 0, 0).astype(bf16)
+        columns = slice(position * own, (position + 1) * own)
+        down = dot_at(hidden_ref[:, columns], d_out_ref[...], 0, 0).astype(bf16)
+        for row, column, rows, width, to, start in down_pieces(own, n_ref.shape[1], wide):
+            grad_ref[place, block + to : block + to + rows, start : start + width] = down[
+                row : row + rows, column : column + width
+            ]
 
 
 def feed_forward_grads(at, n, d_both, hidden, d_out, count):
     rows, width = n.shape
     ff = hidden.shape[1]
-    return on_chip(
+    (out,) = on_chip(
         feed_forward_grads_kernel,
-        [like(bf16, count, width // count, 2 * ff), like(bf16, count, ff // count, width)],
+        [like(bf16, count, width // count + ff // count * width // (2 * ff), 2 * ff)],
         [at, n, d_both, hidden, d_out],
         6 * rows * width * ff,
         name="feed_forward_grads",
-    )
+        room=32,
+    )
+    return out
+
+
+def joined_grads_kernel(at_ref, left_ref, right_ref, grad_ref):
+    count, block, _ = grad_ref.shape
+    for position in range(count):
+        rows = slice(position * block, (position + 1) * block)
+        grad_ref[at_ref[count + position]] = dot_at(
+            left_ref[rows, :], right_ref[...], 1, 0
+        ).astype(bf16)
+
+
+def joined_grads(at, left, right, count):
+    width, rows = left.shape
+    (out,) = on_chip(
+        joined_grads_kernel,
+        [like(bf16, count, width // count, right.shape[1])],
+        [at, left, right],
+        2 * rows * width * right.shape[1],
+        name="joined_grads",
+    )
+    return out
 
 
 def split_heads_kernel(at_ref, own_ref, other_ref, weight_ref, d_mid_ref, heads_ref):
@@ -859,7 +960,7 @@
         [at, joined],
         2 * tokens * width * columns,
         blocks=blocks,
-        scratch=[pltpu.VMEM((tokens, width), bf16), pltpu.SemaphoreType.DMA((len(blocks),))],
+        scratch=[pltpu.VMEM((tokens, width), bf16), pltpu.SemaphoreType.DMA((2 * len(blocks),))],
         name="heads_grad",
     )
     return out
@@ -899,20 +1000,33 @@
     )
 
 
-def layer_output_kernel(count, at_ref, hidden_ref, weight_ref, kept_ref, away_ref, out_ref):
-    out_ref[...] = dot_at(hidden_ref[...], weight_ref[...], 1, 0)
-    part_rows(at_ref, count, out_ref, kept_ref, away_ref)
-
-
-def layer_output(at, hidden, weight, count):
-    ff, width = weight.shape
+def layer_output_kernel(first, at_ref, hidden_ref, *refs):
+    blocks, (kept_ref, away_ref, out_ref, down_ref, sem_ref) = refs[:-5], refs[-5:]
+    copies = down_copies(at_ref, blocks, first, down_ref, sem_ref)
+    for copy in copies:
+        copy.start()
+    for copy in copies:
+        copy.wait()
+    out_ref[...] = dot_at(hidden_ref[...], down_ref[...], 1, 0)
+    part_rows(at_ref, len(blocks), out_ref, kept_ref, away_ref)
+
+
+def layer_output(at, hidden, blocks, first, width):
+    ff = hidden.shape[1]
     rows = hidden.shape[0] // 4
+    count = len(blocks)
+    pieces = len(down_pieces(ff // count, width, 2 * ff))
     return on_chip(
-        functools.partial(layer_output_kernel, count),
+        functools.partial(layer_output_kernel, first),
         [like(f32, 2, rows, width), like(bf16, 2, rows, width)],
-        [at, hidden, weight],
+        [at, hidden],
         0,
-        scratch=[pltpu.VMEM((4 * rows, width), f32)],
+        blocks=blocks,
+        scratch=[
+            pltpu.VMEM((4 * rows, width), f32),
+            pltpu.VMEM((ff, width), bf16),
+            pltpu.SemaphoreType.DMA((count * pieces,)),
+        ],
         name="layer_output",
     )
 
@@ -920,13 +1034,12 @@
 def query_rows_kernel(
     at_ref, terms_ref, gain_ref, query_ref, key_ref, value_ref, d_query, d_key, d_value, d_gain
 ):
-    half = HEAD_SIZE // 2
     pieces = ([], [], [])
-    for head in range(terms_ref.shape[0] // 2):
-        part = terms_ref[2 * head].astype(f32) + terms_ref[2 * head + 1].astype(f32)
-        pieces[0].append(part[:, :HEAD_SIZE])
-        pieces[1].append(part[:, HEAD_SIZE : HEAD_SIZE + half])
-        pieces[2].append(part[:, HEAD_SIZE + half :])
+    for group in range(terms_ref.shape[0] // 2):
+        part = terms_ref[2 * group].astype(f32) + terms_ref[2 * group + 1].astype(f32)
+        pieces[0].append(part[:, : 2 * HEAD_SIZE])
+        pieces[1].append(part[:, 2 * HEAD_SIZE : 3 * HEAD_SIZE])
+        pieces[2].append(part[:, 3 * HEAD_SIZE :])
     gain = gain_ref[...]
     rows_sum = None
     outs = (d_query, d_key, d_value)
@@ -955,7 +1068,8 @@
 
 
 def pair_rows_kernel(
-    size, count, at_ref, terms_ref, gain_ref, gate_ref, up_ref, d_gate, d_up, d_gain
+    size, count, at_ref, terms_ref, down_terms, gain_ref, gate_ref, up_ref,
+    d_gate, d_up, d_gain, d_down,
 ):
     gain = gain_ref[...]
     core = at_ref[2 * count]
@@ -974,17 +1088,31 @@
                     grad * weight_ref[:, columns].astype(f32), axis=1, keepdims=True
                 )
     d_gain[...] = rows_sum
-
-
-def pair_rows_grads(at, terms, gain, gate, up, size, count):
+    for row, column, rows, columns, to, place in down_pieces(*d_down.shape, down_terms.shape[1]):
+        d_down[row : row + rows, column : column + columns] = down_terms[
+            to : to + rows, place : place + columns
+        ]
+
+
+def pair_rows_grads(at, terms, down_terms, gain, gate, up, size, count):
     own = gate.shape[0]
     return on_chip(
         functools.partial(pair_rows_kernel, size, count),
-        [like(f32, *gate.shape), like(f32, *up.shape), like(f32, own, 1)],
-        [at, terms, gain, gate, up],
+        [
+            like(f32, *gate.shape),
+            like(f32, *up.shape),
+            like(f32, own, 1),
+            like(f32, size, down_terms.size // size),
+        ],
+        [at, terms, down_terms, gain, gate, up],
         terms.size,
         name="pair_rows_grads",
     )
+
+
+ring_axes = ("z", "x")
+owner_axes = ("z", "x", "core", "y")
+head_axes = ("z", "x", "y")
 
 
 def ring_of(count):
@@ -1027,58 +1155,59 @@
             ahead, behind = ahead[:half], behind[half:]
         if others:
             ahead, behind = lax.optimization_barrier((ahead, behind) + others)[:2]
-        self.ahead = lax.ppermute(ahead, "d", self.forward)
-        self.behind = lax.ppermute(behind, "d", self.backward)
-
-    def settle(self, *others):
-        out = lax.optimization_barrier((self.ahead, self.behind) + others)
-        self.ahead, self.behind = out[:2]
+        self.pending = [
+            lax.ppermute(ahead, ring_axes, self.forward),
+            lax.ppermute(behind, ring_axes, self.backward),
+        ]
+
+    def land(self, arrived):
+        self.ahead, self.behind = arrived
         if self.hops == self.count // 2:
-            self.parts[self.hops] = jnp.concatenate(out[:2], axis=0)
+            self.parts[self.hops] = jnp.concatenate(arrived, axis=0)
         else:
             self.parts[self.count - self.hops] = self.ahead
             self.parts[self.hops] = self.behind
-        return out[2] if len(others) == 1 else out[2:]
 
 
 class ScatterRing:
-    def __init__(self, terms, count):
+    def __init__(self, term, count):
         self.count = count
-        self.terms = terms
+        self.term = term
         self.forward, self.backward = ring_of(count)
-        self.ahead = [self.part(t, count - 1, 0) for t in terms]
-        self.behind = [self.part(t, 1, 1) for t in terms]
+        self.rows = term.shape[1] // 2
+        far = term[count // 2]
+        self.ahead, self.behind = far[: self.rows], far[self.rows :]
         self.hops = 0
 
-    def part(self, term, at, side):
-        half = term.shape[1] // 2
-        return term[at % self.count, side * half : (side + 1) * half]
-
-    def start(self, *others):
+    def start(self):
         self.hops += 1
-        ahead, behind = self.ahead, self.behind
-        if others:
-            ahead, behind = lax.optimization_barrier((ahead, behind) + others)[:2]
-        self.ahead = [lax.ppermute(a, "d", self.forward) for a in ahead]
-        self.behind = [lax.ppermute(b, "d", self.backward) for b in behind]
-
-    def settle(self, *others):
-        out = lax.optimization_barrier((self.ahead, self.behind) + others)
-        ahead, behind = out[:2]
-        kind = f32 if self.hops == self.count - 1 else bf16
-        place = self.count - 1 - self.hops
-        self.ahead = [
-            (a.astype(f32) + self.part(t, place, 0).astype(f32)).astype(kind)
-            for a, t in zip(ahead, self.terms)
+        self.pending = [
+            lax.ppermute(self.ahead, ring_axes, self.forward),
+            lax.ppermute(self.behind, ring_axes, self.backward),
         ]
-        self.behind = [
-            (b.astype(f32) + self.part(t, 1 + self.hops, 1).astype(f32)).astype(kind)
-            for b, t in zip(behind, self.terms)
-        ]
-        return out[2] if len(others) == 1 else out[2:]
-
-    def sums(self):
-        return [jnp.concatenate([a, b], axis=0) for a, b in zip(self.ahead, self.behind)]
+
+    def land(self, arrived):
+        ahead, behind = (value.astype(f32) for value in arrived)
+        left = self.count // 2 - self.hops
+        if left == 0:
+            self.total = self.term[0].astype(f32) + ahead + behind
+            return
+        if self.hops == 1:
+            edges = ((0, self.rows, 0), (self.rows, 0, 0))
+            ahead, behind = (
+                lax.pad(value, jnp.float32(0), (edge,) + ((0, 0, 0),) * (value.ndim - 1))
+                for value, edge in zip((ahead, behind), (edges[0], edges[1]))
+            )
+        self.ahead = (self.term[left].astype(f32) + ahead).astype(bf16)
+        self.behind = (self.term[self.count - left].astype(f32) + behind).astype(bf16)
+
+
+def settle(moves, *others):
+    moving = tuple(tuple(move.pending) for move in moves)
+    out = lax.optimization_barrier((moving, others))
+    for move, arrived in zip(moves, out[0]):
+        move.land(list(arrived))
+    return out[1][0] if len(others) == 1 else out[1]
 
 
 def swap(values, axis):
@@ -1156,7 +1285,7 @@
     gain1 = norm_gain1.astype(f32)[:, None]
     gain2 = norm_gain2.astype(f32)[:, None]
 
-    place = place_of(lax.axis_index("d"), count)
+    place = place_of(lax.axis_index(ring_axes), count)
     steps = jnp.arange(count, dtype=jnp.int32)
     core = lax.axis_index("core")
     seq = lax.axis_index("y")
@@ -1175,56 +1304,47 @@
     sine = jnp.sin(angle)
 
     own_rows = tokens[0].astype(f32)
-    n1_ring = GatherRing((own_rows * inverse_rms(own_rows)).astype(bf16), count)
+    n1_kept, n1_away = normed_halves(at, tokens[0], count)
+    n1_other = swap(n1_away, "core")
+    half_width = width // 2
+    n1_ring = GatherRing(
+        jnp.concatenate([n1_kept, n1_other, w_out[:, :half_width], w_out[:, half_width:]], axis=0),
+        count,
+    )
     n1_ring.start()
-    out_ring = GatherRing(w_out, count)
-    out_ring.start()
     head_cols = head_columns(at, gain1, w_query, key_weight, value_weight)
-    head_weight = all_to_all(head_cols, ("d", "core", "y")).reshape(width, 2 * HEAD_SIZE)
-    out_ring.settle()
-    head_cols = n1_ring.settle(head_cols)
+    head_weight = all_to_all(head_cols, head_axes).reshape(half_width, 4 * HEAD_SIZE)
+    pair_cols = pair_columns(at, gain2, w_gate, w_up, ff_own)
+    head_cols, pair_cols = settle([n1_ring], head_cols, pair_cols)
     n1_ring.start()
-    out_ring.start()
     tokens_pair = both_rows(tokens[0], head_cols)
-    pair_cols = pair_columns(at, gain2, w_gate, w_up, ff_own)
-    out_ring.settle()
-    head_weight, tokens_pair, pair_cols = n1_ring.settle(head_weight, tokens_pair, pair_cols)
+    head_weight, tokens_pair = settle([n1_ring], head_weight, tokens_pair)
     n1_ring.start()
-    out_ring.start()
     pair_rows = all_to_all(pair_cols, ("core", "y")).reshape(group, 2 * count * ff_own)
-    out_ring.settle()
-    n1_ring.settle()
+    settle([n1_ring])
     n1_ring.start()
-    out_ring.start()
-    out_ring.settle()
-    pair_rows = n1_ring.settle(pair_rows)
-    n1_blocks = n1_ring.parts + [swap(part, "core") for part in n1_ring.parts]
-
-    pair_ring = GatherRing(pair_rows, count)
-    pair_ring.start(n1_blocks[count // 2])
-    down_ring = GatherRing(w_down, count)
-    down_ring.start(n1_blocks[count // 2])
-    q, kv_own = project_heads(at, head_weight, cosine, sine, n1_blocks)
-    kv_other = swap(kv_own, "core")
-    cotangent_pair = both_rows(after(cotangent[0], pair_rows), kv_own)
+    ff_rows = pack_down(at, w_down, pair_rows)
+    ff_rows = settle([n1_ring], ff_rows)
+
+    gather = GatherRing(ff_rows, count)
+    gather.start()
+    kept, away = project_heads(at, head_weight, n1_ring.parts, rows)
+    cotangent_pair = both_rows(after(cotangent[0], ff_rows), kept)
+    mixed_send, mixed, prob, q, k, v = heads_forward(
+        at, kept, swap(away, "core"), cosine, sine, count
+    )
+    mixed_send, cotangent_pair = settle([gather], mixed_send, cotangent_pair)
+    gather.start()
+    mixed_low = all_to_all(mixed_send, head_axes)
     cotangent_other = swap(cotangent_pair, "core")
-    mixed_send, mixed, prob, k, v = heads_forward(at, q, kv_own, kv_other, cosine, sine, count)
-    mixed_send = pair_ring.settle(mixed_send)
-    down_ring.settle()
-    pair_ring.start()
-    down_ring.start()
-    mixed_low = all_to_all(mixed_send, ("d", "y"))
-    mixed_low, cotangent_other = pair_ring.settle(mixed_low, cotangent_other)
-    down_ring.settle()
-    pair_ring.start()
-    down_ring.start()
-    out_weight, mixed_low, kept, away = project_out(at, mixed_low, out_ring.parts, 0)
-    branch = core_sum(kept, away)
-    branch = both_rows_sum(branch)
-    down_ring.settle()
-    branch = pair_ring.settle(branch)
-    pair_ring.start()
-    down_ring.start()
+    mixed_low, cotangent_other = settle([gather], mixed_low, cotangent_other)
+    gather.start()
+    out_weight, mixed_low, kept, away = project_out(at, mixed_low, n1_ring.parts, 2 * rows, own)
+    branch = both_rows_sum(core_sum(kept, away))
+    qkv_cols = query_columns(at, gain1, w_query, key_weight, value_weight)
+    qkv_rows = all_to_all(after(qkv_cols, mixed_low), ("core", "y"))
+    branch, qkv_rows = settle([gather], branch, qkv_rows)
+    gather.start()
     inputs = tokens_pair.astype(f32)
     middle = inputs + branch
 
@@ -1232,33 +1352,23 @@
     n2_pair = middle * r2
     n2_own = n2_pair.astype(bf16)
     n2_other = swap(n2_own, "core")
-    down_ring.settle()
-    d_out, down_weight, d_hidden = hidden_gradient(
-        at, cotangent_pair, cotangent_other, down_ring.parts, ff_own
-    )
-    n2_own, n2_other, d_hidden = pair_ring.settle(n2_own, n2_other, d_hidden)
-    qkv_cols = query_columns(at, gain1, w_query, key_weight, value_weight)
-    qkv_rows = all_to_all(after(qkv_cols, pair_rows), ("core", "y"))
-    qkv_rows = qkv_rows.reshape(group, count * HEAD_SIZE)
-    n2_own, qkv_rows = tie(n2_own, qkv_rows)
-    qkv_ring = GatherRing(qkv_rows, count)
+    n2_own, n2_other = settle([gather], n2_own, n2_other)
+    qkv_ring = GatherRing(qkv_rows.reshape(group, count * HEAD_SIZE), count)
+    qkv_ring.start(n2_own)
+    n2, d_out, hidden, d_both, kept, away = feed_forward(
+        at, n2_own, n2_other, cotangent_pair, cotangent_other, gather.parts, count * ff_own
+    )
+    kept, away = settle([qkv_ring], kept, away)
     qkv_ring.start()
-    n2, hidden, d_both, kept, away = feed_forward(at, n2_own, n2_other, d_hidden, pair_ring.parts)
-    d_n2 = qkv_ring.settle(core_sum(kept, away))
+    d_n2 = core_sum(kept, away)
+    grads = feed_forward_grads(at, n2, d_both, after(hidden, d_n2), d_out, count)
+    d_normed2 = both_rows_sum(d_n2)
+    grads = settle([qkv_ring], grads)
+    scatter = ScatterRing(grads, count)
+    scatter.start()
+    d_normed2 = settle([scatter], d_normed2)
+    scatter.start()
     qkv_ring.start()
-    grad_both, grad_down = feed_forward_grads(
-        at, n2, d_both, after(hidden, d_n2), d_out, count
-    )
-    d_normed2 = both_rows_sum(d_n2)
-    grad_down = qkv_ring.settle(grad_down)
-    qkv_ring.start()
-    ff_ring = ScatterRing([grad_both, grad_down], count)
-    qkv_ring.settle()
-    qkv_ring.start()
-    ff_ring.start()
-    qkv_ring.settle()
-    d_normed2 = ff_ring.settle(d_normed2)
-    ff_ring.start()
     d_middle = cotangent_pair.astype(f32) + r2 * (
         d_normed2 - n2_pair * jnp.mean(d_normed2 * n2_pair, axis=-1, keepdims=True)
     )
@@ -1266,30 +1376,34 @@
     d_mid_own = d_middle.astype(bf16)
     d_mid_other = swap(d_mid_own, "core")
     d_mid, d_mixed = split_heads(at, d_mid_own, d_mid_other, out_weight, count)
-    d_mixed = all_to_all(d_mixed, ("d", "y"))
-    d_mixed = ff_ring.settle(d_mixed)
-    ff_ring.start()
-    grad_out = dot_at(after(mixed_low, d_mixed), d_mid, 1, 0).astype(bf16)
-    owned_out = all_to_all(grad_out.reshape(count, own, width), "d")
-    d_q, kept, away = heads_backward(at, q, k, v, prob, mixed, d_mixed, cosine, sine, count)
-    d_qkv, joined = heads_send(at, d_q, kept, swap(away, "core"), count)
-    d_qkv, owned_out = ff_ring.settle(d_qkv, owned_out)
-    ff_ring.start()
-    d_qkv = all_to_all(d_qkv, ("d", "y"))
-    grad_heads = heads_grad(at, joined, n1_blocks)
-    grad_heads = ff_ring.settle(grad_heads)
-    ff_ring.start()
-    grad_heads, d_qkv = ff_ring.settle(grad_heads, d_qkv)
-    ff_ring.start()
-    grad_heads = all_to_all(grad_heads.reshape(4 * count, own, 2 * HEAD_SIZE), ("d", "core", "y"))
+    d_mixed = all_to_all(d_mixed, head_axes)
+    out_grads = joined_grads(at, mixed_low, d_mid, count)
+    kept_out, away_out = layer_output(
+        at, after(hidden, d_mid), gather.parts, group, width
+    )
+    d_mixed, out_grads, kept_out, away_out = settle(
+        [scatter, qkv_ring], d_mixed, out_grads, kept_out, away_out
+    )
+    out_scatter = ScatterRing(out_grads, count)
+    scatter.start()
+    out_scatter.start()
+    qkv_ring.start()
+    kept, away = heads_backward(at, q, k, v, prob, mixed, d_mixed, cosine, sine, count)
+    out_rows = own_rows_sum(core_sum(kept_out, away_out))
+    kept, away, out_rows = settle([scatter, out_scatter, qkv_ring], kept, away, out_rows)
+    scatter.start()
+    out_scatter.start()
+    d_qkv, joined = heads_send(at, kept, swap(away, "core"), count)
+    d_qkv = all_to_all(d_qkv, head_axes)
+    grad_heads = heads_grad(at, joined, n1_ring.parts)
+    grad_heads, d_qkv = settle([out_scatter], grad_heads, d_qkv)
+    out_scatter.start()
+    grad_heads = all_to_all(grad_heads.reshape(2 * count, own, 4 * HEAD_SIZE), head_axes)
     kept, away = heads_input(at, d_qkv, qkv_ring.parts)
+    kept, away = settle([scatter, out_scatter], kept, away)
+    out_scatter.start()
+    own_both = own_columns(scatter.total[:group].astype(bf16).reshape(2, 2, own, -1))
     d_normed1 = own_rows_sum(core_sum(kept, away))
-    ff_ring.settle()
-    ff_ring.start()
-    ff_ring.settle()
-    owned_both, owned_down = ff_ring.sums()
-    own_both = own_columns(owned_both.astype(bf16).reshape(2, 2, own, -1))
-    kept, away = layer_output(at, hidden, down_weight, count)
     d_middle_own, middle_own = (
         lax.dynamic_index_in_dim(value, seq, 0, False) for value in (d_middle, middle)
     )
@@ -1298,11 +1412,11 @@
     input_grad = d_middle_own + r1 * (
         d_normed1 - n1_wide * jnp.mean(d_normed1 * n1_wide, axis=-1, keepdims=True)
     )
-    result = middle_own + own_rows_sum(core_sum(kept, away))
-    grad_heads, own_both = tie(grad_heads, own_both)
-    owned_out = jnp.sum(owned_out.astype(f32), axis=0)
-    grad_gate, grad_up, grad_gain2 = pair_rows_grads(
-        at, own_both, gain2, w_gate, w_up, ff_own, count
+    result = middle_own + out_rows
+    grad_heads, own_both = settle([out_scatter], grad_heads, own_both)
+    owned_out = out_scatter.total
+    grad_gate, grad_up, grad_gain2, owned_down = pair_rows_grads(
+        at, own_both, scatter.total[group:], gain2, w_gate, w_up, ff_own, count
     )
     grad_query, grad_key, grad_value, grad_gain1 = query_rows_grads(
         at, grad_heads, gain1, w_query, key_weight, value_weight
@@ -1324,11 +1438,10 @@
 
 def by_heads(mesh):
     count = mesh.shape["ctx"] // 2
-    parts = Mesh(mesh.devices.reshape(count, 2, 2), ("d", "core", "y"))
-    owner = ("d", "core", "y")
-    row_spec = P("y", ("d", "core"), None)
-    in_specs = (row_spec, row_spec) + (P(owner),) * 9
-    out_specs = (row_spec, row_spec) + (P(owner),) * 9
+    parts = Mesh(mesh.devices.reshape(count // 2, 2, 2, 2), owner_axes)
+    row_spec = P("y", ("z", "x", "core"), None)
+    in_specs = (row_spec, row_spec) + (P(owner_axes),) * 9
+    out_specs = (row_spec, row_spec) + (P(owner_axes),) * 9
     return jax.shard_map(
         functools.partial(head_layer, count),
         mesh=parts,

time: 502 us -> 441 us (0.88)
  waiting for transfers between devices: 184 us -> 144 us
  starting transfers between devices: 122 us -> 84.2 us
  blocking collectives: 0 us -> 35.3 us
  Pallas kernels: 83.3 us -> 77.3 us
  other arithmetic: 49.6 us -> 43.7 us
    ppermute x68 -> x40, waiting for transfers between devices: 172 us -> 100 us  [the longest x12 52.9 us: start(): lax.ppermute(ahead, ring_axes, self.forward)]
    all_to_all x0 -> x1, blocking collectives: none -> 35.3 us  [all_to_all(): return lax.all_to_all(values, axes, 0, 0, tiled=True)]
    ppermute x68 -> x40, starting transfers between devices: 69.7 us -> 43.6 us  [the longest x12 17.4 us: start(): lax.ppermute(behind, ring_axes, self.backward)]
    ppermute x25 -> x18, waiting for transfers between devices: 10.8 us -> 35 us  [swap(): return lax.ppermute(values, axis, [(0, 1), (1, 0)])]
    all_to_all x8 -> x6, starting transfers between devices: 40.1 us -> 32.2 us  [all_to_all(): return lax.all_to_all(values, axes, 0, 0, tiled=True)]
    all_to_all x8 -> x6, waiting for transfers between devices: 0.98 us -> 8.39 us  [all_to_all(): return lax.all_to_all(values, axes, 0, 0, tiled=True)]
    convert_element_type x13 -> x6, other arithmetic: 21.4 us -> 14.4 us  [land(): (self.term[self.count - left].astype(f32) + behind).astype(bf16)]
    pallas_call x17 -> x19, Pallas kernels: 83.3 us -> 77.3 us  [on_chip(): pl.pallas_call(kernel, out_shape=tuple(out_shape), in_specs=[pl.BlockSpec...]
  transfers between devices with their start and end apart: 101 -> 64, of which waited for: 38 -> 28; matrix products, arithmetic and copies ran while one was open for 10% -> 11% of each run, Pallas kernels for 12% -> 17%
where the time goes in v4:
time: 441 us; the launch traced here: 436 us
  waiting for transfers between devices  144 us (33%)
  starting transfers between devices  84.2 us (19%)
  Pallas kernels  77.3 us (18%)
  local copies, waits for them, and re-layouts  49.8 us (11%)
  other arithmetic  43.7 us (10%)
  blocking collectives  35.3 us (8%)
    pallas_call x19, Pallas kernels, on_chip(): pl.pallas_call(kernel, out_shape=tuple(out_shape), in_specs=[pl.BlockSpec...  77.3 us
    ppermute x12, waiting for transfers between devices, start(): lax.ppermute(ahead, ring_axes, self.forward)  52.9 us
    unnamed x200, local copies, waits for them, and re-layouts  38.4 us
    ppermute x8, waiting for transfers between devices, start(): lax.ppermute(self.ahead, ring_axes, self.forward)  37.9 us
    all_to_all x1, blocking collectives, all_to_all(): return lax.all_to_all(values, axes, 0, 0, tiled=True)  35.3 us
    ppermute x18, waiting for transfers between devices, swap(): return lax.ppermute(values, axis, [(0, 1), (1, 0)])  35 us
    all_to_all x6, starting transfers between devices, all_to_all(): return lax.all_to_all(values, axes, 0, 0, tiled=True)  32.2 us
    ppermute x12, starting transfers between devices, start(): lax.ppermute(behind, ring_axes, self.backward)  17.4 us
  transfers between devices with their start and end apart: 64, of which 28 were waited for; matrix products, arithmetic and copies ran while one was open for 11% of the time, Pallas kernels for 17%

profile of v4, /device:TPU:10, one launch (start us, length us, event | category | flops | bytes accessed | tf_op | source)
XLA Modules:
  0.0 436.1 jit_solution(5036314232649063807)
XLA Ops:
  9.6 6.4 %all-to-all-start = ((bf16[16,48,384]{2,1,0:T(8,128)(2,1)}), bf16[16,48,384]{2,1,0:T(8,128)(2,1)}, u32[]{:S(2)}, u32[]{:S(2)}) async-start(bf16[16,48,384]{2,1,0:T(8,128)(2,1)} %head_columns.1), calls=%async_computation | async-start | bytes 1179648 | tf_op jit(solution)/shard_map/all_to_all | solution.py:1254
  17.8 3.8 collective-permute-done.1.refs_7_
  27.7 7.6 %all-to-all-done = bf16[16,48,384]{2,1,0:T(8,128)(2,1)} async-done(((bf16[16,48,384]{2,1,0:T(8,128)(2,1)}), bf16[16,48,384]{2,1,0:T(8,128)(2,1)}, u32[]{:S(2)}, u32[]{:S(2)}) %all-to-all-start) | async-done | bytes 589856 | tf_op jit(solution)/shard_map/all_to_all | solution.py:1254
  35.3 9.2 %collective-permute-done.3.refs_6_ = bf16[352,768]{1,0:T(8,128)(2,1)S(1)} collective-permute-done((bf16[352,768]{1,0:T(8,128)(2,1)S(1)}, bf16[352,768]{1,0:T(8,128)(2,1)S(1)}, u32[]{:S(2)}, u32[]{:S(2)}) %collective-permute-start.3) | collective-permute-done | bytes 540704 | tf_op jit(solution)/shard_map/ppermute | solution.py:1159
  47.3 4.2 all-to-all-start.1
  51.5 7.2 %collective-permute-done.6.refs_5_ = bf16[352,768]{1,0:T(8,128)(2,1)S(1)} collective-permute-done((bf16[352,768]{1,0:T(8,128)(2,1)S(1)}, bf16[352,768]{1,0:T(8,128)(2,1)S(1)}, u32[]{:S(2)}, u32[]{:S(2)}) %collective-permute-start.6) | collective-permute-done | bytes 540704 | tf_op jit(solution)/shard_map/ppermute | solution.py:1159
  73.7 6.8 %project_heads.1 = (f32[288,2048]{1,0:T(8,128)S(1)}, bf16[288,2048]{1,0:T(8,128)(2,1)S(1)}) custom-call(s32[18]{0:T(128)S(1)} %pad_add_fusion.at_ref, bf16[768,384]{1,0:T(8,128)(2,1)} %bitcast.5.weight_ref, bf16[352,768]{1,0:T(8,128)(2,1)S(1)} %pad_maximum_fusion.3.refs_0_, bf16[352,768]{1,0:T(8,128)(2,1)} %collective-permute-done.2.refs_1_, ...), custom_call_target="tpu_custom_call" | custom-call | flops 1207959552 | bytes 8454216 | tf_op jit(solution)/shard_map/project_heads/pallas_call | solution.py:491
  83.5 8.0 %heads_forward.1 = (bf16[16,48,256]{2,1,0:T(8,128)(2,1)S(1)}, f32[96,2048]{1,0:T(8,128)S(1)}, bf16[9216,256]{1,0:T(8,128)(2,1)S(1)}, bf16[96,2048]{1,0:T(8,128)(...) custom-call(s32[18]{0:T(128)S(1)} %pad_add_fusion.at_ref, ...), custom_call_target="tpu_custom_call" | custom-call | flops 905969664 | bytes 11403336 | tf_op jit(solution)/shard_map/heads_forward/pallas_call | solution.py:491
  99.4 35.3 %all_to_all.35.heads_ref = bf16[16,48,256]{2,1,0:T(8,128)(2,1)S(1)} all-to-all(bf16[16,48,256]{2,1,0:T(8,128)(2,1)S(1)} %get-tuple-element.146), channel_id=1, replica_groups=mesh['z'=4,'x'=2,'core'=2,'y'=2] {'z','x','y'}, dimensions={0} | all-to-all | bytes 786432 | tf_op jit(solution)/shard_map/all_to_all | solution.py:1254
  146.3 4.1 all-to-all-start.3
  150.4 12.3 %collective-permute-done.20 = bf16[2,128,1536]{2,1,0:T(8,128)(2,1)} collective-permute-done((bf16[2,128,1536]{2,1,0:T(8,128)(2,1)}, bf16[2,128,1536]{2,1,0:T(8,128)(2,1)}, u32[]{:S(2)}, u32[]{:S(2)}) %collective-permute-start.20) | collective-permute-done | bytes 786464 | tf_op jit(solution)/shard_map/ppermute | solution.py:1214
  166.0 4.5 %collective-permute-done.17.refs_5_ = bf16[288,2048]{1,0:T(8,128)(2,1)} collective-permute-done((bf16[288,2048]{1,0:T(8,128)(2,1)}, bf16[288,2048]{1,0:T(8,128)(2,1)}, u32[]{:S(2)}, u32[]{:S(2)}) %collective-permute-start.17) | collective-permute-done | bytes 1179680 | tf_op jit(solution)/shard_map/ppermute | solution.py:1159
  178.5 12.1 %collective-permute-done.21 = bf16[144,2048]{1,0:T(8,128)(2,1)S(1)} collective-permute-done((bf16[144,2048]{1,0:T(8,128)(2,1)S(1)}, bf16[144,2048]{1,0:T(8,128)(2,1)S(1)}, u32[]{:S(2)}, u32[]{:S(2)}) %collective-permute-start.21) | collective-permute-done | bytes 589856 | tf_op jit(solution)/shard_map/ppermute | solution.py:1159
  194.1 14.5 %feed_forward.1 = (bf16[512,1536]{1,0:T(8,128)(2,1)}, bf16[512,1536]{1,0:T(8,128)(2,1)}, bf16[512,1024]{1,0:T(8,128)(2,1)S(1)}, bf16[512,2048]{1,0:T(8,128)(2,1)...) custom-call(s32[18]{0:T(128)S(1)} %pad_add_fusion.at_ref, ...), custom_call_target="tpu_custom_call" | custom-call | flops 8053063680 | bytes 21233736 | tf_op jit(solution)/shard_map/feed_forward/pallas_call | solution.py:491
  215.7 5.7 %feed_forward_grads.1 = bf16[8,288,2048]{2,1,0:T(8,128)(2,1)S(1)} custom-call(s32[18]{0:T(128)S(1)} %pad_add_fusion.at_ref, bf16[512,1536]{1,0:T(8,128)(2,1)S(1)} %copy-done.82, bf16[512,2048]{1,0:T(8,128)(2,1)S(1)} %copy-done.81, bf16[512,1024]{1,0:T(8,128)(2,1)S(1)} %get-tuple-element.186.hidden_ref, bf16[512,1536]{1,0:T(8,128)(2,1)S(1)} %copy-done.83), custom_call_target="tpu_custom_call" | custom-call | flops 4831838208 | bytes 15728712 | tf_op jit(solution)/shard_map/feed_forward_grads/pallas_call | solution.py:491
  223.7 8.7 %collective-permute-done.31 = bf16[2,128,1536]{2,1,0:T(8,128)(2,1)S(1)} collective-permute-done((bf16[2,128,1536]{2,1,0:T(8,128)(2,1)S(1)}, bf16[2,128,1536]{2,1,0:T(8,128)(2,1)S(1)}, u32[]{:S(2)}, u32[]{:S(2)}) %collective-permute-start.31) | collective-permute-done | bytes 786464 | tf_op jit(solution)/shard_map/ppermute | solution.py:1214
  232.6 4.2 collective-permute-done.29
  247.0 6.2 %all-to-all-start.4 = ((bf16[16,48,256]{2,1,0:T(8,128)(2,1)}), bf16[16,48,256]{2,1,0:T(8,128)(2,1)}, u32[]{:S(2)}, u32[]{:S(2)}) async-start(bf16[16,48,256]{2,1,0:T(8,128)(2,1)} %copy-done.67), calls=%async_computation.4 | async-start | bytes 786432 | tf_op jit(solution)/shard_map/all_to_all | solution.py:1254
  261.5 4.6 %layer_output.1 = (f32[2,128,1536]{2,1,0:T(8,128)S(1)}, bf16[2,128,1536]{2,1,0:T(8,128)(2,1)S(1)}) custom-call(s32[18]{0:T(128)S(1)} %pad_add_fusion.at_ref, bf16[512,1024]{1,0:T(8,128)(2,1)S(1)} %copy-done.50, bf16[288,2048]{1,0:T(8,128)(2,1)S(1)} %copy-done.15, bf16[288,2048]{1,0:T(8,128)(2,1)S(1)} %copy-done.48, ...), custom_call_target="tpu_custom_call" | custom-call | bytes 12845128 | tf_op jit(solution)/shard_map/layer_output/pallas_call | solution.py:491
  271.1 13.9 %collective-permute-done.34.refs_5_ = bf16[192,768]{1,0:T(8,128)(2,1)} collective-permute-done((bf16[192,768]{1,0:T(8,128)(2,1)}, bf16[192,768]{1,0:T(8,128)(2,1)}, u32[]{:S(2)}, u32[]{:S(2)}) %collective-permute-start.34) | collective-permute-done | bytes 294944 | tf_op jit(solution)/shard_map/ppermute | solution.py:1159
  299.4 8.0 %heads_backward.1 = (f32[288,2048]{1,0:T(8,128)S(1)}, bf16[288,2048]{1,0:T(8,128)(2,1)}) custom-call(s32[18]{0:T(128)S(1)} %pad_add_fusion.at_ref, bf16[96,2048]{1,0:T(8,128)(2,1)S(1)} %copy-done.61, bf16[96,2048]{1,0:T(8,128)(2,1)S(1)} %copy-done.63, bf16[96,2048]{1,0:T(8,128)(2,1)S(1)} %copy-done.65, bf16[9216,256]{1,0:T(8,128)(2,1)S(1)} %copy-done.11, ...), custom_call_target="tpu_custom_call" | custom-call | flops 1811939328 | bytes 11403336 | tf_op jit(solution)/shard_map/heads_backward/pallas_call | solution.py:491
  309.8 12.4 %collective-permute-done.39 = bf16[24,1536]{1,0:T(8,128)(2,1)S(1)} collective-permute-done((bf16[24,1536]{1,0:T(8,128)(2,1)S(1)}, bf16[24,1536]{1,0:T(8,128)(2,1)S(1)}, u32[]{:S(2)}, u32[]{:S(2)}) %collective-permute-start.39) | collective-permute-done | bytes 73760 | tf_op jit(solution)/shard_map/ppermute | solution.py:1185
  324.9 4.3 collective-permute-done.40
  338.6 5.9 %all-to-all-start.5 = ((bf16[16,96,256]{2,1,0:T(8,128)(2,1)}), bf16[16,96,256]{2,1,0:T(8,128)(2,1)}, u32[]{:S(2)}, u32[]{:S(2)}) async-start(bf16[16,96,256]{2,1,0:T(8,128)(2,1)} %copy-done.51), calls=%async_computation.5 | async-start | bytes 1572864 | tf_op jit(solution)/shard_map/all_to_all | solution.py:1254
  347.8 4.8 %fusion.1 = (bf16[288,2048]{1,0:T(8,128)(2,1)}, bf16[288,2048]{1,0:T(8,128)(2,1)}) fusion(bf16[288,2048]{1,0:T(8,128)(2,1)} %collective-permute-done.38, bf16[8,288,2048]{2,1,0:T(8,128)(2,1)} %copy-done.2, bf16[288,2048]{1,0:T(8,128)(2,1)} %collective-permute-done.37), kind=kLoop, calls=%fused_computation.3 | loop fusion | flops 4718592 | bytes 7077888 | tf_op jit(solution)/shard_map/convert_element_type | solution.py:1202
  354.6 7.3 %heads_grad.1 = bf16[768,384]{1,0:T(8,128)(2,1)} custom-call(s32[18]{0:T(128)S(1)} %pad_add_fusion.at_ref, bf16[384,2048]{1,0:T(8,128)(2,1)S(1)} %copy-done.30, bf16[352,768]{1,0:T(8,128)(2,1)S(1)} %pad_maximum_fusion.3.refs_0_, bf16[352,768]{1,0:T(8,128)(2,1)} %collective-permute-done.2.refs_1_, bf16[352,768]{1,0:T(8,128)(2,1)S(1)} %copy-done.9, ...), custom_call_target="tpu_custom_call" | custom-call | flops 1207959552 | bytes 6488136 | tf_op jit(solution)/shard_map/heads_grad/pallas_call | solution.py:491
  362.0 5.8 %collective-permute-done.47 = bf16[48,1536]{1,0:T(8,128)(2,1)S(1)} collective-permute-done((bf16[48,1536]{1,0:T(8,128)(2,1)S(1)}, bf16[48,1536]{1,0:T(8,128)(2,1)S(1)}, u32[]{:S(2)}, u32[]{:S(2)}) %collective-permute-start.47) | collective-permute-done | bytes 147488 | tf_op jit(solution)/shard_map/ppermute | solution.py:1185
  373.8 5.4 %all-to-all-start.6 = ((bf16[16,48,384]{2,1,0:T(8,128)(2,1)}), bf16[16,48,384]{2,1,0:T(8,128)(2,1)}, u32[]{:S(2)}, u32[]{:S(2)}) async-start(bf16[16,48,384]{2,1,0:T(8,128)(2,1)} %bitcast.37), calls=%async_computation.6 | async-start | bytes 1179648 | tf_op jit(solution)/shard_map/all_to_all | solution.py:1254
  383.1 4.0 heads_input.1
  387.1 8.4 %collective-permute-done.45 = bf16[288,2048]{1,0:T(8,128)(2,1)} collective-permute-done((bf16[288,2048]{1,0:T(8,128)(2,1)}, bf16[288,2048]{1,0:T(8,128)(2,1)}, u32[]{:S(2)}, u32[]{:S(2)}) %collective-permute-start.45) | collective-permute-done | bytes 1179680 | tf_op jit(solution)/shard_map/ppermute | solution.py:1185
  395.6 7.0 %collective-permute-done.50 = bf16[48,1536]{1,0:T(8,128)(2,1)} collective-permute-done((bf16[48,1536]{1,0:T(8,128)(2,1)}, bf16[48,1536]{1,0:T(8,128)(2,1)}, u32[]{:S(2)}, u32[]{:S(2)}) %collective-permute-start.50) | collective-permute-done | bytes 147488 | tf_op jit(solution)/shard_map/ppermute | solution.py:1185
  411.1 6.8 %collective-permute-done.56 = bf16[2,48,2048]{2,1,0:T(8,128)(2,1)S(1)} collective-permute-done((bf16[2,48,2048]{2,1,0:T(8,128)(2,1)S(1)}, bf16[2,48,2048]{2,1,0:T(8,128)(2,1)S(1)}, u32[]{:S(2)}, u32[]{:S(2)}) %collective-permute-start.56) | collective-permute-done | bytes 393248 | tf_op jit(solution)/shard_map/ppermute | solution.py:1214
  (377 shorter events, 174.8 us)
Async XLA Ops:
  9.6 25.7 %all-to-all-start = ((bf16[16,48,384]{2,1,0:T(8,128)(2,1)}), bf16[16,48,384]{2,1,0:T(8,128)(2,1)}, u32[]{:S(2)}, u32[]{:S(2)}) async-start(bf16[16,48,384]{2,1,0:T(8,128)(2,1)} %head_columns.1), calls=%async_computation | async-start | bytes 1179648 | tf_op jit(solution)/shard_map/all_to_all | solution.py:1254
  21.6 22.8 %collective-permute-start.3 = (bf16[352,768]{1,0:T(8,128)(2,1)S(1)}, bf16[352,768]{1,0:T(8,128)(2,1)S(1)}, u32[]{:S(2)}, u32[]{:S(2)}) collective-permute-start(bf16[352,768]{1,0:T(8,128)(2,1)S(1)} %collective-permute-done.1.refs_7_), channel_id=1, source_target_pairs={{0,8},{8,16},{16,24},{24,28},{28,20},{20,12},{12,4},{4,0},{1,9},{9... | collective-permute-start | bytes 1622024 | tf_op jit(solution)/shard_map/ppermute | solution.py:1159
  22.0 22.5 %collective-permute-start.4 = (bf16[352,768]{1,0:T(8,128)(2,1)}, bf16[352,768]{1,0:T(8,128)(2,1)S(1)}, u32[]{:S(2)}, u32[]{:S(2)}) collective-permute-start(bf16[352,768]{1,0:T(8,128)(2,1)} %collective-permute-done.2.refs_1_), channel_id=1, source_target_pairs={{8,0},{16,8},{24,16},{28,24},{20,28},{12,20},{4,12},{0,4},{9,1},{1... | collective-permute-start | bytes 1622024 | tf_op jit(solution)/shard_map/ppermute | solution.py:1160
  68.6 26.0 %collective-permute-start.10 = (bf16[288,2048]{1,0:T(8,128)(2,1)S(1)}, bf16[288,2048]{1,0:T(8,128)(2,1)S(1)}, u32[]{:S(2)}, u32[]{:S(2)}) collective-permute-start(bf16[288,2048]{1,0:T(8,128)(2,1)S(1)} %pack_down.1.refs_0_), channel_id=1, source_target_pairs={{0,8},{8,16},{16,24},{24,28},{28,20},{20,12},{12,4},{4,0},{1,9},{9... | collective-permute-start | bytes 3538952 | tf_op jit(solution)/shard_map/ppermute | solution.py:1159
  70.3 24.9 %collective-permute-start.11 = (bf16[288,2048]{1,0:T(8,128)(2,1)S(1)}, bf16[288,2048]{1,0:T(8,128)(2,1)S(1)}, u32[]{:S(2)}, u32[]{:S(2)}) collective-permute-start(bf16[288,2048]{1,0:T(8,128)(2,1)S(1)} %pack_down.1.refs_0_), channel_id=1, source_target_pairs={{8,0},{16,8},{24,16},{28,24},{20,28},{12,20},{4,12},{0,4},{9,1},{1... | collective-permute-start | bytes 3538952 | tf_op jit(solution)/shard_map/ppermute | solution.py:1160
  95.2 39.5 %collective-permute-start.14 = (bf16[288,2048]{1,0:T(8,128)(2,1)S(1)}, bf16[288,2048]{1,0:T(8,128)(2,1)}, u32[]{:S(2)}, u32[]{:S(2)}) collective-permute-start(bf16[288,2048]{1,0:T(8,128)(2,1)S(1)} %collective-permute-done.10.refs_7_), channel_id=1, source_target_pairs={{0,8},{8,16},{16,24},{24,28},{28,20},{20,12},{12,4},{4,0},{1,9},{9... | collective-permute-start | bytes 3538952 | tf_op jit(solution)/shard_map/ppermute | solution.py:1159
  97.5 37.2 %collective-permute-start.15 = (bf16[288,2048]{1,0:T(8,128)(2,1)S(1)}, bf16[288,2048]{1,0:T(8,128)(2,1)}, u32[]{:S(2)}, u32[]{:S(2)}) collective-permute-start(bf16[288,2048]{1,0:T(8,128)(2,1)S(1)} %collective-permute-done.11.refs_1_), channel_id=1, source_target_pairs={{8,0},{16,8},{24,16},{28,24},{20,28},{12,20},{4,12},{0,4},{9,1},{1... | collective-permute-start | bytes 3538952 | tf_op jit(solution)/shard_map/ppermute | solution.py:1160
  99.4 35.3 %collective-permute-start.16 = (bf16[2,128,1536]{2,1,0:T(8,128)(2,1)S(1)}, bf16[2,128,1536]{2,1,0:T(8,128)(2,1)S(1)}, u32[]{:S(2)}, u32[]{:S(2)}) collective-permute-start(bf16[2,128,1536]{2,1,0:T(8,128)(2,1)S(1)} %pad_maximum_fusion.1.d_own_ref), channel_id=1, source_target_pairs={{0,2},{2,0},{1,3},{3,1},{4,6},{6,4},{5,7},{7,5},{8,10},{10,8},{9,1... | collective-permute-start | bytes 2359304 | tf_op jit(solution)/shard_map/ppermute | solution.py:1214
  142.0 20.7 %collective-permute-start.20 = (bf16[2,128,1536]{2,1,0:T(8,128)(2,1)}, bf16[2,128,1536]{2,1,0:T(8,128)(2,1)}, u32[]{:S(2)}, u32[]{:S(2)}) collective-permute-start(bf16[2,128,1536]{2,1,0:T(8,128)(2,1)} %fusion.7), channel_id=1, source_target_pairs={{0,1},{1,0},{2,3},{3,2},{4,5},{5,4},{6,7},{7,6},{8,9},{9,8},{10,11... | collective-permute-start | bytes 2359304 | tf_op jit(solution)/shard_map/ppermute | solution.py:1214
  142.5 28.0 %collective-permute-start.17 = (bf16[288,2048]{1,0:T(8,128)(2,1)}, bf16[288,2048]{1,0:T(8,128)(2,1)}, u32[]{:S(2)}, u32[]{:S(2)}) collective-permute-start(bf16[288,2048]{1,0:T(8,128)(2,1)} %collective-permute-done.14.refs_6_), channel_id=1, source_target_pairs={{0,8},{8,16},{16,24},{24,28},{28,20},{20,12},{12,4},{4,0},{1,9},{9... | collective-permute-start | bytes 3538952 | tf_op jit(solution)/shard_map/ppermute | solution.py:1159
  143.5 27.9 %collective-permute-start.18 = (bf16[288,2048]{1,0:T(8,128)(2,1)}, bf16[288,2048]{1,0:T(8,128)(2,1)}, u32[]{:S(2)}, u32[]{:S(2)}) collective-permute-start(bf16[288,2048]{1,0:T(8,128)(2,1)} %collective-permute-done.15.refs_2_), channel_id=1, source_target_pairs={{8,0},{16,8},{24,16},{28,24},{20,28},{12,20},{4,12},{0,4},{9,1},{1... | collective-permute-start | bytes 3538952 | tf_op jit(solution)/shard_map/ppermute | solution.py:1160
  146.3 19.7 %all-to-all-start.3 = ((bf16[4,48,768]{2,1,0:T(8,128)(2,1)}), bf16[4,48,768]{2,1,0:T(8,128)(2,1)}, u32[]{:S(2)}, u32[]{:S(2)}) async-start(bf16[4,48,768]{2,1,0:T(8,128)(2,1)} %copy-done.42), calls=%async_computation.3 | async-start | bytes 589824 | tf_op jit(solution)/shard_map/all_to_all | solution.py:1254
  173.4 18.4 %collective-permute-start.23 = (bf16[2,128,1536]{2,1,0:T(8,128)(2,1)S(1)}, bf16[2,128,1536]{2,1,0:T(8,128)(2,1)S(1)}, u32[]{:S(2)}, u32[]{:S(2)}) collective-permute-start(bf16[2,128,1536]{2,1,0:T(8,128)(2,1)S(1)} %multiply_convert_fusion.own_ref), channel_id=1, source_target_pairs={{0,2},{2,0},{1,3},{3,1},{4,6},{6,4},{5,7},{7,5},{8,10},{10,8},{9,1... | collective-permute-start | bytes 2359304 | tf_op jit(solution)/shard_map/ppermute | solution.py:1214
  212.7 19.6 %collective-permute-start.31 = (bf16[2,128,1536]{2,1,0:T(8,128)(2,1)S(1)}, bf16[2,128,1536]{2,1,0:T(8,128)(2,1)S(1)}, u32[]{:S(2)}, u32[]{:S(2)}) collective-permute-start(bf16[2,128,1536]{2,1,0:T(8,128)(2,1)S(1)} %get-tuple-element.241), channel_id=1, source_target_pairs={{0,1},{1,0},{2,3},{3,2},{4,5},{5,4},{6,7},{7,6},{8,9},{9,8},{10,11... | collective-permute-start | bytes 2359304 | tf_op jit(solution)/shard_map/ppermute | solution.py:1214
  241.6 43.4 %collective-permute-start.32 = (bf16[288,2048]{1,0:T(8,128)(2,1)}, bf16[288,2048]{1,0:T(8,128)(2,1)}, u32[]{:S(2)}, u32[]{:S(2)}) collective-permute-start(bf16[288,2048]{1,0:T(8,128)(2,1)} %get-tuple-element.250), channel_id=1, source_target_pairs={{0,8},{8,16},{16,24},{24,28},{28,20},{20,12},{12,4},{4,0},{1,9},{9... | collective-permute-start | bytes 3538952 | tf_op jit(solution)/shard_map/ppermute | solution.py:1185
  242.7 42.4 %collective-permute-start.33 = (bf16[288,2048]{1,0:T(8,128)(2,1)}, bf16[288,2048]{1,0:T(8,128)(2,1)}, u32[]{:S(2)}, u32[]{:S(2)}) collective-permute-start(bf16[288,2048]{1,0:T(8,128)(2,1)} %get-tuple-element.249), channel_id=1, source_target_pairs={{8,0},{16,8},{24,16},{28,24},{20,28},{12,20},{4,12},{0,4},{9,1},{1... | collective-permute-start | bytes 3538952 | tf_op jit(solution)/shard_map/ppermute | solution.py:1186
  247.0 38.0 %all-to-all-start.4 = ((bf16[16,48,256]{2,1,0:T(8,128)(2,1)}), bf16[16,48,256]{2,1,0:T(8,128)(2,1)}, u32[]{:S(2)}, u32[]{:S(2)}) async-start(bf16[16,48,256]{2,1,0:T(8,128)(2,1)} %copy-done.67), calls=%async_computation.4 | async-start | bytes 786432 | tf_op jit(solution)/shard_map/all_to_all | solution.py:1254
  253.2 31.8 %collective-permute-start.34 = (bf16[192,768]{1,0:T(8,128)(2,1)}, bf16[192,768]{1,0:T(8,128)(2,1)}, u32[]{:S(2)}, u32[]{:S(2)}) collective-permute-start(bf16[192,768]{1,0:T(8,128)(2,1)} %copy-done.74), channel_id=1, source_target_pairs={{0,8},{8,16},{16,24},{24,28},{28,20},{20,12},{12,4},{4,0},{1,9},{9... | collective-permute-start | bytes 884744 | tf_op jit(solution)/shard_map/ppermute | solution.py:1159
  253.7 31.3 %collective-permute-start.35 = (bf16[192,768]{1,0:T(8,128)(2,1)}, bf16[192,768]{1,0:T(8,128)(2,1)}, u32[]{:S(2)}, u32[]{:S(2)}) collective-permute-start(bf16[192,768]{1,0:T(8,128)(2,1)} %copy-done.76), channel_id=1, source_target_pairs={{8,0},{16,8},{24,16},{28,24},{20,28},{12,20},{4,12},{0,4},{9,1},{1... | collective-permute-start | bytes 884744 | tf_op jit(solution)/shard_map/ppermute | solution.py:1160
  288.6 40.6 %collective-permute-start.37 = (bf16[288,2048]{1,0:T(8,128)(2,1)S(1)}, bf16[288,2048]{1,0:T(8,128)(2,1)}, u32[]{:S(2)}, u32[]{:S(2)}) collective-permute-start(bf16[288,2048]{1,0:T(8,128)(2,1)S(1)} %get-tuple-element.248), channel_id=1, source_target_pairs={{0,8},{8,16},{16,24},{24,28},{28,20},{20,12},{12,4},{4,0},{1,9},{9... | collective-permute-start | bytes 3538952 | tf_op jit(solution)/shard_map/ppermute | solution.py:1185
  289.1 40.1 %collective-permute-start.38 = (bf16[288,2048]{1,0:T(8,128)(2,1)S(1)}, bf16[288,2048]{1,0:T(8,128)(2,1)}, u32[]{:S(2)}, u32[]{:S(2)}) collective-permute-start(bf16[288,2048]{1,0:T(8,128)(2,1)S(1)} %get-tuple-element.247), channel_id=1, source_target_pairs={{8,0},{16,8},{24,16},{28,24},{20,28},{12,20},{4,12},{0,4},{9,1},{1... | collective-permute-start | bytes 3538952 | tf_op jit(solution)/shard_map/ppermute | solution.py:1186
  292.1 37.1 %collective-permute-start.41 = (bf16[96,768]{1,0:T(8,128)(2,1)S(1)}, bf16[96,768]{1,0:T(8,128)(2,1)S(1)}, u32[]{:S(2)}, u32[]{:S(2)}) collective-permute-start(bf16[96,768]{1,0:T(8,128)(2,1)S(1)} %slice.121), channel_id=1, source_target_pairs={{0,8},{8,16},{16,24},{24,28},{28,20},{20,12},{12,4},{4,0},{1,9},{9... | collective-permute-start | bytes 442376 | tf_op jit(solution)/shard_map/ppermute | solution.py:1159
  293.7 30.2 %collective-permute-start.44 = (bf16[128,1536]{1,0:T(8,128)(2,1)S(1)}, bf16[128,1536]{1,0:T(8,128)(2,1)S(1)}, u32[]{:S(2)}, u32[]{:S(2)}) collective-permute-start(bf16[128,1536]{1,0:T(8,128)(2,1)S(1)} %fusion.17), channel_id=1, source_target_pairs={{0,1},{1,0},{2,3},{3,2},{4,5},{5,4},{6,7},{7,6},{8,9},{9,8},{10,11... | collective-permute-start | bytes 1179656 | tf_op jit(solution)/shard_map/ppermute | solution.py:1214
  295.4 26.8 %collective-permute-start.39 = (bf16[24,1536]{1,0:T(8,128)(2,1)S(1)}, bf16[24,1536]{1,0:T(8,128)(2,1)S(1)}, u32[]{:S(2)}, u32[]{:S(2)}) collective-permute-start(bf16[24,1536]{1,0:T(8,128)(2,1)S(1)} %get-tuple-element.260), channel_id=1, source_target_pairs={{0,8},{8,16},{16,24},{24,28},{28,20},{20,12},{12,4},{4,0},{1,9},{9... | collective-permute-start | bytes 221192 | tf_op jit(solution)/shard_map/ppermute | solution.py:1185
  338.6 29.1 %all-to-all-start.5 = ((bf16[16,96,256]{2,1,0:T(8,128)(2,1)}), bf16[16,96,256]{2,1,0:T(8,128)(2,1)}, u32[]{:S(2)}, u32[]{:S(2)}) async-start(bf16[16,96,256]{2,1,0:T(8,128)(2,1)} %copy-done.51), calls=%async_computation.5 | async-start | bytes 1572864 | tf_op jit(solution)/shard_map/all_to_all | solution.py:1254
  345.7 22.1 %collective-permute-start.47 = (bf16[48,1536]{1,0:T(8,128)(2,1)S(1)}, bf16[48,1536]{1,0:T(8,128)(2,1)S(1)}, u32[]{:S(2)}, u32[]{:S(2)}) collective-permute-start(bf16[48,1536]{1,0:T(8,128)(2,1)S(1)} %get-tuple-element.258), channel_id=1, source_target_pairs={{0,8},{8,16},{16,24},{24,28},{28,20},{20,12},{12,4},{4,0},{1,9},{9... | collective-permute-start | bytes 442376 | tf_op jit(solution)/shard_map/ppermute | solution.py:1185
  346.3 21.5 %collective-permute-start.48 = (bf16[48,1536]{1,0:T(8,128)(2,1)S(1)}, bf16[48,1536]{1,0:T(8,128)(2,1)S(1)}, u32[]{:S(2)}, u32[]{:S(2)}) collective-permute-start(bf16[48,1536]{1,0:T(8,128)(2,1)S(1)} %get-tuple-element.257), channel_id=1, source_target_pairs={{8,0},{16,8},{24,16},{28,24},{20,28},{12,20},{4,12},{0,4},{9,1},{1... | collective-permute-start | bytes 442376 | tf_op jit(solution)/shard_map/ppermute | solution.py:1186
  352.6 43.0 %collective-permute-start.45 = (bf16[288,2048]{1,0:T(8,128)(2,1)}, bf16[288,2048]{1,0:T(8,128)(2,1)}, u32[]{:S(2)}, u32[]{:S(2)}) collective-permute-start(bf16[288,2048]{1,0:T(8,128)(2,1)} %get-tuple-element.246), channel_id=1, source_target_pairs={{0,8},{8,16},{16,24},{24,28},{28,20},{20,12},{12,4},{4,0},{1,9},{9... | collective-permute-start | bytes 3538952 | tf_op jit(solution)/shard_map/ppermute | solution.py:1185
  353.1 42.5 %collective-permute-start.46 = (bf16[288,2048]{1,0:T(8,128)(2,1)}, bf16[288,2048]{1,0:T(8,128)(2,1)}, u32[]{:S(2)}, u32[]{:S(2)}) collective-permute-start(bf16[288,2048]{1,0:T(8,128)(2,1)} %get-tuple-element.245), channel_id=1, source_target_pairs={{8,0},{16,8},{24,16},{28,24},{20,28},{12,20},{4,12},{0,4},{9,1},{1... | collective-permute-start | bytes 3538952 | tf_op jit(solution)/shard_map/ppermute | solution.py:1186
  369.5 33.1 %collective-permute-start.50 = (bf16[48,1536]{1,0:T(8,128)(2,1)}, bf16[48,1536]{1,0:T(8,128)(2,1)}, u32[]{:S(2)}, u32[]{:S(2)}) collective-permute-start(bf16[48,1536]{1,0:T(8,128)(2,1)} %get-tuple-element.256), channel_id=1, source_target_pairs={{0,8},{8,16},{16,24},{24,28},{28,20},{20,12},{12,4},{4,0},{1,9},{9... | collective-permute-start | bytes 442376 | tf_op jit(solution)/shard_map/ppermute | solution.py:1185
  369.5 33.1 %collective-permute-start.51 = (bf16[48,1536]{1,0:T(8,128)(2,1)}, bf16[48,1536]{1,0:T(8,128)(2,1)}, u32[]{:S(2)}, u32[]{:S(2)}) collective-permute-start(bf16[48,1536]{1,0:T(8,128)(2,1)} %get-tuple-element.255), channel_id=1, source_target_pairs={{8,0},{16,8},{24,16},{28,24},{20,28},{12,20},{4,12},{0,4},{9,1},{1... | collective-permute-start | bytes 442376 | tf_op jit(solution)/shard_map/ppermute | solution.py:1186
  373.8 48.9 %all-to-all-start.6 = ((bf16[16,48,384]{2,1,0:T(8,128)(2,1)}), bf16[16,48,384]{2,1,0:T(8,128)(2,1)}, u32[]{:S(2)}, u32[]{:S(2)}) async-start(bf16[16,48,384]{2,1,0:T(8,128)(2,1)} %bitcast.37), calls=%async_computation.6 | async-start | bytes 1179648 | tf_op jit(solution)/shard_map/all_to_all | solution.py:1254
  (131 other events, 1017.5 us)

commit v5 on v4

--- a/solution.py
+++ b/solution.py
@@ -447,41 +447,25 @@
     )
 
 
-def heads_send_kernel(count, at_ref, kept_ref, other_ref, send_ref, joined_ref, d_kv_ref):
+def heads_join_kernel(count, at_ref, kept_ref, other_ref, joined_ref):
     core = at_ref[2 * count]
     size = kept_ref.shape[0] // 3
-    half = size // 2
-    quarter = half // 2
-    step = send_ref.shape[2]
-    d_kv_ref[...] = kept_ref[size:, :] + other_ref[size:, :].astype(f32)
     joined_ref[pl.ds(pl.multiple_of(core * size, size), size), :] = kept_ref[:size, :].astype(bf16)
     joined_ref[pl.ds(pl.multiple_of((1 - core) * size, size), size), :] = other_ref[:size, :]
-    joined_ref[2 * size :, :] = d_kv_ref[...].astype(bf16)
-    for block in range(count):
-        columns = slice(block * step, (block + 1) * step)
-        for side in range(2):
-            start = pl.multiple_of(core * half + side * quarter, quarter)
-            send_ref[2 * block + side] = jnp.concatenate(
-                [
-                    kept_ref[side * half : (side + 1) * half, columns],
-                    d_kv_ref[pl.ds(start, quarter), columns],
-                    d_kv_ref[pl.ds(start + size, quarter), columns],
-                ],
-                axis=0,
-            ).astype(bf16)
-
-
-def heads_send(at, kept, other, count):
+    d_kv = kept_ref[size:, :] + other_ref[size:, :].astype(f32)
+    joined_ref[2 * size :, :] = d_kv.astype(bf16)
+
+
+def heads_join(at, kept, other, count):
     size, tokens = kept.shape
-    size = size // 3
-    return on_chip(
-        functools.partial(heads_send_kernel, count),
-        [like(bf16, 2 * count, size, tokens // count), like(bf16, 4 * size, tokens)],
+    (out,) = on_chip(
+        functools.partial(heads_join_kernel, count),
+        [like(bf16, size // 3 * 4, tokens)],
         [at, kept, other],
-        8 * kept.size,
-        scratch=[pltpu.VMEM((2 * size, tokens), f32)],
-        name="heads_send",
-    )
+        4 * kept.size,
+        name="heads_join",
+    )
+    return out
 
 
 def on_chip(kernel, out_shape, args, flops, blocks=(), scratch=(), name=None, room=24):
@@ -539,36 +523,6 @@
         away_ref[seq] = whole_ref[core_rows(at_ref, count, rows, seq, True), :].astype(bf16)
 
 
-def query_columns_kernel(at_ref, gain_ref, query_ref, key_ref, value_ref, out_ref):
-    gain = gain_ref[...]
-    query = query_ref[...].astype(f32) * gain
-    key = key_ref[...].astype(f32) * gain
-    value = value_ref[...].astype(f32) * gain
-    half = HEAD_SIZE // 2
-    quarter = HEAD_SIZE // 4
-    groups = out_ref.shape[2] // HEAD_SIZE
-    for t in range(4):
-        pieces = []
-        for group in range(groups):
-            place = 4 * group + t
-            pieces.append(query[:, place * half : (place + 1) * half])
-            pieces.append(key[:, place * quarter : (place + 1) * quarter])
-            pieces.append(value[:, place * quarter : (place + 1) * quarter])
-        out_ref[t] = jnp.concatenate(pieces, axis=1).astype(bf16)
-
-
-def query_columns(at, gain, query, key, value):
-    own, width = query.shape
-    (out,) = on_chip(
-        query_columns_kernel,
-        [like(bf16, 4, own, (width + 2 * key.shape[1]) // 4)],
-        [at, gain, query, key, value],
-        own * width,
-        name="query_columns",
-    )
-    return out
-
-
 def pair_columns_kernel(size, at_ref, gain_ref, gate_ref, up_ref, out_ref):
     gain = gain_ref[...]
     half = out_ref.shape[2] // 2
@@ -598,9 +552,9 @@
     query = query_ref[...].astype(f32) * gain
     key = key_ref[...].astype(f32) * gain
     value = value_ref[...].astype(f32) * gain
-    for group in range(out_ref.shape[0] // 2):
+    for group in range(out_ref.shape[0]):
         shared = slice(group * HEAD_SIZE, (group + 1) * HEAD_SIZE)
-        columns = jnp.concatenate(
+        out_ref[group] = jnp.concatenate(
             [
                 query[:, 2 * group * HEAD_SIZE : 2 * (group + 1) * HEAD_SIZE],
                 key[:, shared],
@@ -608,15 +562,13 @@
             ],
             axis=1,
         ).astype(bf16)
-        out_ref[2 * group] = columns
-        out_ref[2 * group + 1] = columns
 
 
 def head_columns(at, gain, query, key, value):
     own, width = query.shape
     (out,) = on_chip(
         head_columns_kernel,
-        [like(bf16, width // HEAD_SIZE, own, 4 * HEAD_SIZE)],
+        [like(bf16, width // HEAD_SIZE // 2, own, 4 * HEAD_SIZE)],
         [at, gain, query, key, value],
         own * width,
         name="head_columns",
@@ -669,14 +621,20 @@
     return copies
 
 
-def project_heads_kernel(at_ref, weight_ref, *refs):
-    blocks, (kept_ref, away_ref, n_ref, out_ref, sem_ref) = refs[:-5], refs[-5:]
+def project_heads_kernel(at_ref, own_ref, other_ref, *refs):
+    blocks, (kept_ref, away_ref, weight_ref, n_ref, out_ref, sem_ref) = refs[:-6], refs[-6:]
     copies = sequence_copies(at_ref, blocks, n_ref, sem_ref)
     for copy in copies:
         copy.start()
+    core = at_ref[2 * len(blocks)]
+    seq = at_ref[2 * len(blocks) + 1]
+    own = own_ref.shape[1]
+    for position in range(len(blocks)):
+        for ref, side in ((own_ref, seq), (other_ref, 1 - seq)):
+            start = pl.multiple_of((2 * position + side) * own, own)
+            weight_ref[pl.ds(start, own), :] = ref[position]
     for copy in copies:
         copy.wait()
-    core = at_ref[2 * len(blocks)]
     size = kept_ref.shape[0] // 3
     out_ref[...] = dot_at(weight_ref[...], n_ref[...], 0, 1)
     kept_ref[:size, :] = out_ref[pl.ds(pl.multiple_of(core * size, size), size), :]
@@ -686,15 +644,20 @@
     away_ref[size:, :] = out_ref[2 * size :, :].astype(bf16)
 
 
-def project_heads(at, weight, blocks, rows):
+def project_heads(at, weight_own, weight_other, blocks, rows):
     count = len(blocks)
-    width, columns = weight.shape
+    _, own, columns = weight_own.shape
+    width = 2 * count * own
     tokens = 2 * count * rows
     size = columns // 4
     return on_chip(
         project_heads_kernel,
-        [like(f32, 3 * size, tokens), like(bf16, 3 * size, tokens)],
-        [at, weight],
+        [
+            like(f32, 3 * size, tokens),
+            like(bf16, 3 * size, tokens),
+            like(bf16, width, columns),
+        ],
+        [at, weight_own, weight_other],
         2 * columns * tokens * width,
         blocks=blocks,
         scratch=[
@@ -809,22 +772,25 @@
 
 
 def feed_forward_kernel(step, at_ref, own_ref, other_ref, d_own_ref, d_other_ref, *refs):
-    blocks = refs[:-11]
-    n_ref, d_out_ref, hidden_ref, d_both_ref, kept_ref, away_ref = refs[-11:-5]
-    d_n_ref, whole_ref, down_ref, sem_ref, down_sem_ref = refs[-5:]
+    blocks = refs[:-12]
+    n_ref, d_out_ref, hidden_ref, d_both_ref, kept_ref, away_ref = refs[-12:-6]
+    d_n_ref, d_hidden_ref, whole_ref, down_ref, sem_ref, down_sem_ref = refs[-6:]
     ff = hidden_ref.shape[1]
     first = whole_ref.shape[0] // len(blocks)
-    copies = down_copies(at_ref, blocks, first, down_ref, down_sem_ref)
-    copies += block_copies(at_ref, blocks, whole_ref, sem_ref)
-    for copy in copies:
+    down = down_copies(at_ref, blocks, first, down_ref, down_sem_ref)
+    whole = block_copies(at_ref, blocks, whole_ref, sem_ref)
+    for copy in down + whole:
         copy.start()
     join_rows(at_ref, len(blocks), own_ref, other_ref, n_ref)
     join_rows(at_ref, len(blocks), d_own_ref, d_other_ref, d_out_ref)
-    for copy in copies:
+    for copy in down:
+        copy.wait()
+    d_hidden_ref[...] = dot_at(d_out_ref[...], down_ref[...], 1, 1).astype(bf16)
+    for copy in whole:
         copy.wait()
     for begin in range(0, n_ref.shape[0], step):
         rows = slice(begin, begin + step)
-        d_hidden = dot_at(d_out_ref[rows, :], down_ref[...], 1, 1)
+        d_hidden = d_hidden_ref[rows, :].astype(f32)
         both = dot_at(n_ref[rows, :], whole_ref[...], 1, 0)
         gate = both[:, :ff]
         upper = both[:, ff:]
@@ -856,6 +822,7 @@
         blocks=blocks,
         scratch=[
             pltpu.VMEM((4 * rows, width), f32),
+            pltpu.VMEM((4 * rows, ff), bf16),
             pltpu.VMEM((width, 2 * ff), bf16),
             pltpu.VMEM((ff, width), bf16),
             pltpu.SemaphoreType.DMA((count,)),
@@ -966,38 +933,56 @@
     return out
 
 
-def heads_input_kernel(at_ref, heads_ref, *refs):
-    blocks = refs[:-6]
-    kept_ref, away_ref, out_ref, joined_ref, weight_ref, sem_ref = refs[-6:]
-    copies = block_copies(at_ref, blocks, weight_ref, sem_ref)
-    for copy in copies:
-        copy.start()
-    join_heads(heads_ref, joined_ref)
-    for copy in copies:
-        copy.wait()
-    out_ref[...] = dot_at(joined_ref[...], weight_ref[...], 0, 1)
-    part_rows(at_ref, len(blocks), out_ref, kept_ref, away_ref)
-
-
-def heads_input(at, heads, blocks):
-    count = len(blocks)
-    block, columns = blocks[0].shape
-    rows = heads.shape[2] // 2
-    width = count * block
-    return on_chip(
+def heads_input_kernel(at_ref, joined_ref, weight_ref, out_ref):
+    count, rows, _ = out_ref.shape
+    for position in range(count):
+        columns = slice(position * rows, (position + 1) * rows)
+        out_ref[at_ref[count + position]] = dot_at(
+            joined_ref[:, columns], weight_ref[...], 0, 1
+        ).astype(bf16)
+
+
+def heads_input(at, joined, weight, count):
+    width, columns = weight.shape
+    tokens = joined.shape[1]
+    (out,) = on_chip(
         heads_input_kernel,
-        [like(f32, 2, rows, width), like(bf16, 2, rows, width)],
-        [at, heads],
-        0,
-        blocks=blocks,
-        scratch=[
-            pltpu.VMEM((4 * rows, width), f32),
-            pltpu.VMEM((columns, 4 * rows), bf16),
-            pltpu.VMEM((width, columns), bf16),
-            pltpu.SemaphoreType.DMA((count,)),
-        ],
+        [like(bf16, count, tokens // count, width)],
+        [at, joined, weight],
+        2 * tokens * width * columns,
         name="heads_input",
     )
+    return out
+
+
+def input_rows_kernel(count, at_ref, kept_ref, other_ref, rows_ref, d_middle_ref, out_ref):
+    core = at_ref[2 * count]
+    kept = kept_ref[...]
+    other = other_ref[...].astype(f32)
+    first = jnp.where(core == 0, kept, other)
+    second = jnp.where(core == 0, other, kept)
+    size = kept.shape[1] // count
+    pieces = []
+    for i in range(count):
+        pieces.append(first[:, i * size : (i + 1) * size])
+        pieces.append(second[:, i * size : (i + 1) * size])
+    d_normed = jnp.concatenate(pieces, axis=1)
+    rows = rows_ref[...].astype(f32)
+    inverse = lax.rsqrt(jnp.mean(rows * rows, axis=-1, keepdims=True) + norm_eps)
+    normed = rows * inverse
+    mean = jnp.mean(d_normed * normed, axis=-1, keepdims=True)
+    out_ref[...] = d_middle_ref[...] + inverse * (d_normed - normed * mean)
+
+
+def input_rows(at, kept, other, rows, d_middle, count):
+    (out,) = on_chip(
+        functools.partial(input_rows_kernel, count),
+        [like(f32, *rows.shape)],
+        [at, kept, other, rows, d_middle],
+        8 * rows.size,
+        name="input_rows",
+    )
+    return out
 
 
 def layer_output_kernel(first, at_ref, hidden_ref, *refs):
@@ -1170,8 +1155,9 @@
 
 
 class ScatterRing:
-    def __init__(self, term, count):
+    def __init__(self, term, count, pieces=1):
         self.count = count
+        self.pieces = pieces
         self.term = term
         self.forward, self.backward = ring_of(count)
         self.rows = term.shape[1] // 2
@@ -1189,17 +1175,37 @@
     def land(self, arrived):
         ahead, behind = (value.astype(f32) for value in arrived)
         left = self.count // 2 - self.hops
-        if left == 0:
-            self.total = self.term[0].astype(f32) + ahead + behind
-            return
         if self.hops == 1:
             edges = ((0, self.rows, 0), (self.rows, 0, 0))
             ahead, behind = (
                 lax.pad(value, jnp.float32(0), (edge,) + ((0, 0, 0),) * (value.ndim - 1))
                 for value, edge in zip((ahead, behind), (edges[0], edges[1]))
             )
-        self.ahead = (self.term[left].astype(f32) + ahead).astype(bf16)
-        self.behind = (self.term[self.count - left].astype(f32) + behind).astype(bf16)
+        sides = ((self.term[left], ahead), (self.term[self.count - left], behind))
+        if left > 1:
+            self.ahead, self.behind = ((t.astype(f32) + v).astype(bf16) for t, v in sides)
+            return
+        rows = self.term.shape[1]
+        self.lasts = []
+        for piece in range(self.pieces):
+            cut = slice(piece * rows // self.pieces, (piece + 1) * rows // self.pieces)
+            ends = [(t[cut].astype(f32) + v[cut]).astype(bf16) for t, v in sides]
+            self.lasts.append(LastHop(self, self.term[0, cut], ends))
+
+
+class LastHop:
+    def __init__(self, ring, own, ends):
+        self.ring, self.own, self.ends = ring, own, ends
+
+    def start(self):
+        ahead, behind = self.ends
+        self.pending = [
+            lax.ppermute(ahead, ring_axes, self.ring.forward),
+            lax.ppermute(behind, ring_axes, self.ring.backward),
+        ]
+
+    def land(self, arrived):
+        self.total = self.own.astype(f32) + arrived[0].astype(f32) + arrived[1].astype(f32)
 
 
 def settle(moves, *others):
@@ -1313,22 +1319,23 @@
     )
     n1_ring.start()
     head_cols = head_columns(at, gain1, w_query, key_weight, value_weight)
-    head_weight = all_to_all(head_cols, head_axes).reshape(half_width, 4 * HEAD_SIZE)
+    weight_own = all_to_all(head_cols, ring_axes)
     pair_cols = pair_columns(at, gain2, w_gate, w_up, ff_own)
     head_cols, pair_cols = settle([n1_ring], head_cols, pair_cols)
     n1_ring.start()
     tokens_pair = both_rows(tokens[0], head_cols)
-    head_weight, tokens_pair = settle([n1_ring], head_weight, tokens_pair)
+    weight_own, tokens_pair = settle([n1_ring], weight_own, tokens_pair)
     n1_ring.start()
+    weight_other = swap(weight_own, "y")
     pair_rows = all_to_all(pair_cols, ("core", "y")).reshape(group, 2 * count * ff_own)
     settle([n1_ring])
     n1_ring.start()
     ff_rows = pack_down(at, w_down, pair_rows)
-    ff_rows = settle([n1_ring], ff_rows)
+    ff_rows, weight_other = settle([n1_ring], ff_rows, weight_other)
 
     gather = GatherRing(ff_rows, count)
     gather.start()
-    kept, away = project_heads(at, head_weight, n1_ring.parts, rows)
+    kept, away, head_weight = project_heads(at, weight_own, weight_other, n1_ring.parts, rows)
     cotangent_pair = both_rows(after(cotangent[0], ff_rows), kept)
     mixed_send, mixed, prob, q, k, v = heads_forward(
         at, kept, swap(away, "core"), cosine, sine, count
@@ -1341,9 +1348,7 @@
     gather.start()
     out_weight, mixed_low, kept, away = project_out(at, mixed_low, n1_ring.parts, 2 * rows, own)
     branch = both_rows_sum(core_sum(kept, away))
-    qkv_cols = query_columns(at, gain1, w_query, key_weight, value_weight)
-    qkv_rows = all_to_all(after(qkv_cols, mixed_low), ("core", "y"))
-    branch, qkv_rows = settle([gather], branch, qkv_rows)
+    branch = settle([gather], branch)
     gather.start()
     inputs = tokens_pair.astype(f32)
     middle = inputs + branch
@@ -1353,22 +1358,16 @@
     n2_own = n2_pair.astype(bf16)
     n2_other = swap(n2_own, "core")
     n2_own, n2_other = settle([gather], n2_own, n2_other)
-    qkv_ring = GatherRing(qkv_rows.reshape(group, count * HEAD_SIZE), count)
-    qkv_ring.start(n2_own)
     n2, d_out, hidden, d_both, kept, away = feed_forward(
         at, n2_own, n2_other, cotangent_pair, cotangent_other, gather.parts, count * ff_own
     )
-    kept, away = settle([qkv_ring], kept, away)
-    qkv_ring.start()
     d_n2 = core_sum(kept, away)
     grads = feed_forward_grads(at, n2, d_both, after(hidden, d_n2), d_out, count)
     d_normed2 = both_rows_sum(d_n2)
-    grads = settle([qkv_ring], grads)
-    scatter = ScatterRing(grads, count)
+    scatter = ScatterRing(grads, count, pieces=2)
     scatter.start()
     d_normed2 = settle([scatter], d_normed2)
     scatter.start()
-    qkv_ring.start()
     d_middle = cotangent_pair.astype(f32) + r2 * (
         d_normed2 - n2_pair * jnp.mean(d_normed2 * n2_pair, axis=-1, keepdims=True)
     )
@@ -1382,45 +1381,53 @@
         at, after(hidden, d_mid), gather.parts, group, width
     )
     d_mixed, out_grads, kept_out, away_out = settle(
-        [scatter, qkv_ring], d_mixed, out_grads, kept_out, away_out
+        [scatter], d_mixed, out_grads, kept_out, away_out
     )
     out_scatter = ScatterRing(out_grads, count)
     scatter.start()
     out_scatter.start()
-    qkv_ring.start()
     kept, away = heads_backward(at, q, k, v, prob, mixed, d_mixed, cosine, sine, count)
     out_rows = own_rows_sum(core_sum(kept_out, away_out))
-    kept, away, out_rows = settle([scatter, out_scatter, qkv_ring], kept, away, out_rows)
-    scatter.start()
+    kept, away, out_rows = settle([scatter, out_scatter], kept, away, out_rows)
+    early, late = scatter.lasts
+    early.start()
     out_scatter.start()
-    d_qkv, joined = heads_send(at, kept, swap(away, "core"), count)
-    d_qkv = all_to_all(d_qkv, head_axes)
+    joined = heads_join(at, kept, swap(away, "core"), count)
+    d_n1 = heads_input(at, joined, head_weight, count)
     grad_heads = heads_grad(at, joined, n1_ring.parts)
-    grad_heads, d_qkv = settle([out_scatter], grad_heads, d_qkv)
+    d_n1, grad_heads = settle([early, out_scatter], d_n1, grad_heads)
+    d_n1_ring = ScatterRing(d_n1, count)
+    d_n1_ring.start()
+    late.start()
     out_scatter.start()
     grad_heads = all_to_all(grad_heads.reshape(2 * count, own, 4 * HEAD_SIZE), head_axes)
-    kept, away = heads_input(at, d_qkv, qkv_ring.parts)
-    kept, away = settle([scatter, out_scatter], kept, away)
-    out_scatter.start()
-    own_both = own_columns(scatter.total[:group].astype(bf16).reshape(2, 2, own, -1))
-    d_normed1 = own_rows_sum(core_sum(kept, away))
+    settle([d_n1_ring])
+    d_n1_ring.start()
+    grad_heads = settle([late, out_scatter, d_n1_ring], grad_heads)
+    d_n1_ring.start()
+    (out_last,) = out_scatter.lasts
+    out_last.start()
+    owned = jnp.concatenate([early.total, late.total], axis=0)
+    own_both = own_columns(owned[:group].astype(bf16).reshape(2, 2, own, -1))
+    grad_query, grad_key, grad_value, grad_gain1 = query_rows_grads(
+        at, grad_heads, gain1, w_query, key_weight, value_weight
+    )
+    grad_query, own_both = settle([d_n1_ring, out_last], grad_query, own_both)
+    (d_n1_last,) = d_n1_ring.lasts
+    d_n1_last.start()
+    grad_gate, grad_up, grad_gain2, owned_down = pair_rows_grads(
+        at, own_both, owned[group:], gain2, w_gate, w_up, ff_own, count
+    )
+    grad_gate = settle([d_n1_last], grad_gate)
     d_middle_own, middle_own = (
         lax.dynamic_index_in_dim(value, seq, 0, False) for value in (d_middle, middle)
     )
-    r1 = inverse_rms(own_rows)
-    n1_wide = own_rows * r1
-    input_grad = d_middle_own + r1 * (
-        d_normed1 - n1_wide * jnp.mean(d_normed1 * n1_wide, axis=-1, keepdims=True)
-    )
+    by_core = d_n1_last.total.reshape(2, rows, half_width)
+    other = swap(lax.dynamic_index_in_dim(by_core, 1 - core, 0, False).astype(bf16), "core")
+    kept = lax.dynamic_index_in_dim(by_core, core, 0, False)
+    input_grad = input_rows(at, kept, other, tokens[0], d_middle_own, count)
     result = middle_own + out_rows
-    grad_heads, own_both = settle([out_scatter], grad_heads, own_both)
-    owned_out = out_scatter.total
-    grad_gate, grad_up, grad_gain2, owned_down = pair_rows_grads(
-        at, own_both, scatter.total[group:], gain2, w_gate, w_up, ff_own, count
-    )
-    grad_query, grad_key, grad_value, grad_gain1 = query_rows_grads(
-        at, grad_heads, gain1, w_query, key_weight, value_weight
-    )
+    owned_out = out_last.total
     return (
         result.astype(bf16)[None],
         input_grad[None],

time: 441 us -> 420 us (0.952)
  local copies, waits for them, and re-layouts: 49.8 us -> 40.4 us
  starting transfers between devices: 84.2 us -> 75.8 us
  other arithmetic: 43.7 us -> 38 us
    ppermute x12 -> x8, waiting for transfers between devices: 52.9 us -> 40.5 us  [start(): lax.ppermute(ahead, ring_axes, self.forward)]
    all_to_all x6 -> x4, starting transfers between devices: 32.2 us -> 23 us  [all_to_all(): return lax.all_to_all(values, axes, 0, 0, tiled=True)]
    ppermute x0 -> x8, waiting for transfers between devices: none -> 9.2 us  [the longest x4 9.13 us: start(): lax.ppermute(ahead, ring_axes, self.ring.forward)]
    ppermute x0 -> x8, starting transfers between devices: none -> 8.15 us  [the longest x4 6.7 us: start(): lax.ppermute(behind, ring_axes, self.ring.backward)]
    ppermute x8 -> x9, waiting for transfers between devices: 37.9 us -> 44.4 us  [start(): lax.ppermute(self.ahead, ring_axes, self.forward)]
    ppermute x12 -> x8, starting transfers between devices: 17.4 us -> 11.1 us  [start(): lax.ppermute(behind, ring_axes, self.backward)]
    unnamed x200 -> x188, local copies, waits for them, and re-layouts: 38.4 us -> 32.6 us
    ppermute x18, waiting for transfers between devices: 35 us -> 40 us  [swap(): return lax.ppermute(values, axis, [(0, 1), (1, 0)])]
  transfers between devices with their start and end apart: 64 -> 64, of which waited for: 28 -> 31; matrix products, arithmetic and copies ran while one was open for 11% -> 9% of each run, Pallas kernels for 17% -> 13%
where the time goes in v5:
time: 420 us; the launch traced here: 412 us
  waiting for transfers between devices  147 us (35%)
  starting transfers between devices  75.8 us (18%)
  Pallas kernels  74.1 us (18%)
  local copies, waits for them, and re-layouts  40.4 us (10%)
  other arithmetic  38 us (9%)
  blocking collectives  35.3 us (8%)
    pallas_call x19, Pallas kernels, on_chip(): pl.pallas_call(kernel, out_shape=tuple(out_shape), in_specs=[pl.BlockSpec...  74.1 us
    ppermute x9, waiting for transfers between devices, start(): lax.ppermute(self.ahead, ring_axes, self.forward)  44.4 us
    ppermute x8, waiting for transfers between devices, start(): lax.ppermute(ahead, ring_axes, self.forward)  40.5 us
    ppermute x18, waiting for transfers between devices, swap(): return lax.ppermute(values, axis, [(0, 1), (1, 0)])  40 us
    all_to_all x1, blocking collectives, all_to_all(): return lax.all_to_all(values, axes, 0, 0, tiled=True)  35.3 us
    unnamed x188, local copies, waits for them, and re-layouts  32.6 us
    all_to_all x4, starting transfers between devices, all_to_all(): return lax.all_to_all(values, axes, 0, 0, tiled=True)  23 us
    ppermute x9, starting transfers between devices, start(): lax.ppermute(self.behind, ring_axes, self.backward)  11.9 us
  transfers between devices with their start and end apart: 64, of which 31 were waited for; matrix products, arithmetic and copies ran while one was open for 9% of the time, Pallas kernels for 13%

profile of v5, /device:TPU:10, one launch (start us, length us, event | category | flops | bytes accessed | tf_op | source)
XLA Modules:
  0.0 412.2 jit_solution(13227272695315089441)
XLA Ops:
  9.2 6.2 %all-to-all-start = ((bf16[8,48,384]{2,1,0:T(8,128)(2,1)}), bf16[8,48,384]{2,1,0:T(8,128)(2,1)S(1)}, u32[]{:S(2)}, u32[]{:S(2)}) async-start(bf16[8,48,384]{2,1,0:T(8,128)(2,1)} %head_columns.1), calls=%async_computation | async-start | bytes 589824 | tf_op jit(solution)/shard_map/all_to_all | solution.py:1260
  20.6 3.1 collective-permute-start.4
  25.8 10.4 %collective-permute-done.3.refs_6_ = bf16[352,768]{1,0:T(8,128)(2,1)S(1)} collective-permute-done((bf16[352,768]{1,0:T(8,128)(2,1)S(1)}, bf16[352,768]{1,0:T(8,128)(2,1)S(1)}, u32[]{:S(2)}, u32[]{:S(2)}) %collective-permute-start.3) | collective-permute-done | bytes 540704 | tf_op jit(solution)/shard_map/ppermute | solution.py:1144
  38.3 4.2 %all-to-all-start.1 = ((bf16[4,48,2048]{2,1,0:T(8,128)(2,1)}), bf16[4,48,2048]{2,1,0:T(8,128)(2,1)}, u32[]{:S(2)}, u32[]{:S(2)}) async-start(bf16[4,48,2048]{2,1,0:T(8,128)(2,1)} %copy-done.14), calls=%async_computation.1 | async-start | bytes 1572864 | tf_op jit(solution)/shard_map/all_to_all | solution.py:1260
  44.5 5.3 %collective-permute-done.6.refs_5_ = bf16[352,768]{1,0:T(8,128)(2,1)S(1)} collective-permute-done((bf16[352,768]{1,0:T(8,128)(2,1)S(1)}, bf16[352,768]{1,0:T(8,128)(2,1)S(1)}, u32[]{:S(2)}, u32[]{:S(2)}) %collective-permute-start.6) | collective-permute-done | bytes 540704 | tf_op jit(solution)/shard_map/ppermute | solution.py:1144
  57.0 3.6 collective-permute-done.10.other_ref
  67.1 6.7 %project_heads.1 = (f32[288,2048]{1,0:T(8,128)S(1)}, bf16[288,2048]{1,0:T(8,128)(2,1)S(1)}, bf16[768,384]{1,0:T(8,128)(2,1)S(1)}) custom-call(s32[18]{0:T(128)S(1)} %pad_add_fusion.at_ref, bf16[8,48,384]{2,1,0:T(8,128)(2,1)S(1)} %all-to-all-done.own_ref, bf16[8,48,384]{2,1,0:T(8,128)(2,1)} %collective-permute-done.10.other_ref, ...), custom_call_target="tpu_custom_call" | custom-call | flops 1207959552 | bytes 9044040 | tf_op jit(solution)/shard_map/project_heads/pallas_call | solution.py:475
  76.8 7.9 %heads_forward.1 = (bf16[16,48,256]{2,1,0:T(8,128)(2,1)S(1)}, f32[96,2048]{1,0:T(8,128)S(1)}, bf16[9216,256]{1,0:T(8,128)(2,1)S(1)}, bf16[96,2048]{1,0:T(8,128)(...) custom-call(s32[18]{0:T(128)S(1)} %pad_add_fusion.at_ref, ...), custom_call_target="tpu_custom_call" | custom-call | flops 905969664 | bytes 11403336 | tf_op jit(solution)/shard_map/heads_forward/pallas_call | solution.py:475
  90.7 35.3 %all_to_all.25.heads_ref = bf16[16,48,256]{2,1,0:T(8,128)(2,1)S(1)} all-to-all(bf16[16,48,256]{2,1,0:T(8,128)(2,1)S(1)} %get-tuple-element.140), channel_id=1, replica_groups=mesh['z'=4,'x'=2,'core'=2,'y'=2] {'z','x','y'}, dimensions={0} | all-to-all | bytes 786432 | tf_op jit(solution)/shard_map/all_to_all | solution.py:1260
  126.0 3.0 project_out.1
  134.2 17.1 %collective-permute-done.21 = bf16[2,128,1536]{2,1,0:T(8,128)(2,1)S(1)} collective-permute-done((bf16[2,128,1536]{2,1,0:T(8,128)(2,1)S(1)}, bf16[2,128,1536]{2,1,0:T(8,128)(2,1)S(1)}, u32[]{:S(2)}, u32[]{:S(2)}) %collective-permute-start.21) | collective-permute-done | bytes 786464 | tf_op jit(solution)/shard_map/ppermute | solution.py:1220
  151.6 8.3 %collective-permute-done.18.refs_5_ = bf16[288,2048]{1,0:T(8,128)(2,1)S(1)} collective-permute-done((bf16[288,2048]{1,0:T(8,128)(2,1)S(1)}, bf16[288,2048]{1,0:T(8,128)(2,1)S(1)}, u32[]{:S(2)}, u32[]{:S(2)}) %collective-permute-start.18) | collective-permute-done | bytes 1179680 | tf_op jit(solution)/shard_map/ppermute | solution.py:1144
  163.4 13.6 %collective-permute-done.22 = bf16[144,2048]{1,0:T(8,128)(2,1)S(1)} collective-permute-done((bf16[144,2048]{1,0:T(8,128)(2,1)S(1)}, bf16[144,2048]{1,0:T(8,128)(2,1)S(1)}, u32[]{:S(2)}, u32[]{:S(2)}) %collective-permute-start.22) | collective-permute-done | bytes 589856 | tf_op jit(solution)/shard_map/ppermute | solution.py:1144
  177.6 14.0 %feed_forward.1 = (bf16[512,1536]{1,0:T(8,128)(2,1)}, bf16[512,1536]{1,0:T(8,128)(2,1)}, bf16[512,1024]{1,0:T(8,128)(2,1)S(1)}, bf16[512,2048]{1,0:T(8,128)(2,1)...) custom-call(s32[18]{0:T(128)S(1)} %pad_add_fusion.at_ref, ...), custom_call_target="tpu_custom_call" | custom-call | flops 8053063680 | bytes 21233736 | tf_op jit(solution)/shard_map/feed_forward/pallas_call | solution.py:475
  198.5 5.9 %feed_forward_grads.1 = bf16[8,288,2048]{2,1,0:T(8,128)(2,1)S(1)} custom-call(s32[18]{0:T(128)S(1)} %pad_add_fusion.at_ref, bf16[512,1536]{1,0:T(8,128)(2,1)S(1)} %copy-done.71, bf16[512,2048]{1,0:T(8,128)(2,1)S(1)} %copy-done.70, bf16[512,1024]{1,0:T(8,128)(2,1)S(1)} %get-tuple-element.169.hidden_ref, bf16[512,1536]{1,0:T(8,128)(2,1)S(1)} %copy-done.72), custom_call_target="tpu_custom_call" | custom-call | flops 4831838208 | bytes 15728712 | tf_op jit(solution)/shard_map/feed_forward_grads/pallas_call | solution.py:475
  206.6 8.7 %collective-permute-done.28 = bf16[2,128,1536]{2,1,0:T(8,128)(2,1)S(1)} collective-permute-done((bf16[2,128,1536]{2,1,0:T(8,128)(2,1)S(1)}, bf16[2,128,1536]{2,1,0:T(8,128)(2,1)S(1)}, u32[]{:S(2)}, u32[]{:S(2)}) %collective-permute-start.28) | collective-permute-done | bytes 786464 | tf_op jit(solution)/shard_map/ppermute | solution.py:1220
  215.6 4.1 collective-permute-done.26
  230.0 6.1 %all-to-all-start.3 = ((bf16[16,48,256]{2,1,0:T(8,128)(2,1)}), bf16[16,48,256]{2,1,0:T(8,128)(2,1)}, u32[]{:S(2)}, u32[]{:S(2)}) async-start(bf16[16,48,256]{2,1,0:T(8,128)(2,1)} %copy-done.56), calls=%async_computation.3 | async-start | bytes 786432 | tf_op jit(solution)/shard_map/all_to_all | solution.py:1260
  247.4 3.8 layer_output.1
  252.4 2.8 joined_grads.1
  256.3 6.9 %all-to-all-done.3.back_ref = bf16[16,48,256]{2,1,0:T(8,128)(2,1)} async-done(((bf16[16,48,256]{2,1,0:T(8,128)(2,1)}), bf16[16,48,256]{2,1,0:T(8,128)(2,1)}, u32[]{:S(2)}, u32[]{:S(2)}) %all-to-all-start.3) | async-done | bytes 393248 | tf_op jit(solution)/shard_map/all_to_all | solution.py:1260
  263.1 3.5 fusion
  277.2 6.9 %heads_backward.1 = (f32[288,2048]{1,0:T(8,128)S(1)}, bf16[288,2048]{1,0:T(8,128)(2,1)S(1)}) custom-call(s32[18]{0:T(128)S(1)} %pad_add_fusion.at_ref, bf16[96,2048]{1,0:T(8,128)(2,1)S(1)} %copy-done.50, bf16[96,2048]{1,0:T(8,128)(2,1)S(1)} %copy-done.52, bf16[96,2048]{1,0:T(8,128)(2,1)S(1)} %copy-done.54, bf16[9216,256]{1,0:T(8,128)(2,1)S(1)} %copy-done.6, ...), custom_call_target="tpu_custom_call" | custom-call | flops 1811939328 | bytes 11403336 | tf_op jit(solution)/shard_map/heads_backward/pallas_call | solution.py:475
  285.1 11.6 %collective-permute-done.34 = bf16[24,1536]{1,0:T(8,128)(2,1)S(1)} collective-permute-done((bf16[24,1536]{1,0:T(8,128)(2,1)S(1)}, bf16[24,1536]{1,0:T(8,128)(2,1)S(1)}, u32[]{:S(2)}, u32[]{:S(2)}) %collective-permute-start.34) | collective-permute-done | bytes 73760 | tf_op jit(solution)/shard_map/ppermute | solution.py:1171
  298.0 3.4 fusion.6
  307.3 6.5 %heads_grad.1 = bf16[768,384]{1,0:T(8,128)(2,1)S(1)} custom-call(s32[18]{0:T(128)S(1)} %pad_add_fusion.at_ref, bf16[384,2048]{1,0:T(8,128)(2,1)S(1)} %heads_join.1.joined_ref, bf16[352,768]{1,0:T(8,128)(2,1)S(1)} %pad_maximum_fusion.4.refs_0_, bf16[352,768]{1,0:T(8,128)(2,1)S(1)} %collective-permute-done.2.refs_1_, ...), custom_call_target="tpu_custom_call" | custom-call | flops 1207959552 | bytes 6488136 | tf_op jit(solution)/shard_map/heads_grad/pallas_call | solution.py:475
  317.1 3.2 collective-permute-done.40
  321.0 6.5 %all-to-all-start.4 = ((bf16[16,48,384]{2,1,0:T(8,128)(2,1)}), bf16[16,48,384]{2,1,0:T(8,128)(2,1)}, u32[]{:S(2)}, u32[]{:S(2)}) async-start(bf16[16,48,384]{2,1,0:T(8,128)(2,1)} %bitcast.157), calls=%async_computation.4 | async-start | bytes 1179648 | tf_op jit(solution)/shard_map/all_to_all | solution.py:1260
  331.6 15.1 %collective-permute-done.47 = bf16[128,768]{1,0:T(8,128)(2,1)S(1)} collective-permute-done((bf16[128,768]{1,0:T(8,128)(2,1)S(1)}, bf16[128,768]{1,0:T(8,128)(2,1)S(1)}, u32[]{:S(2)}, u32[]{:S(2)}) %collective-permute-start.47) | collective-permute-done | bytes 196640 | tf_op jit(solution)/shard_map/ppermute | solution.py:1171
  351.5 8.0 %collective-permute-done.43 = bf16[144,2048]{1,0:T(8,128)(2,1)} collective-permute-done((bf16[144,2048]{1,0:T(8,128)(2,1)}, bf16[144,2048]{1,0:T(8,128)(2,1)}, u32[]{:S(2)}, u32[]{:S(2)}) %collective-permute-start.43) | collective-permute-done | bytes 589856 | tf_op jit(solution)/shard_map/ppermute | solution.py:1203
  359.7 10.3 %collective-permute-done.45 = bf16[48,1536]{1,0:T(8,128)(2,1)} collective-permute-done((bf16[48,1536]{1,0:T(8,128)(2,1)}, bf16[48,1536]{1,0:T(8,128)(2,1)}, u32[]{:S(2)}, u32[]{:S(2)}) %collective-permute-start.45) | collective-permute-done | bytes 147488 | tf_op jit(solution)/shard_map/ppermute | solution.py:1171
  378.7 4.3 %collective-permute-done.55 = bf16[2,48,2048]{2,1,0:T(8,128)(2,1)S(1)} collective-permute-done((bf16[2,48,2048]{2,1,0:T(8,128)(2,1)S(1)}, bf16[2,48,2048]{2,1,0:T(8,128)(2,1)S(1)}, u32[]{:S(2)}, u32[]{:S(2)}) %collective-permute-start.55) | collective-permute-done | bytes 393248 | tf_op jit(solution)/shard_map/ppermute | solution.py:1220
  (365 shorter events, 153.6 us)
Async XLA Ops:
  4.5 16.1 %collective-permute-start.2 = (bf16[352,768]{1,0:T(8,128)(2,1)S(1)}, bf16[352,768]{1,0:T(8,128)(2,1)S(1)}, u32[]{:S(2)}, u32[]{:S(2)}) collective-permute-start(bf16[352,768]{1,0:T(8,128)(2,1)S(1)} %pad_maximum_fusion.4.refs_0_), channel_id=1, source_target_pairs={{8,0},{16,8},{24,16},{28,24},{20,28},{12,20},{4,12},{0,4},{9,1},{1... | collective-permute-start | bytes 1622024 | tf_op jit(solution)/shard_map/ppermute | solution.py:1145
  9.2 16.6 %all-to-all-start = ((bf16[8,48,384]{2,1,0:T(8,128)(2,1)}), bf16[8,48,384]{2,1,0:T(8,128)(2,1)S(1)}, u32[]{:S(2)}, u32[]{:S(2)}) async-start(bf16[8,48,384]{2,1,0:T(8,128)(2,1)} %head_columns.1), calls=%async_computation | async-start | bytes 589824 | tf_op jit(solution)/shard_map/all_to_all | solution.py:1260
  38.3 16.4 %all-to-all-start.1 = ((bf16[4,48,2048]{2,1,0:T(8,128)(2,1)}), bf16[4,48,2048]{2,1,0:T(8,128)(2,1)}, u32[]{:S(2)}, u32[]{:S(2)}) async-start(bf16[4,48,2048]{2,1,0:T(8,128)(2,1)} %copy-done.14), calls=%async_computation.1 | async-start | bytes 1572864 | tf_op jit(solution)/shard_map/all_to_all | solution.py:1260
  42.5 18.0 %collective-permute-start.10 = (bf16[8,48,384]{2,1,0:T(8,128)(2,1)S(1)}, bf16[8,48,384]{2,1,0:T(8,128)(2,1)}, u32[]{:S(2)}, u32[]{:S(2)}) collective-permute-start(bf16[8,48,384]{2,1,0:T(8,128)(2,1)S(1)} %all-to-all-done.own_ref), channel_id=1, source_target_pairs={{0,1},{1,0},{2,3},{3,2},{4,5},{5,4},{6,7},{7,6},{8,9},{9,8},{10,11... | collective-permute-start | bytes 884744 | tf_op jit(solution)/shard_map/ppermute | solution.py:1220
  60.5 27.6 %collective-permute-start.11 = (bf16[288,2048]{1,0:T(8,128)(2,1)S(1)}, bf16[288,2048]{1,0:T(8,128)(2,1)S(1)}, u32[]{:S(2)}, u32[]{:S(2)}) collective-permute-start(bf16[288,2048]{1,0:T(8,128)(2,1)S(1)} %pack_down.1.refs_0_), channel_id=1, source_target_pairs={{0,8},{8,16},{16,24},{24,28},{28,20},{20,12},{12,4},{4,0},{1,9},{9... | collective-permute-start | bytes 3538952 | tf_op jit(solution)/shard_map/ppermute | solution.py:1144
  61.7 26.9 %collective-permute-start.12 = (bf16[288,2048]{1,0:T(8,128)(2,1)S(1)}, bf16[288,2048]{1,0:T(8,128)(2,1)S(1)}, u32[]{:S(2)}, u32[]{:S(2)}) collective-permute-start(bf16[288,2048]{1,0:T(8,128)(2,1)S(1)} %pack_down.1.refs_0_), channel_id=1, source_target_pairs={{8,0},{16,8},{24,16},{28,24},{20,28},{12,20},{4,12},{0,4},{9,1},{1... | collective-permute-start | bytes 3538952 | tf_op jit(solution)/shard_map/ppermute | solution.py:1145
  88.6 37.4 %collective-permute-start.15 = (bf16[288,2048]{1,0:T(8,128)(2,1)S(1)}, bf16[288,2048]{1,0:T(8,128)(2,1)S(1)}, u32[]{:S(2)}, u32[]{:S(2)}) collective-permute-start(bf16[288,2048]{1,0:T(8,128)(2,1)S(1)} %collective-permute-done.11.refs_7_), channel_id=1, source_target_pairs={{0,8},{8,16},{16,24},{24,28},{28,20},{20,12},{12,4},{4,0},{1,9},{9... | collective-permute-start | bytes 3538952 | tf_op jit(solution)/shard_map/ppermute | solution.py:1144
  90.5 35.5 %collective-permute-start.16 = (bf16[288,2048]{1,0:T(8,128)(2,1)S(1)}, bf16[288,2048]{1,0:T(8,128)(2,1)S(1)}, u32[]{:S(2)}, u32[]{:S(2)}) collective-permute-start(bf16[288,2048]{1,0:T(8,128)(2,1)S(1)} %collective-permute-done.12.refs_1_), channel_id=1, source_target_pairs={{8,0},{16,8},{24,16},{28,24},{20,28},{12,20},{4,12},{0,4},{9,1},{1... | collective-permute-start | bytes 3538952 | tf_op jit(solution)/shard_map/ppermute | solution.py:1145
  90.7 35.4 %collective-permute-start.17 = (bf16[2,128,1536]{2,1,0:T(8,128)(2,1)S(1)}, bf16[2,128,1536]{2,1,0:T(8,128)(2,1)S(1)}, u32[]{:S(2)}, u32[]{:S(2)}) collective-permute-start(bf16[2,128,1536]{2,1,0:T(8,128)(2,1)S(1)} %pad_maximum_fusion.2.d_own_ref), channel_id=1, source_target_pairs={{0,2},{2,0},{1,3},{3,1},{4,6},{6,4},{5,7},{7,5},{8,10},{10,8},{9,1... | collective-permute-start | bytes 2359304 | tf_op jit(solution)/shard_map/ppermute | solution.py:1220
  131.7 19.6 %collective-permute-start.21 = (bf16[2,128,1536]{2,1,0:T(8,128)(2,1)S(1)}, bf16[2,128,1536]{2,1,0:T(8,128)(2,1)S(1)}, u32[]{:S(2)}, u32[]{:S(2)}) collective-permute-start(bf16[2,128,1536]{2,1,0:T(8,128)(2,1)S(1)} %fusion.11), channel_id=1, source_target_pairs={{0,1},{1,0},{2,3},{3,2},{4,5},{5,4},{6,7},{7,6},{8,9},{9,8},{10,11... | collective-permute-start | bytes 2359304 | tf_op jit(solution)/shard_map/ppermute | solution.py:1220
  132.2 27.7 %collective-permute-start.18 = (bf16[288,2048]{1,0:T(8,128)(2,1)S(1)}, bf16[288,2048]{1,0:T(8,128)(2,1)S(1)}, u32[]{:S(2)}, u32[]{:S(2)}) collective-permute-start(bf16[288,2048]{1,0:T(8,128)(2,1)S(1)} %collective-permute-done.15.refs_6_), channel_id=1, source_target_pairs={{0,8},{8,16},{16,24},{24,28},{28,20},{20,12},{12,4},{4,0},{1,9},{9... | collective-permute-start | bytes 3538952 | tf_op jit(solution)/shard_map/ppermute | solution.py:1144
  133.1 27.4 %collective-permute-start.19 = (bf16[288,2048]{1,0:T(8,128)(2,1)S(1)}, bf16[288,2048]{1,0:T(8,128)(2,1)S(1)}, u32[]{:S(2)}, u32[]{:S(2)}) collective-permute-start(bf16[288,2048]{1,0:T(8,128)(2,1)S(1)} %collective-permute-done.16.refs_2_), channel_id=1, source_target_pairs={{8,0},{16,8},{24,16},{28,24},{20,28},{12,20},{4,12},{0,4},{9,1},{1... | collective-permute-start | bytes 3538952 | tf_op jit(solution)/shard_map/ppermute | solution.py:1145
  161.1 16.3 %collective-permute-start.24 = (bf16[2,128,1536]{2,1,0:T(8,128)(2,1)S(1)}, bf16[2,128,1536]{2,1,0:T(8,128)(2,1)S(1)}, u32[]{:S(2)}, u32[]{:S(2)}) collective-permute-start(bf16[2,128,1536]{2,1,0:T(8,128)(2,1)S(1)} %multiply_convert_fusion.own_ref), channel_id=1, source_target_pairs={{0,2},{2,0},{1,3},{3,1},{4,6},{6,4},{5,7},{7,5},{8,10},{10,8},{9,1... | collective-permute-start | bytes 2359304 | tf_op jit(solution)/shard_map/ppermute | solution.py:1220
  195.7 19.6 %collective-permute-start.28 = (bf16[2,128,1536]{2,1,0:T(8,128)(2,1)S(1)}, bf16[2,128,1536]{2,1,0:T(8,128)(2,1)S(1)}, u32[]{:S(2)}, u32[]{:S(2)}) collective-permute-start(bf16[2,128,1536]{2,1,0:T(8,128)(2,1)S(1)} %get-tuple-element.229), channel_id=1, source_target_pairs={{0,1},{1,0},{2,3},{3,2},{4,5},{5,4},{6,7},{7,6},{8,9},{9,8},{10,11... | collective-permute-start | bytes 2359304 | tf_op jit(solution)/shard_map/ppermute | solution.py:1220
  224.5 31.7 %collective-permute-start.29 = (bf16[288,2048]{1,0:T(8,128)(2,1)}, bf16[288,2048]{1,0:T(8,128)(2,1)}, u32[]{:S(2)}, u32[]{:S(2)}) collective-permute-start(bf16[288,2048]{1,0:T(8,128)(2,1)} %get-tuple-element.243), channel_id=1, source_target_pairs={{0,8},{8,16},{16,24},{24,28},{28,20},{20,12},{12,4},{4,0},{1,9},{9... | collective-permute-start | bytes 3538952 | tf_op jit(solution)/shard_map/ppermute | solution.py:1171
  225.6 30.7 %collective-permute-start.30 = (bf16[288,2048]{1,0:T(8,128)(2,1)}, bf16[288,2048]{1,0:T(8,128)(2,1)}, u32[]{:S(2)}, u32[]{:S(2)}) collective-permute-start(bf16[288,2048]{1,0:T(8,128)(2,1)} %get-tuple-element.242), channel_id=1, source_target_pairs={{8,0},{16,8},{24,16},{28,24},{20,28},{12,20},{4,12},{0,4},{9,1},{1... | collective-permute-start | bytes 3538952 | tf_op jit(solution)/shard_map/ppermute | solution.py:1172
  230.0 33.2 %all-to-all-start.3 = ((bf16[16,48,256]{2,1,0:T(8,128)(2,1)}), bf16[16,48,256]{2,1,0:T(8,128)(2,1)}, u32[]{:S(2)}, u32[]{:S(2)}) async-start(bf16[16,48,256]{2,1,0:T(8,128)(2,1)} %copy-done.56), calls=%async_computation.3 | async-start | bytes 786432 | tf_op jit(solution)/shard_map/all_to_all | solution.py:1260
  266.6 30.8 %collective-permute-start.32 = (bf16[288,2048]{1,0:T(8,128)(2,1)S(1)}, bf16[288,2048]{1,0:T(8,128)(2,1)S(1)}, u32[]{:S(2)}, u32[]{:S(2)}) collective-permute-start(bf16[288,2048]{1,0:T(8,128)(2,1)S(1)} %get-tuple-element.241), channel_id=1, source_target_pairs={{0,8},{8,16},{16,24},{24,28},{28,20},{20,12},{12,4},{4,0},{1,9},{9... | collective-permute-start | bytes 3538952 | tf_op jit(solution)/shard_map/ppermute | solution.py:1171
  267.7 29.7 %collective-permute-start.33 = (bf16[288,2048]{1,0:T(8,128)(2,1)S(1)}, bf16[288,2048]{1,0:T(8,128)(2,1)S(1)}, u32[]{:S(2)}, u32[]{:S(2)}) collective-permute-start(bf16[288,2048]{1,0:T(8,128)(2,1)S(1)} %get-tuple-element.240), channel_id=1, source_target_pairs={{8,0},{16,8},{24,16},{28,24},{20,28},{12,20},{4,12},{0,4},{9,1},{1... | collective-permute-start | bytes 3538952 | tf_op jit(solution)/shard_map/ppermute | solution.py:1172
  272.4 24.3 %collective-permute-start.34 = (bf16[24,1536]{1,0:T(8,128)(2,1)S(1)}, bf16[24,1536]{1,0:T(8,128)(2,1)S(1)}, u32[]{:S(2)}, u32[]{:S(2)}) collective-permute-start(bf16[24,1536]{1,0:T(8,128)(2,1)S(1)} %get-tuple-element.261), channel_id=1, source_target_pairs={{0,8},{8,16},{16,24},{24,28},{28,20},{20,12},{12,4},{4,0},{1,9},{9... | collective-permute-start | bytes 221192 | tf_op jit(solution)/shard_map/ppermute | solution.py:1171
  273.3 24.0 %collective-permute-start.35 = (bf16[24,1536]{1,0:T(8,128)(2,1)S(1)}, bf16[24,1536]{1,0:T(8,128)(2,1)S(1)}, u32[]{:S(2)}, u32[]{:S(2)}) collective-permute-start(bf16[24,1536]{1,0:T(8,128)(2,1)S(1)} %get-tuple-element.260), channel_id=1, source_target_pairs={{8,0},{16,8},{24,16},{28,24},{20,28},{12,20},{4,12},{0,4},{9,1},{1... | collective-permute-start | bytes 221192 | tf_op jit(solution)/shard_map/ppermute | solution.py:1172
  301.4 18.9 %collective-permute-start.38 = (bf16[144,2048]{1,0:T(8,128)(2,1)S(1)}, bf16[144,2048]{1,0:T(8,128)(2,1)}, u32[]{:S(2)}, u32[]{:S(2)}) collective-permute-start(bf16[144,2048]{1,0:T(8,128)(2,1)S(1)} %get-tuple-element.239), channel_id=1, source_target_pairs={{0,8},{8,16},{16,24},{24,28},{28,20},{20,12},{12,4},{4,0},{1,9},{9... | collective-permute-start | bytes 1769480 | tf_op jit(solution)/shard_map/ppermute | solution.py:1203
  301.7 18.6 %collective-permute-start.39 = (bf16[144,2048]{1,0:T(8,128)(2,1)S(1)}, bf16[144,2048]{1,0:T(8,128)(2,1)}, u32[]{:S(2)}, u32[]{:S(2)}) collective-permute-start(bf16[144,2048]{1,0:T(8,128)(2,1)S(1)} %get-tuple-element.233), channel_id=1, source_target_pairs={{8,0},{16,8},{24,16},{28,24},{20,28},{12,20},{4,12},{0,4},{9,1},{1... | collective-permute-start | bytes 1769480 | tf_op jit(solution)/shard_map/ppermute | solution.py:1204
  304.4 15.8 %collective-permute-start.40 = (bf16[48,1536]{1,0:T(8,128)(2,1)S(1)}, bf16[48,1536]{1,0:T(8,128)(2,1)S(1)}, u32[]{:S(2)}, u32[]{:S(2)}) collective-permute-start(bf16[48,1536]{1,0:T(8,128)(2,1)S(1)} %get-tuple-element.259), channel_id=1, source_target_pairs={{0,8},{8,16},{16,24},{24,28},{28,20},{20,12},{12,4},{4,0},{1,9},{9... | collective-permute-start | bytes 442376 | tf_op jit(solution)/shard_map/ppermute | solution.py:1171
  321.0 49.0 %all-to-all-start.4 = ((bf16[16,48,384]{2,1,0:T(8,128)(2,1)}), bf16[16,48,384]{2,1,0:T(8,128)(2,1)}, u32[]{:S(2)}, u32[]{:S(2)}) async-start(bf16[16,48,384]{2,1,0:T(8,128)(2,1)} %bitcast.157), calls=%async_computation.4 | async-start | bytes 1179648 | tf_op jit(solution)/shard_map/all_to_all | solution.py:1260
  327.5 19.2 %collective-permute-start.47 = (bf16[128,768]{1,0:T(8,128)(2,1)S(1)}, bf16[128,768]{1,0:T(8,128)(2,1)S(1)}, u32[]{:S(2)}, u32[]{:S(2)}) collective-permute-start(bf16[128,768]{1,0:T(8,128)(2,1)S(1)} %get-tuple-element.253), channel_id=1, source_target_pairs={{0,8},{8,16},{16,24},{24,28},{28,20},{20,12},{12,4},{4,0},{1,9},{9... | collective-permute-start | bytes 589832 | tf_op jit(solution)/shard_map/ppermute | solution.py:1171
  328.1 18.6 %collective-permute-start.48 = (bf16[128,768]{1,0:T(8,128)(2,1)S(1)}, bf16[128,768]{1,0:T(8,128)(2,1)S(1)}, u32[]{:S(2)}, u32[]{:S(2)}) collective-permute-start(bf16[128,768]{1,0:T(8,128)(2,1)S(1)} %get-tuple-element.252), channel_id=1, source_target_pairs={{8,0},{16,8},{24,16},{28,24},{20,28},{12,20},{4,12},{0,4},{9,1},{1... | collective-permute-start | bytes 589832 | tf_op jit(solution)/shard_map/ppermute | solution.py:1172
  329.6 29.9 %collective-permute-start.43 = (bf16[144,2048]{1,0:T(8,128)(2,1)}, bf16[144,2048]{1,0:T(8,128)(2,1)}, u32[]{:S(2)}, u32[]{:S(2)}) collective-permute-start(bf16[144,2048]{1,0:T(8,128)(2,1)} %get-tuple-element.238), channel_id=1, source_target_pairs={{0,8},{8,16},{16,24},{24,28},{28,20},{20,12},{12,4},{4,0},{1,9},{9... | collective-permute-start | bytes 1769480 | tf_op jit(solution)/shard_map/ppermute | solution.py:1203
  330.2 29.5 %collective-permute-start.44 = (bf16[144,2048]{1,0:T(8,128)(2,1)}, bf16[144,2048]{1,0:T(8,128)(2,1)}, u32[]{:S(2)}, u32[]{:S(2)}) collective-permute-start(bf16[144,2048]{1,0:T(8,128)(2,1)} %get-tuple-element.234), channel_id=1, source_target_pairs={{8,0},{16,8},{24,16},{28,24},{20,28},{12,20},{4,12},{0,4},{9,1},{1... | collective-permute-start | bytes 1769480 | tf_op jit(solution)/shard_map/ppermute | solution.py:1204
  347.7 22.3 %collective-permute-start.49 = (bf16[256,768]{1,0:T(8,128)(2,1)}, bf16[256,768]{1,0:T(8,128)(2,1)S(1)}, u32[]{:S(2)}, u32[]{:S(2)}) collective-permute-start(bf16[256,768]{1,0:T(8,128)(2,1)} %get-tuple-element.251), channel_id=1, source_target_pairs={{0,8},{8,16},{16,24},{24,28},{28,20},{20,12},{12,4},{4,0},{1,9},{9... | collective-permute-start | bytes 1179656 | tf_op jit(solution)/shard_map/ppermute | solution.py:1171
  347.7 22.3 %collective-permute-start.50 = (bf16[256,768]{1,0:T(8,128)(2,1)}, bf16[256,768]{1,0:T(8,128)(2,1)}, u32[]{:S(2)}, u32[]{:S(2)}) collective-permute-start(bf16[256,768]{1,0:T(8,128)(2,1)} %get-tuple-element.250), channel_id=1, source_target_pairs={{8,0},{16,8},{24,16},{28,24},{20,28},{12,20},{4,12},{0,4},{9,1},{1... | collective-permute-start | bytes 1179656 | tf_op jit(solution)/shard_map/ppermute | solution.py:1172
  351.5 18.5 %collective-permute-start.45 = (bf16[48,1536]{1,0:T(8,128)(2,1)}, bf16[48,1536]{1,0:T(8,128)(2,1)}, u32[]{:S(2)}, u32[]{:S(2)}) collective-permute-start(bf16[48,1536]{1,0:T(8,128)(2,1)} %get-tuple-element.257), channel_id=1, source_target_pairs={{0,8},{8,16},{16,24},{24,28},{28,20},{20,12},{12,4},{4,0},{1,9},{9... | collective-permute-start | bytes 442376 | tf_op jit(solution)/shard_map/ppermute | solution.py:1171
  (125 other events, 1430.4 us)

commit v6 on v5

--- a/solution.py
+++ b/solution.py
@@ -957,7 +957,7 @@
 
 def input_rows_kernel(count, at_ref, kept_ref, other_ref, rows_ref, d_middle_ref, out_ref):
     core = at_ref[2 * count]
-    kept = kept_ref[...]
+    kept = kept_ref[core]
     other = other_ref[...].astype(f32)
     first = jnp.where(core == 0, kept, other)
     second = jnp.where(core == 0, other, kept)
@@ -971,7 +971,8 @@
     inverse = lax.rsqrt(jnp.mean(rows * rows, axis=-1, keepdims=True) + norm_eps)
     normed = rows * inverse
     mean = jnp.mean(d_normed * normed, axis=-1, keepdims=True)
-    out_ref[...] = d_middle_ref[...] + inverse * (d_normed - normed * mean)
+    d_middle = d_middle_ref[at_ref[2 * count + 1]]
+    out_ref[...] = d_middle + inverse * (d_normed - normed * mean)
 
 
 def input_rows(at, kept, other, rows, d_middle, count):
@@ -1173,23 +1174,21 @@
         ]
 
     def land(self, arrived):
-        ahead, behind = (value.astype(f32) for value in arrived)
+        ahead, behind = arrived
         left = self.count // 2 - self.hops
         if self.hops == 1:
-            edges = ((0, self.rows, 0), (self.rows, 0, 0))
-            ahead, behind = (
-                lax.pad(value, jnp.float32(0), (edge,) + ((0, 0, 0),) * (value.ndim - 1))
-                for value, edge in zip((ahead, behind), (edges[0], edges[1]))
-            )
+            rest = ((0, 0, 0),) * (ahead.ndim - 1)
+            ahead = lax.pad(ahead, bf16(0), ((0, self.rows, 0),) + rest)
+            behind = lax.pad(behind, bf16(0), ((self.rows, 0, 0),) + rest)
         sides = ((self.term[left], ahead), (self.term[self.count - left], behind))
         if left > 1:
-            self.ahead, self.behind = ((t.astype(f32) + v).astype(bf16) for t, v in sides)
+            self.ahead, self.behind = (t + v for t, v in sides)
             return
         rows = self.term.shape[1]
         self.lasts = []
         for piece in range(self.pieces):
             cut = slice(piece * rows // self.pieces, (piece + 1) * rows // self.pieces)
-            ends = [(t[cut].astype(f32) + v[cut]).astype(bf16) for t, v in sides]
+            ends = [t[cut] + v[cut] for t, v in sides]
             self.lasts.append(LastHop(self, self.term[0, cut], ends))
 
 
@@ -1328,10 +1327,10 @@
     n1_ring.start()
     weight_other = swap(weight_own, "y")
     pair_rows = all_to_all(pair_cols, ("core", "y")).reshape(group, 2 * count * ff_own)
-    settle([n1_ring])
+    pair_rows = settle([n1_ring], pair_rows)
     n1_ring.start()
     ff_rows = pack_down(at, w_down, pair_rows)
-    ff_rows, weight_other = settle([n1_ring], ff_rows, weight_other)
+    ff_rows = settle([n1_ring], ff_rows)
 
     gather = GatherRing(ff_rows, count)
     gather.start()
@@ -1393,40 +1392,36 @@
     early.start()
     out_scatter.start()
     joined = heads_join(at, kept, swap(away, "core"), count)
-    d_n1 = heads_input(at, joined, head_weight, count)
     grad_heads = heads_grad(at, joined, n1_ring.parts)
-    d_n1, grad_heads = settle([early, out_scatter], d_n1, grad_heads)
+    d_n1 = heads_input(at, after(joined, grad_heads), head_weight, count)
     d_n1_ring = ScatterRing(d_n1, count)
     d_n1_ring.start()
+    grad_heads = settle([early, out_scatter, d_n1_ring], grad_heads)
     late.start()
+    d_n1_ring.start()
     out_scatter.start()
-    grad_heads = all_to_all(grad_heads.reshape(2 * count, own, 4 * HEAD_SIZE), head_axes)
-    settle([d_n1_ring])
-    d_n1_ring.start()
-    grad_heads = settle([late, out_scatter, d_n1_ring], grad_heads)
+    grad_heads = settle([late, d_n1_ring, out_scatter], grad_heads)
     d_n1_ring.start()
     (out_last,) = out_scatter.lasts
     out_last.start()
+    grad_heads = all_to_all(grad_heads.reshape(2 * count, own, 4 * HEAD_SIZE), head_axes)
     owned = jnp.concatenate([early.total, late.total], axis=0)
+    owned = after(owned, d_n1_ring.ahead, d_n1_ring.behind)
     own_both = own_columns(owned[:group].astype(bf16).reshape(2, 2, own, -1))
-    grad_query, grad_key, grad_value, grad_gain1 = query_rows_grads(
-        at, grad_heads, gain1, w_query, key_weight, value_weight
-    )
-    grad_query, own_both = settle([d_n1_ring, out_last], grad_query, own_both)
+    own_both = settle([d_n1_ring], own_both)
     (d_n1_last,) = d_n1_ring.lasts
     d_n1_last.start()
     grad_gate, grad_up, grad_gain2, owned_down = pair_rows_grads(
         at, own_both, owned[group:], gain2, w_gate, w_up, ff_own, count
     )
-    grad_gate = settle([d_n1_last], grad_gate)
-    d_middle_own, middle_own = (
-        lax.dynamic_index_in_dim(value, seq, 0, False) for value in (d_middle, middle)
+    grad_gate, grad_heads = settle([d_n1_last, out_last], grad_gate, grad_heads)
+    grad_query, grad_key, grad_value, grad_gain1 = query_rows_grads(
+        at, grad_heads, gain1, w_query, key_weight, value_weight
     )
     by_core = d_n1_last.total.reshape(2, rows, half_width)
     other = swap(lax.dynamic_index_in_dim(by_core, 1 - core, 0, False).astype(bf16), "core")
-    kept = lax.dynamic_index_in_dim(by_core, core, 0, False)
-    input_grad = input_rows(at, kept, other, tokens[0], d_middle_own, count)
-    result = middle_own + out_rows
+    input_grad = input_rows(at, by_core, other, tokens[0], d_middle, count)
+    result = lax.dynamic_index_in_dim(middle, seq, 0, False) + out_rows
     owned_out = out_last.total
     return (
         result.astype(bf16)[None],

time: 420 us -> 401 us (0.955)
  local copies, waits for them, and re-layouts: 40.4 us -> 31.5 us
  other arithmetic: 38 us -> 31.2 us
    ppermute x9, waiting for transfers between devices: 44.4 us -> 25.7 us  [start(): lax.ppermute(self.ahead, ring_axes, self.forward)]
    convert_element_type x11 -> x0, other arithmetic: 16.8 us -> none  [the longest x6 10.5 us: land(): (t.astype(f32) + v).astype(bf16)]
    add x0 -> x9, other arithmetic: none -> 11.9 us  [the longest x6 6.05 us: land(): self.ahead, self.behind = (t + v for t, v in sides)]
    ppermute x9, waiting for transfers between devices: 1.61 us -> 10.7 us  [start(): lax.ppermute(self.behind, ring_axes, self.backward)]
    ppermute x4, waiting for transfers between devices: 9.13 us -> 18 us  [start(): lax.ppermute(ahead, ring_axes, self.ring.forward)]
    ppermute x18, waiting for transfers between devices: 40 us -> 32.8 us  [swap(): return lax.ppermute(values, axis, [(0, 1), (1, 0)])]
    unnamed x188 -> x170, local copies, waits for them, and re-layouts: 32.6 us -> 27.8 us
    ppermute x9, starting transfers between devices: 5.21 us -> 9.88 us  [start(): lax.ppermute(self.ahead, ring_axes, self.forward)]
  transfers between devices with their start and end apart: 64 -> 64, of which waited for: 31 -> 36; matrix products, arithmetic and copies ran while one was open for 9% -> 6% of each run, Pallas kernels for 13% -> 14%
where the time goes in v6:
time: 401 us; the launch traced here: 395 us
  waiting for transfers between devices  144 us (36%)
  starting transfers between devices  77.3 us (19%)
  Pallas kernels  74.7 us (19%)
  blocking collectives  33.9 us (8%)
  local copies, waits for them, and re-layouts  31.5 us (8%)
  other arithmetic  31.2 us (8%)
    pallas_call x19, Pallas kernels, on_chip(): pl.pallas_call(kernel, out_shape=tuple(out_shape), in_specs=[pl.BlockSpec...  74.7 us
    ppermute x8, waiting for transfers between devices, start(): lax.ppermute(ahead, ring_axes, self.forward)  40 us
    all_to_all x1, blocking collectives, all_to_all(): return lax.all_to_all(values, axes, 0, 0, tiled=True)  33.9 us
    ppermute x18, waiting for transfers between devices, swap(): return lax.ppermute(values, axis, [(0, 1), (1, 0)])  32.8 us
    unnamed x170, local copies, waits for them, and re-layouts  27.8 us
    ppermute x9, waiting for transfers between devices, start(): lax.ppermute(self.ahead, ring_axes, self.forward)  25.7 us
    all_to_all x4, starting transfers between devices, all_to_all(): return lax.all_to_all(values, axes, 0, 0, tiled=True)  22.1 us
    ppermute x4, waiting for transfers between devices, start(): lax.ppermute(ahead, ring_axes, self.ring.forward)  18 us
  transfers between devices with their start and end apart: 64, of which 36 were waited for; matrix products, arithmetic and copies ran while one was open for 6% of the time, Pallas kernels for 14%

profile of v6, /device:TPU:10, one launch (start us, length us, event | category | flops | bytes accessed | tf_op | source)
XLA Modules:
  0.0 395.0 jit_solution(15404206586955310485)
XLA Ops:
  9.2 6.2 %all-to-all-start = ((bf16[8,48,384]{2,1,0:T(8,128)(2,1)}), bf16[8,48,384]{2,1,0:T(8,128)(2,1)S(1)}, u32[]{:S(2)}, u32[]{:S(2)}) async-start(bf16[8,48,384]{2,1,0:T(8,128)(2,1)} %head_columns.1), calls=%async_computation | async-start | bytes 589824 | tf_op jit(solution)/shard_map/all_to_all | solution.py:1259
  20.6 3.1 collective-permute-start.4
  25.7 4.2 %all-to-all-start.1 = ((bf16[4,48,2048]{2,1,0:T(8,128)(2,1)}), bf16[4,48,2048]{2,1,0:T(8,128)(2,1)}, u32[]{:S(2)}, u32[]{:S(2)}) async-start(bf16[4,48,2048]{2,1,0:T(8,128)(2,1)} %pair_columns.1), calls=%async_computation.1 | async-start | bytes 1572864 | tf_op jit(solution)/shard_map/all_to_all | solution.py:1259
  30.8 5.4 %collective-permute-done.3.refs_6_ = bf16[352,768]{1,0:T(8,128)(2,1)S(1)} collective-permute-done((bf16[352,768]{1,0:T(8,128)(2,1)S(1)}, bf16[352,768]{1,0:T(8,128)(2,1)S(1)}, u32[]{:S(2)}, u32[]{:S(2)}) %collective-permute-start.3) | collective-permute-done | bytes 540704 | tf_op jit(solution)/shard_map/ppermute | solution.py:1145
  38.3 3.3 all-to-all-done.1
  41.6 8.2 %collective-permute-done.6.refs_5_ = bf16[352,768]{1,0:T(8,128)(2,1)S(1)} collective-permute-done((bf16[352,768]{1,0:T(8,128)(2,1)S(1)}, bf16[352,768]{1,0:T(8,128)(2,1)S(1)}, u32[]{:S(2)}, u32[]{:S(2)}) %collective-permute-start.6) | collective-permute-done | bytes 540704 | tf_op jit(solution)/shard_map/ppermute | solution.py:1145
  63.5 6.3 %project_heads.1 = (f32[288,2048]{1,0:T(8,128)S(1)}, bf16[288,2048]{1,0:T(8,128)(2,1)S(1)}, bf16[768,384]{1,0:T(8,128)(2,1)S(1)}) custom-call(s32[18]{0:T(128)S(1)} %pad_add_fusion.at_ref, bf16[8,48,384]{2,1,0:T(8,128)(2,1)S(1)} %all-to-all-done.own_ref, bf16[8,48,384]{2,1,0:T(8,128)(2,1)S(1)} %collective-permute-done.12.other_ref, ...), custom_call_target="tpu_custom_call" | custom-call | flops 1207959552 | bytes 9044040 | tf_op jit(solution)/shard_map/project_heads/pallas_call | solution.py:475
  72.8 8.0 %heads_forward.1 = (bf16[16,48,256]{2,1,0:T(8,128)(2,1)S(1)}, f32[96,2048]{1,0:T(8,128)S(1)}, bf16[9216,256]{1,0:T(8,128)(2,1)S(1)}, bf16[96,2048]{1,0:T(8,128)(...) custom-call(s32[18]{0:T(128)S(1)} %pad_add_fusion.at_ref, ...), custom_call_target="tpu_custom_call" | custom-call | flops 905969664 | bytes 11403336 | tf_op jit(solution)/shard_map/heads_forward/pallas_call | solution.py:475
  87.1 33.9 %all_to_all.25.heads_ref = bf16[16,48,256]{2,1,0:T(8,128)(2,1)S(1)} all-to-all(bf16[16,48,256]{2,1,0:T(8,128)(2,1)S(1)} %get-tuple-element.141), channel_id=1, replica_groups=mesh['z'=4,'x'=2,'core'=2,'y'=2] {'z','x','y'}, dimensions={0} | all-to-all | bytes 786432 | tf_op jit(solution)/shard_map/all_to_all | solution.py:1259
  121.1 3.0 project_out.1
  130.3 16.0 %collective-permute-done.21 = bf16[2,128,1536]{2,1,0:T(8,128)(2,1)S(1)} collective-permute-done((bf16[2,128,1536]{2,1,0:T(8,128)(2,1)S(1)}, bf16[2,128,1536]{2,1,0:T(8,128)(2,1)S(1)}, u32[]{:S(2)}, u32[]{:S(2)}) %collective-permute-start.21) | collective-permute-done | bytes 786464 | tf_op jit(solution)/shard_map/ppermute | solution.py:1219
  146.7 9.4 %collective-permute-done.18.refs_5_ = bf16[288,2048]{1,0:T(8,128)(2,1)S(1)} collective-permute-done((bf16[288,2048]{1,0:T(8,128)(2,1)S(1)}, bf16[288,2048]{1,0:T(8,128)(2,1)S(1)}, u32[]{:S(2)}, u32[]{:S(2)}) %collective-permute-start.18) | collective-permute-done | bytes 1179680 | tf_op jit(solution)/shard_map/ppermute | solution.py:1145
  159.5 13.6 %collective-permute-done.22 = bf16[144,2048]{1,0:T(8,128)(2,1)S(1)} collective-permute-done((bf16[144,2048]{1,0:T(8,128)(2,1)S(1)}, bf16[144,2048]{1,0:T(8,128)(2,1)S(1)}, u32[]{:S(2)}, u32[]{:S(2)}) %collective-permute-start.22) | collective-permute-done | bytes 589856 | tf_op jit(solution)/shard_map/ppermute | solution.py:1145
  173.7 13.9 %feed_forward.1 = (bf16[512,1536]{1,0:T(8,128)(2,1)}, bf16[512,1536]{1,0:T(8,128)(2,1)}, bf16[512,1024]{1,0:T(8,128)(2,1)S(1)}, bf16[512,2048]{1,0:T(8,128)(2,1)...) custom-call(s32[18]{0:T(128)S(1)} %pad_add_fusion.at_ref, ...), custom_call_target="tpu_custom_call" | custom-call | flops 8053063680 | bytes 21233736 | tf_op jit(solution)/shard_map/feed_forward/pallas_call | solution.py:475
  193.9 5.9 %feed_forward_grads.1 = bf16[8,288,2048]{2,1,0:T(8,128)(2,1)S(1)} custom-call(s32[18]{0:T(128)S(1)} %pad_add_fusion.at_ref, bf16[512,1536]{1,0:T(8,128)(2,1)S(1)} %copy-done.69, bf16[512,2048]{1,0:T(8,128)(2,1)S(1)} %copy-done.68, bf16[512,1024]{1,0:T(8,128)(2,1)S(1)} %get-tuple-element.170.hidden_ref, bf16[512,1536]{1,0:T(8,128)(2,1)S(1)} %copy-done.70), custom_call_target="tpu_custom_call" | custom-call | flops 4831838208 | bytes 15728712 | tf_op jit(solution)/shard_map/feed_forward_grads/pallas_call | solution.py:475
  202.0 9.5 %collective-permute-done.28 = bf16[2,128,1536]{2,1,0:T(8,128)(2,1)S(1)} collective-permute-done((bf16[2,128,1536]{2,1,0:T(8,128)(2,1)S(1)}, bf16[2,128,1536]{2,1,0:T(8,128)(2,1)S(1)}, u32[]{:S(2)}, u32[]{:S(2)}) %collective-permute-start.28) | collective-permute-done | bytes 786464 | tf_op jit(solution)/shard_map/ppermute | solution.py:1219
  211.7 3.7 collective-permute-done.26
  225.6 6.1 %all-to-all-start.3 = ((bf16[16,48,256]{2,1,0:T(8,128)(2,1)}), bf16[16,48,256]{2,1,0:T(8,128)(2,1)}, u32[]{:S(2)}, u32[]{:S(2)}) async-start(bf16[16,48,256]{2,1,0:T(8,128)(2,1)} %copy-done.56), calls=%async_computation.3 | async-start | bytes 786432 | tf_op jit(solution)/shard_map/all_to_all | solution.py:1259
  243.1 3.8 layer_output.1
  248.1 2.8 joined_grads.1
  252.0 7.0 %all-to-all-done.3.back_ref = bf16[16,48,256]{2,1,0:T(8,128)(2,1)} async-done(((bf16[16,48,256]{2,1,0:T(8,128)(2,1)}), bf16[16,48,256]{2,1,0:T(8,128)(2,1)}, u32[]{:S(2)}, u32[]{:S(2)}) %all-to-all-start.3) | async-done | bytes 393248 | tf_op jit(solution)/shard_map/all_to_all | solution.py:1259
  258.9 2.7 fusion
  270.8 7.0 %heads_backward.1 = (f32[288,2048]{1,0:T(8,128)S(1)}, bf16[288,2048]{1,0:T(8,128)(2,1)S(1)}) custom-call(s32[18]{0:T(128)S(1)} %pad_add_fusion.at_ref, bf16[96,2048]{1,0:T(8,128)(2,1)S(1)} %copy-done.50, bf16[96,2048]{1,0:T(8,128)(2,1)S(1)} %copy-done.52, bf16[96,2048]{1,0:T(8,128)(2,1)S(1)} %copy-done.54, bf16[9216,256]{1,0:T(8,128)(2,1)S(1)} %copy-done.7, ...), custom_call_target="tpu_custom_call" | custom-call | flops 1811939328 | bytes 11403336 | tf_op jit(solution)/shard_map/heads_backward/pallas_call | solution.py:475
  278.8 12.9 %collective-permute-done.34 = bf16[24,1536]{1,0:T(8,128)(2,1)S(1)} collective-permute-done((bf16[24,1536]{1,0:T(8,128)(2,1)S(1)}, bf16[24,1536]{1,0:T(8,128)(2,1)S(1)}, u32[]{:S(2)}, u32[]{:S(2)}) %collective-permute-start.34) | collective-permute-done | bytes 73760 | tf_op jit(solution)/shard_map/ppermute | solution.py:1172
  297.7 6.6 %heads_grad.1 = bf16[768,384]{1,0:T(8,128)(2,1)S(1)} custom-call(s32[18]{0:T(128)S(1)} %pad_add_fusion.at_ref, bf16[384,2048]{1,0:T(8,128)(2,1)S(1)} %heads_join.1.joined_ref, bf16[352,768]{1,0:T(8,128)(2,1)S(1)} %pad_maximum_fusion.4.refs_0_, bf16[352,768]{1,0:T(8,128)(2,1)S(1)} %collective-permute-done.2.refs_1_, ...), custom_call_target="tpu_custom_call" | custom-call | flops 1207959552 | bytes 6488136 | tf_op jit(solution)/shard_map/heads_grad/pallas_call | solution.py:475
  311.3 7.3 %collective-permute-done.44 = bf16[48,1536]{1,0:T(8,128)(2,1)S(1)} collective-permute-done((bf16[48,1536]{1,0:T(8,128)(2,1)S(1)}, bf16[48,1536]{1,0:T(8,128)(2,1)S(1)}, u32[]{:S(2)}, u32[]{:S(2)}) %collective-permute-start.44) | collective-permute-done | bytes 147488 | tf_op jit(solution)/shard_map/ppermute | solution.py:1173
  324.1 10.8 %collective-permute-done.39 = bf16[144,2048]{1,0:T(8,128)(2,1)S(1)} collective-permute-done((bf16[144,2048]{1,0:T(8,128)(2,1)S(1)}, bf16[144,2048]{1,0:T(8,128)(2,1)S(1)}, u32[]{:S(2)}, u32[]{:S(2)}) %collective-permute-start.39) | collective-permute-done | bytes 589856 | tf_op jit(solution)/shard_map/ppermute | solution.py:1202
  336.1 8.3 %collective-permute-done.49 = bf16[48,1536]{1,0:T(8,128)(2,1)S(1)} collective-permute-done((bf16[48,1536]{1,0:T(8,128)(2,1)S(1)}, bf16[48,1536]{1,0:T(8,128)(2,1)S(1)}, u32[]{:S(2)}, u32[]{:S(2)}) %collective-permute-start.49) | collective-permute-done | bytes 147488 | tf_op jit(solution)/shard_map/ppermute | solution.py:1172
  353.0 5.6 %all-to-all-start.4 = ((bf16[16,48,384]{2,1,0:T(8,128)(2,1)}), bf16[16,48,384]{2,1,0:T(8,128)(2,1)}, u32[]{:S(2)}, u32[]{:S(2)}) async-start(bf16[16,48,384]{2,1,0:T(8,128)(2,1)} %bitcast.148), calls=%async_computation.4 | async-start | bytes 1179648 | tf_op jit(solution)/shard_map/all_to_all | solution.py:1259
  368.9 2.7 collective-permute-start.56
  377.9 6.1 %collective-permute-done.55 = bf16[256,768]{1,0:T(8,128)(2,1)} collective-permute-done((bf16[256,768]{1,0:T(8,128)(2,1)}, bf16[256,768]{1,0:T(8,128)(2,1)}, u32[]{:S(2)}, u32[]{:S(2)}) %collective-permute-start.55) | collective-permute-done | bytes 393248 | tf_op jit(solution)/shard_map/ppermute | solution.py:1202
  391.9 2.6 input_rows.1
  (344 shorter events, 146.8 us)
Async XLA Ops:
  4.5 16.1 %collective-permute-start.2 = (bf16[352,768]{1,0:T(8,128)(2,1)S(1)}, bf16[352,768]{1,0:T(8,128)(2,1)S(1)}, u32[]{:S(2)}, u32[]{:S(2)}) collective-permute-start(bf16[352,768]{1,0:T(8,128)(2,1)S(1)} %pad_maximum_fusion.4.refs_0_), channel_id=1, source_target_pairs={{8,0},{16,8},{24,16},{28,24},{20,28},{12,20},{4,12},{0,4},{9,1},{1... | collective-permute-start | bytes 1622024 | tf_op jit(solution)/shard_map/ppermute | solution.py:1146
  9.2 16.5 %all-to-all-start = ((bf16[8,48,384]{2,1,0:T(8,128)(2,1)}), bf16[8,48,384]{2,1,0:T(8,128)(2,1)S(1)}, u32[]{:S(2)}, u32[]{:S(2)}) async-start(bf16[8,48,384]{2,1,0:T(8,128)(2,1)} %head_columns.1), calls=%async_computation | async-start | bytes 589824 | tf_op jit(solution)/shard_map/all_to_all | solution.py:1259
  20.6 15.7 %collective-permute-start.3 = (bf16[352,768]{1,0:T(8,128)(2,1)S(1)}, bf16[352,768]{1,0:T(8,128)(2,1)S(1)}, u32[]{:S(2)}, u32[]{:S(2)}) collective-permute-start(bf16[352,768]{1,0:T(8,128)(2,1)S(1)} %collective-permute-done.1.refs_7_), channel_id=1, source_target_pairs={{0,8},{8,16},{16,24},{24,28},{28,20},{20,12},{12,4},{4,0},{1,9},{9... | collective-permute-start | bytes 1622024 | tf_op jit(solution)/shard_map/ppermute | solution.py:1145
  20.6 15.7 %collective-permute-start.4 = (bf16[352,768]{1,0:T(8,128)(2,1)S(1)}, bf16[352,768]{1,0:T(8,128)(2,1)}, u32[]{:S(2)}, u32[]{:S(2)}) collective-permute-start(bf16[352,768]{1,0:T(8,128)(2,1)S(1)} %collective-permute-done.2.refs_1_), channel_id=1, source_target_pairs={{8,0},{16,8},{24,16},{28,24},{20,28},{12,20},{4,12},{0,4},{9,1},{1... | collective-permute-start | bytes 1622024 | tf_op jit(solution)/shard_map/ppermute | solution.py:1146
  25.7 15.9 %all-to-all-start.1 = ((bf16[4,48,2048]{2,1,0:T(8,128)(2,1)}), bf16[4,48,2048]{2,1,0:T(8,128)(2,1)}, u32[]{:S(2)}, u32[]{:S(2)}) async-start(bf16[4,48,2048]{2,1,0:T(8,128)(2,1)} %pair_columns.1), calls=%async_computation.1 | async-start | bytes 1572864 | tf_op jit(solution)/shard_map/all_to_all | solution.py:1259
  58.4 25.3 %collective-permute-start.10 = (bf16[288,2048]{1,0:T(8,128)(2,1)S(1)}, bf16[288,2048]{1,0:T(8,128)(2,1)S(1)}, u32[]{:S(2)}, u32[]{:S(2)}) collective-permute-start(bf16[288,2048]{1,0:T(8,128)(2,1)S(1)} %pack_down.1.refs_0_), channel_id=1, source_target_pairs={{0,8},{8,16},{16,24},{24,28},{28,20},{20,12},{12,4},{4,0},{1,9},{9... | collective-permute-start | bytes 3538952 | tf_op jit(solution)/shard_map/ppermute | solution.py:1145
  60.1 25.0 %collective-permute-start.11 = (bf16[288,2048]{1,0:T(8,128)(2,1)S(1)}, bf16[288,2048]{1,0:T(8,128)(2,1)S(1)}, u32[]{:S(2)}, u32[]{:S(2)}) collective-permute-start(bf16[288,2048]{1,0:T(8,128)(2,1)S(1)} %pack_down.1.refs_0_), channel_id=1, source_target_pairs={{8,0},{16,8},{24,16},{28,24},{20,28},{12,20},{4,12},{0,4},{9,1},{1... | collective-permute-start | bytes 3538952 | tf_op jit(solution)/shard_map/ppermute | solution.py:1146
  85.1 36.0 %collective-permute-start.15 = (bf16[288,2048]{1,0:T(8,128)(2,1)S(1)}, bf16[288,2048]{1,0:T(8,128)(2,1)S(1)}, u32[]{:S(2)}, u32[]{:S(2)}) collective-permute-start(bf16[288,2048]{1,0:T(8,128)(2,1)S(1)} %collective-permute-done.10.refs_7_), channel_id=1, source_target_pairs={{0,8},{8,16},{16,24},{24,28},{28,20},{20,12},{12,4},{4,0},{1,9},{9... | collective-permute-start | bytes 3538952 | tf_op jit(solution)/shard_map/ppermute | solution.py:1145
  85.7 35.3 %collective-permute-start.16 = (bf16[288,2048]{1,0:T(8,128)(2,1)S(1)}, bf16[288,2048]{1,0:T(8,128)(2,1)S(1)}, u32[]{:S(2)}, u32[]{:S(2)}) collective-permute-start(bf16[288,2048]{1,0:T(8,128)(2,1)S(1)} %collective-permute-done.11.refs_1_), channel_id=1, source_target_pairs={{8,0},{16,8},{24,16},{28,24},{20,28},{12,20},{4,12},{0,4},{9,1},{1... | collective-permute-start | bytes 3538952 | tf_op jit(solution)/shard_map/ppermute | solution.py:1146
  87.1 33.9 %collective-permute-start.17 = (bf16[2,128,1536]{2,1,0:T(8,128)(2,1)S(1)}, bf16[2,128,1536]{2,1,0:T(8,128)(2,1)S(1)}, u32[]{:S(2)}, u32[]{:S(2)}) collective-permute-start(bf16[2,128,1536]{2,1,0:T(8,128)(2,1)S(1)} %pad_maximum_fusion.2.d_own_ref), channel_id=1, source_target_pairs={{0,2},{2,0},{1,3},{3,1},{4,6},{6,4},{5,7},{7,5},{8,10},{10,8},{9,1... | collective-permute-start | bytes 2359304 | tf_op jit(solution)/shard_map/ppermute | solution.py:1219
  126.7 19.6 %collective-permute-start.21 = (bf16[2,128,1536]{2,1,0:T(8,128)(2,1)S(1)}, bf16[2,128,1536]{2,1,0:T(8,128)(2,1)S(1)}, u32[]{:S(2)}, u32[]{:S(2)}) collective-permute-start(bf16[2,128,1536]{2,1,0:T(8,128)(2,1)S(1)} %fusion.6), channel_id=1, source_target_pairs={{0,1},{1,0},{2,3},{3,2},{4,5},{5,4},{6,7},{7,6},{8,9},{9,8},{10,11... | collective-permute-start | bytes 2359304 | tf_op jit(solution)/shard_map/ppermute | solution.py:1219
  128.3 27.7 %collective-permute-start.18 = (bf16[288,2048]{1,0:T(8,128)(2,1)S(1)}, bf16[288,2048]{1,0:T(8,128)(2,1)S(1)}, u32[]{:S(2)}, u32[]{:S(2)}) collective-permute-start(bf16[288,2048]{1,0:T(8,128)(2,1)S(1)} %collective-permute-done.15.refs_6_), channel_id=1, source_target_pairs={{0,8},{8,16},{16,24},{24,28},{28,20},{20,12},{12,4},{4,0},{1,9},{9... | collective-permute-start | bytes 3538952 | tf_op jit(solution)/shard_map/ppermute | solution.py:1145
  129.3 27.4 %collective-permute-start.19 = (bf16[288,2048]{1,0:T(8,128)(2,1)S(1)}, bf16[288,2048]{1,0:T(8,128)(2,1)S(1)}, u32[]{:S(2)}, u32[]{:S(2)}) collective-permute-start(bf16[288,2048]{1,0:T(8,128)(2,1)S(1)} %collective-permute-done.16.refs_2_), channel_id=1, source_target_pairs={{8,0},{16,8},{24,16},{28,24},{20,28},{12,20},{4,12},{0,4},{9,1},{1... | collective-permute-start | bytes 3538952 | tf_op jit(solution)/shard_map/ppermute | solution.py:1146
  157.2 16.3 %collective-permute-start.24 = (bf16[2,128,1536]{2,1,0:T(8,128)(2,1)S(1)}, bf16[2,128,1536]{2,1,0:T(8,128)(2,1)S(1)}, u32[]{:S(2)}, u32[]{:S(2)}) collective-permute-start(bf16[2,128,1536]{2,1,0:T(8,128)(2,1)S(1)} %multiply_convert_fusion.own_ref), channel_id=1, source_target_pairs={{0,2},{2,0},{1,3},{3,1},{4,6},{6,4},{5,7},{7,5},{8,10},{10,8},{9,1... | collective-permute-start | bytes 2359304 | tf_op jit(solution)/shard_map/ppermute | solution.py:1219
  157.3 15.8 %collective-permute-start.22 = (bf16[144,2048]{1,0:T(8,128)(2,1)S(1)}, bf16[144,2048]{1,0:T(8,128)(2,1)S(1)}, u32[]{:S(2)}, u32[]{:S(2)}) collective-permute-start(bf16[144,2048]{1,0:T(8,128)(2,1)S(1)} %slice.176), channel_id=1, source_target_pairs={{0,8},{8,16},{16,24},{24,28},{28,20},{20,12},{12,4},{4,0},{1,9},{9... | collective-permute-start | bytes 1769480 | tf_op jit(solution)/shard_map/ppermute | solution.py:1145
  191.8 19.6 %collective-permute-start.28 = (bf16[2,128,1536]{2,1,0:T(8,128)(2,1)S(1)}, bf16[2,128,1536]{2,1,0:T(8,128)(2,1)S(1)}, u32[]{:S(2)}, u32[]{:S(2)}) collective-permute-start(bf16[2,128,1536]{2,1,0:T(8,128)(2,1)S(1)} %get-tuple-element.229), channel_id=1, source_target_pairs={{0,1},{1,0},{2,3},{3,2},{4,5},{5,4},{6,7},{7,6},{8,9},{9,8},{10,11... | collective-permute-start | bytes 2359304 | tf_op jit(solution)/shard_map/ppermute | solution.py:1219
  220.2 31.8 %collective-permute-start.29 = (bf16[288,2048]{1,0:T(8,128)(2,1)}, bf16[288,2048]{1,0:T(8,128)(2,1)}, u32[]{:S(2)}, u32[]{:S(2)}) collective-permute-start(bf16[288,2048]{1,0:T(8,128)(2,1)} %get-tuple-element.244), channel_id=1, source_target_pairs={{0,8},{8,16},{16,24},{24,28},{28,20},{20,12},{12,4},{4,0},{1,9},{9... | collective-permute-start | bytes 3538952 | tf_op jit(solution)/shard_map/ppermute | solution.py:1172
  221.7 30.3 %collective-permute-start.30 = (bf16[288,2048]{1,0:T(8,128)(2,1)}, bf16[288,2048]{1,0:T(8,128)(2,1)}, u32[]{:S(2)}, u32[]{:S(2)}) collective-permute-start(bf16[288,2048]{1,0:T(8,128)(2,1)} %get-tuple-element.243), channel_id=1, source_target_pairs={{8,0},{16,8},{24,16},{28,24},{20,28},{12,20},{4,12},{0,4},{9,1},{1... | collective-permute-start | bytes 3538952 | tf_op jit(solution)/shard_map/ppermute | solution.py:1173
  225.6 33.3 %all-to-all-start.3 = ((bf16[16,48,256]{2,1,0:T(8,128)(2,1)}), bf16[16,48,256]{2,1,0:T(8,128)(2,1)}, u32[]{:S(2)}, u32[]{:S(2)}) async-start(bf16[16,48,256]{2,1,0:T(8,128)(2,1)} %copy-done.56), calls=%async_computation.3 | async-start | bytes 786432 | tf_op jit(solution)/shard_map/all_to_all | solution.py:1259
  261.6 30.8 %collective-permute-start.32 = (bf16[288,2048]{1,0:T(8,128)(2,1)S(1)}, bf16[288,2048]{1,0:T(8,128)(2,1)S(1)}, u32[]{:S(2)}, u32[]{:S(2)}) collective-permute-start(bf16[288,2048]{1,0:T(8,128)(2,1)S(1)} %get-tuple-element.242), channel_id=1, source_target_pairs={{0,8},{8,16},{16,24},{24,28},{28,20},{20,12},{12,4},{4,0},{1,9},{9... | collective-permute-start | bytes 3538952 | tf_op jit(solution)/shard_map/ppermute | solution.py:1172
  262.7 29.7 %collective-permute-start.33 = (bf16[288,2048]{1,0:T(8,128)(2,1)S(1)}, bf16[288,2048]{1,0:T(8,128)(2,1)S(1)}, u32[]{:S(2)}, u32[]{:S(2)}) collective-permute-start(bf16[288,2048]{1,0:T(8,128)(2,1)S(1)} %get-tuple-element.241), channel_id=1, source_target_pairs={{8,0},{16,8},{24,16},{28,24},{20,28},{12,20},{4,12},{0,4},{9,1},{1... | collective-permute-start | bytes 3538952 | tf_op jit(solution)/shard_map/ppermute | solution.py:1173
  266.2 25.5 %collective-permute-start.34 = (bf16[24,1536]{1,0:T(8,128)(2,1)S(1)}, bf16[24,1536]{1,0:T(8,128)(2,1)S(1)}, u32[]{:S(2)}, u32[]{:S(2)}) collective-permute-start(bf16[24,1536]{1,0:T(8,128)(2,1)S(1)} %get-tuple-element.262), channel_id=1, source_target_pairs={{0,8},{8,16},{16,24},{24,28},{28,20},{20,12},{12,4},{4,0},{1,9},{9... | collective-permute-start | bytes 221192 | tf_op jit(solution)/shard_map/ppermute | solution.py:1172
  267.1 25.2 %collective-permute-start.35 = (bf16[24,1536]{1,0:T(8,128)(2,1)S(1)}, bf16[24,1536]{1,0:T(8,128)(2,1)S(1)}, u32[]{:S(2)}, u32[]{:S(2)}) collective-permute-start(bf16[24,1536]{1,0:T(8,128)(2,1)S(1)} %get-tuple-element.261), channel_id=1, source_target_pairs={{8,0},{16,8},{24,16},{28,24},{20,28},{12,20},{4,12},{0,4},{9,1},{1... | collective-permute-start | bytes 221192 | tf_op jit(solution)/shard_map/ppermute | solution.py:1173
  292.5 17.2 %collective-permute-start.43 = (bf16[48,1536]{1,0:T(8,128)(2,1)S(1)}, bf16[48,1536]{1,0:T(8,128)(2,1)S(1)}, u32[]{:S(2)}, u32[]{:S(2)}) collective-permute-start(bf16[48,1536]{1,0:T(8,128)(2,1)S(1)} %get-tuple-element.260), channel_id=1, source_target_pairs={{0,8},{8,16},{16,24},{24,28},{28,20},{20,12},{12,4},{4,0},{1,9},{9... | collective-permute-start | bytes 442376 | tf_op jit(solution)/shard_map/ppermute | solution.py:1172
  294.8 25.0 %collective-permute-start.41 = (bf16[144,2048]{1,0:T(8,128)(2,1)S(1)}, bf16[144,2048]{1,0:T(8,128)(2,1)S(1)}, u32[]{:S(2)}, u32[]{:S(2)}) collective-permute-start(bf16[144,2048]{1,0:T(8,128)(2,1)S(1)} %get-tuple-element.240), channel_id=1, source_target_pairs={{0,8},{8,16},{16,24},{24,28},{28,20},{20,12},{12,4},{4,0},{1,9},{9... | collective-permute-start | bytes 1769480 | tf_op jit(solution)/shard_map/ppermute | solution.py:1202
  296.1 24.6 %collective-permute-start.42 = (bf16[144,2048]{1,0:T(8,128)(2,1)S(1)}, bf16[144,2048]{1,0:T(8,128)(2,1)S(1)}, u32[]{:S(2)}, u32[]{:S(2)}) collective-permute-start(bf16[144,2048]{1,0:T(8,128)(2,1)S(1)} %get-tuple-element.233), channel_id=1, source_target_pairs={{8,0},{16,8},{24,16},{28,24},{20,28},{12,20},{4,12},{0,4},{9,1},{1... | collective-permute-start | bytes 1769480 | tf_op jit(solution)/shard_map/ppermute | solution.py:1203
  318.6 16.3 %collective-permute-start.39 = (bf16[144,2048]{1,0:T(8,128)(2,1)S(1)}, bf16[144,2048]{1,0:T(8,128)(2,1)S(1)}, u32[]{:S(2)}, u32[]{:S(2)}) collective-permute-start(bf16[144,2048]{1,0:T(8,128)(2,1)S(1)} %get-tuple-element.239), channel_id=1, source_target_pairs={{0,8},{8,16},{16,24},{24,28},{28,20},{20,12},{12,4},{4,0},{1,9},{9... | collective-permute-start | bytes 1769480 | tf_op jit(solution)/shard_map/ppermute | solution.py:1202
  319.8 16.3 %collective-permute-start.40 = (bf16[144,2048]{1,0:T(8,128)(2,1)S(1)}, bf16[144,2048]{1,0:T(8,128)(2,1)S(1)}, u32[]{:S(2)}, u32[]{:S(2)}) collective-permute-start(bf16[144,2048]{1,0:T(8,128)(2,1)S(1)} %get-tuple-element.234), channel_id=1, source_target_pairs={{8,0},{16,8},{24,16},{28,24},{20,28},{12,20},{4,12},{0,4},{9,1},{1... | collective-permute-start | bytes 1769480 | tf_op jit(solution)/shard_map/ppermute | solution.py:1203
  320.8 24.5 %collective-permute-start.47 = (bf16[256,768]{1,0:T(8,128)(2,1)S(1)}, bf16[256,768]{1,0:T(8,128)(2,1)S(1)}, u32[]{:S(2)}, u32[]{:S(2)}) collective-permute-start(bf16[256,768]{1,0:T(8,128)(2,1)S(1)} %get-tuple-element.252), channel_id=1, source_target_pairs={{0,8},{8,16},{16,24},{24,28},{28,20},{20,12},{12,4},{4,0},{1,9},{9... | collective-permute-start | bytes 1179656 | tf_op jit(solution)/shard_map/ppermute | solution.py:1172
  322.0 23.3 %collective-permute-start.48 = (bf16[256,768]{1,0:T(8,128)(2,1)S(1)}, bf16[256,768]{1,0:T(8,128)(2,1)S(1)}, u32[]{:S(2)}, u32[]{:S(2)}) collective-permute-start(bf16[256,768]{1,0:T(8,128)(2,1)S(1)} %get-tuple-element.251), channel_id=1, source_target_pairs={{8,0},{16,8},{24,16},{28,24},{20,28},{12,20},{4,12},{0,4},{9,1},{1... | collective-permute-start | bytes 1179656 | tf_op jit(solution)/shard_map/ppermute | solution.py:1173
  322.9 21.5 %collective-permute-start.49 = (bf16[48,1536]{1,0:T(8,128)(2,1)S(1)}, bf16[48,1536]{1,0:T(8,128)(2,1)S(1)}, u32[]{:S(2)}, u32[]{:S(2)}) collective-permute-start(bf16[48,1536]{1,0:T(8,128)(2,1)S(1)} %get-tuple-element.258), channel_id=1, source_target_pairs={{0,8},{8,16},{16,24},{24,28},{28,20},{20,12},{12,4},{4,0},{1,9},{9... | collective-permute-start | bytes 442376 | tf_op jit(solution)/shard_map/ppermute | solution.py:1172
  353.0 24.9 %all-to-all-start.4 = ((bf16[16,48,384]{2,1,0:T(8,128)(2,1)}), bf16[16,48,384]{2,1,0:T(8,128)(2,1)}, u32[]{:S(2)}, u32[]{:S(2)}) async-start(bf16[16,48,384]{2,1,0:T(8,128)(2,1)} %bitcast.148), calls=%async_computation.4 | async-start | bytes 1179648 | tf_op jit(solution)/shard_map/all_to_all | solution.py:1259
  (116 other events, 1376.0 us)

commit v7 on v6

--- a/solution.py
+++ b/solution.py
@@ -833,20 +833,50 @@
     )
 
 
+def packed_grads(n_ref, d_both_ref, hidden_ref, d_out_ref, position, block, own, wide):
+    columns = slice(position * block, (position + 1) * block)
+    yield 0, block, 0, wide, dot_at(n_ref[:, columns], d_both_ref[...], 0, 0).astype(bf16)
+    columns = slice(position * own, (position + 1) * own)
+    down = dot_at(hidden_ref[:, columns], d_out_ref[...], 0, 0).astype(bf16)
+    for row, column, rows, width, to, start in down_pieces(own, n_ref.shape[1], wide):
+        yield block + to, rows, start, width, down[row : row + rows, column : column + width]
+
+
+def far_grads_kernel(count, at_ref, n_ref, d_both_ref, hidden_ref, d_out_ref, grad_ref):
+    wide = grad_ref.shape[1]
+    block = n_ref.shape[1] // count
+    own = hidden_ref.shape[1] // count
+    for position in range(count):
+
+        @pl.when(at_ref[count // 2] == position)
+        def _(position=position):
+            refs = (n_ref, d_both_ref, hidden_ref, d_out_ref)
+            for to, rows, start, width, part in packed_grads(*refs, position, block, own, wide):
+                grad_ref[to : to + rows, start : start + width] = part
+
+
+def far_grads(at, n, d_both, hidden, d_out, count):
+    rows, width = n.shape
+    ff = hidden.shape[1]
+    (out,) = on_chip(
+        functools.partial(far_grads_kernel, count),
+        [like(bf16, width // count + ff // count * width // (2 * ff), 2 * ff)],
+        [at, n, d_both, hidden, d_out],
+        6 * rows * width * ff // count,
+        name="far_grads",
+    )
+    return out
+
+
 def feed_forward_grads_kernel(at_ref, n_ref, d_both_ref, hidden_ref, d_out_ref, grad_ref):
     count, _, wide = grad_ref.shape
     block = n_ref.shape[1] // count
     own = hidden_ref.shape[1] // count
     for position in range(count):
         place = at_ref[count + position]
-        columns = slice(position * block, (position + 1) * block)
-        grad_ref[place, :block, :] = dot_at(n_ref[:, columns], d_both_ref[...], 0, 0).astype(bf16)
-        columns = slice(position * own, (position + 1) * own)
-        down = dot_at(hidden_ref[:, columns], d_out_ref[...], 0, 0).astype(bf16)
-        for row, column, rows, width, to, start in down_pieces(own, n_ref.shape[1], wide):
-            grad_ref[place, block + to : block + to + rows, start : start + width] = down[
-                row : row + rows, column : column + width
-            ]
+        refs = (n_ref, d_both_ref, hidden_ref, d_out_ref)
+        for to, rows, start, width, part in packed_grads(*refs, position, block, own, wide):
+            grad_ref[place, to : to + rows, start : start + width] = part
 
 
 def feed_forward_grads(at, n, d_both, hidden, d_out, count):
@@ -1156,13 +1186,11 @@
 
 
 class ScatterRing:
-    def __init__(self, term, count, pieces=1):
+    def __init__(self, far, count, pieces=1):
         self.count = count
         self.pieces = pieces
-        self.term = term
         self.forward, self.backward = ring_of(count)
-        self.rows = term.shape[1] // 2
-        far = term[count // 2]
+        self.rows = far.shape[0] // 2
         self.ahead, self.behind = far[: self.rows], far[self.rows :]
         self.hops = 0
 
@@ -1204,7 +1232,11 @@
         ]
 
     def land(self, arrived):
-        self.total = self.own.astype(f32) + arrived[0].astype(f32) + arrived[1].astype(f32)
+        self.arrived = arrived
+
+    def total(self, *others):
+        ahead, behind = lax.optimization_barrier(tuple(self.arrived) + others)[:2]
+        return self.own.astype(f32) + ahead.astype(f32) + behind.astype(f32)
 
 
 def settle(moves, *others):
@@ -1361,11 +1393,13 @@
         at, n2_own, n2_other, cotangent_pair, cotangent_other, gather.parts, count * ff_own
     )
     d_n2 = core_sum(kept, away)
-    grads = feed_forward_grads(at, n2, d_both, after(hidden, d_n2), d_out, count)
+    hidden = after(hidden, d_n2)
     d_normed2 = both_rows_sum(d_n2)
-    scatter = ScatterRing(grads, count, pieces=2)
+    far = far_grads(at, n2, d_both, hidden, d_out, count)
+    scatter = ScatterRing(far, count, pieces=2)
     scatter.start()
-    d_normed2 = settle([scatter], d_normed2)
+    scatter.term = feed_forward_grads(at, n2, d_both, after(hidden, far), d_out, count)
+    scatter.term = settle([scatter], scatter.term)
     scatter.start()
     d_middle = cotangent_pair.astype(f32) + r2 * (
         d_normed2 - n2_pair * jnp.mean(d_normed2 * n2_pair, axis=-1, keepdims=True)
@@ -1382,31 +1416,36 @@
     d_mixed, out_grads, kept_out, away_out = settle(
         [scatter], d_mixed, out_grads, kept_out, away_out
     )
-    out_scatter = ScatterRing(out_grads, count)
+    out_scatter = ScatterRing(out_grads[count // 2], count)
+    out_scatter.term = out_grads
     scatter.start()
     out_scatter.start()
     kept, away = heads_backward(at, q, k, v, prob, mixed, d_mixed, cosine, sine, count)
-    out_rows = own_rows_sum(core_sum(kept_out, away_out))
-    kept, away, out_rows = settle([scatter, out_scatter], kept, away, out_rows)
+    kept, away = settle([scatter, out_scatter], kept, away)
     early, late = scatter.lasts
     early.start()
     out_scatter.start()
+    away = after(away, *early.ends)
     joined = heads_join(at, kept, swap(away, "core"), count)
     grad_heads = heads_grad(at, joined, n1_ring.parts)
     d_n1 = heads_input(at, after(joined, grad_heads), head_weight, count)
-    d_n1_ring = ScatterRing(d_n1, count)
+    d_n1_ring = ScatterRing(d_n1[count // 2], count)
+    d_n1_ring.term = d_n1
     d_n1_ring.start()
-    grad_heads = settle([early, out_scatter, d_n1_ring], grad_heads)
+    away_out = after(away_out, joined)
+    out_rows = core_sum(kept_out, away_out)
+    grad_heads, out_rows = settle([early, out_scatter, d_n1_ring], grad_heads, out_rows)
     late.start()
     d_n1_ring.start()
     out_scatter.start()
-    grad_heads = settle([late, d_n1_ring, out_scatter], grad_heads)
+    out_rows = own_rows_sum(out_rows)
+    grad_heads, out_rows = settle([late, d_n1_ring, out_scatter], grad_heads, out_rows)
     d_n1_ring.start()
     (out_last,) = out_scatter.lasts
     out_last.start()
     grad_heads = all_to_all(grad_heads.reshape(2 * count, own, 4 * HEAD_SIZE), head_axes)
-    owned = jnp.concatenate([early.total, late.total], axis=0)
-    owned = after(owned, d_n1_ring.ahead, d_n1_ring.behind)
+    sent = (d_n1_ring.ahead, d_n1_ring.behind)
+    owned = jnp.concatenate([early.total(*sent), late.total(*sent)], axis=0)
     own_both = own_columns(owned[:group].astype(bf16).reshape(2, 2, own, -1))
     own_both = settle([d_n1_ring], own_both)
     (d_n1_last,) = d_n1_ring.lasts
@@ -1418,11 +1457,11 @@
     grad_query, grad_key, grad_value, grad_gain1 = query_rows_grads(
         at, grad_heads, gain1, w_query, key_weight, value_weight
     )
-    by_core = d_n1_last.total.reshape(2, rows, half_width)
+    by_core = d_n1_last.total().reshape(2, rows, half_width)
     other = swap(lax.dynamic_index_in_dim(by_core, 1 - core, 0, False).astype(bf16), "core")
     input_grad = input_rows(at, by_core, other, tokens[0], d_middle, count)
     result = lax.dynamic_index_in_dim(middle, seq, 0, False) + out_rows
-    owned_out = out_last.total
+    owned_out = out_last.total()
     return (
         result.astype(bf16)[None],
         input_grad[None],

time: 401 us -> 396 us (0.988)
  waiting for transfers between devices: 144 us -> 137 us
    ppermute x9, waiting for transfers between devices: 10.7 us -> 29.6 us  [start(): lax.ppermute(self.behind, ring_axes, self.backward)]
    ppermute x9, waiting for transfers between devices: 25.7 us -> 7.51 us  [start(): lax.ppermute(self.ahead, ring_axes, self.forward)]
    ppermute x4, waiting for transfers between devices: 18 us -> 4.67 us  [start(): lax.ppermute(ahead, ring_axes, self.ring.forward)]
    ppermute x8, waiting for transfers between devices: 5.06 us -> 18 us  [start(): lax.ppermute(behind, ring_axes, self.backward)]
    ppermute x4, waiting for transfers between devices: 0.8 us -> 12.9 us  [start(): lax.ppermute(behind, ring_axes, self.ring.backward)]
    ppermute x8, waiting for transfers between devices: 40 us -> 28.1 us  [start(): lax.ppermute(ahead, ring_axes, self.forward)]
    ppermute x18, waiting for transfers between devices: 32.8 us -> 25.2 us  [swap(): return lax.ppermute(values, axis, [(0, 1), (1, 0)])]
    pallas_call x19 -> x20, Pallas kernels: 74.7 us -> 77.7 us  [on_chip(): pl.pallas_call(kernel, out_shape=tuple(out_shape), in_specs=[pl.BlockSpec...]
  transfers between devices with their start and end apart: 64 -> 64, of which waited for: 36 -> 40; matrix products, arithmetic and copies ran while one was open for 6% -> 5% of each run, Pallas kernels for 14% -> 14%
where the time goes in v7:
time: 396 us; the launch traced here: 391 us
  waiting for transfers between devices  137 us (35%)
  Pallas kernels  77.7 us (20%)
  starting transfers between devices  75.9 us (19%)
  local copies, waits for them, and re-layouts  33.5 us (8%)
  blocking collectives  33.1 us (8%)
  other arithmetic  32 us (8%)
    pallas_call x20, Pallas kernels, on_chip(): pl.pallas_call(kernel, out_shape=tuple(out_shape), in_specs=[pl.BlockSpec...  77.7 us
    all_to_all x1, blocking collectives, all_to_all(): return lax.all_to_all(values, axes, 0, 0, tiled=True)  33.1 us
    unnamed x184, local copies, waits for them, and re-layouts  30.1 us
    ppermute x9, waiting for transfers between devices, start(): lax.ppermute(self.behind, ring_axes, self.backward)  29.6 us
    ppermute x8, waiting for transfers between devices, start(): lax.ppermute(ahead, ring_axes, self.forward)  28.1 us
    ppermute x18, waiting for transfers between devices, swap(): return lax.ppermute(values, axis, [(0, 1), (1, 0)])  25.2 us
    all_to_all x4, starting transfers between devices, all_to_all(): return lax.all_to_all(values, axes, 0, 0, tiled=True)  23 us
    ppermute x8, waiting for transfers between devices, start(): lax.ppermute(behind, ring_axes, self.backward)  18 us
  transfers between devices with their start and end apart: 64, of which 40 were waited for; matrix products, arithmetic and copies ran while one was open for 5% of the time, Pallas kernels for 14%

profile of v7, /device:TPU:10, one launch (start us, length us, event | category | flops | bytes accessed | tf_op | source)
XLA Modules:
  0.0 391.3 jit_solution(5754688000046967891)
XLA Ops:
  9.2 6.2 %all-to-all-start = ((bf16[8,48,384]{2,1,0:T(8,128)(2,1)}), bf16[8,48,384]{2,1,0:T(8,128)(2,1)S(1)}, u32[]{:S(2)}, u32[]{:S(2)}) async-start(bf16[8,48,384]{2,1,0:T(8,128)(2,1)} %head_columns.1), calls=%async_computation | async-start | bytes 589824 | tf_op jit(solution)/shard_map/all_to_all | solution.py:1291
  17.2 2.9 collective-permute-done.2.refs_1_
  26.5 4.2 %all-to-all-start.1 = ((bf16[4,48,2048]{2,1,0:T(8,128)(2,1)}), bf16[4,48,2048]{2,1,0:T(8,128)(2,1)}, u32[]{:S(2)}, u32[]{:S(2)}) async-start(bf16[4,48,2048]{2,1,0:T(8,128)(2,1)} %pair_columns.1), calls=%async_computation.1 | async-start | bytes 1572864 | tf_op jit(solution)/shard_map/all_to_all | solution.py:1291
  31.7 5.9 %collective-permute-done.3.refs_6_ = bf16[352,768]{1,0:T(8,128)(2,1)S(1)} collective-permute-done((bf16[352,768]{1,0:T(8,128)(2,1)S(1)}, bf16[352,768]{1,0:T(8,128)(2,1)S(1)}, u32[]{:S(2)}, u32[]{:S(2)}) %collective-permute-start.3) | collective-permute-done | bytes 540704 | tf_op jit(solution)/shard_map/ppermute | solution.py:1175
  39.6 2.9 all-to-all-done.1
  42.4 8.4 %collective-permute-done.6.refs_5_ = bf16[352,768]{1,0:T(8,128)(2,1)S(1)} collective-permute-done((bf16[352,768]{1,0:T(8,128)(2,1)S(1)}, bf16[352,768]{1,0:T(8,128)(2,1)S(1)}, u32[]{:S(2)}, u32[]{:S(2)}) %collective-permute-start.6) | collective-permute-done | bytes 540704 | tf_op jit(solution)/shard_map/ppermute | solution.py:1175
  64.5 6.3 %project_heads.1 = (f32[288,2048]{1,0:T(8,128)S(1)}, bf16[288,2048]{1,0:T(8,128)(2,1)S(1)}, bf16[768,384]{1,0:T(8,128)(2,1)S(1)}) custom-call(s32[18]{0:T(128)S(1)} %pad_add_fusion.at_ref, bf16[8,48,384]{2,1,0:T(8,128)(2,1)S(1)} %all-to-all-done.own_ref, bf16[8,48,384]{2,1,0:T(8,128)(2,1)S(1)} %collective-permute-done.12.other_ref, ...), custom_call_target="tpu_custom_call" | custom-call | flops 1207959552 | bytes 9044040 | tf_op jit(solution)/shard_map/project_heads/pallas_call | solution.py:475
  73.8 8.0 %heads_forward.1 = (bf16[16,48,256]{2,1,0:T(8,128)(2,1)S(1)}, f32[96,2048]{1,0:T(8,128)S(1)}, bf16[9216,256]{1,0:T(8,128)(2,1)S(1)}, bf16[96,2048]{1,0:T(8,128)(...) custom-call(s32[18]{0:T(128)S(1)} %pad_add_fusion.at_ref, ...), custom_call_target="tpu_custom_call" | custom-call | flops 905969664 | bytes 11403336 | tf_op jit(solution)/shard_map/heads_forward/pallas_call | solution.py:475
  87.0 33.1 %all_to_all.25.heads_ref = bf16[16,48,256]{2,1,0:T(8,128)(2,1)S(1)} all-to-all(bf16[16,48,256]{2,1,0:T(8,128)(2,1)S(1)} %get-tuple-element.152), channel_id=1, replica_groups=mesh['z'=4,'x'=2,'core'=2,'y'=2] {'z','x','y'}, dimensions={0} | all-to-all | bytes 786432 | tf_op jit(solution)/shard_map/all_to_all | solution.py:1291
  120.2 3.0 project_out.1
  130.3 15.9 %collective-permute-done.21 = bf16[2,128,1536]{2,1,0:T(8,128)(2,1)S(1)} collective-permute-done((bf16[2,128,1536]{2,1,0:T(8,128)(2,1)S(1)}, bf16[2,128,1536]{2,1,0:T(8,128)(2,1)S(1)}, u32[]{:S(2)}, u32[]{:S(2)}) %collective-permute-start.21) | collective-permute-done | bytes 786464 | tf_op jit(solution)/shard_map/ppermute | solution.py:1251
  146.4 9.4 %collective-permute-done.18.refs_5_ = bf16[288,2048]{1,0:T(8,128)(2,1)S(1)} collective-permute-done((bf16[288,2048]{1,0:T(8,128)(2,1)S(1)}, bf16[288,2048]{1,0:T(8,128)(2,1)S(1)}, u32[]{:S(2)}, u32[]{:S(2)}) %collective-permute-start.18) | collective-permute-done | bytes 1179680 | tf_op jit(solution)/shard_map/ppermute | solution.py:1175
  160.3 12.7 %collective-permute-done.23 = bf16[144,2048]{1,0:T(8,128)(2,1)S(1)} collective-permute-done((bf16[144,2048]{1,0:T(8,128)(2,1)S(1)}, bf16[144,2048]{1,0:T(8,128)(2,1)S(1)}, u32[]{:S(2)}, u32[]{:S(2)}) %collective-permute-start.23) | collective-permute-done | bytes 589856 | tf_op jit(solution)/shard_map/ppermute | solution.py:1176
  174.1 13.8 %feed_forward.1 = (bf16[512,1536]{1,0:T(8,128)(2,1)}, bf16[512,1536]{1,0:T(8,128)(2,1)}, bf16[512,1024]{1,0:T(8,128)(2,1)S(1)}, bf16[512,2048]{1,0:T(8,128)(2,1)...) custom-call(s32[18]{0:T(128)S(1)} %pad_add_fusion.at_ref, ...), custom_call_target="tpu_custom_call" | custom-call | flops 8053063680 | bytes 21233736 | tf_op jit(solution)/shard_map/feed_forward/pallas_call | solution.py:475
  198.0 5.7 %feed_forward_grads.1 = bf16[8,288,2048]{2,1,0:T(8,128)(2,1)S(1)} custom-call(s32[18]{0:T(128)S(1)} %pad_add_fusion.at_ref, bf16[512,1536]{1,0:T(8,128)(2,1)S(1)} %copy-done.38, bf16[512,2048]{1,0:T(8,128)(2,1)S(1)} %copy-done.29, bf16[512,1024]{1,0:T(8,128)(2,1)S(1)} %get-tuple-element.182.hidden_ref, bf16[512,1536]{1,0:T(8,128)(2,1)S(1)} %copy-done.40), custom_call_target="tpu_custom_call" | custom-call | flops 4831838208 | bytes 15728712 | tf_op jit(solution)/shard_map/feed_forward_grads/pallas_call | solution.py:475
  203.7 7.7 %collective-permute-done.27 = bf16[144,2048]{1,0:T(8,128)(2,1)S(1)} collective-permute-done((bf16[144,2048]{1,0:T(8,128)(2,1)S(1)}, bf16[144,2048]{1,0:T(8,128)(2,1)S(1)}, u32[]{:S(2)}, u32[]{:S(2)}) %collective-permute-start.27) | collective-permute-done | bytes 589856 | tf_op jit(solution)/shard_map/ppermute | solution.py:1201
  221.6 7.3 %all-to-all-start.3 = ((bf16[16,48,256]{2,1,0:T(8,128)(2,1)}), bf16[16,48,256]{2,1,0:T(8,128)(2,1)}, u32[]{:S(2)}, u32[]{:S(2)}) async-start(bf16[16,48,256]{2,1,0:T(8,128)(2,1)} %copy-done.62), calls=%async_computation.3 | async-start | bytes 786432 | tf_op jit(solution)/shard_map/all_to_all | solution.py:1291
  240.3 3.8 layer_output.1
  245.2 2.8 joined_grads.1
  249.1 6.2 %all-to-all-done.3.back_ref = bf16[16,48,256]{2,1,0:T(8,128)(2,1)} async-done(((bf16[16,48,256]{2,1,0:T(8,128)(2,1)}), bf16[16,48,256]{2,1,0:T(8,128)(2,1)}, u32[]{:S(2)}, u32[]{:S(2)}) %all-to-all-start.3) | async-done | bytes 393248 | tf_op jit(solution)/shard_map/all_to_all | solution.py:1291
  255.3 2.7 bitcast_add_fusion
  265.5 8.0 %heads_backward.1 = (f32[288,2048]{1,0:T(8,128)S(1)}, bf16[288,2048]{1,0:T(8,128)(2,1)}) custom-call(s32[18]{0:T(128)S(1)} %pad_add_fusion.at_ref, bf16[96,2048]{1,0:T(8,128)(2,1)S(1)} %copy-done.56, bf16[96,2048]{1,0:T(8,128)(2,1)S(1)} %copy-done.58, bf16[96,2048]{1,0:T(8,128)(2,1)S(1)} %copy-done.60, bf16[9216,256]{1,0:T(8,128)(2,1)S(1)} %copy-done.7, ...), custom_call_target="tpu_custom_call" | custom-call | flops 1811939328 | bytes 11403336 | tf_op jit(solution)/shard_map/heads_backward/pallas_call | solution.py:475
  273.5 13.2 %collective-permute-done.35 = bf16[24,1536]{1,0:T(8,128)(2,1)S(1)} collective-permute-done((bf16[24,1536]{1,0:T(8,128)(2,1)S(1)}, bf16[24,1536]{1,0:T(8,128)(2,1)S(1)}, u32[]{:S(2)}, u32[]{:S(2)}) %collective-permute-start.35) | collective-permute-done | bytes 73760 | tf_op jit(solution)/shard_map/ppermute | solution.py:1201
  286.9 3.2 bitcast_add_fusion.4
  299.1 6.5 %heads_grad.1 = bf16[768,384]{1,0:T(8,128)(2,1)S(1)} custom-call(s32[18]{0:T(128)S(1)} %pad_add_fusion.at_ref, bf16[384,2048]{1,0:T(8,128)(2,1)S(1)} %heads_join.1.joined_ref, bf16[352,768]{1,0:T(8,128)(2,1)S(1)} %pad_maximum_fusion.4.refs_0_, bf16[352,768]{1,0:T(8,128)(2,1)S(1)} %collective-permute-done.2.refs_1_, ...), custom_call_target="tpu_custom_call" | custom-call | flops 1207959552 | bytes 6488136 | tf_op jit(solution)/shard_map/heads_grad/pallas_call | solution.py:475
  314.2 3.0 collective-permute-done.44
  322.1 7.7 %collective-permute-done.37 = bf16[144,2048]{1,0:T(8,128)(2,1)S(1)} collective-permute-done((bf16[144,2048]{1,0:T(8,128)(2,1)S(1)}, bf16[144,2048]{1,0:T(8,128)(2,1)S(1)}, u32[]{:S(2)}, u32[]{:S(2)}) %collective-permute-start.37) | collective-permute-done | bytes 589856 | tf_op jit(solution)/shard_map/ppermute | solution.py:1231
  334.7 5.3 %collective-permute-done.47 = bf16[256,768]{1,0:T(8,128)(2,1)S(1)} collective-permute-done((bf16[256,768]{1,0:T(8,128)(2,1)S(1)}, bf16[256,768]{1,0:T(8,128)(2,1)S(1)}, u32[]{:S(2)}, u32[]{:S(2)}) %collective-permute-start.47) | collective-permute-done | bytes 393248 | tf_op jit(solution)/shard_map/ppermute | solution.py:1201
  342.5 2.8 fusion.29
  349.0 5.2 %all-to-all-start.4 = ((bf16[16,48,384]{2,1,0:T(8,128)(2,1)}), bf16[16,48,384]{2,1,0:T(8,128)(2,1)}, u32[]{:S(2)}, u32[]{:S(2)}) async-start(bf16[16,48,384]{2,1,0:T(8,128)(2,1)} %bitcast.129), calls=%async_computation.4 | async-start | bytes 1179648 | tf_op jit(solution)/shard_map/all_to_all | solution.py:1291
  374.7 3.7 collective-permute-done.56
  388.5 2.6 input_rows.1
  (357 shorter events, 159.4 us)
Async XLA Ops:
  4.0 16.1 %collective-permute-start.2 = (bf16[352,768]{1,0:T(8,128)(2,1)S(1)}, bf16[352,768]{1,0:T(8,128)(2,1)S(1)}, u32[]{:S(2)}, u32[]{:S(2)}) collective-permute-start(bf16[352,768]{1,0:T(8,128)(2,1)S(1)} %pad_maximum_fusion.4.refs_0_), channel_id=1, source_target_pairs={{8,0},{16,8},{24,16},{28,24},{20,28},{12,20},{4,12},{0,4},{9,1},{1... | collective-permute-start | bytes 1622024 | tf_op jit(solution)/shard_map/ppermute | solution.py:1176
  5.6 15.6 %collective-permute-start.1 = (bf16[352,768]{1,0:T(8,128)(2,1)S(1)}, bf16[352,768]{1,0:T(8,128)(2,1)S(1)}, u32[]{:S(2)}, u32[]{:S(2)}) collective-permute-start(bf16[352,768]{1,0:T(8,128)(2,1)S(1)} %pad_maximum_fusion.4.refs_0_), channel_id=1, source_target_pairs={{0,8},{8,16},{16,24},{24,28},{28,20},{20,12},{12,4},{4,0},{1,9},{9... | collective-permute-start | bytes 1622024 | tf_op jit(solution)/shard_map/ppermute | solution.py:1175
  9.2 17.3 %all-to-all-start = ((bf16[8,48,384]{2,1,0:T(8,128)(2,1)}), bf16[8,48,384]{2,1,0:T(8,128)(2,1)S(1)}, u32[]{:S(2)}, u32[]{:S(2)}) async-start(bf16[8,48,384]{2,1,0:T(8,128)(2,1)} %head_columns.1), calls=%async_computation | async-start | bytes 589824 | tf_op jit(solution)/shard_map/all_to_all | solution.py:1291
  21.2 16.4 %collective-permute-start.3 = (bf16[352,768]{1,0:T(8,128)(2,1)S(1)}, bf16[352,768]{1,0:T(8,128)(2,1)S(1)}, u32[]{:S(2)}, u32[]{:S(2)}) collective-permute-start(bf16[352,768]{1,0:T(8,128)(2,1)S(1)} %collective-permute-done.1.refs_7_), channel_id=1, source_target_pairs={{0,8},{8,16},{16,24},{24,28},{28,20},{20,12},{12,4},{4,0},{1,9},{9... | collective-permute-start | bytes 1622024 | tf_op jit(solution)/shard_map/ppermute | solution.py:1175
  21.3 16.3 %collective-permute-start.4 = (bf16[352,768]{1,0:T(8,128)(2,1)S(1)}, bf16[352,768]{1,0:T(8,128)(2,1)}, u32[]{:S(2)}, u32[]{:S(2)}) collective-permute-start(bf16[352,768]{1,0:T(8,128)(2,1)S(1)} %collective-permute-done.2.refs_1_), channel_id=1, source_target_pairs={{8,0},{16,8},{24,16},{28,24},{20,28},{12,20},{4,12},{0,4},{9,1},{1... | collective-permute-start | bytes 1622024 | tf_op jit(solution)/shard_map/ppermute | solution.py:1176
  26.5 15.9 %all-to-all-start.1 = ((bf16[4,48,2048]{2,1,0:T(8,128)(2,1)}), bf16[4,48,2048]{2,1,0:T(8,128)(2,1)}, u32[]{:S(2)}, u32[]{:S(2)}) async-start(bf16[4,48,2048]{2,1,0:T(8,128)(2,1)} %pair_columns.1), calls=%async_computation.1 | async-start | bytes 1572864 | tf_op jit(solution)/shard_map/all_to_all | solution.py:1291
  59.3 24.6 %collective-permute-start.11 = (bf16[288,2048]{1,0:T(8,128)(2,1)S(1)}, bf16[288,2048]{1,0:T(8,128)(2,1)S(1)}, u32[]{:S(2)}, u32[]{:S(2)}) collective-permute-start(bf16[288,2048]{1,0:T(8,128)(2,1)S(1)} %pack_down.1.refs_0_), channel_id=1, source_target_pairs={{8,0},{16,8},{24,16},{28,24},{20,28},{12,20},{4,12},{0,4},{9,1},{1... | collective-permute-start | bytes 3538952 | tf_op jit(solution)/shard_map/ppermute | solution.py:1176
  59.9 25.1 %collective-permute-start.10 = (bf16[288,2048]{1,0:T(8,128)(2,1)S(1)}, bf16[288,2048]{1,0:T(8,128)(2,1)S(1)}, u32[]{:S(2)}, u32[]{:S(2)}) collective-permute-start(bf16[288,2048]{1,0:T(8,128)(2,1)S(1)} %pack_down.1.refs_0_), channel_id=1, source_target_pairs={{0,8},{8,16},{16,24},{24,28},{28,20},{20,12},{12,4},{4,0},{1,9},{9... | collective-permute-start | bytes 3538952 | tf_op jit(solution)/shard_map/ppermute | solution.py:1175
  85.0 35.2 %collective-permute-start.15 = (bf16[288,2048]{1,0:T(8,128)(2,1)S(1)}, bf16[288,2048]{1,0:T(8,128)(2,1)S(1)}, u32[]{:S(2)}, u32[]{:S(2)}) collective-permute-start(bf16[288,2048]{1,0:T(8,128)(2,1)S(1)} %collective-permute-done.10.refs_7_), channel_id=1, source_target_pairs={{0,8},{8,16},{16,24},{24,28},{28,20},{20,12},{12,4},{4,0},{1,9},{9... | collective-permute-start | bytes 3538952 | tf_op jit(solution)/shard_map/ppermute | solution.py:1175
  86.2 33.9 %collective-permute-start.16 = (bf16[288,2048]{1,0:T(8,128)(2,1)S(1)}, bf16[288,2048]{1,0:T(8,128)(2,1)S(1)}, u32[]{:S(2)}, u32[]{:S(2)}) collective-permute-start(bf16[288,2048]{1,0:T(8,128)(2,1)S(1)} %collective-permute-done.11.refs_1_), channel_id=1, source_target_pairs={{8,0},{16,8},{24,16},{28,24},{20,28},{12,20},{4,12},{0,4},{9,1},{1... | collective-permute-start | bytes 3538952 | tf_op jit(solution)/shard_map/ppermute | solution.py:1176
  87.0 33.1 %collective-permute-start.17 = (bf16[2,128,1536]{2,1,0:T(8,128)(2,1)S(1)}, bf16[2,128,1536]{2,1,0:T(8,128)(2,1)S(1)}, u32[]{:S(2)}, u32[]{:S(2)}) collective-permute-start(bf16[2,128,1536]{2,1,0:T(8,128)(2,1)S(1)} %pad_maximum_fusion.2.d_own_ref), channel_id=1, source_target_pairs={{0,2},{2,0},{1,3},{3,1},{4,6},{6,4},{5,7},{7,5},{8,10},{10,8},{9,1... | collective-permute-start | bytes 2359304 | tf_op jit(solution)/shard_map/ppermute | solution.py:1251
  126.5 19.6 %collective-permute-start.21 = (bf16[2,128,1536]{2,1,0:T(8,128)(2,1)S(1)}, bf16[2,128,1536]{2,1,0:T(8,128)(2,1)S(1)}, u32[]{:S(2)}, u32[]{:S(2)}) collective-permute-start(bf16[2,128,1536]{2,1,0:T(8,128)(2,1)S(1)} %fusion.5), channel_id=1, source_target_pairs={{0,1},{1,0},{2,3},{3,2},{4,5},{5,4},{6,7},{7,6},{8,9},{9,8},{10,11... | collective-permute-start | bytes 2359304 | tf_op jit(solution)/shard_map/ppermute | solution.py:1251
  128.1 27.7 %collective-permute-start.18 = (bf16[288,2048]{1,0:T(8,128)(2,1)S(1)}, bf16[288,2048]{1,0:T(8,128)(2,1)S(1)}, u32[]{:S(2)}, u32[]{:S(2)}) collective-permute-start(bf16[288,2048]{1,0:T(8,128)(2,1)S(1)} %collective-permute-done.15.refs_6_), channel_id=1, source_target_pairs={{0,8},{8,16},{16,24},{24,28},{28,20},{20,12},{12,4},{4,0},{1,9},{9... | collective-permute-start | bytes 3538952 | tf_op jit(solution)/shard_map/ppermute | solution.py:1175
  129.0 27.6 %collective-permute-start.19 = (bf16[288,2048]{1,0:T(8,128)(2,1)S(1)}, bf16[288,2048]{1,0:T(8,128)(2,1)S(1)}, u32[]{:S(2)}, u32[]{:S(2)}) collective-permute-start(bf16[288,2048]{1,0:T(8,128)(2,1)S(1)} %collective-permute-done.16.refs_2_), channel_id=1, source_target_pairs={{8,0},{16,8},{24,16},{28,24},{20,28},{12,20},{4,12},{0,4},{9,1},{1... | collective-permute-start | bytes 3538952 | tf_op jit(solution)/shard_map/ppermute | solution.py:1176
  157.1 16.8 %collective-permute-start.24 = (bf16[2,128,1536]{2,1,0:T(8,128)(2,1)S(1)}, bf16[2,128,1536]{2,1,0:T(8,128)(2,1)S(1)}, u32[]{:S(2)}, u32[]{:S(2)}) collective-permute-start(bf16[2,128,1536]{2,1,0:T(8,128)(2,1)S(1)} %multiply_convert_fusion.own_ref), channel_id=1, source_target_pairs={{0,2},{2,0},{1,3},{3,1},{4,6},{6,4},{5,7},{7,5},{8,10},{10,8},{9,1... | collective-permute-start | bytes 2359304 | tf_op jit(solution)/shard_map/ppermute | solution.py:1251
  192.1 19.9 %collective-permute-start.30 = (bf16[2,128,1536]{2,1,0:T(8,128)(2,1)S(1)}, bf16[2,128,1536]{2,1,0:T(8,128)(2,1)S(1)}, u32[]{:S(2)}, u32[]{:S(2)}) collective-permute-start(bf16[2,128,1536]{2,1,0:T(8,128)(2,1)S(1)} %get-tuple-element.253), channel_id=1, source_target_pairs={{0,1},{1,0},{2,3},{3,2},{4,5},{5,4},{6,7},{7,6},{8,9},{9,8},{10,11... | collective-permute-start | bytes 2359304 | tf_op jit(solution)/shard_map/ppermute | solution.py:1251
  195.9 15.4 %collective-permute-start.27 = (bf16[144,2048]{1,0:T(8,128)(2,1)S(1)}, bf16[144,2048]{1,0:T(8,128)(2,1)S(1)}, u32[]{:S(2)}, u32[]{:S(2)}) collective-permute-start(bf16[144,2048]{1,0:T(8,128)(2,1)S(1)} %get-tuple-element.284), channel_id=1, source_target_pairs={{8,0},{16,8},{24,16},{28,24},{20,28},{12,20},{4,12},{0,4},{9,1},{1... | collective-permute-start | bytes 1769480 | tf_op jit(solution)/shard_map/ppermute | solution.py:1201
  196.9 15.1 %collective-permute-start.26 = (bf16[144,2048]{1,0:T(8,128)(2,1)S(1)}, bf16[144,2048]{1,0:T(8,128)(2,1)S(1)}, u32[]{:S(2)}, u32[]{:S(2)}) collective-permute-start(bf16[144,2048]{1,0:T(8,128)(2,1)S(1)} %get-tuple-element.285), channel_id=1, source_target_pairs={{0,8},{8,16},{16,24},{24,28},{28,20},{20,12},{12,4},{4,0},{1,9},{9... | collective-permute-start | bytes 1769480 | tf_op jit(solution)/shard_map/ppermute | solution.py:1200
  216.1 33.0 %collective-permute-start.29 = (bf16[288,2048]{1,0:T(8,128)(2,1)}, bf16[288,2048]{1,0:T(8,128)(2,1)}, u32[]{:S(2)}, u32[]{:S(2)}) collective-permute-start(bf16[288,2048]{1,0:T(8,128)(2,1)} %get-tuple-element.266), channel_id=1, source_target_pairs={{8,0},{16,8},{24,16},{28,24},{20,28},{12,20},{4,12},{0,4},{9,1},{1... | collective-permute-start | bytes 3538952 | tf_op jit(solution)/shard_map/ppermute | solution.py:1201
  217.9 31.2 %collective-permute-start.28 = (bf16[288,2048]{1,0:T(8,128)(2,1)}, bf16[288,2048]{1,0:T(8,128)(2,1)}, u32[]{:S(2)}, u32[]{:S(2)}) collective-permute-start(bf16[288,2048]{1,0:T(8,128)(2,1)} %get-tuple-element.267), channel_id=1, source_target_pairs={{0,8},{8,16},{16,24},{24,28},{28,20},{20,12},{12,4},{4,0},{1,9},{9... | collective-permute-start | bytes 3538952 | tf_op jit(solution)/shard_map/ppermute | solution.py:1200
  221.6 33.7 %all-to-all-start.3 = ((bf16[16,48,256]{2,1,0:T(8,128)(2,1)}), bf16[16,48,256]{2,1,0:T(8,128)(2,1)}, u32[]{:S(2)}, u32[]{:S(2)}) async-start(bf16[16,48,256]{2,1,0:T(8,128)(2,1)} %copy-done.62), calls=%async_computation.3 | async-start | bytes 786432 | tf_op jit(solution)/shard_map/all_to_all | solution.py:1291
  258.1 28.9 %collective-permute-start.33 = (bf16[288,2048]{1,0:T(8,128)(2,1)S(1)}, bf16[288,2048]{1,0:T(8,128)(2,1)S(1)}, u32[]{:S(2)}, u32[]{:S(2)}) collective-permute-start(bf16[288,2048]{1,0:T(8,128)(2,1)S(1)} %get-tuple-element.264), channel_id=1, source_target_pairs={{8,0},{16,8},{24,16},{28,24},{20,28},{12,20},{4,12},{0,4},{9,1},{1... | collective-permute-start | bytes 3538952 | tf_op jit(solution)/shard_map/ppermute | solution.py:1201
  258.4 28.6 %collective-permute-start.32 = (bf16[288,2048]{1,0:T(8,128)(2,1)S(1)}, bf16[288,2048]{1,0:T(8,128)(2,1)S(1)}, u32[]{:S(2)}, u32[]{:S(2)}) collective-permute-start(bf16[288,2048]{1,0:T(8,128)(2,1)S(1)} %get-tuple-element.265), channel_id=1, source_target_pairs={{0,8},{8,16},{16,24},{24,28},{28,20},{20,12},{12,4},{4,0},{1,9},{9... | collective-permute-start | bytes 3538952 | tf_op jit(solution)/shard_map/ppermute | solution.py:1200
  261.1 25.6 %collective-permute-start.35 = (bf16[24,1536]{1,0:T(8,128)(2,1)S(1)}, bf16[24,1536]{1,0:T(8,128)(2,1)S(1)}, u32[]{:S(2)}, u32[]{:S(2)}) collective-permute-start(bf16[24,1536]{1,0:T(8,128)(2,1)S(1)} %get-tuple-element.282), channel_id=1, source_target_pairs={{8,0},{16,8},{24,16},{28,24},{20,28},{12,20},{4,12},{0,4},{9,1},{1... | collective-permute-start | bytes 221192 | tf_op jit(solution)/shard_map/ppermute | solution.py:1201
  261.4 25.6 %collective-permute-start.34 = (bf16[24,1536]{1,0:T(8,128)(2,1)S(1)}, bf16[24,1536]{1,0:T(8,128)(2,1)S(1)}, u32[]{:S(2)}, u32[]{:S(2)}) collective-permute-start(bf16[24,1536]{1,0:T(8,128)(2,1)S(1)} %get-tuple-element.283), channel_id=1, source_target_pairs={{0,8},{8,16},{16,24},{24,28},{28,20},{20,12},{12,4},{4,0},{1,9},{9... | collective-permute-start | bytes 221192 | tf_op jit(solution)/shard_map/ppermute | solution.py:1200
  290.2 23.2 %collective-permute-start.40 = (bf16[144,2048]{1,0:T(8,128)(2,1)}, bf16[144,2048]{1,0:T(8,128)(2,1)S(1)}, u32[]{:S(2)}, u32[]{:S(2)}) collective-permute-start(bf16[144,2048]{1,0:T(8,128)(2,1)} %get-tuple-element.257), channel_id=1, source_target_pairs={{8,0},{16,8},{24,16},{28,24},{20,28},{12,20},{4,12},{0,4},{9,1},{1... | collective-permute-start | bytes 1769480 | tf_op jit(solution)/shard_map/ppermute | solution.py:1231
  292.0 22.2 %collective-permute-start.39 = (bf16[144,2048]{1,0:T(8,128)(2,1)}, bf16[144,2048]{1,0:T(8,128)(2,1)S(1)}, u32[]{:S(2)}, u32[]{:S(2)}) collective-permute-start(bf16[144,2048]{1,0:T(8,128)(2,1)} %get-tuple-element.263), channel_id=1, source_target_pairs={{0,8},{8,16},{16,24},{24,28},{28,20},{20,12},{12,4},{4,0},{1,9},{9... | collective-permute-start | bytes 1769480 | tf_op jit(solution)/shard_map/ppermute | solution.py:1230
  312.1 17.6 %collective-permute-start.37 = (bf16[144,2048]{1,0:T(8,128)(2,1)S(1)}, bf16[144,2048]{1,0:T(8,128)(2,1)S(1)}, u32[]{:S(2)}, u32[]{:S(2)}) collective-permute-start(bf16[144,2048]{1,0:T(8,128)(2,1)S(1)} %copy-done.82), channel_id=1, source_target_pairs={{8,0},{16,8},{24,16},{28,24},{20,28},{12,20},{4,12},{0,4},{9,1},{1... | collective-permute-start | bytes 1769480 | tf_op jit(solution)/shard_map/ppermute | solution.py:1231
  313.4 19.4 %collective-permute-start.36 = (bf16[144,2048]{1,0:T(8,128)(2,1)S(1)}, bf16[144,2048]{1,0:T(8,128)(2,1)S(1)}, u32[]{:S(2)}, u32[]{:S(2)}) collective-permute-start(bf16[144,2048]{1,0:T(8,128)(2,1)S(1)} %copy-done.81), channel_id=1, source_target_pairs={{0,8},{8,16},{16,24},{24,28},{28,20},{20,12},{12,4},{4,0},{1,9},{9... | collective-permute-start | bytes 1769480 | tf_op jit(solution)/shard_map/ppermute | solution.py:1230
  347.4 15.5 %collective-permute-start.51 = (bf16[256,768]{1,0:T(8,128)(2,1)}, bf16[256,768]{1,0:T(8,128)(2,1)}, u32[]{:S(2)}, u32[]{:S(2)}) collective-permute-start(bf16[256,768]{1,0:T(8,128)(2,1)} %get-tuple-element.271), channel_id=1, source_target_pairs={{0,8},{8,16},{16,24},{24,28},{28,20},{20,12},{12,4},{4,0},{1,9},{9... | collective-permute-start | bytes 1179656 | tf_op jit(solution)/shard_map/ppermute | solution.py:1200
  349.0 25.6 %all-to-all-start.4 = ((bf16[16,48,384]{2,1,0:T(8,128)(2,1)}), bf16[16,48,384]{2,1,0:T(8,128)(2,1)}, u32[]{:S(2)}, u32[]{:S(2)}) async-start(bf16[16,48,384]{2,1,0:T(8,128)(2,1)} %bitcast.129), calls=%async_computation.4 | async-start | bytes 1179648 | tf_op jit(solution)/shard_map/all_to_all | solution.py:1291
  365.1 15.5 %collective-permute-start.55 = (bf16[256,768]{1,0:T(8,128)(2,1)}, bf16[256,768]{1,0:T(8,128)(2,1)}, u32[]{:S(2)}, u32[]{:S(2)}) collective-permute-start(bf16[256,768]{1,0:T(8,128)(2,1)} %get-tuple-element.269), channel_id=1, source_target_pairs={{0,8},{8,16},{16,24},{24,28},{28,20},{20,12},{12,4},{4,0},{1,9},{9... | collective-permute-start | bytes 1179656 | tf_op jit(solution)/shard_map/ppermute | solution.py:1230
  (123 other events, 1385.3 us)

commit v8 on v7

--- a/solution.py
+++ b/solution.py
@@ -808,7 +808,7 @@
     count = len(blocks)
     pieces = len(down_pieces(ff // count, width, 2 * ff))
     return on_chip(
-        functools.partial(feed_forward_kernel, min(256, 4 * rows)),
+        functools.partial(feed_forward_kernel, 4 * rows),
         [
             like(bf16, 4 * rows, width),
             like(bf16, 4 * rows, width),
@@ -1374,12 +1374,12 @@
     mixed_send, cotangent_pair = settle([gather], mixed_send, cotangent_pair)
     gather.start()
     mixed_low = all_to_all(mixed_send, head_axes)
-    cotangent_other = swap(cotangent_pair, "core")
-    mixed_low, cotangent_other = settle([gather], mixed_low, cotangent_other)
+    mixed_low = settle([gather], mixed_low)
     gather.start()
     out_weight, mixed_low, kept, away = project_out(at, mixed_low, n1_ring.parts, 2 * rows, own)
     branch = both_rows_sum(core_sum(kept, away))
-    branch = settle([gather], branch)
+    cotangent_other = swap(after(cotangent_pair, mixed_low), "core")
+    branch, cotangent_other = settle([gather], branch, cotangent_other)
     gather.start()
     inputs = tokens_pair.astype(f32)
     middle = inputs + branch

time: 396 us -> 397 us (level)
  transfers between devices with their start and end apart: 64 -> 64, of which waited for: 40 -> 39; matrix products, arithmetic and copies ran while one was open for 5% -> 5% of each run, Pallas kernels for 14% -> 14%
where the time goes in v8:
time: 397 us; the launch traced here: 392 us
  waiting for transfers between devices  137 us (35%)
  Pallas kernels  77.7 us (20%)
  starting transfers between devices  75.9 us (19%)
  local copies, waits for them, and re-layouts  33.9 us (9%)
  blocking collectives  33.7 us (8%)
  other arithmetic  32.2 us (8%)
    pallas_call x20, Pallas kernels, on_chip(): pl.pallas_call(kernel, out_shape=tuple(out_shape), in_specs=[pl.BlockSpec...  77.7 us
    all_to_all x1, blocking collectives, all_to_all(): return lax.all_to_all(values, axes, 0, 0, tiled=True)  33.7 us
    unnamed x184, local copies, waits for them, and re-layouts  30.6 us
    ppermute x9, waiting for transfers between devices, start(): lax.ppermute(self.behind, ring_axes, self.backward)  29.5 us
    ppermute x8, waiting for transfers between devices, start(): lax.ppermute(ahead, ring_axes, self.forward)  28.1 us
    ppermute x18, waiting for transfers between devices, swap(): return lax.ppermute(values, axis, [(0, 1), (1, 0)])  25.2 us
    all_to_all x4, starting transfers between devices, all_to_all(): return lax.all_to_all(values, axes, 0, 0, tiled=True)  23 us
    ppermute x8, waiting for transfers between devices, start(): lax.ppermute(behind, ring_axes, self.backward)  17.5 us
  transfers between devices with their start and end apart: 64, of which 39 were waited for; matrix products, arithmetic and copies ran while one was open for 5% of the time, Pallas kernels for 14%

profile of v8, /device:TPU:10, one launch (start us, length us, event | category | flops | bytes accessed | tf_op | source)
XLA Modules:
  0.0 391.9 jit_solution(5406821686019032819)
XLA Ops:
  9.2 6.2 %all-to-all-start = ((bf16[8,48,384]{2,1,0:T(8,128)(2,1)}), bf16[8,48,384]{2,1,0:T(8,128)(2,1)S(1)}, u32[]{:S(2)}, u32[]{:S(2)}) async-start(bf16[8,48,384]{2,1,0:T(8,128)(2,1)} %head_columns.1), calls=%async_computation | async-start | bytes 589824 | tf_op jit(solution)/shard_map/all_to_all | solution.py:1291
  17.2 2.9 collective-permute-done.2.refs_1_
  26.5 4.2 %all-to-all-start.1 = ((bf16[4,48,2048]{2,1,0:T(8,128)(2,1)}), bf16[4,48,2048]{2,1,0:T(8,128)(2,1)}, u32[]{:S(2)}, u32[]{:S(2)}) async-start(bf16[4,48,2048]{2,1,0:T(8,128)(2,1)} %pair_columns.1), calls=%async_computation.1 | async-start | bytes 1572864 | tf_op jit(solution)/shard_map/all_to_all | solution.py:1291
  31.7 5.9 %collective-permute-done.3.refs_6_ = bf16[352,768]{1,0:T(8,128)(2,1)S(1)} collective-permute-done((bf16[352,768]{1,0:T(8,128)(2,1)S(1)}, bf16[352,768]{1,0:T(8,128)(2,1)S(1)}, u32[]{:S(2)}, u32[]{:S(2)}) %collective-permute-start.3) | collective-permute-done | bytes 540704 | tf_op jit(solution)/shard_map/ppermute | solution.py:1175
  39.6 2.9 all-to-all-done.1
  42.4 8.4 %collective-permute-done.6.refs_5_ = bf16[352,768]{1,0:T(8,128)(2,1)S(1)} collective-permute-done((bf16[352,768]{1,0:T(8,128)(2,1)S(1)}, bf16[352,768]{1,0:T(8,128)(2,1)S(1)}, u32[]{:S(2)}, u32[]{:S(2)}) %collective-permute-start.6) | collective-permute-done | bytes 540704 | tf_op jit(solution)/shard_map/ppermute | solution.py:1175
  64.5 6.3 %project_heads.1 = (f32[288,2048]{1,0:T(8,128)S(1)}, bf16[288,2048]{1,0:T(8,128)(2,1)S(1)}, bf16[768,384]{1,0:T(8,128)(2,1)S(1)}) custom-call(s32[18]{0:T(128)S(1)} %pad_add_fusion.at_ref, bf16[8,48,384]{2,1,0:T(8,128)(2,1)S(1)} %all-to-all-done.own_ref, bf16[8,48,384]{2,1,0:T(8,128)(2,1)S(1)} %collective-permute-done.12.other_ref, ...), custom_call_target="tpu_custom_call" | custom-call | flops 1207959552 | bytes 9044040 | tf_op jit(solution)/shard_map/project_heads/pallas_call | solution.py:475
  73.8 8.0 %heads_forward.1 = (bf16[16,48,256]{2,1,0:T(8,128)(2,1)S(1)}, f32[96,2048]{1,0:T(8,128)S(1)}, bf16[9216,256]{1,0:T(8,128)(2,1)S(1)}, bf16[96,2048]{1,0:T(8,128)(...) custom-call(s32[18]{0:T(128)S(1)} %pad_add_fusion.at_ref, ...), custom_call_target="tpu_custom_call" | custom-call | flops 905969664 | bytes 11403336 | tf_op jit(solution)/shard_map/heads_forward/pallas_call | solution.py:475
  87.0 33.7 %all_to_all.25.heads_ref = bf16[16,48,256]{2,1,0:T(8,128)(2,1)S(1)} all-to-all(bf16[16,48,256]{2,1,0:T(8,128)(2,1)S(1)} %get-tuple-element.153), channel_id=1, replica_groups=mesh['z'=4,'x'=2,'core'=2,'y'=2] {'z','x','y'}, dimensions={0} | all-to-all | bytes 786432 | tf_op jit(solution)/shard_map/all_to_all | solution.py:1291
  120.8 3.0 project_out.1
  130.9 15.9 %collective-permute-done.20 = bf16[2,128,1536]{2,1,0:T(8,128)(2,1)S(1)} collective-permute-done((bf16[2,128,1536]{2,1,0:T(8,128)(2,1)S(1)}, bf16[2,128,1536]{2,1,0:T(8,128)(2,1)S(1)}, u32[]{:S(2)}, u32[]{:S(2)}) %collective-permute-start.20) | collective-permute-done | bytes 786464 | tf_op jit(solution)/shard_map/ppermute | solution.py:1251
  147.0 9.4 %collective-permute-done.17.refs_5_ = bf16[288,2048]{1,0:T(8,128)(2,1)S(1)} collective-permute-done((bf16[288,2048]{1,0:T(8,128)(2,1)S(1)}, bf16[288,2048]{1,0:T(8,128)(2,1)S(1)}, u32[]{:S(2)}, u32[]{:S(2)}) %collective-permute-start.17) | collective-permute-done | bytes 1179680 | tf_op jit(solution)/shard_map/ppermute | solution.py:1175
  160.8 12.8 %collective-permute-done.23 = bf16[144,2048]{1,0:T(8,128)(2,1)S(1)} collective-permute-done((bf16[144,2048]{1,0:T(8,128)(2,1)S(1)}, bf16[144,2048]{1,0:T(8,128)(2,1)S(1)}, u32[]{:S(2)}, u32[]{:S(2)}) %collective-permute-start.23) | collective-permute-done | bytes 589856 | tf_op jit(solution)/shard_map/ppermute | solution.py:1176
  174.7 13.7 %feed_forward.1 = (bf16[512,1536]{1,0:T(8,128)(2,1)}, bf16[512,1536]{1,0:T(8,128)(2,1)}, bf16[512,1024]{1,0:T(8,128)(2,1)S(1)}, bf16[512,2048]{1,0:T(8,128)(2,1)...) custom-call(s32[18]{0:T(128)S(1)} %pad_add_fusion.at_ref, ...), custom_call_target="tpu_custom_call" | custom-call | flops 8053063680 | bytes 21233736 | tf_op jit(solution)/shard_map/feed_forward/pallas_call | solution.py:475
  198.5 5.7 %feed_forward_grads.1 = bf16[8,288,2048]{2,1,0:T(8,128)(2,1)S(1)} custom-call(s32[18]{0:T(128)S(1)} %pad_add_fusion.at_ref, bf16[512,1536]{1,0:T(8,128)(2,1)S(1)} %copy-done.38, bf16[512,2048]{1,0:T(8,128)(2,1)S(1)} %copy-done.29, bf16[512,1024]{1,0:T(8,128)(2,1)S(1)} %get-tuple-element.184.hidden_ref, bf16[512,1536]{1,0:T(8,128)(2,1)S(1)} %copy-done.40), custom_call_target="tpu_custom_call" | custom-call | flops 4831838208 | bytes 15728712 | tf_op jit(solution)/shard_map/feed_forward_grads/pallas_call | solution.py:475
  204.2 7.7 %collective-permute-done.27 = bf16[144,2048]{1,0:T(8,128)(2,1)S(1)} collective-permute-done((bf16[144,2048]{1,0:T(8,128)(2,1)S(1)}, bf16[144,2048]{1,0:T(8,128)(2,1)S(1)}, u32[]{:S(2)}, u32[]{:S(2)}) %collective-permute-start.27) | collective-permute-done | bytes 589856 | tf_op jit(solution)/shard_map/ppermute | solution.py:1201
  222.1 7.3 %all-to-all-start.3 = ((bf16[16,48,256]{2,1,0:T(8,128)(2,1)}), bf16[16,48,256]{2,1,0:T(8,128)(2,1)}, u32[]{:S(2)}, u32[]{:S(2)}) async-start(bf16[16,48,256]{2,1,0:T(8,128)(2,1)} %copy-done.62), calls=%async_computation.3 | async-start | bytes 786432 | tf_op jit(solution)/shard_map/all_to_all | solution.py:1291
  240.8 3.8 layer_output.1
  245.8 2.8 joined_grads.1
  249.7 6.3 %all-to-all-done.3.back_ref = bf16[16,48,256]{2,1,0:T(8,128)(2,1)} async-done(((bf16[16,48,256]{2,1,0:T(8,128)(2,1)}), bf16[16,48,256]{2,1,0:T(8,128)(2,1)}, u32[]{:S(2)}, u32[]{:S(2)}) %all-to-all-start.3) | async-done | bytes 393248 | tf_op jit(solution)/shard_map/all_to_all | solution.py:1291
  256.0 2.7 bitcast_add_fusion
  266.2 8.1 %heads_backward.1 = (f32[288,2048]{1,0:T(8,128)S(1)}, bf16[288,2048]{1,0:T(8,128)(2,1)}) custom-call(s32[18]{0:T(128)S(1)} %pad_add_fusion.at_ref, bf16[96,2048]{1,0:T(8,128)(2,1)S(1)} %copy-done.56, bf16[96,2048]{1,0:T(8,128)(2,1)S(1)} %copy-done.58, bf16[96,2048]{1,0:T(8,128)(2,1)S(1)} %copy-done.60, bf16[9216,256]{1,0:T(8,128)(2,1)S(1)} %copy-done.7, ...), custom_call_target="tpu_custom_call" | custom-call | flops 1811939328 | bytes 11403336 | tf_op jit(solution)/shard_map/heads_backward/pallas_call | solution.py:475
  274.2 13.1 %collective-permute-done.35 = bf16[24,1536]{1,0:T(8,128)(2,1)S(1)} collective-permute-done((bf16[24,1536]{1,0:T(8,128)(2,1)S(1)}, bf16[24,1536]{1,0:T(8,128)(2,1)S(1)}, u32[]{:S(2)}, u32[]{:S(2)}) %collective-permute-start.35) | collective-permute-done | bytes 73760 | tf_op jit(solution)/shard_map/ppermute | solution.py:1201
  287.6 3.3 bitcast_add_fusion.4
  299.8 6.5 %heads_grad.1 = bf16[768,384]{1,0:T(8,128)(2,1)S(1)} custom-call(s32[18]{0:T(128)S(1)} %pad_add_fusion.at_ref, bf16[384,2048]{1,0:T(8,128)(2,1)S(1)} %heads_join.1.joined_ref, bf16[352,768]{1,0:T(8,128)(2,1)S(1)} %pad_maximum_fusion.4.refs_0_, bf16[352,768]{1,0:T(8,128)(2,1)S(1)} %collective-permute-done.2.refs_1_, ...), custom_call_target="tpu_custom_call" | custom-call | flops 1207959552 | bytes 6488136 | tf_op jit(solution)/shard_map/heads_grad/pallas_call | solution.py:475
  314.9 3.0 collective-permute-done.44
  322.8 7.7 %collective-permute-done.37 = bf16[144,2048]{1,0:T(8,128)(2,1)S(1)} collective-permute-done((bf16[144,2048]{1,0:T(8,128)(2,1)S(1)}, bf16[144,2048]{1,0:T(8,128)(2,1)S(1)}, u32[]{:S(2)}, u32[]{:S(2)}) %collective-permute-start.37) | collective-permute-done | bytes 589856 | tf_op jit(solution)/shard_map/ppermute | solution.py:1231
  335.4 5.3 %collective-permute-done.47 = bf16[256,768]{1,0:T(8,128)(2,1)S(1)} collective-permute-done((bf16[256,768]{1,0:T(8,128)(2,1)S(1)}, bf16[256,768]{1,0:T(8,128)(2,1)S(1)}, u32[]{:S(2)}, u32[]{:S(2)}) %collective-permute-start.47) | collective-permute-done | bytes 393248 | tf_op jit(solution)/shard_map/ppermute | solution.py:1201
  343.1 2.8 fusion.29
  349.7 5.2 %all-to-all-start.4 = ((bf16[16,48,384]{2,1,0:T(8,128)(2,1)}), bf16[16,48,384]{2,1,0:T(8,128)(2,1)}, u32[]{:S(2)}, u32[]{:S(2)}) async-start(bf16[16,48,384]{2,1,0:T(8,128)(2,1)} %bitcast.129), calls=%async_computation.4 | async-start | bytes 1179648 | tf_op jit(solution)/shard_map/all_to_all | solution.py:1291
  375.3 3.7 collective-permute-done.56
  389.1 2.6 input_rows.1
  (357 shorter events, 159.2 us)
Async XLA Ops:
  4.0 16.1 %collective-permute-start.2 = (bf16[352,768]{1,0:T(8,128)(2,1)S(1)}, bf16[352,768]{1,0:T(8,128)(2,1)S(1)}, u32[]{:S(2)}, u32[]{:S(2)}) collective-permute-start(bf16[352,768]{1,0:T(8,128)(2,1)S(1)} %pad_maximum_fusion.4.refs_0_), channel_id=1, source_target_pairs={{8,0},{16,8},{24,16},{28,24},{20,28},{12,20},{4,12},{0,4},{9,1},{1... | collective-permute-start | bytes 1622024 | tf_op jit(solution)/shard_map/ppermute | solution.py:1176
  5.6 15.6 %collective-permute-start.1 = (bf16[352,768]{1,0:T(8,128)(2,1)S(1)}, bf16[352,768]{1,0:T(8,128)(2,1)S(1)}, u32[]{:S(2)}, u32[]{:S(2)}) collective-permute-start(bf16[352,768]{1,0:T(8,128)(2,1)S(1)} %pad_maximum_fusion.4.refs_0_), channel_id=1, source_target_pairs={{0,8},{8,16},{16,24},{24,28},{28,20},{20,12},{12,4},{4,0},{1,9},{9... | collective-permute-start | bytes 1622024 | tf_op jit(solution)/shard_map/ppermute | solution.py:1175
  9.2 17.3 %all-to-all-start = ((bf16[8,48,384]{2,1,0:T(8,128)(2,1)}), bf16[8,48,384]{2,1,0:T(8,128)(2,1)S(1)}, u32[]{:S(2)}, u32[]{:S(2)}) async-start(bf16[8,48,384]{2,1,0:T(8,128)(2,1)} %head_columns.1), calls=%async_computation | async-start | bytes 589824 | tf_op jit(solution)/shard_map/all_to_all | solution.py:1291
  21.2 16.4 %collective-permute-start.3 = (bf16[352,768]{1,0:T(8,128)(2,1)S(1)}, bf16[352,768]{1,0:T(8,128)(2,1)S(1)}, u32[]{:S(2)}, u32[]{:S(2)}) collective-permute-start(bf16[352,768]{1,0:T(8,128)(2,1)S(1)} %collective-permute-done.1.refs_7_), channel_id=1, source_target_pairs={{0,8},{8,16},{16,24},{24,28},{28,20},{20,12},{12,4},{4,0},{1,9},{9... | collective-permute-start | bytes 1622024 | tf_op jit(solution)/shard_map/ppermute | solution.py:1175
  21.3 16.3 %collective-permute-start.4 = (bf16[352,768]{1,0:T(8,128)(2,1)S(1)}, bf16[352,768]{1,0:T(8,128)(2,1)}, u32[]{:S(2)}, u32[]{:S(2)}) collective-permute-start(bf16[352,768]{1,0:T(8,128)(2,1)S(1)} %collective-permute-done.2.refs_1_), channel_id=1, source_target_pairs={{8,0},{16,8},{24,16},{28,24},{20,28},{12,20},{4,12},{0,4},{9,1},{1... | collective-permute-start | bytes 1622024 | tf_op jit(solution)/shard_map/ppermute | solution.py:1176
  26.5 15.9 %all-to-all-start.1 = ((bf16[4,48,2048]{2,1,0:T(8,128)(2,1)}), bf16[4,48,2048]{2,1,0:T(8,128)(2,1)}, u32[]{:S(2)}, u32[]{:S(2)}) async-start(bf16[4,48,2048]{2,1,0:T(8,128)(2,1)} %pair_columns.1), calls=%async_computation.1 | async-start | bytes 1572864 | tf_op jit(solution)/shard_map/all_to_all | solution.py:1291
  59.3 24.7 %collective-permute-start.11 = (bf16[288,2048]{1,0:T(8,128)(2,1)S(1)}, bf16[288,2048]{1,0:T(8,128)(2,1)S(1)}, u32[]{:S(2)}, u32[]{:S(2)}) collective-permute-start(bf16[288,2048]{1,0:T(8,128)(2,1)S(1)} %pack_down.1.refs_0_), channel_id=1, source_target_pairs={{8,0},{16,8},{24,16},{28,24},{20,28},{12,20},{4,12},{0,4},{9,1},{1... | collective-permute-start | bytes 3538952 | tf_op jit(solution)/shard_map/ppermute | solution.py:1176
  59.9 25.1 %collective-permute-start.10 = (bf16[288,2048]{1,0:T(8,128)(2,1)S(1)}, bf16[288,2048]{1,0:T(8,128)(2,1)S(1)}, u32[]{:S(2)}, u32[]{:S(2)}) collective-permute-start(bf16[288,2048]{1,0:T(8,128)(2,1)S(1)} %pack_down.1.refs_0_), channel_id=1, source_target_pairs={{0,8},{8,16},{16,24},{24,28},{28,20},{20,12},{12,4},{4,0},{1,9},{9... | collective-permute-start | bytes 3538952 | tf_op jit(solution)/shard_map/ppermute | solution.py:1175
  85.0 35.7 %collective-permute-start.15 = (bf16[288,2048]{1,0:T(8,128)(2,1)S(1)}, bf16[288,2048]{1,0:T(8,128)(2,1)S(1)}, u32[]{:S(2)}, u32[]{:S(2)}) collective-permute-start(bf16[288,2048]{1,0:T(8,128)(2,1)S(1)} %collective-permute-done.10.refs_7_), channel_id=1, source_target_pairs={{0,8},{8,16},{16,24},{24,28},{28,20},{20,12},{12,4},{4,0},{1,9},{9... | collective-permute-start | bytes 3538952 | tf_op jit(solution)/shard_map/ppermute | solution.py:1175
  86.2 34.5 %collective-permute-start.16 = (bf16[288,2048]{1,0:T(8,128)(2,1)S(1)}, bf16[288,2048]{1,0:T(8,128)(2,1)S(1)}, u32[]{:S(2)}, u32[]{:S(2)}) collective-permute-start(bf16[288,2048]{1,0:T(8,128)(2,1)S(1)} %collective-permute-done.11.refs_1_), channel_id=1, source_target_pairs={{8,0},{16,8},{24,16},{28,24},{20,28},{12,20},{4,12},{0,4},{9,1},{1... | collective-permute-start | bytes 3538952 | tf_op jit(solution)/shard_map/ppermute | solution.py:1176
  127.1 19.6 %collective-permute-start.20 = (bf16[2,128,1536]{2,1,0:T(8,128)(2,1)S(1)}, bf16[2,128,1536]{2,1,0:T(8,128)(2,1)S(1)}, u32[]{:S(2)}, u32[]{:S(2)}) collective-permute-start(bf16[2,128,1536]{2,1,0:T(8,128)(2,1)S(1)} %fusion.5), channel_id=1, source_target_pairs={{0,1},{1,0},{2,3},{3,2},{4,5},{5,4},{6,7},{7,6},{8,9},{9,8},{10,11... | collective-permute-start | bytes 2359304 | tf_op jit(solution)/shard_map/ppermute | solution.py:1251
  128.7 27.7 %collective-permute-start.17 = (bf16[288,2048]{1,0:T(8,128)(2,1)S(1)}, bf16[288,2048]{1,0:T(8,128)(2,1)S(1)}, u32[]{:S(2)}, u32[]{:S(2)}) collective-permute-start(bf16[288,2048]{1,0:T(8,128)(2,1)S(1)} %collective-permute-done.15.refs_6_), channel_id=1, source_target_pairs={{0,8},{8,16},{16,24},{24,28},{28,20},{20,12},{12,4},{4,0},{1,9},{9... | collective-permute-start | bytes 3538952 | tf_op jit(solution)/shard_map/ppermute | solution.py:1175
  129.6 27.6 %collective-permute-start.18 = (bf16[288,2048]{1,0:T(8,128)(2,1)S(1)}, bf16[288,2048]{1,0:T(8,128)(2,1)S(1)}, u32[]{:S(2)}, u32[]{:S(2)}) collective-permute-start(bf16[288,2048]{1,0:T(8,128)(2,1)S(1)} %collective-permute-done.16.refs_2_), channel_id=1, source_target_pairs={{8,0},{16,8},{24,16},{28,24},{20,28},{12,20},{4,12},{0,4},{9,1},{1... | collective-permute-start | bytes 3538952 | tf_op jit(solution)/shard_map/ppermute | solution.py:1176
  130.9 16.2 %collective-permute-start.21 = (bf16[2,128,1536]{2,1,0:T(8,128)(2,1)S(1)}, bf16[2,128,1536]{2,1,0:T(8,128)(2,1)S(1)}, u32[]{:S(2)}, u32[]{:S(2)}) collective-permute-start(bf16[2,128,1536]{2,1,0:T(8,128)(2,1)S(1)} %pad_maximum_fusion.2.d_own_ref), channel_id=1, source_target_pairs={{0,2},{2,0},{1,3},{3,1},{4,6},{6,4},{5,7},{7,5},{8,10},{10,8},{9,1... | collective-permute-start | bytes 2359304 | tf_op jit(solution)/shard_map/ppermute | solution.py:1251
  157.7 16.8 %collective-permute-start.24 = (bf16[2,128,1536]{2,1,0:T(8,128)(2,1)S(1)}, bf16[2,128,1536]{2,1,0:T(8,128)(2,1)S(1)}, u32[]{:S(2)}, u32[]{:S(2)}) collective-permute-start(bf16[2,128,1536]{2,1,0:T(8,128)(2,1)S(1)} %multiply_convert_fusion.own_ref), channel_id=1, source_target_pairs={{0,2},{2,0},{1,3},{3,1},{4,6},{6,4},{5,7},{7,5},{8,10},{10,8},{9,1... | collective-permute-start | bytes 2359304 | tf_op jit(solution)/shard_map/ppermute | solution.py:1251
  192.6 19.9 %collective-permute-start.30 = (bf16[2,128,1536]{2,1,0:T(8,128)(2,1)S(1)}, bf16[2,128,1536]{2,1,0:T(8,128)(2,1)S(1)}, u32[]{:S(2)}, u32[]{:S(2)}) collective-permute-start(bf16[2,128,1536]{2,1,0:T(8,128)(2,1)S(1)} %get-tuple-element.255), channel_id=1, source_target_pairs={{0,1},{1,0},{2,3},{3,2},{4,5},{5,4},{6,7},{7,6},{8,9},{9,8},{10,11... | collective-permute-start | bytes 2359304 | tf_op jit(solution)/shard_map/ppermute | solution.py:1251
  196.5 15.4 %collective-permute-start.27 = (bf16[144,2048]{1,0:T(8,128)(2,1)S(1)}, bf16[144,2048]{1,0:T(8,128)(2,1)S(1)}, u32[]{:S(2)}, u32[]{:S(2)}) collective-permute-start(bf16[144,2048]{1,0:T(8,128)(2,1)S(1)} %get-tuple-element.286), channel_id=1, source_target_pairs={{8,0},{16,8},{24,16},{28,24},{20,28},{12,20},{4,12},{0,4},{9,1},{1... | collective-permute-start | bytes 1769480 | tf_op jit(solution)/shard_map/ppermute | solution.py:1201
  197.5 15.1 %collective-permute-start.26 = (bf16[144,2048]{1,0:T(8,128)(2,1)S(1)}, bf16[144,2048]{1,0:T(8,128)(2,1)S(1)}, u32[]{:S(2)}, u32[]{:S(2)}) collective-permute-start(bf16[144,2048]{1,0:T(8,128)(2,1)S(1)} %get-tuple-element.287), channel_id=1, source_target_pairs={{0,8},{8,16},{16,24},{24,28},{28,20},{20,12},{12,4},{4,0},{1,9},{9... | collective-permute-start | bytes 1769480 | tf_op jit(solution)/shard_map/ppermute | solution.py:1200
  216.8 32.9 %collective-permute-start.29 = (bf16[288,2048]{1,0:T(8,128)(2,1)}, bf16[288,2048]{1,0:T(8,128)(2,1)}, u32[]{:S(2)}, u32[]{:S(2)}) collective-permute-start(bf16[288,2048]{1,0:T(8,128)(2,1)} %get-tuple-element.268), channel_id=1, source_target_pairs={{8,0},{16,8},{24,16},{28,24},{20,28},{12,20},{4,12},{0,4},{9,1},{1... | collective-permute-start | bytes 3538952 | tf_op jit(solution)/shard_map/ppermute | solution.py:1201
  218.5 31.2 %collective-permute-start.28 = (bf16[288,2048]{1,0:T(8,128)(2,1)}, bf16[288,2048]{1,0:T(8,128)(2,1)}, u32[]{:S(2)}, u32[]{:S(2)}) collective-permute-start(bf16[288,2048]{1,0:T(8,128)(2,1)} %get-tuple-element.269), channel_id=1, source_target_pairs={{0,8},{8,16},{16,24},{24,28},{28,20},{20,12},{12,4},{4,0},{1,9},{9... | collective-permute-start | bytes 3538952 | tf_op jit(solution)/shard_map/ppermute | solution.py:1200
  222.1 33.8 %all-to-all-start.3 = ((bf16[16,48,256]{2,1,0:T(8,128)(2,1)}), bf16[16,48,256]{2,1,0:T(8,128)(2,1)}, u32[]{:S(2)}, u32[]{:S(2)}) async-start(bf16[16,48,256]{2,1,0:T(8,128)(2,1)} %copy-done.62), calls=%async_computation.3 | async-start | bytes 786432 | tf_op jit(solution)/shard_map/all_to_all | solution.py:1291
  258.7 28.9 %collective-permute-start.33 = (bf16[288,2048]{1,0:T(8,128)(2,1)S(1)}, bf16[288,2048]{1,0:T(8,128)(2,1)S(1)}, u32[]{:S(2)}, u32[]{:S(2)}) collective-permute-start(bf16[288,2048]{1,0:T(8,128)(2,1)S(1)} %get-tuple-element.266), channel_id=1, source_target_pairs={{8,0},{16,8},{24,16},{28,24},{20,28},{12,20},{4,12},{0,4},{9,1},{1... | collective-permute-start | bytes 3538952 | tf_op jit(solution)/shard_map/ppermute | solution.py:1201
  259.0 28.6 %collective-permute-start.32 = (bf16[288,2048]{1,0:T(8,128)(2,1)S(1)}, bf16[288,2048]{1,0:T(8,128)(2,1)S(1)}, u32[]{:S(2)}, u32[]{:S(2)}) collective-permute-start(bf16[288,2048]{1,0:T(8,128)(2,1)S(1)} %get-tuple-element.267), channel_id=1, source_target_pairs={{0,8},{8,16},{16,24},{24,28},{28,20},{20,12},{12,4},{4,0},{1,9},{9... | collective-permute-start | bytes 3538952 | tf_op jit(solution)/shard_map/ppermute | solution.py:1200
  261.7 25.6 %collective-permute-start.35 = (bf16[24,1536]{1,0:T(8,128)(2,1)S(1)}, bf16[24,1536]{1,0:T(8,128)(2,1)S(1)}, u32[]{:S(2)}, u32[]{:S(2)}) collective-permute-start(bf16[24,1536]{1,0:T(8,128)(2,1)S(1)} %get-tuple-element.284), channel_id=1, source_target_pairs={{8,0},{16,8},{24,16},{28,24},{20,28},{12,20},{4,12},{0,4},{9,1},{1... | collective-permute-start | bytes 221192 | tf_op jit(solution)/shard_map/ppermute | solution.py:1201
  262.0 25.6 %collective-permute-start.34 = (bf16[24,1536]{1,0:T(8,128)(2,1)S(1)}, bf16[24,1536]{1,0:T(8,128)(2,1)S(1)}, u32[]{:S(2)}, u32[]{:S(2)}) collective-permute-start(bf16[24,1536]{1,0:T(8,128)(2,1)S(1)} %get-tuple-element.285), channel_id=1, source_target_pairs={{0,8},{8,16},{16,24},{24,28},{28,20},{20,12},{12,4},{4,0},{1,9},{9... | collective-permute-start | bytes 221192 | tf_op jit(solution)/shard_map/ppermute | solution.py:1200
  290.9 23.2 %collective-permute-start.40 = (bf16[144,2048]{1,0:T(8,128)(2,1)}, bf16[144,2048]{1,0:T(8,128)(2,1)S(1)}, u32[]{:S(2)}, u32[]{:S(2)}) collective-permute-start(bf16[144,2048]{1,0:T(8,128)(2,1)} %get-tuple-element.259), channel_id=1, source_target_pairs={{8,0},{16,8},{24,16},{28,24},{20,28},{12,20},{4,12},{0,4},{9,1},{1... | collective-permute-start | bytes 1769480 | tf_op jit(solution)/shard_map/ppermute | solution.py:1231
  292.7 22.2 %collective-permute-start.39 = (bf16[144,2048]{1,0:T(8,128)(2,1)}, bf16[144,2048]{1,0:T(8,128)(2,1)S(1)}, u32[]{:S(2)}, u32[]{:S(2)}) collective-permute-start(bf16[144,2048]{1,0:T(8,128)(2,1)} %get-tuple-element.265), channel_id=1, source_target_pairs={{0,8},{8,16},{16,24},{24,28},{28,20},{20,12},{12,4},{4,0},{1,9},{9... | collective-permute-start | bytes 1769480 | tf_op jit(solution)/shard_map/ppermute | solution.py:1230
  312.8 17.6 %collective-permute-start.37 = (bf16[144,2048]{1,0:T(8,128)(2,1)S(1)}, bf16[144,2048]{1,0:T(8,128)(2,1)S(1)}, u32[]{:S(2)}, u32[]{:S(2)}) collective-permute-start(bf16[144,2048]{1,0:T(8,128)(2,1)S(1)} %copy-done.82), channel_id=1, source_target_pairs={{8,0},{16,8},{24,16},{28,24},{20,28},{12,20},{4,12},{0,4},{9,1},{1... | collective-permute-start | bytes 1769480 | tf_op jit(solution)/shard_map/ppermute | solution.py:1231
  314.1 19.4 %collective-permute-start.36 = (bf16[144,2048]{1,0:T(8,128)(2,1)S(1)}, bf16[144,2048]{1,0:T(8,128)(2,1)S(1)}, u32[]{:S(2)}, u32[]{:S(2)}) collective-permute-start(bf16[144,2048]{1,0:T(8,128)(2,1)S(1)} %copy-done.81), channel_id=1, source_target_pairs={{0,8},{8,16},{16,24},{24,28},{28,20},{20,12},{12,4},{4,0},{1,9},{9... | collective-permute-start | bytes 1769480 | tf_op jit(solution)/shard_map/ppermute | solution.py:1230
  348.1 15.5 %collective-permute-start.51 = (bf16[256,768]{1,0:T(8,128)(2,1)}, bf16[256,768]{1,0:T(8,128)(2,1)}, u32[]{:S(2)}, u32[]{:S(2)}) collective-permute-start(bf16[256,768]{1,0:T(8,128)(2,1)} %get-tuple-element.273), channel_id=1, source_target_pairs={{0,8},{8,16},{16,24},{24,28},{28,20},{20,12},{12,4},{4,0},{1,9},{9... | collective-permute-start | bytes 1179656 | tf_op jit(solution)/shard_map/ppermute | solution.py:1200
  349.7 25.6 %all-to-all-start.4 = ((bf16[16,48,384]{2,1,0:T(8,128)(2,1)}), bf16[16,48,384]{2,1,0:T(8,128)(2,1)}, u32[]{:S(2)}, u32[]{:S(2)}) async-start(bf16[16,48,384]{2,1,0:T(8,128)(2,1)} %bitcast.129), calls=%async_computation.4 | async-start | bytes 1179648 | tf_op jit(solution)/shard_map/all_to_all | solution.py:1291
  365.8 15.5 %collective-permute-start.55 = (bf16[256,768]{1,0:T(8,128)(2,1)}, bf16[256,768]{1,0:T(8,128)(2,1)}, u32[]{:S(2)}, u32[]{:S(2)}) collective-permute-start(bf16[256,768]{1,0:T(8,128)(2,1)} %get-tuple-element.271), channel_id=1, source_target_pairs={{0,8},{8,16},{16,24},{24,28},{28,20},{20,12},{12,4},{4,0},{1,9},{9... | collective-permute-start | bytes 1179656 | tf_op jit(solution)/shard_map/ppermute | solution.py:1230
  (123 other events, 1344.4 us)
